TPU v7x, 32 devices: a whole 2x2x4 slice. The times are simulated.
32 devices in a mesh: seq: 4 (over y, x), chan: 8 (over z, core).
Axes of the slice: x: 2, y: 2, z: 4, core: 2. Of those that a mesh axis runs over, the one named last changes fastest.
Arguments:
- tokens: bfloat16 [16, 2048, 1024], P(None, 'seq', 'chan'), may hold values from -6 to 6
- cotangent: bfloat16 [16, 2048, 1024], P(None, 'seq', 'chan'), may hold values from -6 to 6
- doc_starts: int32 [16, 8], P('chan'), may hold values from 0 to 2048, as said below
- lengths: int32 [16], P('chan'), may hold values from 1024 to 2048, as said below
- norm1_gain: float32 [1024], replicated, may hold values from 0.5 to 1.5
- recur_input: bfloat16 [1024, 1536], replicated, may hold values from -0.1875 to 0.1875
- recur_gate: bfloat16 [1024, 1536], replicated, may hold values from -0.1875 to 0.1875
- conv_kernel: float32 [4, 1536], replicated, may hold values from -3 to 3
- conv_bias: float32 [1536], replicated, may hold values from -3 to 3
- lru_gates: bfloat16 [1536, 192], replicated, may hold values from -0.625 to 0.625
- lru_bias: float32 [2, 1536], replicated, may hold values from -4 to 4
- lru_decay: float32 [1536], replicated, may hold values from 3 to 9
- recur_out: bfloat16 [1536, 1024], replicated, may hold values from -0.21875 to 0.21875
- norm2_gain: float32 [1024], replicated, may hold values from 0.5 to 1.5
- mlp_gate: bfloat16 [1024, 3072], replicated, may hold values from -0.1875 to 0.1875
- mlp_up: bfloat16 [1024, 3072], replicated, may hold values from -0.1875 to 0.1875
- mlp_down: bfloat16 [3072, 1024], replicated, may hold values from -0.15625 to 0.15625
Outputs:
- output: bfloat16 [16, 2048, 1024], P(None, 'seq', 'chan')
- grad_tokens: bfloat16 [16, 2048, 1024], P(None, 'seq', 'chan')
- grad_norm1_gain: float32 [1024], P(('seq', 'chan'))
- grad_recur_input: float32 [1024, 1536], P(('seq', 'chan'))
- grad_recur_gate: float32 [1024, 1536], P(('seq', 'chan'))
- grad_conv_kernel: float32 [4, 1536], P(None, ('seq', 'chan'))
- grad_conv_bias: float32 [1536], P(('seq', 'chan'))
- grad_lru_gates: float32 [1536, 192], P(('seq', 'chan'))
- grad_lru_bias: float32 [2, 1536], P(None, ('seq', 'chan'))
- grad_lru_decay: float32 [1536], P(('seq', 'chan'))
- grad_recur_out: float32 [1536, 1024], P(('seq', 'chan'))
- grad_norm2_gain: float32 [1024], P(('seq', 'chan'))
- grad_mlp_gate: float32 [1024, 3072], P(('seq', 'chan'))
- grad_mlp_up: float32 [1024, 3072], P(('seq', 'chan'))
- grad_mlp_down: float32 [3072, 1024], P(('seq', 'chan'))
Inputs may be any that keep to these rules, and one draw needn't show every extreme that they name: `doc_starts`: each row's list ascends from 0; unused slots hold 2048. `lengths`: some row has length 2048.
All inputs are finite; a program needn't handle non-finite values.
Results may differ from a plain program's by a relative error of at most 0.0095.
Values may be sent and summed in bfloat16 or wider, within the bound.
A program may use at most 320 MiB of HBM per device.

v0:
```python
import jax
import jax.numpy as jnp
from jax import lax
from jax.sharding import PartitionSpec as P

H = 16


EPS = 1e-06
ROOT_FLOOR = 1e-06
LANES = 128


def prefix(value, axis, join, neutral, backward):
    count, mine = (lax.axis_size(axis), lax.axis_index(axis))
    pieces = jax.tree.map(lambda part: lax.all_gather(part, axis), value)
    if backward:
        pieces = jax.tree.map(lambda part: part[::-1], pieces)
        mine = count - 1 - mine
    subtotal = jax.tree.map(
        lambda part, zero: jnp.full_like(part, 0) + jnp.asarray(zero, part.dtype), value, neutral
    )

    def hop(position, subtotal):
        longer = join(subtotal, jax.tree.map(lambda part: part[position], pieces))
        return jax.tree.map(lambda new, old: jnp.where(position < mine, new, old), longer, subtotal)

    return lax.fori_loop(0, count - 1, hop, subtotal)


def passed_along(value, axis, steps):
    count = lax.axis_size(axis)
    leading, last = (max(0, -steps), min(count, count - steps))
    return lax.ppermute(value, axis, [(source, source + steps) for source in range(leading, last)])


def as_sent(x):
    return jax.tree.map(lambda a: a.astype(jnp.bfloat16) if a.dtype == jnp.float32 else a, x)


def trans_dot(left, right):
    return lax.dot_general(
        left, right, (((0,), (0,)), ((), ())), preferred_element_type=jnp.float32
    )


def back_dot(left, right):
    return lax.dot_general(
        left, right, (((1,), (1,)), ((), ())), preferred_element_type=jnp.float32
    )


def fwd_dot(left, right):
    return jnp.dot(left, right, preferred_element_type=jnp.float32)


def gelu_fn(value):
    return jax.nn.gelu(value, approximate=True)


def pair_join(earlier, later):
    return (earlier[0] * later[0], later[0] * earlier[1] + later[1])


def local_scan(factors, values):
    return lax.associative_scan(pair_join, (factors, values), axis=1)


def norm_back(grad_norm, normed, inverse, gain):
    scaled = grad_norm * gain
    mean_term = jnp.mean(scaled * normed, axis=1, keepdims=True)
    return (inverse * (scaled - normed * mean_term), jnp.sum(grad_norm * normed, axis=0))


def lane_rows(matrix):
    return matrix.reshape(-1, LANES)


def carry_forward(summary):
    identity = (jnp.ones_like(summary[0]), jnp.zeros_like(summary[1]))
    return prefix(summary, "seq", pair_join, identity, False)[1]


def carry_backward(summary):
    identity = (jnp.ones_like(summary[0]), jnp.zeros_like(summary[1]))
    return prefix(summary, "seq", pair_join, identity, True)[1]


def body(
    tokens,
    cotangent,
    doc_starts,
    lengths,
    norm1_gain,
    recur_input,
    recur_gate,
    conv_kernel,
    conv_bias,
    lru_gates,
    lru_bias,
    lru_decay,
    recur_out,
    norm2_gain,
    mlp_gate,
    mlp_up,
    mlp_down,
):
    seq_x, seq_g = (
        lax.all_to_all(tokens, "chan", split_axis=0, concat_axis=2, tiled=True),
        lax.all_to_all(cotangent, "chan", split_axis=0, concat_axis=2, tiled=True),
    )
    row_count, block_len, model_dim = seq_x.shape
    tok_count = row_count * block_len
    rec_width = recur_input.shape[1]
    ffn_width = mlp_gate.shape[1]
    head_count = H
    head_size = rec_width // head_count
    tap_count = conv_kernel.shape[0]
    rim_size = tap_count - 1
    seq_index = lax.axis_index("seq")
    position = seq_index * block_len + jnp.arange(block_len, dtype=jnp.int32)
    bounds = jnp.concatenate([doc_starts, lengths[:, None]], axis=1)
    is_before = bounds[:, None, :] <= position[None, :, None]
    seg_start = jnp.max(jnp.where(is_before, bounds[:, None, :], 0), axis=2)
    at_start = (seg_start == position[None, :])[:, :, None]
    is_valid = (position[None, :] < lengths[:, None]).reshape(tok_count, 1)
    flat_x = seq_x.reshape(tok_count, model_dim).astype(jnp.float32)
    inv_one = lax.rsqrt(jnp.mean(flat_x * flat_x, axis=1, keepdims=True) + EPS)
    normed_one = flat_x * inv_one
    normed_low = (normed_one * norm1_gain).astype(jnp.bfloat16)
    branch_pre = fwd_dot(normed_low, recur_input)
    gate_pre = fwd_dot(normed_low, recur_gate)
    gate_act = gelu_fn(gate_pre)
    branch_rows = branch_pre.reshape(row_count, block_len, rec_width)
    prev_rim = passed_along(
        branch_rows[:, block_len - rim_size :, :].astype(jnp.bfloat16), "seq", 1
    ).astype(jnp.float32)
    extended = jnp.concatenate([prev_rim, branch_rows], axis=1)
    conv_sum = jnp.zeros_like(branch_rows) + conv_bias
    tap_masks = []
    for offset in range(tap_count):
        tap_keep = (position[None, :] - offset >= seg_start)[:, :, None]
        tap_masks.append(tap_keep)
        window = extended[:, rim_size - offset : rim_size - offset + block_len, :]
        conv_sum = conv_sum + conv_kernel[offset] * jnp.where(tap_keep, window, 0.0)
    lru_in = conv_sum.astype(jnp.bfloat16)
    lru_heads = lru_in.reshape(tok_count, head_count, head_size)
    gate_blocks = lru_gates.reshape(head_count, head_size, 2 * head_size)
    gate_both = jnp.einsum(
        "thi,hij->thj", lru_heads, gate_blocks, preferred_element_type=jnp.float32
    )
    rate_pre = gate_both[:, :, :head_size].reshape(tok_count, rec_width) + lru_bias[0]
    input_pre = gate_both[:, :, head_size:].reshape(tok_count, rec_width) + lru_bias[1]
    rate_gate = jax.nn.sigmoid(rate_pre)
    input_gate = jax.nn.sigmoid(input_pre)
    soft_decay = jax.nn.softplus(-lru_decay)
    log_decay = -8.0 * rate_gate * soft_decay
    decay_rate = jnp.exp(log_decay)
    root_arg = -jnp.expm1(2.0 * log_decay)
    root_live = root_arg > ROOT_FLOOR
    root_term = jnp.sqrt(jnp.maximum(root_arg, ROOT_FLOOR))
    start_flat = at_start.reshape(tok_count, 1)
    decay_coef = jnp.where(start_flat, 0.0, decay_rate)
    scale_in = jnp.where(start_flat, 1.0, root_term)
    lru_value = lru_in.reshape(tok_count, rec_width).astype(jnp.float32)
    lru_drive = scale_in * input_gate * lru_value
    coef_rows = decay_coef.reshape(row_count, block_len, rec_width)
    drive_rows = lru_drive.reshape(row_count, block_len, rec_width)
    cum_coef, local_state = local_scan(coef_rows, drive_rows)
    carry_in = carry_forward((cum_coef[:, -1, :], local_state[:, -1, :]))
    state_rows = local_state + cum_coef * carry_in[:, None, :]
    state_flat = state_rows.reshape(tok_count, rec_width)
    mixed_low = (state_flat * gate_act).astype(jnp.bfloat16)
    resid_one = flat_x + fwd_dot(mixed_low, recur_out)
    inv_two = lax.rsqrt(jnp.mean(resid_one * resid_one, axis=1, keepdims=True) + EPS)
    normed_two = resid_one * inv_two
    normed_low2 = (normed_two * norm2_gain).astype(jnp.bfloat16)
    mlp_gate_pre = fwd_dot(normed_low2, mlp_gate)
    mlp_up_pre = fwd_dot(normed_low2, mlp_up)
    gelu_gate = gelu_fn(mlp_gate_pre)
    hidden_low = (gelu_gate * mlp_up_pre).astype(jnp.bfloat16)
    result = (resid_one + fwd_dot(hidden_low, mlp_down)).astype(jnp.bfloat16)
    output = lax.all_to_all(
        result.reshape(row_count, block_len, model_dim),
        "chan",
        split_axis=2,
        concat_axis=0,
        tiled=True,
    )
    grad_out = jnp.where(is_valid, seq_g.reshape(tok_count, model_dim).astype(jnp.float32), 0.0)
    grad_low = grad_out.astype(jnp.bfloat16)
    grad_down = trans_dot(hidden_low, grad_low)
    grad_hidden = back_dot(grad_low, mlp_down)
    _, gelu_pull = jax.vjp(gelu_fn, mlp_gate_pre)
    mgate_low = gelu_pull(grad_hidden * mlp_up_pre)[0].astype(jnp.bfloat16)
    mup_low = (grad_hidden * gelu_gate).astype(jnp.bfloat16)
    grad_mgate = trans_dot(normed_low2, mgate_low)
    grad_mup = trans_dot(normed_low2, mup_low)
    grad_norm2 = back_dot(mgate_low, mlp_gate) + back_dot(mup_low, mlp_up)
    resid_part, grad_gain2 = norm_back(grad_norm2, normed_two, inv_two, norm2_gain)
    grad_resid = grad_out + resid_part
    resid_low = grad_resid.astype(jnp.bfloat16)
    grad_rout = trans_dot(mixed_low, resid_low)
    grad_mixed = back_dot(resid_low, recur_out)
    grad_state = grad_mixed * gate_act
    _, act_pull = jax.vjp(gelu_fn, gate_pre)
    gate_low = act_pull(grad_mixed * state_flat)[0].astype(jnp.bfloat16)
    next_coef = jnp.concatenate([coef_rows[:, 1:, :], jnp.ones_like(coef_rows[:, :1, :])], axis=1)
    flip_cum, flip_local = local_scan(
        jnp.flip(next_coef, 1), jnp.flip(grad_state.reshape(row_count, block_len, rec_width), 1)
    )
    back_cum = jnp.flip(flip_cum, 1)
    back_local = jnp.flip(flip_local, 1)
    carry_out = carry_backward((cum_coef[:, -1, :], coef_rows[:, 0, :] * back_local[:, 0, :]))
    adjoint = back_local + back_cum * carry_out[:, None, :]
    prev_state = jnp.concatenate([carry_in[:, None, :], state_rows[:, :-1, :]], axis=1)
    grad_coef = (adjoint * prev_state).reshape(tok_count, rec_width)
    adjoint_flat = adjoint.reshape(tok_count, rec_width)
    grad_scale = adjoint_flat * input_gate * lru_value
    grad_igate = adjoint_flat * scale_in * lru_value
    grad_value = adjoint_flat * scale_in * input_gate
    root_pull = jnp.where(root_live, grad_scale * decay_rate * decay_rate / root_term, 0.0)
    grad_log = jnp.where(start_flat, 0.0, grad_coef * decay_rate - root_pull)
    grad_decay = -jax.nn.sigmoid(-lru_decay) * jnp.sum(grad_log * (-8.0 * rate_gate), axis=0)
    rate_low = (grad_log * (-8.0 * soft_decay) * rate_gate * (1.0 - rate_gate)).astype(jnp.bfloat16)
    input_low = (grad_igate * input_gate * (1.0 - input_gate)).astype(jnp.bfloat16)
    grad_lbias = jnp.stack(
        [
            jnp.sum(rate_low.astype(jnp.float32), axis=0),
            jnp.sum(input_low.astype(jnp.float32), axis=0),
        ]
    )
    pre_heads = jnp.concatenate(
        [
            rate_low.reshape(tok_count, head_count, head_size),
            input_low.reshape(tok_count, head_count, head_size),
        ],
        axis=2,
    )
    grad_lgates = jnp.einsum(
        "thi,thj->hij", lru_heads, pre_heads, preferred_element_type=jnp.float32
    ).reshape(rec_width, 2 * head_size)
    grad_value = grad_value + jnp.einsum(
        "thj,hij->thi", pre_heads, gate_blocks, preferred_element_type=jnp.float32
    ).reshape(tok_count, rec_width)
    grad_conv_rows = grad_value.reshape(row_count, block_len, rec_width)
    grad_cbias = jnp.sum(grad_value, axis=0)
    grad_ext = jnp.zeros_like(extended)
    kernel_grads = []
    for offset in range(tap_count):
        masked = jnp.where(tap_masks[offset], grad_conv_rows, 0.0)
        window = extended[:, rim_size - offset : rim_size - offset + block_len, :]
        kernel_grads.append(jnp.sum(masked * window, axis=(0, 1)))
        grad_ext = grad_ext + jnp.pad(
            conv_kernel[offset] * masked, ((0, 0), (rim_size - offset, offset), (0, 0))
        )
    grad_ckernel = jnp.stack(kernel_grads)
    from_next = passed_along(as_sent(grad_ext[:, :rim_size, :]), "seq", -1)
    grad_branch = grad_ext[:, rim_size:, :] + jnp.pad(
        from_next, ((0, 0), (block_len - rim_size, 0), (0, 0))
    )
    branch_low = grad_branch.reshape(tok_count, rec_width).astype(jnp.bfloat16)
    grad_rin = trans_dot(normed_low, branch_low)
    grad_rgate = trans_dot(normed_low, gate_low)
    grad_norm1 = back_dot(branch_low, recur_input) + back_dot(gate_low, recur_gate)
    input_part, grad_gain1 = norm_back(grad_norm1, normed_one, inv_one, norm1_gain)
    grad_x = (grad_resid + input_part).astype(jnp.bfloat16).reshape(row_count, block_len, model_dim)
    grad_tokens = lax.all_to_all(grad_x, "chan", split_axis=2, concat_axis=0, tiled=True)
    terms = (
        grad_gain1,
        lane_rows(grad_rin),
        lane_rows(grad_rgate),
        grad_ckernel,
        grad_cbias,
        grad_lgates,
        grad_lbias,
        grad_decay,
        lane_rows(grad_rout),
        grad_gain2,
        lane_rows(grad_mgate),
        lane_rows(grad_mup),
        lane_rows(grad_down),
    )
    summed = (
        lax.psum_scatter(terms[0], ("seq", "chan"), scatter_dimension=0, tiled=True),
        lax.psum_scatter(terms[1], ("seq", "chan"), scatter_dimension=0, tiled=True),
        lax.psum_scatter(terms[2], ("seq", "chan"), scatter_dimension=0, tiled=True),
        lax.psum_scatter(terms[3], ("seq", "chan"), scatter_dimension=1, tiled=True),
        lax.psum_scatter(terms[4], ("seq", "chan"), scatter_dimension=0, tiled=True),
        lax.psum_scatter(terms[5], ("seq", "chan"), scatter_dimension=0, tiled=True),
        lax.psum_scatter(terms[6], ("seq", "chan"), scatter_dimension=1, tiled=True),
        lax.psum_scatter(terms[7], ("seq", "chan"), scatter_dimension=0, tiled=True),
        lax.psum_scatter(terms[8], ("seq", "chan"), scatter_dimension=0, tiled=True),
        lax.psum_scatter(terms[9], ("seq", "chan"), scatter_dimension=0, tiled=True),
        lax.psum_scatter(terms[10], ("seq", "chan"), scatter_dimension=0, tiled=True),
        lax.psum_scatter(terms[11], ("seq", "chan"), scatter_dimension=0, tiled=True),
        lax.psum_scatter(terms[12], ("seq", "chan"), scatter_dimension=0, tiled=True),
    )
    (
        sum_gain1,
        sum_rin,
        sum_rgate,
        sum_ckernel,
        sum_cbias,
        sum_lgates,
        sum_lbias,
        sum_decay,
        sum_rout,
        sum_gain2,
        sum_mgate,
        sum_mup,
        sum_down,
    ) = summed
    return (
        output,
        grad_tokens,
        sum_gain1,
        sum_rin.reshape(-1, rec_width),
        sum_rgate.reshape(-1, rec_width),
        sum_ckernel,
        sum_cbias,
        sum_lgates,
        sum_lbias,
        sum_decay,
        sum_rout.reshape(-1, model_dim),
        sum_gain2,
        sum_mgate.reshape(-1, ffn_width),
        sum_mup.reshape(-1, ffn_width),
        sum_down.reshape(-1, model_dim),
    )


def solution(mesh):
    return jax.shard_map(
        body,
        mesh=mesh,
        in_specs=(
            P(None, "seq", "chan"),
            P(None, "seq", "chan"),
            P("chan", None),
            P("chan"),
            P(),
            P(),
            P(),
            P(),
            P(),
            P(),
            P(),
            P(),
            P(),
            P(),
            P(),
            P(),
            P(),
        ),
        out_specs=(
            P(None, "seq", "chan"),
            P(None, "seq", "chan"),
            P(("seq", "chan")),
            P(("seq", "chan"), None),
            P(("seq", "chan"), None),
            P(None, ("seq", "chan")),
            P(("seq", "chan")),
            P(("seq", "chan"), None),
            P(None, ("seq", "chan")),
            P(("seq", "chan")),
            P(("seq", "chan"), None),
            P(("seq", "chan")),
            P(("seq", "chan"), None),
            P(("seq", "chan"), None),
            P(("seq", "chan"), None),
        ),
        check_vma=False,
    )
```

profile of v0, /device:TPU:0, one launch (start us, length us, event | category | flops | bytes accessed | tf_op | source)
XLA Modules:
  0.0 2506.6 jit_solution(3925583040898510700)
XLA Ops:
  7.2 55.8 %all_to_all.54 = bf16[16,512,128]{2,1,0:T(8,128)(2,1)} all-to-all(bf16[16,512,128]{2,1,0:T(8,128)(2,1)} %param.21), channel_id=1, replica_groups=mesh['seq'=4,'chan'=8] {'chan'}, dimensions={0} | all-to-all | bytes 4194304 | tf_op jit(solution)/shard_map/all_to_all | solution.py:109
  102.5 14.1 all-to-all-done.2
  731.9 26.0 %multiply_convert_fusion = (bf16[1024,3072]{1,0:T(8,128)(2,1)}, bf16[1024,3072]{1,0:T(8,128)(2,1)}, bf16[1024,3072]{1,0:T(8,128)(2,1)}) fusion(f32[1024,3072]{1,0:T(8,128)} %fusion.102, f32[1024,3072]{1,0:T(8,128)} %fusion.103, bf16[3072,1024]{1,0:T(8,128)(2,1)} %param.37, f32[128,8,8,128]{3,2,1,0:T(8,128)} %bitcast.166, pred[1024]{0:T(1024)(128)(4,1)S(1)} %copy-done.112), kind=kOutput, calls=%fused_computation.15 | convolution fusion | flops 6525288448 | bytes 54526976 | tf_op jit(solution)/shard_map/dot_general | solution.py:48
  840.3 24.7 slice.717
  865.0 15.8 slice.710
  880.8 24.9 slice.712
  905.8 15.8 slice.714
  1018.6 16.7 slice.708
  1035.4 25.4 %slice.778 = f32[2,255,1536]{2,1,0:T(8,128)} reverse(f32[2,255,1536]{2,1,0:T(8,128)} %slice.777), dimensions={1} | reverse | bytes 6266880 | tf_op jit(solution)/shard_map/slice | solution.py:66
  1167.7 48.7 %rev.15 = f32[2,512,1536]{2,1,0:T(8,128)} reverse(f32[2,512,1536]{2,1,0:T(8,128)} %add.759), dimensions={1} | reverse | bytes 12582912 | tf_op jit(solution)/shard_map/jit(_flip)/rev | solution.py:213
  1254.7 48.8 %rev.16 = f32[2,512,1536]{2,1,0:T(8,128)} reverse(f32[2,512,1536]{2,1,0:T(8,128)} %add.768), dimensions={1} | reverse | bytes 12582912 | tf_op jit(solution)/shard_map/jit(_flip)/rev | solution.py:212
  1303.5 20.5 multiply_reduce_fusion
  1364.8 15.9 fusion.31
  1380.7 15.1 add_reduce_fusion
  1415.5 23.5 multiply_reduce_fusion.3
  1548.5 14.1 reshape.537
  1631.5 42.3 %all-to-all-done.1 = bf16[2,512,1024]{1,0,2:T(2,128)(2,1)} async-done(((bf16[2,512,1024]{1,0,2:T(2,128)(2,1)}), bf16[2,512,1024]{1,0,2:T(2,128)(2,1)}, u32[]{:S(2)}, u32[]{:S(2)}) %all-to-all-start.1) | async-done | bytes 2097184 | tf_op jit(solution)/shard_map/all_to_all | solution.py:183
  1686.2 61.3 %all-reduce.83 = (f32[1024]{0:T(1024)S(1)}, f32[1536]{0:T(1024)S(1)}, f32[1536]{0:T(1024)S(1)}, f32[1024]{0:T(1024)S(1)}) all-reduce(f32[1024]{0:T(1024)S(1)} %get-tuple-element.250, f32[1536]{0:T(1024)S(1)} %reduce_sum.138, f32[1536]{0:T(1024)S(1)} %negate_multiply_fusion, ...), channel_id=5, replica_groups=mesh['seq'=4,'chan'=8] {'seq','chan'}, use_global_device_ids=true, to_apply=%region_10.11.clone | all-reduce | flops 5120 | bytes 40960
  1765.2 29.6 %reduce-scatter.16.cloned.1.call-done = f32[384,128]{1,0:T(8,128)} async-done(((f32[12288,128]{1,0:T(8,128)}), f32[384,128]{1,0:T(8,128)}) %reduce-scatter.16.cloned.1.call-update) | async-done | bytes 196624 | tf_op jit(solution)/shard_map/reduce_scatter | solution.py:287
  1796.4 117.6 %reduce-scatter.14.cloned.1.call-done = f32[384,128]{1,0:T(8,128)} async-done(((f32[12288,128]{1,0:T(8,128)}), f32[384,128]{1,0:T(8,128)}) %reduce-scatter.14.cloned.1.call-update) | async-done | bytes 196624 | tf_op jit(solution)/shard_map/reduce_scatter | solution.py:286
  1915.7 159.8 %reduce-scatter.26.cloned.1.call-done = f32[768,128]{1,0:T(8,128)} async-done(((f32[24576,128]{1,0:T(8,128)}), f32[768,128]{1,0:T(8,128)}) %reduce-scatter.26.cloned.1.call-update) | async-done | bytes 393232 | tf_op jit(solution)/shard_map/reduce_scatter | solution.py:297
  2077.3 158.6 %reduce-scatter.24.cloned.1.call-done = f32[768,128]{1,0:T(8,128)} async-done(((f32[24576,128]{1,0:T(8,128)}), f32[768,128]{1,0:T(8,128)}) %reduce-scatter.24.cloned.1.call-update) | async-done | bytes 393232 | tf_op jit(solution)/shard_map/reduce_scatter | solution.py:296
  2237.8 160.0 %reduce-scatter.22.cloned.1.call-done = f32[768,128]{1,0:T(8,128)} async-done(((f32[24576,128]{1,0:T(8,128)}), f32[768,128]{1,0:T(8,128)}) %reduce-scatter.22.cloned.1.call-update) | async-done | bytes 393232 | tf_op jit(solution)/shard_map/reduce_scatter | solution.py:295
  2399.6 100.2 %reduce-scatter.18.cloned.1.call-done = f32[48,192]{1,0:T(8,128)} async-done(((f32[1536,192]{1,0:T(8,128)}), f32[48,192]{1,0:T(8,128)}) %reduce-scatter.18.cloned.1.call-update) | async-done | bytes 36880 | tf_op jit(solution)/shard_map/reduce_scatter | solution.py:290
  (697 shorter events, 1257.3 us)
Async XLA Ops:
  7.2 699.7 %copy-start = (bf16[1536,1024]{1,0:T(8,128)(2,1)S(1)}, bf16[1536,1024]{1,0:T(8,128)(2,1)}, u32[]{:S(2)}) copy-start(bf16[1536,1024]{1,0:T(8,128)(2,1)} %param.33) | copy-start | bytes 9437188
  7.2 60.4 %copy-start.117 = (s32[2]{0:T(128)S(1)}, s32[2]{0:T(128)}, u32[]{:S(2)}) copy-start(s32[2]{0:T(128)} %param.24) | copy-start | bytes 28
  7.2 60.5 %copy-start.116 = (s32[2,8]{1,0:T(2,128)S(1)}, s32[2,8]{1,0:T(2,128)}, u32[]{:S(2)}) copy-start(s32[2,8]{1,0:T(2,128)} %param.23) | copy-start | bytes 196
  7.2 60.8 %copy-start.103 = (f32[4,1536]{1,0:T(4,128)S(1)}, f32[4,1536]{1,0:T(4,128)}, u32[]{:S(2)}) copy-start(f32[4,1536]{1,0:T(4,128)} %param.28) | copy-start | bytes 73732
  7.2 60.8 %copy-start.98 = (f32[1536]{0:T(1024)S(1)}, f32[1536]{0:T(1024)}, u32[]{:S(2)}) copy-start(f32[1536]{0:T(1024)} %param.32) | copy-start | bytes 18436
  63.0 53.6 %all-to-all-start.2 = ((bf16[16,512,128]{2,1,0:T(8,128)(2,1)}), bf16[16,512,128]{2,1,0:T(8,128)(2,1)}, u32[]{:S(2)}, u32[]{:S(2)}) async-start(bf16[16,512,128]{2,1,0:T(8,128)(2,1)} %param.22), calls=%async_computation.2 | async-start | bytes 4194304 | tf_op jit(solution)/shard_map/all_to_all | solution.py:110
  67.5 1617.1 %reduce-scatter.30.cloned.1.call-start = ((), (), s32[]{:S(2)}) async-start(), calls=%async_computation.21 | async-start | bytes 811008
  68.1 134.0 %copy-start.58 = (f32[1536]{0:T(1024)}, f32[1536]{0:T(1024)S(1)}, u32[]{:S(2)}) copy-start(f32[1536]{0:T(1024)S(1)} %fusion.78) | copy-start | bytes 18436
  68.2 133.9 %copy-start.68 = (pred[2,512]{1,0:T(4,128)(4,1)}, pred[2,512]{1,0:T(4,128)(4,1)S(1)}, u32[]{:S(2)}) copy-start(pred[2,512]{1,0:T(4,128)(4,1)S(1)} %get-tuple-element.380) | copy-start | bytes 3076
  93.0 28.5 %collective-permute-start = (bf16[2,3,1536]{2,1,0:T(4,128)(2,1)S(1)}, bf16[2,3,1536]{2,1,0:T(4,128)(2,1)S(1)}, u32[]{:S(2)}, u32[]{:S(2)}) collective-permute-start(bf16[2,3,1536]{2,1,0:T(4,128)(2,1)S(1)} %slice.1091), channel_id=1, source_target_pairs={{0,8},{8,16},{16,24},{1,9},{9,17},{17,25},{2,10},{10,18},{18,26},{... | collective-permute-start | bytes 55304 | tf_op jit(solution)/shard_map/ppermute | solution.py:34
  96.4 105.7 %copy-start.54 = (f32[1536]{0:T(1024)}, f32[1536]{0:T(1024)S(1)}, u32[]{:S(2)}) copy-start(f32[1536]{0:T(1024)S(1)} %get-tuple-element.256) | copy-start | bytes 18436
  96.4 105.7 %copy-start.56 = (f32[1536]{0:T(1024)}, f32[1536]{0:T(1024)S(1)}, u32[]{:S(2)}) copy-start(f32[1536]{0:T(1024)S(1)} %get-tuple-element.257) | copy-start | bytes 18436
  1325.3 424.5 %reduce-scatter.28.cloned.1.call-start = ((), (), s32[]{:S(2)}) async-start(), calls=%async_computation.20 | async-start | bytes 811008
  1440.3 323.3 %reduce-scatter.20.cloned.1.call-start = ((), (), s32[]{:S(2)}) async-start(), calls=%async_computation.16 | async-start | bytes 6488064 | tf_op jit(solution)/shard_map/reduce_scatter | solution.py:293
  1456.7 338.1 %reduce-scatter.16.cloned.1.call-start = ((), (), s32[]{:S(2)}) async-start(), calls=%async_computation.14 | async-start | bytes 6488064 | tf_op jit(solution)/shard_map/reduce_scatter | solution.py:287
  1474.4 439.7 %reduce-scatter.14.cloned.1.call-start = ((), (), s32[]{:S(2)}) async-start(), calls=%async_computation.13 | async-start | bytes 6488064 | tf_op jit(solution)/shard_map/reduce_scatter | solution.py:286
  1489.1 5.9 collective-permute-start.1
  1508.2 567.4 %reduce-scatter.26.cloned.1.call-start = ((), (), s32[]{:S(2)}) async-start(), calls=%async_computation.19 | async-start | bytes 12976128 | tf_op jit(solution)/shard_map/reduce_scatter | solution.py:297
  1536.0 700.0 %reduce-scatter.24.cloned.1.call-start = ((), (), s32[]{:S(2)}) async-start(), calls=%async_computation.18 | async-start | bytes 12976128 | tf_op jit(solution)/shard_map/reduce_scatter | solution.py:296
  1562.7 835.1 %reduce-scatter.22.cloned.1.call-start = ((), (), s32[]{:S(2)}) async-start(), calls=%async_computation.17 | async-start | bytes 12976128 | tf_op jit(solution)/shard_map/reduce_scatter | solution.py:295
  1607.5 66.4 %all-to-all-start.1 = ((bf16[2,512,1024]{1,0,2:T(2,128)(2,1)}), bf16[2,512,1024]{1,0,2:T(2,128)(2,1)}, u32[]{:S(2)}, u32[]{:S(2)}) async-start(bf16[2,512,1024]{1,0,2:T(2,128)(2,1)} %copy.85), calls=%async_computation.1 | async-start | bytes 4194304 | tf_op jit(solution)/shard_map/all_to_all | solution.py:183
  1673.9 83.5 %all-to-all-start.3 = ((bf16[2,512,1024]{1,0,2:T(2,128)(2,1)}), bf16[2,512,1024]{1,0,2:T(2,128)(2,1)}, u32[]{:S(2)}, u32[]{:S(2)}) async-start(bf16[2,512,1024]{1,0,2:T(2,128)(2,1)} %copy.92), calls=%async_computation.3 | async-start | bytes 4194304 | tf_op jit(solution)/shard_map/all_to_all | solution.py:268
  1678.3 821.5 %reduce-scatter.18.cloned.1.call-start = ((), (), s32[]{:S(2)}) async-start(), calls=%async_computation.15 | async-start | bytes 1622016 | tf_op jit(solution)/shard_map/reduce_scatter | solution.py:290
  1684.5 815.3 %copy-start.1 = (bf16[1536,1024]{1,0:T(8,128)(2,1)S(1)}, bf16[1536,1024]{1,0:T(8,128)(2,1)}, u32[]{:S(2)}) copy-start(bf16[1536,1024]{1,0:T(8,128)(2,1)} %param.33) | copy-start | bytes 9437188
  (116 other events, 1931.1 us)
Sparse Core Ops, SparseCore 0:
  1325.4 93.3 reduce-scatter.29
  1440.4 93.3 reduce-scatter.27
  1539.4 135.9 reduce-scatter.19
  1681.8 112.9 reduce-scatter.15
  1800.3 113.7 reduce-scatter.13
  1921.0 154.5 reduce-scatter.25
  2081.6 154.3 reduce-scatter.23
  2243.1 154.7 reduce-scatter.21
  2403.6 96.1 reduce-scatter.17
where the time goes:
time: 2540 us; the launch traced here: 2510 us
  local copies, waits for them, and re-layouts  1020 us (40%)
  waiting for transfers between devices  787 us (31%)
  other arithmetic  302 us (12%)
  matrix products  219 us (9%)
  blocking collectives  141 us (6%)
    slice x125, local copies, waits for them, and re-layouts, local_scan(): return lax.associative_scan(pair_join, (factors, values), axis=1)  467 us
    pad x64, local copies, waits for them, and re-layouts, local_scan(): return lax.associative_scan(pair_join, (factors, values), axis=1)  182 us
    reduce_scatter x1, waiting for transfers between devices, body(): lax.psum_scatter(terms[10], ('seq', 'chan'), scatter_dimension=0, tiled=T...  160 us
    reduce_scatter x1, waiting for transfers between devices, body(): lax.psum_scatter(terms[12], ('seq', 'chan'), scatter_dimension=0, tiled=T...  160 us
    reduce_scatter x1, waiting for transfers between devices, body(): lax.psum_scatter(terms[11], ('seq', 'chan'), scatter_dimension=0, tiled=T...  159 us
    reduce_scatter x1, waiting for transfers between devices, body(): lax.psum_scatter(terms[1], ('seq', 'chan'), scatter_dimension=0, tiled=True)  118 us
    reduce_scatter x1, waiting for transfers between devices, body(): lax.psum_scatter(terms[5], ('seq', 'chan'), scatter_dimension=0, tiled=True)  100 us
    dot_general x6, matrix products, back_dot(): lax.dot_general(left, right, (((1,), (1,)), ((), ())), preferred_element_...  72.7 us
  transfers between devices with their start and end apart: 14, of which 9 were waited for; matrix products, arithmetic and copies ran while one was open for 14% of the time, Pallas kernels for 0%

commit v1 on v0

--- a/solution.py
+++ b/solution.py
@@ -1,6 +1,11 @@
+import functools
+import math
+
 import jax
 import jax.numpy as jnp
 from jax import lax
+from jax.experimental import pallas as pl
+from jax.experimental.pallas import tpu as pltpu
 from jax.sharding import PartitionSpec as P
 
 H = 16
@@ -9,6 +14,468 @@
 EPS = 1e-06
 ROOT_FLOOR = 1e-06
 LANES = 128
+SUBLANES = 8
+STEP = 16
+VMEM_BYTES = 56 * 1024 * 1024
+
+
+def sigmoid(value):
+    return 0.5 * jnp.tanh(0.5 * value) + 0.5
+
+
+GELU_C = 0.7978845608
+GELU_A = 0.044715
+
+
+def gelu_pair(value):
+    square = value * value
+    inner = jnp.tanh(value * (GELU_C + (GELU_C * GELU_A) * square))
+    half = 0.5 + 0.5 * inner
+    slope = GELU_C + (3.0 * GELU_C * GELU_A) * square
+    return (value * half, half + 0.5 * value * (1.0 - inner * inner) * slope)
+
+
+def root_argument(log_decay, decay):
+    y = 2.0 * log_decay
+    series = 1.0 + y * (1.0 / 7.0)
+    for divisor in (6.0, 5.0, 4.0, 3.0, 2.0):
+        series = 1.0 + (y * (1.0 / divisor)) * series
+    return jnp.where(y > -0.25, -y * series, 1.0 - decay * decay)
+
+
+def across(column, width):
+    return jnp.concatenate([column] * (width // LANES), axis=1)
+
+
+def forward_kernel(
+    branch_ref,
+    rim_ref,
+    dist_ref,
+    par_ref,
+    gates_ref,
+    lru_ref,
+    rate_ref,
+    igate_ref,
+    state_ref,
+    cum_ref,
+    both_ref,
+):
+    rows, length, width = branch_ref.shape
+    taps = [par_ref[k : k + 1, :] for k in range(4)]
+    conv_bias, rate_bias, input_bias, soft = (par_ref[k : k + 1, :] for k in range(4, 8))
+    place = lax.broadcasted_iota(jnp.int32, (SUBLANES, width), 0)
+
+    for row in range(rows):
+
+        def conv_step(index, before, row=row):
+            base = pl.multiple_of(index * STEP, STEP)
+            pieces = []
+            for half in range(STEP // SUBLANES):
+                at = pl.ds(base + half * SUBLANES, SUBLANES)
+                here = branch_ref[row, at, :]
+                dist = across(dist_ref[row, at, :], width)
+                total = conv_bias + taps[0] * here
+                for k in range(1, 4):
+                    shifted = pltpu.roll(jnp.where(place < SUBLANES - k, here, before), k, 0)
+                    total = total + taps[k] * jnp.where(dist >= k, shifted, 0.0)
+                pieces.append(total)
+                before = here
+            lru_ref[row, pl.ds(base, STEP), :] = jnp.concatenate(pieces, axis=0).astype(jnp.bfloat16)
+            return before
+
+        lax.fori_loop(0, length // STEP, conv_step, rim_ref[row])
+
+        piece = min(length, 256)
+
+        def dot_step(index, carry, row=row):
+            at = pl.ds(pl.multiple_of(index * piece, piece), piece)
+            both_ref[row, at, :] = jnp.dot(
+                lru_ref[row, at, :], gates_ref[...], preferred_element_type=jnp.float32
+            )
+            return carry
+
+        lax.fori_loop(0, length // piece, dot_step, 0)
+
+    def scan_step(index, carry):
+        base = pl.multiple_of(index * STEP, STEP)
+        later = []
+        for row in range(rows):
+            run_cum, run_state = carry[row]
+            lru_both = lru_ref[row, pl.ds(base, STEP), :].astype(jnp.float32)
+            for half in range(STEP // SUBLANES):
+                at = pl.ds(base + half * SUBLANES, SUBLANES)
+                lru = lru_both[half * SUBLANES : (half + 1) * SUBLANES]
+                start = across(dist_ref[row, at, :], width) == 0
+                rate = sigmoid(both_ref[row, at, :width] + rate_bias)
+                igate = sigmoid(both_ref[row, at, width:] + input_bias)
+                log_decay = rate * soft
+                decay = jnp.exp(log_decay)
+                arg = jnp.maximum(root_argument(log_decay, decay), ROOT_FLOOR)
+                root = arg * lax.rsqrt(arg)
+                cum = jnp.where(start, 0.0, decay)
+                value = jnp.where(start, 1.0, root) * igate * lru
+                rate_ref[row, at, :] = rate
+                igate_ref[row, at, :] = igate
+                for shift in (1, 2, 4):
+                    live = place >= shift
+                    value = value + cum * jnp.where(live, pltpu.roll(value, shift, 0), 0.0)
+                    cum = cum * jnp.where(live, pltpu.roll(cum, shift, 0), 1.0)
+                value = value + cum * run_state
+                cum = cum * run_cum
+                state_ref[row, at, :] = value
+                cum_ref[row, at, :] = cum
+                run_state = value[SUBLANES - 1 :, :]
+                run_cum = cum[SUBLANES - 1 :, :]
+            later.append((run_cum, run_state))
+        return tuple(later)
+
+    one, zero = (jnp.ones((1, width), jnp.float32), jnp.zeros((1, width), jnp.float32))
+    lax.fori_loop(0, length // STEP, scan_step, tuple((one, zero) for _ in range(rows)))
+
+
+def adjoint_kernel(
+    dmix_ref,
+    pre_ref,
+    state_ref,
+    cum_ref,
+    carry_ref,
+    rate_ref,
+    dist_ref,
+    par_ref,
+    dgate_ref,
+    local_ref,
+    back_ref,
+    first_ref,
+):
+    rows, length, width = dmix_ref.shape
+    soft = par_ref[7:8, :]
+    place = lax.broadcasted_iota(jnp.int32, (SUBLANES, width), 0)
+    last = length // STEP - 1
+
+    def step(index, carry):
+        base = pl.multiple_of((last - index) * STEP, STEP)
+        later = []
+        for row in range(rows):
+            run_cum, run_back = carry[row]
+            entering = carry_ref[row]
+            pieces = []
+            for half in reversed(range(STEP // SUBLANES)):
+                at = pl.ds(base + half * SUBLANES, SUBLANES)
+                start = across(dist_ref[row, at, :], width) == 0
+                state = state_ref[row, at, :] + cum_ref[row, at, :] * entering
+                act, slope = gelu_pair(pre_ref[row, at, :])
+                dmix = dmix_ref[row, at, :]
+                pieces.append(dmix * state * slope)
+                dstate = dmix * act
+                coef = jnp.where(start, 0.0, jnp.exp(rate_ref[row, at, :] * soft))
+                value = coef * dstate
+                for shift in (1, 2, 4):
+                    live = place < SUBLANES - shift
+                    turn = SUBLANES - shift
+                    value = value + coef * jnp.where(live, pltpu.roll(value, turn, 0), 0.0)
+                    coef = coef * jnp.where(live, pltpu.roll(coef, turn, 0), 1.0)
+                value = value + coef * run_back
+                coef = coef * run_cum
+                inside = place < SUBLANES - 1
+                local_ref[row, at, :] = dstate + jnp.where(
+                    inside, pltpu.roll(value, SUBLANES - 1, 0), run_back
+                )
+                back_ref[row, at, :] = jnp.where(inside, pltpu.roll(coef, SUBLANES - 1, 0), run_cum)
+                run_back = value[:1, :]
+                run_cum = coef[:1, :]
+            dgate_ref[row, pl.ds(base, STEP), :] = jnp.concatenate(pieces[::-1], axis=0).astype(
+                jnp.bfloat16
+            )
+            later.append((run_cum, run_back))
+        return tuple(later)
+
+    one, zero = (jnp.ones((1, width), jnp.float32), jnp.zeros((1, width), jnp.float32))
+    done = lax.fori_loop(0, last + 1, step, tuple((one, zero) for _ in range(rows)))
+    for row in range(rows):
+        first_ref[row] = done[row][1]
+
+
+def backward_kernel(
+    head_size,
+    local_ref,
+    back_ref,
+    out_ref,
+    state_ref,
+    cum_ref,
+    in_ref,
+    rate_ref,
+    igate_ref,
+    lru_ref,
+    dist_ref,
+    branch_ref,
+    rim_ref,
+    par_ref,
+    gates_ref,
+    dbranch_ref,
+    tail_ref,
+    head_ref,
+    sums_ref,
+    dgates_ref,
+    both_ref,
+    dconv_ref,
+):
+    rows, length, width = local_ref.shape
+    taps = [par_ref[k : k + 1, :] for k in range(4)]
+    soft = par_ref[7:8, :]
+    place = lax.broadcasted_iota(jnp.int32, (SUBLANES, width), 0)
+    zeros = jnp.zeros((SUBLANES, width), jnp.float32)
+
+    def gate_step(index, carry):
+        sums, earlier = carry
+        decay_sum, rate_sum, input_sum = sums
+        base = pl.multiple_of(index * STEP, STEP)
+        later = []
+        for row in range(rows):
+            before = earlier[row]
+            entering = in_ref[row]
+            leaving = out_ref[row]
+            lru_both = lru_ref[row, pl.ds(base, STEP), :].astype(jnp.float32)
+            drates, dinputs = ([], [])
+            for half in range(STEP // SUBLANES):
+                at = pl.ds(base + half * SUBLANES, SUBLANES)
+                lru = lru_both[half * SUBLANES : (half + 1) * SUBLANES]
+                start = across(dist_ref[row, at, :], width) == 0
+                adjoint = local_ref[row, at, :] + back_ref[row, at, :] * leaving
+                state = state_ref[row, at, :] + cum_ref[row, at, :] * entering
+                previous = jnp.where(place < 1, before, pltpu.roll(state, 1, 0))
+                before = state[SUBLANES - 1 :, :]
+                rate = rate_ref[row, at, :]
+                igate = igate_ref[row, at, :]
+                log_decay = rate * soft
+                decay = jnp.exp(log_decay)
+                arg = root_argument(log_decay, decay)
+                above = arg > ROOT_FLOOR
+                arg = jnp.maximum(arg, ROOT_FLOOR)
+                inverse = lax.rsqrt(arg)
+                scale = jnp.where(start, 1.0, arg * inverse)
+                gated = adjoint * igate
+                dscale = gated * lru
+                pull = jnp.where(above, dscale * decay * decay * inverse, 0.0)
+                dlog = jnp.where(start, 0.0, adjoint * previous * decay - pull)
+                dig = adjoint * scale * lru
+                weighted = dlog * rate
+                decay_sum = decay_sum + weighted
+                drates.append(weighted * soft * (1.0 - rate))
+                dinputs.append(dig * igate * (1.0 - igate))
+                dconv_ref[row, at, :] = gated * scale
+            drate = jnp.concatenate(drates, axis=0).astype(jnp.bfloat16)
+            dinput = jnp.concatenate(dinputs, axis=0).astype(jnp.bfloat16)
+            both_ref[row, pl.ds(base, STEP), :width] = drate
+            both_ref[row, pl.ds(base, STEP), width:] = dinput
+            drate = drate.astype(jnp.float32)
+            dinput = dinput.astype(jnp.float32)
+            rate_sum = rate_sum + (drate[:SUBLANES] + drate[SUBLANES:])
+            input_sum = input_sum + (dinput[:SUBLANES] + dinput[SUBLANES:])
+            later.append(before)
+        return ((decay_sum, rate_sum, input_sum), tuple(later))
+
+    sums, _ = lax.fori_loop(
+        0,
+        length // STEP,
+        gate_step,
+        ((zeros, zeros, zeros), tuple(in_ref[row] for row in range(rows))),
+    )
+    for slot, total in zip((5, 6, 7), (sums[1], sums[2], sums[0])):
+        sums_ref[slot : slot + 1, :] = jnp.sum(total, axis=0, keepdims=True)
+
+    piece = min(length, 256)
+    wide = None
+    for row in range(rows):
+
+        def dot_step(index, carry, row=row):
+            at = pl.ds(pl.multiple_of(index * piece, piece), piece)
+            dconv_ref[row, at, :] += lax.dot_general(
+                both_ref[row, at, :],
+                gates_ref[...],
+                (((1,), (1,)), ((), ())),
+                preferred_element_type=jnp.float32,
+            )
+            return carry
+
+        lax.fori_loop(0, length // piece, dot_step, 0)
+        part = lax.dot_general(
+            lru_ref[row], both_ref[row], (((0,), (0,)), ((), ())), preferred_element_type=jnp.float32
+        )
+        wide = part if wide is None else wide + part
+    row_head = lax.broadcasted_iota(jnp.int32, (width, width), 0) // head_size
+    col_head = lax.broadcasted_iota(jnp.int32, (width, width), 1) // head_size
+    own = row_head == col_head
+    for part in range(2):
+        kept = jnp.where(own, wide[:, part * width : (part + 1) * width], 0.0)
+        folded = kept
+        for other in range(1, width // head_size):
+            folded = folded + pltpu.roll(kept, width - other * head_size, 1)
+        dgates_ref[:, part * LANES : (part + 1) * LANES] = folded[:, :LANES]
+
+    def conv_step(index, carry):
+        sums, following = carry
+        sums = list(sums)
+        base = pl.multiple_of((length // STEP - 1 - index) * STEP, STEP)
+        later = []
+        for row in range(rows):
+            after = following[row]
+            pieces = []
+            for half in reversed(range(STEP // SUBLANES)):
+                at = pl.ds(base + half * SUBLANES, SUBLANES)
+                dist = across(dist_ref[row, at, :], width)
+                branch = branch_ref[row, at, :]
+                here = dconv_ref[row, at, :]
+                total = taps[0] * here
+                sums[0] = sums[0] + here * branch
+                sums[4] = sums[4] + here
+                masked = tuple(jnp.where(dist >= k, here, 0.0) for k in range(1, 4))
+                for k in range(1, 4):
+                    moved = pltpu.roll(
+                        jnp.where(place >= k, masked[k - 1], after[k - 1]), SUBLANES - k, 0
+                    )
+                    total = total + taps[k] * moved
+                    sums[k] = sums[k] + branch * moved
+                after = masked
+                pieces.append(total)
+            whole = jnp.concatenate(pieces[::-1], axis=0)
+            dbranch_ref[row, pl.ds(base, STEP), :] = whole.astype(jnp.bfloat16)
+            later.append(after)
+
+            @pl.when(index == 0)
+            def _(row=row, whole=whole):
+                tail_ref[row] = whole[STEP - SUBLANES :]
+
+        return (tuple(sums), tuple(later))
+
+    sums, firsts = lax.fori_loop(
+        0,
+        length // STEP,
+        conv_step,
+        ((zeros,) * 5, tuple((zeros,) * 3 for _ in range(rows))),
+    )
+    sums = list(sums)
+    for row in range(rows):
+        total = zeros
+        rim = rim_ref[row]
+        for k in range(1, 4):
+            moved = pltpu.roll(jnp.where(place >= k, 0.0, firsts[row][k - 1]), SUBLANES - k, 0)
+            total = total + taps[k] * moved
+            sums[k] = sums[k] + rim * moved
+        head_ref[row] = total
+    for slot in range(5):
+        sums_ref[slot : slot + 1, :] = jnp.sum(sums[slot], axis=0, keepdims=True)
+
+
+def channel_call(kernel, name, arrays, specs, outs, out_specs, scratch, blocks, flops):
+    moved = sum(math.prod(a.shape) * a.dtype.itemsize for a in (*arrays, *outs))
+    return pl.pallas_call(
+        kernel,
+        name=name,
+        grid=(blocks,),
+        in_specs=specs,
+        out_specs=out_specs,
+        out_shape=outs,
+        scratch_shapes=scratch,
+        compiler_params=pltpu.CompilerParams(vmem_limit_bytes=VMEM_BYTES),
+        cost_estimate=pl.CostEstimate(flops=flops, bytes_accessed=moved, transcendentals=0),
+    )(*arrays)
+
+
+class Recurrence:
+    def __init__(self, rows, length, channels, head_size):
+        self.rows, self.length, self.channels = (rows, length, channels)
+        self.head_size = head_size
+        self.width = head_size * LANES // math.gcd(head_size, LANES)
+        self.blocks = channels // self.width
+        self.flops = 2 * rows * length * channels * 2 * self.width
+
+    def tall(self):
+        return pl.BlockSpec((self.rows, self.length, self.width), lambda j: (0, 0, j))
+
+    def short(self, size):
+        return pl.BlockSpec((self.rows, size, self.width), lambda j: (0, 0, j))
+
+    def flat(self, size):
+        return pl.BlockSpec((size, self.width), lambda j: (0, j))
+
+    def dist(self):
+        return pl.BlockSpec((self.rows, self.length, LANES), lambda j: (0, 0, 0))
+
+    def gates(self, columns):
+        return pl.BlockSpec((self.width, columns), lambda j: (j, 0))
+
+    def shape(self, size, dtype):
+        return jax.ShapeDtypeStruct((self.rows, size, self.channels), dtype)
+
+    def widen(self, lru_gates):
+        size, width = (self.head_size, self.width)
+        heads = width // size
+        column = jnp.arange(2 * width)
+        source = (column // width) * size + column % size
+        spread = (jnp.arange(2 * size)[:, None] == source[None, :]).astype(jnp.bfloat16)
+        owner = (column % width) // size
+        mine = (jnp.arange(self.channels) // size) % heads
+        wide = jnp.dot(lru_gates, spread, preferred_element_type=jnp.float32)
+        return jnp.where(mine[:, None] == owner[None, :], wide, 0.0).astype(jnp.bfloat16)
+
+    def forward(self, branch, rim, dist, params, gates):
+        f32 = jnp.float32
+        outs = [self.shape(self.length, d) for d in (jnp.bfloat16, f32, f32, f32, f32)]
+        return channel_call(
+            forward_kernel,
+            "recurrence_forward",
+            (branch, rim, dist, params, gates),
+            [self.tall(), self.short(SUBLANES), self.dist(), self.flat(16), self.gates(2 * self.width)],
+            outs,
+            [self.tall()] * 5,
+            [pltpu.VMEM((self.rows, self.length, 2 * self.width), f32)],
+            self.blocks,
+            self.flops,
+        )
+
+    def adjoint(self, dmix, pre, state, cum, entering, rate, dist, params):
+        f32 = jnp.float32
+        outs = [self.shape(self.length, d) for d in (jnp.bfloat16, f32, f32)] + [self.shape(1, f32)]
+        tall = self.tall()
+        return channel_call(
+            adjoint_kernel,
+            "recurrence_adjoint",
+            (dmix, pre, state, cum, entering, rate, dist, params),
+            [tall, tall, tall, tall, self.short(1), tall, self.dist(), self.flat(16)],
+            outs,
+            [tall, tall, tall, self.short(1)],
+            [],
+            self.blocks,
+            0,
+        )
+
+    def backward(
+        self, local, back, leaving, state, cum, entering, rate, igate, lru, dist, branch, rim, params, gates
+    ):
+        f32 = jnp.float32
+        outs = [
+            self.shape(self.length, jnp.bfloat16),
+            self.shape(SUBLANES, f32),
+            self.shape(SUBLANES, f32),
+            jax.ShapeDtypeStruct((SUBLANES, self.channels), f32),
+            jax.ShapeDtypeStruct((self.channels, 2 * LANES), f32),
+        ]
+        tall, one = (self.tall(), self.short(1))
+        return channel_call(
+            functools.partial(backward_kernel, self.head_size),
+            "recurrence_backward",
+            (local, back, leaving, state, cum, entering, rate, igate, lru, dist, branch, rim, params, gates),
+            [tall, tall, one, tall, tall, one, tall, tall, tall, self.dist(), tall]
+            + [self.short(SUBLANES), self.flat(16), self.gates(2 * self.width)],
+            outs,
+            [tall, self.short(SUBLANES), self.short(SUBLANES), self.flat(SUBLANES), self.gates(2 * LANES)],
+            [
+                pltpu.VMEM((self.rows, self.length, 2 * self.width), jnp.bfloat16),
+                pltpu.VMEM((self.rows, self.length, self.width), f32),
+            ],
+            self.blocks,
+            2 * self.flops,
+        )
 
 
 def prefix(value, axis, join, neutral, backward):
@@ -60,10 +527,6 @@
 
 def pair_join(earlier, later):
     return (earlier[0] * later[0], later[0] * earlier[1] + later[1])
-
-
-def local_scan(factors, values):
-    return lax.associative_scan(pair_join, (factors, values), axis=1)
 
 
 def norm_back(grad_norm, normed, inverse, gain):
@@ -122,7 +585,6 @@
     bounds = jnp.concatenate([doc_starts, lengths[:, None]], axis=1)
     is_before = bounds[:, None, :] <= position[None, :, None]
     seg_start = jnp.max(jnp.where(is_before, bounds[:, None, :], 0), axis=2)
-    at_start = (seg_start == position[None, :])[:, :, None]
     is_valid = (position[None, :] < lengths[:, None]).reshape(tok_count, 1)
     flat_x = seq_x.reshape(tok_count, model_dim).astype(jnp.float32)
     inv_one = lax.rsqrt(jnp.mean(flat_x * flat_x, axis=1, keepdims=True) + EPS)
@@ -132,43 +594,32 @@
     gate_pre = fwd_dot(normed_low, recur_gate)
     gate_act = gelu_fn(gate_pre)
     branch_rows = branch_pre.reshape(row_count, block_len, rec_width)
+    core = Recurrence(row_count, block_len, rec_width, head_size)
     prev_rim = passed_along(
         branch_rows[:, block_len - rim_size :, :].astype(jnp.bfloat16), "seq", 1
     ).astype(jnp.float32)
-    extended = jnp.concatenate([prev_rim, branch_rows], axis=1)
-    conv_sum = jnp.zeros_like(branch_rows) + conv_bias
-    tap_masks = []
-    for offset in range(tap_count):
-        tap_keep = (position[None, :] - offset >= seg_start)[:, :, None]
-        tap_masks.append(tap_keep)
-        window = extended[:, rim_size - offset : rim_size - offset + block_len, :]
-        conv_sum = conv_sum + conv_kernel[offset] * jnp.where(tap_keep, window, 0.0)
-    lru_in = conv_sum.astype(jnp.bfloat16)
-    lru_heads = lru_in.reshape(tok_count, head_count, head_size)
-    gate_blocks = lru_gates.reshape(head_count, head_size, 2 * head_size)
-    gate_both = jnp.einsum(
-        "thi,hij->thj", lru_heads, gate_blocks, preferred_element_type=jnp.float32
-    )
-    rate_pre = gate_both[:, :, :head_size].reshape(tok_count, rec_width) + lru_bias[0]
-    input_pre = gate_both[:, :, head_size:].reshape(tok_count, rec_width) + lru_bias[1]
-    rate_gate = jax.nn.sigmoid(rate_pre)
-    input_gate = jax.nn.sigmoid(input_pre)
+    rim = jnp.pad(prev_rim, ((0, 0), (SUBLANES - rim_size, 0), (0, 0)))
+    dist = jnp.broadcast_to(
+        (position[None, :] - seg_start)[:, :, None], (row_count, block_len, LANES)
+    )
     soft_decay = jax.nn.softplus(-lru_decay)
-    log_decay = -8.0 * rate_gate * soft_decay
-    decay_rate = jnp.exp(log_decay)
-    root_arg = -jnp.expm1(2.0 * log_decay)
-    root_live = root_arg > ROOT_FLOOR
-    root_term = jnp.sqrt(jnp.maximum(root_arg, ROOT_FLOOR))
-    start_flat = at_start.reshape(tok_count, 1)
-    decay_coef = jnp.where(start_flat, 0.0, decay_rate)
-    scale_in = jnp.where(start_flat, 1.0, root_term)
-    lru_value = lru_in.reshape(tok_count, rec_width).astype(jnp.float32)
-    lru_drive = scale_in * input_gate * lru_value
-    coef_rows = decay_coef.reshape(row_count, block_len, rec_width)
-    drive_rows = lru_drive.reshape(row_count, block_len, rec_width)
-    cum_coef, local_state = local_scan(coef_rows, drive_rows)
+    params = jnp.concatenate(
+        [
+            conv_kernel,
+            conv_bias[None],
+            lru_bias,
+            (-8.0 * soft_decay)[None],
+            jnp.zeros((SUBLANES, rec_width), jnp.float32),
+        ],
+        axis=0,
+    )
+    wide_gates = core.widen(lru_gates)
+    lru_in, rate_gate, input_gate, local_state, cum_coef = core.forward(
+        branch_rows, rim, dist, params, wide_gates
+    )
     carry_in = carry_forward((cum_coef[:, -1, :], local_state[:, -1, :]))
-    state_rows = local_state + cum_coef * carry_in[:, None, :]
+    entering = carry_in[:, None, :]
+    state_rows = local_state + cum_coef * entering
     state_flat = state_rows.reshape(tok_count, rec_width)
     mixed_low = (state_flat * gate_act).astype(jnp.bfloat16)
     resid_one = flat_x + fwd_dot(mixed_low, recur_out)
@@ -202,64 +653,46 @@
     resid_low = grad_resid.astype(jnp.bfloat16)
     grad_rout = trans_dot(mixed_low, resid_low)
     grad_mixed = back_dot(resid_low, recur_out)
-    grad_state = grad_mixed * gate_act
-    _, act_pull = jax.vjp(gelu_fn, gate_pre)
-    gate_low = act_pull(grad_mixed * state_flat)[0].astype(jnp.bfloat16)
-    next_coef = jnp.concatenate([coef_rows[:, 1:, :], jnp.ones_like(coef_rows[:, :1, :])], axis=1)
-    flip_cum, flip_local = local_scan(
-        jnp.flip(next_coef, 1), jnp.flip(grad_state.reshape(row_count, block_len, rec_width), 1)
-    )
-    back_cum = jnp.flip(flip_cum, 1)
-    back_local = jnp.flip(flip_local, 1)
-    carry_out = carry_backward((cum_coef[:, -1, :], coef_rows[:, 0, :] * back_local[:, 0, :]))
-    adjoint = back_local + back_cum * carry_out[:, None, :]
-    prev_state = jnp.concatenate([carry_in[:, None, :], state_rows[:, :-1, :]], axis=1)
-    grad_coef = (adjoint * prev_state).reshape(tok_count, rec_width)
-    adjoint_flat = adjoint.reshape(tok_count, rec_width)
-    grad_scale = adjoint_flat * input_gate * lru_value
-    grad_igate = adjoint_flat * scale_in * lru_value
-    grad_value = adjoint_flat * scale_in * input_gate
-    root_pull = jnp.where(root_live, grad_scale * decay_rate * decay_rate / root_term, 0.0)
-    grad_log = jnp.where(start_flat, 0.0, grad_coef * decay_rate - root_pull)
-    grad_decay = -jax.nn.sigmoid(-lru_decay) * jnp.sum(grad_log * (-8.0 * rate_gate), axis=0)
-    rate_low = (grad_log * (-8.0 * soft_decay) * rate_gate * (1.0 - rate_gate)).astype(jnp.bfloat16)
-    input_low = (grad_igate * input_gate * (1.0 - input_gate)).astype(jnp.bfloat16)
-    grad_lbias = jnp.stack(
-        [
-            jnp.sum(rate_low.astype(jnp.float32), axis=0),
-            jnp.sum(input_low.astype(jnp.float32), axis=0),
-        ]
-    )
-    pre_heads = jnp.concatenate(
-        [
-            rate_low.reshape(tok_count, head_count, head_size),
-            input_low.reshape(tok_count, head_count, head_size),
-        ],
-        axis=2,
-    )
-    grad_lgates = jnp.einsum(
-        "thi,thj->hij", lru_heads, pre_heads, preferred_element_type=jnp.float32
-    ).reshape(rec_width, 2 * head_size)
-    grad_value = grad_value + jnp.einsum(
-        "thj,hij->thi", pre_heads, gate_blocks, preferred_element_type=jnp.float32
+    gate_low, back_local, back_cum, first_term = core.adjoint(
+        grad_mixed.reshape(row_count, block_len, rec_width),
+        gate_pre.reshape(row_count, block_len, rec_width),
+        local_state,
+        cum_coef,
+        entering,
+        rate_gate,
+        dist,
+        params,
+    )
+    gate_low = gate_low.reshape(tok_count, rec_width)
+    carry_out = carry_backward((cum_coef[:, -1, :], first_term[:, 0, :]))
+    branch_local, tail, lead, channel_sums, gate_sums = core.backward(
+        back_local,
+        back_cum,
+        carry_out[:, None, :],
+        local_state,
+        cum_coef,
+        entering,
+        rate_gate,
+        input_gate,
+        lru_in,
+        dist,
+        branch_rows,
+        rim,
+        params,
+        wide_gates,
+    )
+    grad_ckernel = channel_sums[:4]
+    grad_cbias = channel_sums[4]
+    grad_lbias = channel_sums[5:7]
+    grad_decay = 8.0 * jax.nn.sigmoid(-lru_decay) * channel_sums[7]
+    grad_lgates = jnp.concatenate(
+        [gate_sums[:, :head_size], gate_sums[:, LANES : LANES + head_size]], axis=1
+    )
+    from_next = passed_along(as_sent(lead[:, SUBLANES - rim_size :, :]), "seq", -1)
+    ending = tail + jnp.pad(from_next.astype(jnp.float32), ((0, 0), (SUBLANES - rim_size, 0), (0, 0)))
+    branch_low = lax.dynamic_update_slice(
+        branch_local, ending.astype(jnp.bfloat16), (0, block_len - SUBLANES, 0)
     ).reshape(tok_count, rec_width)
-    grad_conv_rows = grad_value.reshape(row_count, block_len, rec_width)
-    grad_cbias = jnp.sum(grad_value, axis=0)
-    grad_ext = jnp.zeros_like(extended)
-    kernel_grads = []
-    for offset in range(tap_count):
-        masked = jnp.where(tap_masks[offset], grad_conv_rows, 0.0)
-        window = extended[:, rim_size - offset : rim_size - offset + block_len, :]
-        kernel_grads.append(jnp.sum(masked * window, axis=(0, 1)))
-        grad_ext = grad_ext + jnp.pad(
-            conv_kernel[offset] * masked, ((0, 0), (rim_size - offset, offset), (0, 0))
-        )
-    grad_ckernel = jnp.stack(kernel_grads)
-    from_next = passed_along(as_sent(grad_ext[:, :rim_size, :]), "seq", -1)
-    grad_branch = grad_ext[:, rim_size:, :] + jnp.pad(
-        from_next, ((0, 0), (block_len - rim_size, 0), (0, 0))
-    )
-    branch_low = grad_branch.reshape(tok_count, rec_width).astype(jnp.bfloat16)
     grad_rin = trans_dot(normed_low, branch_low)
     grad_rgate = trans_dot(normed_low, gate_low)
     grad_norm1 = back_dot(branch_low, recur_input) + back_dot(gate_low, recur_gate)

time: 2540 us -> 1530 us (0.60)
  local copies, waits for them, and re-layouts: 1020 us -> 131 us
  other arithmetic: 302 us -> 29.8 us
  waiting for transfers between devices: 787 us -> 942 us
  Pallas kernels: 0 us -> 101 us
  blocking collectives: 141 us -> 87.5 us
  matrix products: 219 us -> 185 us
    slice x130 -> x7, local copies, waits for them, and re-layouts: 483 us -> 6.72 us  [the longest x2 1.81 us: body(): carry_in = carry_forward((cum_coef[:, -1, :], local_state[:, -1, :]))]
    pad x64 -> x0, local copies, waits for them, and re-layouts: 182 us -> none  [local_scan(): return lax.associative_scan(pair_join, (factors, values), axis=1)]
    add x54 -> x1, other arithmetic: 127 us -> 8.71 us  [body(): state_rows = local_state + cum_coef * entering]
    pallas_call x0 -> x3, Pallas kernels: none -> 101 us  [channel_call(): pl.pallas_call(kernel, name=name, grid=(blocks,), in_specs=specs, out_spe...]
    rev x2 -> x0, local copies, waits for them, and re-layouts: 97.5 us -> none  [the longest x1 48.8 us: body(): back_cum = jnp.flip(flip_cum, 1)]
    reduce_scatter x1, waiting for transfers between devices: 29.6 us -> 119 us  [body(): lax.psum_scatter(terms[2], ('seq', 'chan'), scatter_dimension=0, tiled=True)]
    reshape x10 -> x0, local copies, waits for them, and re-layouts: 85.2 us -> none  [the longest x2 19.5 us: body(): grad_value = grad_value + jnp.einsum('thj,hij->thi', pre_heads, gate_bloc...]
    all_to_all x1 -> x0, blocking collectives: 55.8 us -> none  [body(): lax.all_to_all(tokens, 'chan', split_axis=0, concat_axis=2, tiled=True)]
  transfers between devices with their start and end apart: 14 -> 15, of which waited for: 9 -> 11; matrix products, arithmetic and copies ran while one was open for 14% -> 15% of each run, Pallas kernels for 0% -> 0%
where the time goes in v1:
time: 1530 us; the launch traced here: 1520 us
  waiting for transfers between devices  942 us (62%)
  matrix products  185 us (12%)
  local copies, waits for them, and re-layouts  131 us (9%)
  Pallas kernels  101 us (7%)
  blocking collectives  87.5 us (6%)
  other arithmetic  29.8 us (2%)
  starting transfers between devices  25.5 us (2%)
    reduce_scatter x1, waiting for transfers between devices, body(): lax.psum_scatter(terms[10], ('seq', 'chan'), scatter_dimension=0, tiled=T...  160 us
    reduce_scatter x1, waiting for transfers between devices, body(): lax.psum_scatter(terms[12], ('seq', 'chan'), scatter_dimension=0, tiled=T...  160 us
    reduce_scatter x1, waiting for transfers between devices, body(): lax.psum_scatter(terms[11], ('seq', 'chan'), scatter_dimension=0, tiled=T...  159 us
    reduce_scatter x1, waiting for transfers between devices, body(): lax.psum_scatter(terms[2], ('seq', 'chan'), scatter_dimension=0, tiled=True)  119 us
    reduce_scatter x1, waiting for transfers between devices, body(): lax.psum_scatter(terms[1], ('seq', 'chan'), scatter_dimension=0, tiled=True)  118 us
    pallas_call x3, Pallas kernels, channel_call(): pl.pallas_call(kernel, name=name, grid=(blocks,), in_specs=specs, out_spe...  101 us
    reduce_scatter x1, waiting for transfers between devices, body(): lax.psum_scatter(terms[5], ('seq', 'chan'), scatter_dimension=0, tiled=True)  100 us
    dot_general x6, matrix products, back_dot(): lax.dot_general(left, right, (((1,), (1,)), ((), ())), preferred_element_...  65.8 us
  transfers between devices with their start and end apart: 15, of which 11 were waited for; matrix products, arithmetic and copies ran while one was open for 15% of the time, Pallas kernels for 0%

profile of v1, /device:TPU:0, one launch (start us, length us, event | category | flops | bytes accessed | tf_op | source)
XLA Modules:
  0.0 1517.0 jit_solution(6181027096531928887)
XLA Ops:
  14.1 48.9 %all-to-all-done = bf16[16,512,128]{2,1,0:T(8,128)(2,1)} async-done(((bf16[16,512,128]{2,1,0:T(8,128)(2,1)}), bf16[16,512,128]{2,1,0:T(8,128)(2,1)}, u32[]{:S(2)}, u32[]{:S(2)}) %all-to-all-start) | async-done | bytes 2097184 | tf_op jit(solution)/shard_map/all_to_all | solution.py:572
  100.7 15.8 %all-to-all-done.2 = bf16[16,512,128]{2,1,0:T(8,128)(2,1)} async-done(((bf16[16,512,128]{2,1,0:T(8,128)(2,1)}), bf16[16,512,128]{2,1,0:T(8,128)(2,1)}, u32[]{:S(2)}, u32[]{:S(2)}) %all-to-all-start.2) | async-done | bytes 2097184 | tf_op jit(solution)/shard_map/all_to_all | solution.py:573
  123.0 35.0 %recurrence_forward.1 = (bf16[2,512,1536]{2,1,0:T(8,128)(2,1)}, f32[2,512,1536]{2,1,0:T(8,128)}, f32[2,512,1536]{2,1,0:T(8,128)}, f32[2,512,1536]{2,1,0:T(8,128)}, f32[2,512,1536]{2,1,0:T(8,128)}) custom-call(f32[2,512,1536]{2,1,0:T(8,128)} %copy-done.1, f32[2,8,1536]{2,1,0:T(8,128)} %pad_convert_fusion.rim_ref, s32[2,512,128]{2,1,0:T(8,128)} %broadcast_in_dim.42.dist_ref, ...), custom_call_target="tpu_custom_call" | custom-call | flops 2415919104 | bytes 37683200 | tf_op jit(solution)/shard_map/recurrence_forward/pallas_call | solution.py:371
  222.1 26.5 %multiply_convert_fusion = (bf16[1024,3072]{1,0:T(8,128)(2,1)}, bf16[1024,3072]{1,0:T(8,128)(2,1)}, bf16[1024,3072]{1,0:T(8,128)(2,1)}) fusion(f32[1024,3072]{1,0:T(8,128)} %fusion.64, f32[1024,3072]{1,0:T(8,128)} %fusion.65, bf16[3072,1024]{1,0:T(8,128)(2,1)} %param.37, f32[128,8,8,128]{3,2,1,0:T(8,128)} %bitcast.130, pred[1024]{0:T(1024)(128)(4,1)S(1)} %lt.75), kind=kOutput, calls=%fused_computation.15 | convolution fusion | flops 6525288448 | bytes 54526976 | tf_op jit(solution)/shard_map/dot_general | solution.py:515
  248.6 12.2 fusion.66
  260.8 11.2 multiply_reduce_fusion
  279.3 23.5 %recurrence_adjoint.1 = (bf16[2,512,1536]{2,1,0:T(8,128)(2,1)}, f32[2,512,1536]{2,1,0:T(8,128)}, f32[2,512,1536]{2,1,0:T(8,128)}, f32[2,1,1536]{2,1,0:T(1,128)}) custom-call(f32[2,512,1536]{2,1,0:T(8,128)} %bitcast.139, f32[2,512,1536]{2,1,0:T(8,128)} %bitcast.138, f32[2,512,1536]{2,1,0:T(8,128)} %get-tuple-element.217.state_ref, ...), custom_call_target="tpu_custom_call" | custom-call | bytes 47833088 | tf_op jit(solution)/shard_map/recurrence_adjoint/pallas_call | solution.py:371
  313.3 42.8 %recurrence_backward.1 = (bf16[2,512,1536]{2,1,0:T(8,128)(2,1)}, f32[2,8,1536]{2,1,0:T(8,128)}, f32[2,8,1536]{2,1,0:T(8,128)}, f32[8,1536]{1,0:T(8,128)}, f32[1536,256]{1,0:T(8,128)}) custom-call(f32[2,512,1536]{2,1,0:T(8,128)} %get-tuple-element.221.local_ref, f32[2,512,1536]{2,1,0:T(8,128)} %get-tuple-element.222.back_ref, ...), custom_call_target="tpu_custom_call" | custom-call | flops 4831838208 | bytes 55255040 | tf_op jit(solution)/shard_map/recurrence_backward/pallas_call | solution.py:371
  415.5 12.3 fusion.68
  427.7 13.9 reshape.288
  441.7 12.2 fusion.69
  453.9 13.9 reshape.290
  468.2 13.5 fusion.59
  481.7 13.8 reshape.292
  495.5 12.2 add_convert_fusion.1
  537.4 31.5 %all-to-all-done.1 = bf16[2,512,1024]{1,0,2:T(2,128)(2,1)} async-done(((bf16[2,512,1024]{1,0,2:T(2,128)(2,1)}), bf16[2,512,1024]{1,0,2:T(2,128)(2,1)}, u32[]{:S(2)}, u32[]{:S(2)}) %all-to-all-start.1) | async-done | bytes 2097184 | tf_op jit(solution)/shard_map/all_to_all | solution.py:634
  579.0 63.3 %all-reduce.6 = (f32[1024]{0:T(1024)S(1)}, f32[1536]{0:T(1024)S(1)}, f32[1536]{0:T(1024)S(1)}, f32[1024]{0:T(1024)S(1)}) all-reduce(f32[1024]{0:T(1024)S(1)} %get-tuple-element.271, f32[1536]{0:T(1024)S(1)} %get-tuple-element.274, f32[1536]{0:T(1024)S(1)} %multiply_multiply_fusion.4, ...), channel_id=5, replica_groups=mesh['seq'=4,'chan'=8] {'seq','chan'}, use_global_device_ids=true, to_apply=%region_10.11.clone | all-reduce | flops 5120 | bytes 40960
  658.4 27.0 %reduce-scatter.20.cloned.1.call-done = f32[384,128]{1,0:T(8,128)} async-done(((f32[12288,128]{1,0:T(8,128)}), f32[384,128]{1,0:T(8,128)}) %reduce-scatter.20.cloned.1.call-update) | async-done | bytes 196624 | tf_op jit(solution)/shard_map/reduce_scatter | solution.py:726
  687.0 118.6 %reduce-scatter.16.cloned.1.call-done = f32[384,128]{1,0:T(8,128)} async-done(((f32[12288,128]{1,0:T(8,128)}), f32[384,128]{1,0:T(8,128)}) %reduce-scatter.16.cloned.1.call-update) | async-done | bytes 196624 | tf_op jit(solution)/shard_map/reduce_scatter | solution.py:720
  807.2 117.6 %reduce-scatter.14.cloned.1.call-done = f32[384,128]{1,0:T(8,128)} async-done(((f32[12288,128]{1,0:T(8,128)}), f32[384,128]{1,0:T(8,128)}) %reduce-scatter.14.cloned.1.call-update) | async-done | bytes 196624 | tf_op jit(solution)/shard_map/reduce_scatter | solution.py:719
  926.4 159.8 %reduce-scatter.22.cloned.1.call-done = f32[768,128]{1,0:T(8,128)} async-done(((f32[24576,128]{1,0:T(8,128)}), f32[768,128]{1,0:T(8,128)}) %reduce-scatter.22.cloned.1.call-update) | async-done | bytes 393232 | tf_op jit(solution)/shard_map/reduce_scatter | solution.py:728
  1088.1 158.6 %reduce-scatter.24.cloned.1.call-done = f32[768,128]{1,0:T(8,128)} async-done(((f32[24576,128]{1,0:T(8,128)}), f32[768,128]{1,0:T(8,128)}) %reduce-scatter.24.cloned.1.call-update) | async-done | bytes 393232 | tf_op jit(solution)/shard_map/reduce_scatter | solution.py:729
  1248.5 159.7 %reduce-scatter.26.cloned.1.call-done = f32[768,128]{1,0:T(8,128)} async-done(((f32[24576,128]{1,0:T(8,128)}), f32[768,128]{1,0:T(8,128)}) %reduce-scatter.26.cloned.1.call-update) | async-done | bytes 393232 | tf_op jit(solution)/shard_map/reduce_scatter | solution.py:730
  1410.1 100.2 %reduce-scatter.18.cloned.1.call-done = f32[48,192]{1,0:T(8,128)} async-done(((f32[1536,192]{1,0:T(8,128)}), f32[48,192]{1,0:T(8,128)}) %reduce-scatter.18.cloned.1.call-update) | async-done | bytes 36880 | tf_op jit(solution)/shard_map/reduce_scatter | solution.py:723
  (197 shorter events, 260.7 us)
Async XLA Ops:
  7.2 179.9 %copy-start = (bf16[1024,1536]{1,0:T(8,128)(2,1)S(1)}, bf16[1024,1536]{1,0:T(8,128)(2,1)}, u32[]{:S(2)}) copy-start(bf16[1024,1536]{1,0:T(8,128)(2,1)} %param.27) | copy-start | bytes 9437188
  7.2 60.4 %copy-start.12 = (f32[1536]{0:T(1024)S(1)}, f32[1536]{0:T(1024)}, u32[]{:S(2)}) copy-start(f32[1536]{0:T(1024)} %param.32) | copy-start | bytes 18436
  7.2 55.8 %all-to-all-start = ((bf16[16,512,128]{2,1,0:T(8,128)(2,1)}), bf16[16,512,128]{2,1,0:T(8,128)(2,1)}, u32[]{:S(2)}, u32[]{:S(2)}) async-start(bf16[16,512,128]{2,1,0:T(8,128)(2,1)} %param.21), calls=%async_computation | async-start | bytes 4194304 | tf_op jit(solution)/shard_map/all_to_all | solution.py:572
  63.0 53.4 %all-to-all-start.2 = ((bf16[16,512,128]{2,1,0:T(8,128)(2,1)}), bf16[16,512,128]{2,1,0:T(8,128)(2,1)}, u32[]{:S(2)}, u32[]{:S(2)}) async-start(bf16[16,512,128]{2,1,0:T(8,128)(2,1)} %param.22), calls=%async_computation.2 | async-start | bytes 4194304 | tf_op jit(solution)/shard_map/all_to_all | solution.py:573
  67.4 510.2 %reduce-scatter.30.cloned.1.call-start = ((), (), s32[]{:S(2)}) async-start(), calls=%async_computation.21 | async-start | bytes 811008
  86.7 12.6 copy-start.21
  86.7 12.6 copy-start.14
  86.7 12.6 copy-start.20
  95.8 25.5 %collective-permute-start = (bf16[2,3,1536]{2,1,0:T(4,128)(2,1)S(1)}, bf16[2,3,1536]{2,1,0:T(4,128)(2,1)S(1)}, u32[]{:S(2)}, u32[]{:S(2)}) collective-permute-start(bf16[2,3,1536]{2,1,0:T(4,128)(2,1)S(1)} %slice.50), channel_id=1, source_target_pairs={{0,8},{8,16},{16,24},{1,9},{9,17},{17,25},{2,10},{10,18},{18,26},{... | collective-permute-start | bytes 55304 | tf_op jit(solution)/shard_map/ppermute | solution.py:501
  100.7 86.4 %copy-start.18 = (f32[1,4,2,128]{3,1,2,0:T(4,128)}, f32[1,4,2,128]{3,1,2,0:T(4,128)S(1)}, u32[]{:S(2)}) copy-start(f32[1,4,2,128]{3,1,2,0:T(4,128)S(1)} %copy.73) | copy-start | bytes 12292
  248.6 12.2 copy-start.4
  248.6 12.2 copy-start.28
  279.3 31.1 %copy-start.10 = (f32[2,1536]{1,0:T(2,128)S(1)}, f32[2,1536]{1,0:T(2,128)}, u32[]{:S(2)}) copy-start(f32[2,1536]{1,0:T(2,128)} %custom-call.1) | copy-start | bytes 36868
  358.1 286.5 %reduce-scatter.28.cloned.1.call-start = ((), (), s32[]{:S(2)}) async-start(), calls=%async_computation.20 | async-start | bytes 811008
  360.2 325.2 %reduce-scatter.20.cloned.1.call-start = ((), (), s32[]{:S(2)}) async-start(), calls=%async_computation.16 | async-start | bytes 6488064 | tf_op jit(solution)/shard_map/reduce_scatter | solution.py:726
  376.7 428.9 %reduce-scatter.16.cloned.1.call-start = ((), (), s32[]{:S(2)}) async-start(), calls=%async_computation.14 | async-start | bytes 6488064 | tf_op jit(solution)/shard_map/reduce_scatter | solution.py:720
  392.5 532.4 %reduce-scatter.14.cloned.1.call-start = ((), (), s32[]{:S(2)}) async-start(), calls=%async_computation.13 | async-start | bytes 6488064 | tf_op jit(solution)/shard_map/reduce_scatter | solution.py:719
  393.4 5.7 collective-permute-start.1
  415.4 670.9 %reduce-scatter.22.cloned.1.call-start = ((), (), s32[]{:S(2)}) async-start(), calls=%async_computation.17 | async-start | bytes 12976128 | tf_op jit(solution)/shard_map/reduce_scatter | solution.py:728
  441.6 805.1 %reduce-scatter.24.cloned.1.call-start = ((), (), s32[]{:S(2)}) async-start(), calls=%async_computation.18 | async-start | bytes 12976128 | tf_op jit(solution)/shard_map/reduce_scatter | solution.py:729
  467.8 940.5 %reduce-scatter.26.cloned.1.call-start = ((), (), s32[]{:S(2)}) async-start(), calls=%async_computation.19 | async-start | bytes 12976128 | tf_op jit(solution)/shard_map/reduce_scatter | solution.py:730
  513.9 55.0 %all-to-all-start.1 = ((bf16[2,512,1024]{1,0,2:T(2,128)(2,1)}), bf16[2,512,1024]{1,0,2:T(2,128)(2,1)}, u32[]{:S(2)}, u32[]{:S(2)}) async-start(bf16[2,512,1024]{1,0,2:T(2,128)(2,1)} %copy.58), calls=%async_computation.1 | async-start | bytes 4194304 | tf_op jit(solution)/shard_map/all_to_all | solution.py:634
  568.9 83.3 %all-to-all-start.3 = ((bf16[2,512,1024]{1,0,2:T(2,128)(2,1)}), bf16[2,512,1024]{1,0,2:T(2,128)(2,1)}, u32[]{:S(2)}, u32[]{:S(2)}) async-start(bf16[2,512,1024]{1,0,2:T(2,128)(2,1)} %copy.61), calls=%async_computation.3 | async-start | bytes 4194304 | tf_op jit(solution)/shard_map/all_to_all | solution.py:701
  573.3 937.0 %reduce-scatter.18.cloned.1.call-start = ((), (), s32[]{:S(2)}) async-start(), calls=%async_computation.15 | async-start | bytes 1622016 | tf_op jit(solution)/shard_map/reduce_scatter | solution.py:723
  (25 other events, 158.7 us)
Sparse Core Ops, SparseCore 0:
  358.3 93.2 reduce-scatter.29
  456.7 106.9 reduce-scatter.27
  569.3 116.0 reduce-scatter.19
  691.8 113.7 reduce-scatter.15
  811.1 113.6 reduce-scatter.13
  931.7 154.5 reduce-scatter.21
  1092.3 154.3 reduce-scatter.23
  1253.8 154.4 reduce-scatter.25
  1414.1 96.1 reduce-scatter.17

commit v2 on v1

--- a/solution.py
+++ b/solution.py
@@ -478,21 +478,15 @@
         )
 
 
-def prefix(value, axis, join, neutral, backward):
+def carried(factor, value, axis, backward):
     count, mine = (lax.axis_size(axis), lax.axis_index(axis))
-    pieces = jax.tree.map(lambda part: lax.all_gather(part, axis), value)
-    if backward:
-        pieces = jax.tree.map(lambda part: part[::-1], pieces)
-        mine = count - 1 - mine
-    subtotal = jax.tree.map(
-        lambda part, zero: jnp.full_like(part, 0) + jnp.asarray(zero, part.dtype), value, neutral
-    )
-
-    def hop(position, subtotal):
-        longer = join(subtotal, jax.tree.map(lambda part: part[position], pieces))
-        return jax.tree.map(lambda new, old: jnp.where(position < mine, new, old), longer, subtotal)
-
-    return lax.fori_loop(0, count - 1, hop, subtotal)
+    pieces = lax.all_gather(jnp.stack([factor, value]), axis)
+    order = range(count - 1, 0, -1) if backward else range(count - 1)
+    total = jnp.zeros_like(value)
+    for place in order:
+        longer = pieces[place, 0] * total + pieces[place, 1]
+        total = jnp.where(place > mine if backward else place < mine, longer, total)
+    return total
 
 
 def passed_along(value, axis, steps):
@@ -501,14 +495,10 @@
     return lax.ppermute(value, axis, [(source, source + steps) for source in range(leading, last)])
 
 
-def as_sent(x):
-    return jax.tree.map(lambda a: a.astype(jnp.bfloat16) if a.dtype == jnp.float32 else a, x)
-
-
-def trans_dot(left, right):
+def weight_grad(left, right):
     return lax.dot_general(
         left, right, (((0,), (0,)), ((), ())), preferred_element_type=jnp.float32
-    )
+    ).astype(jnp.bfloat16)
 
 
 def back_dot(left, right):
@@ -525,28 +515,46 @@
     return jax.nn.gelu(value, approximate=True)
 
 
-def pair_join(earlier, later):
-    return (earlier[0] * later[0], later[0] * earlier[1] + later[1])
-
-
 def norm_back(grad_norm, normed, inverse, gain):
     scaled = grad_norm * gain
     mean_term = jnp.mean(scaled * normed, axis=1, keepdims=True)
-    return (inverse * (scaled - normed * mean_term), jnp.sum(grad_norm * normed, axis=0))
-
-
-def lane_rows(matrix):
-    return matrix.reshape(-1, LANES)
-
-
-def carry_forward(summary):
-    identity = (jnp.ones_like(summary[0]), jnp.zeros_like(summary[1]))
-    return prefix(summary, "seq", pair_join, identity, False)[1]
-
-
-def carry_backward(summary):
-    identity = (jnp.ones_like(summary[0]), jnp.zeros_like(summary[1]))
-    return prefix(summary, "seq", pair_join, identity, True)[1]
+    return inverse * (scaled - normed * mean_term)
+
+
+def halved(blocks, axis, bit, high, dtype):
+    count = lax.axis_size(axis)
+    mine = (lax.axis_index(axis) >> bit) & 1
+    half = blocks.shape[0] // 2
+    place = 0 if high else 1
+    pairs = blocks.reshape(((2, half) if high else (half, 2)) + blocks.shape[1:])
+    sent = lax.dynamic_index_in_dim(pairs, 1 - mine, place, keepdims=False)
+    kept = lax.dynamic_index_in_dim(pairs, mine, place, keepdims=False)
+    got = lax.ppermute(sent, axis, [(source, source ^ (1 << bit)) for source in range(count)])
+    return (kept.astype(jnp.float32) + got.astype(jnp.float32)).astype(dtype)
+
+
+def bits(axis):
+    return range(lax.axis_size(axis).bit_length() - 1)
+
+
+def core_summed(gradient):
+    devices = lax.axis_size(("seq", "zed", "core"))
+    blocks = gradient.reshape(devices, gradient.shape[0] // devices, gradient.shape[1])
+    return halved(blocks, "core", 0, False, gradient.dtype)
+
+
+def chips_summed(blocks, high):
+    seq, zed = (lax.axis_size("seq"), lax.axis_size("zed"))
+    low = blocks.dtype
+    seq_bits = reversed(bits("seq")) if high else bits("seq")
+    for bit in seq_bits:
+        outer = blocks.shape[0] // zed
+        blocks = blocks.reshape((outer, zed) + blocks.shape[1:])
+        blocks = halved(blocks, "seq", bit, high, low)
+        blocks = blocks.reshape((outer // 2 * zed,) + blocks.shape[2:])
+    for bit in bits("zed"):
+        blocks = halved(blocks, "zed", bit, False, jnp.float32 if bit == bits("zed")[-1] else low)
+    return blocks[0]
 
 
 def body(
@@ -569,8 +577,8 @@
     mlp_down,
 ):
     seq_x, seq_g = (
-        lax.all_to_all(tokens, "chan", split_axis=0, concat_axis=2, tiled=True),
-        lax.all_to_all(cotangent, "chan", split_axis=0, concat_axis=2, tiled=True),
+        lax.all_to_all(tokens, ("zed", "core"), split_axis=0, concat_axis=2, tiled=True),
+        lax.all_to_all(cotangent, ("zed", "core"), split_axis=0, concat_axis=2, tiled=True),
     )
     row_count, block_len, model_dim = seq_x.shape
     tok_count = row_count * block_len
@@ -617,7 +625,7 @@
     lru_in, rate_gate, input_gate, local_state, cum_coef = core.forward(
         branch_rows, rim, dist, params, wide_gates
     )
-    carry_in = carry_forward((cum_coef[:, -1, :], local_state[:, -1, :]))
+    carry_in = carried(cum_coef[:, -1, :], local_state[:, -1, :], "seq", False)
     entering = carry_in[:, None, :]
     state_rows = local_state + cum_coef * entering
     state_flat = state_rows.reshape(tok_count, rec_width)
@@ -633,25 +641,43 @@
     result = (resid_one + fwd_dot(hidden_low, mlp_down)).astype(jnp.bfloat16)
     output = lax.all_to_all(
         result.reshape(row_count, block_len, model_dim),
-        "chan",
+        ("zed", "core"),
         split_axis=2,
         concat_axis=0,
         tiled=True,
     )
     grad_out = jnp.where(is_valid, seq_g.reshape(tok_count, model_dim).astype(jnp.float32), 0.0)
     grad_low = grad_out.astype(jnp.bfloat16)
-    grad_down = trans_dot(hidden_low, grad_low)
+    grad_down = core_summed(weight_grad(hidden_low, grad_low))
     grad_hidden = back_dot(grad_low, mlp_down)
     _, gelu_pull = jax.vjp(gelu_fn, mlp_gate_pre)
     mgate_low = gelu_pull(grad_hidden * mlp_up_pre)[0].astype(jnp.bfloat16)
     mup_low = (grad_hidden * gelu_gate).astype(jnp.bfloat16)
-    grad_mgate = trans_dot(normed_low2, mgate_low)
-    grad_mup = trans_dot(normed_low2, mup_low)
+    grad_mgate = core_summed(weight_grad(normed_low2, mgate_low))
+    grad_mup = core_summed(weight_grad(normed_low2, mup_low))
+    chips = grad_down.shape[0]
+    parts = [
+        jnp.swapaxes(part.reshape(chips, part.shape[1], -1, model_dim), 1, 2).reshape(
+            chips, -1, model_dim
+        )
+        for part in (grad_mgate, grad_mup)
+    ]
+    merged = jnp.concatenate([*parts, grad_down], axis=1)
+    own = lax.psum_scatter(merged, ("seq", "zed"), scatter_dimension=0, tiled=True)[0]
+    own = own.astype(jnp.float32)
+    own_rows = model_dim // (2 * chips)
+    count = parts[0].shape[1]
+
+    def unfolded(part):
+        return jnp.swapaxes(part.reshape(-1, own_rows, model_dim), 0, 1).reshape(own_rows, -1)
+
+    sum_mgate, sum_mup = (unfolded(own[:count]), unfolded(own[count : 2 * count]))
+    sum_down = own[2 * count :]
     grad_norm2 = back_dot(mgate_low, mlp_gate) + back_dot(mup_low, mlp_up)
-    resid_part, grad_gain2 = norm_back(grad_norm2, normed_two, inv_two, norm2_gain)
+    resid_part = norm_back(grad_norm2, normed_two, inv_two, norm2_gain)
     grad_resid = grad_out + resid_part
     resid_low = grad_resid.astype(jnp.bfloat16)
-    grad_rout = trans_dot(mixed_low, resid_low)
+    sum_rout = chips_summed(core_summed(weight_grad(mixed_low, resid_low)), True)
     grad_mixed = back_dot(resid_low, recur_out)
     gate_low, back_local, back_cum, first_term = core.adjoint(
         grad_mixed.reshape(row_count, block_len, rec_width),
@@ -664,7 +690,7 @@
         params,
     )
     gate_low = gate_low.reshape(tok_count, rec_width)
-    carry_out = carry_backward((cum_coef[:, -1, :], first_term[:, 0, :]))
+    carry_out = carried(cum_coef[:, -1, :], first_term[:, 0, :], "seq", True)
     branch_local, tail, lead, channel_sums, gate_sums = core.backward(
         back_local,
         back_cum,
@@ -681,127 +707,90 @@
         params,
         wide_gates,
     )
-    grad_ckernel = channel_sums[:4]
-    grad_cbias = channel_sums[4]
-    grad_lbias = channel_sums[5:7]
-    grad_decay = 8.0 * jax.nn.sigmoid(-lru_decay) * channel_sums[7]
-    grad_lgates = jnp.concatenate(
-        [gate_sums[:, :head_size], gate_sums[:, LANES : LANES + head_size]], axis=1
-    )
-    from_next = passed_along(as_sent(lead[:, SUBLANES - rim_size :, :]), "seq", -1)
+    spare = jnp.swapaxes(channel_sums, 0, 1)
+    small = jnp.concatenate(
+        [gate_sums[:, :head_size], spare, gate_sums[:, head_size + SUBLANES :]], axis=1
+    )
+    own_small = chips_summed(core_summed(small), True)
+    sum_lgates = jnp.concatenate(
+        [own_small[:, :head_size], own_small[:, LANES : LANES + head_size]], axis=1
+    )
+    own_sums = jnp.swapaxes(own_small[:, head_size : head_size + SUBLANES], 0, 1)
+    from_next = passed_along(
+        lead[:, SUBLANES - rim_size :, :].astype(jnp.bfloat16), "seq", -1
+    )
     ending = tail + jnp.pad(from_next.astype(jnp.float32), ((0, 0), (SUBLANES - rim_size, 0), (0, 0)))
     branch_low = lax.dynamic_update_slice(
         branch_local, ending.astype(jnp.bfloat16), (0, block_len - SUBLANES, 0)
     ).reshape(tok_count, rec_width)
-    grad_rin = trans_dot(normed_low, branch_low)
-    grad_rgate = trans_dot(normed_low, gate_low)
+    sum_rin = chips_summed(core_summed(weight_grad(normed_low, branch_low)), False)
+    sum_rgate = chips_summed(core_summed(weight_grad(normed_low, gate_low)), False)
     grad_norm1 = back_dot(branch_low, recur_input) + back_dot(gate_low, recur_gate)
-    input_part, grad_gain1 = norm_back(grad_norm1, normed_one, inv_one, norm1_gain)
+    input_part = norm_back(grad_norm1, normed_one, inv_one, norm1_gain)
     grad_x = (grad_resid + input_part).astype(jnp.bfloat16).reshape(row_count, block_len, model_dim)
-    grad_tokens = lax.all_to_all(grad_x, "chan", split_axis=2, concat_axis=0, tiled=True)
-    terms = (
-        grad_gain1,
-        lane_rows(grad_rin),
-        lane_rows(grad_rgate),
-        grad_ckernel,
-        grad_cbias,
-        grad_lgates,
-        grad_lbias,
-        grad_decay,
-        lane_rows(grad_rout),
-        grad_gain2,
-        lane_rows(grad_mgate),
-        lane_rows(grad_mup),
-        lane_rows(grad_down),
-    )
-    summed = (
-        lax.psum_scatter(terms[0], ("seq", "chan"), scatter_dimension=0, tiled=True),
-        lax.psum_scatter(terms[1], ("seq", "chan"), scatter_dimension=0, tiled=True),
-        lax.psum_scatter(terms[2], ("seq", "chan"), scatter_dimension=0, tiled=True),
-        lax.psum_scatter(terms[3], ("seq", "chan"), scatter_dimension=1, tiled=True),
-        lax.psum_scatter(terms[4], ("seq", "chan"), scatter_dimension=0, tiled=True),
-        lax.psum_scatter(terms[5], ("seq", "chan"), scatter_dimension=0, tiled=True),
-        lax.psum_scatter(terms[6], ("seq", "chan"), scatter_dimension=1, tiled=True),
-        lax.psum_scatter(terms[7], ("seq", "chan"), scatter_dimension=0, tiled=True),
-        lax.psum_scatter(terms[8], ("seq", "chan"), scatter_dimension=0, tiled=True),
-        lax.psum_scatter(terms[9], ("seq", "chan"), scatter_dimension=0, tiled=True),
-        lax.psum_scatter(terms[10], ("seq", "chan"), scatter_dimension=0, tiled=True),
-        lax.psum_scatter(terms[11], ("seq", "chan"), scatter_dimension=0, tiled=True),
-        lax.psum_scatter(terms[12], ("seq", "chan"), scatter_dimension=0, tiled=True),
-    )
-    (
+    grad_tokens = lax.all_to_all(grad_x, ("zed", "core"), split_axis=2, concat_axis=0, tiled=True)
+    device = lax.axis_index(("seq", "zed", "core"))
+
+    def mine(array, size, axis=0):
+        return lax.dynamic_slice_in_dim(array, device * size, size, axis)
+
+    def weighed(weight, gradient):
+        return jnp.sum(mine(weight, own_rows).astype(jnp.float32) * gradient, axis=1)
+
+    sum_gain1 = (weighed(recur_input, sum_rin) + weighed(recur_gate, sum_rgate)) / mine(
+        norm1_gain, own_rows
+    )
+    sum_gain2 = (weighed(mlp_gate, sum_mgate) + weighed(mlp_up, sum_mup)) / mine(
+        norm2_gain, own_rows
+    )
+    own_channels = own_sums.shape[1]
+    sum_decay = 8.0 * jax.nn.sigmoid(-mine(lru_decay, own_channels)) * own_sums[7]
+    return (
+        output,
+        grad_tokens,
         sum_gain1,
         sum_rin,
         sum_rgate,
-        sum_ckernel,
-        sum_cbias,
+        own_sums[:4],
+        own_sums[4],
         sum_lgates,
-        sum_lbias,
+        own_sums[5:7],
         sum_decay,
         sum_rout,
         sum_gain2,
         sum_mgate,
         sum_mup,
         sum_down,
-    ) = summed
-    return (
-        output,
-        grad_tokens,
-        sum_gain1,
-        sum_rin.reshape(-1, rec_width),
-        sum_rgate.reshape(-1, rec_width),
-        sum_ckernel,
-        sum_cbias,
-        sum_lgates,
-        sum_lbias,
-        sum_decay,
-        sum_rout.reshape(-1, model_dim),
-        sum_gain2,
-        sum_mgate.reshape(-1, ffn_width),
-        sum_mup.reshape(-1, ffn_width),
-        sum_down.reshape(-1, model_dim),
     )
 
 
 def solution(mesh):
+    seq, chan = (mesh.shape["seq"], mesh.shape["chan"])
+    chips = jax.sharding.Mesh(mesh.devices.reshape(seq, chan // 2, 2), ("seq", "zed", "core"))
+    chan = ("zed", "core")
+    every = ("seq", "zed", "core")
+    activations = P(None, "seq", chan)
+    rows, columns, vector = (P(every, None), P(None, every), P(every))
     return jax.shard_map(
         body,
-        mesh=mesh,
-        in_specs=(
-            P(None, "seq", "chan"),
-            P(None, "seq", "chan"),
-            P("chan", None),
-            P("chan"),
-            P(),
-            P(),
-            P(),
-            P(),
-            P(),
-            P(),
-            P(),
-            P(),
-            P(),
-            P(),
-            P(),
-            P(),
-            P(),
-        ),
+        mesh=chips,
+        in_specs=(activations, activations, P(chan, None), P(chan)) + (P(),) * 13,
         out_specs=(
-            P(None, "seq", "chan"),
-            P(None, "seq", "chan"),
-            P(("seq", "chan")),
-            P(("seq", "chan"), None),
-            P(("seq", "chan"), None),
-            P(None, ("seq", "chan")),
-            P(("seq", "chan")),
-            P(("seq", "chan"), None),
-            P(None, ("seq", "chan")),
-            P(("seq", "chan")),
-            P(("seq", "chan"), None),
-            P(("seq", "chan")),
-            P(("seq", "chan"), None),
-            P(("seq", "chan"), None),
-            P(("seq", "chan"), None),
+            activations,
+            activations,
+            vector,
+            rows,
+            rows,
+            columns,
+            vector,
+            rows,
+            columns,
+            vector,
+            rows,
+            vector,
+            rows,
+            rows,
+            rows,
         ),
         check_vma=False,
     )

time: 1530 us -> 738 us (0.48)
  waiting for transfers between devices: 942 us -> 195 us
  blocking collectives: 87.5 us -> 17 us
  other arithmetic: 29.8 us -> 68.6 us
  starting transfers between devices: 25.5 us -> 58.4 us
  local copies, waits for them, and re-layouts: 131 us -> 107 us
  matrix products: 185 us -> 166 us
    reduce_scatter x7 -> x1, waiting for transfers between devices: 842 us -> 0.01 us  [body(): lax.psum_scatter(merged, ('seq', 'zed'), scatter_dimension=0, tiled=True)[0]]
    ppermute x0 -> x23, waiting for transfers between devices: none -> 131 us  [halved(): lax.ppermute(sent, axis, [(source, source ^ 1 << bit) for source in range...]
    unnamed x1 -> x0, blocking collectives: 63.3 us -> none
    reshape x12 -> x4, local copies, waits for them, and re-layouts: 72.9 us -> 20.8 us  [the longest x2 20.2 us: body(): part.reshape(chips, part.shape[1], -1, model_dim)]
    ppermute x0 -> x23, starting transfers between devices: none -> 33.8 us  [halved(): lax.ppermute(sent, axis, [(source, source ^ 1 << bit) for source in range...]
    all_to_all x4, waiting for transfers between devices: 96.1 us -> 64.6 us  [the longest x1 48.9 us: body(): lax.all_to_all(tokens, ('zed', 'core'), split_axis=0, concat_axis=2, tile...]
    convert_element_type x0 -> x16, other arithmetic: none -> 26.9 us  [the longest x15 26.8 us: halved(): return (kept.astype(jnp.float32) + got.astype(jnp.float32)).astype(dtype)]
    dot_general x6, matrix products: 64.6 us -> 44.3 us  [weight_grad(): lax.dot_general(left, right, (((0,), (0,)), ((), ())), preferred_element_...]
  transfers between devices with their start and end apart: 15 -> 30, of which waited for: 11 -> 15; matrix products, arithmetic and copies ran while one was open for 15% -> 29% of each run, Pallas kernels for 0% -> 9%
where the time goes in v2:
time: 738 us; the launch traced here: 729 us
  waiting for transfers between devices  195 us (26%)
  matrix products  166 us (22%)
  local copies, waits for them, and re-layouts  107 us (14%)
  Pallas kernels  101 us (14%)
  other arithmetic  68.6 us (9%)
  starting transfers between devices  58.4 us (8%)
  blocking collectives  17 us (2%)
  between operations  15.3 us (2%)
    ppermute x23, waiting for transfers between devices, halved(): lax.ppermute(sent, axis, [(source, source ^ 1 << bit) for source in range...  131 us
    pallas_call x3, Pallas kernels, channel_call(): pl.pallas_call(kernel, name=name, grid=(blocks,), in_specs=specs, out_spe...  101 us
    dot_general x6, matrix products, back_dot(): lax.dot_general(left, right, (((1,), (1,)), ((), ())), preferred_element_...  69.6 us
    all_to_all x1, waiting for transfers between devices, body(): lax.all_to_all(tokens, ('zed', 'core'), split_axis=0, concat_axis=2, tile...  48.9 us
    dot_general x6, matrix products, fwd_dot(): return jnp.dot(left, right, preferred_element_type=jnp.float32)  48.8 us
    dot_general x6, matrix products, weight_grad(): lax.dot_general(left, right, (((0,), (0,)), ((), ())), preferred_element_...  44.3 us
    ppermute x23, starting transfers between devices, halved(): lax.ppermute(sent, axis, [(source, source ^ 1 << bit) for source in range...  33.8 us
    convert_element_type x15, other arithmetic, halved(): return (kept.astype(jnp.float32) + got.astype(jnp.float32)).astype(dtype)  26.8 us
  transfers between devices with their start and end apart: 30, of which 15 were waited for; matrix products, arithmetic and copies ran while one was open for 29% of the time, Pallas kernels for 9%

profile of v2, /device:TPU:0, one launch (start us, length us, event | category | flops | bytes accessed | tf_op | source)
XLA Modules:
  0.0 728.9 jit_solution(2245336190043248057)
XLA Ops:
  14.1 48.9 %all-to-all-done = bf16[16,512,128]{2,1,0:T(8,128)(2,1)} async-done(((bf16[16,512,128]{2,1,0:T(8,128)(2,1)}), bf16[16,512,128]{2,1,0:T(8,128)(2,1)}, u32[]{:S(2)}, u32[]{:S(2)}) %all-to-all-start) | async-done | bytes 2097184 | tf_op jit(solution)/shard_map/all_to_all | solution.py:580
  100.7 15.7 %all-to-all-done.2 = bf16[16,512,128]{2,1,0:T(8,128)(2,1)} async-done(((bf16[16,512,128]{2,1,0:T(8,128)(2,1)}), bf16[16,512,128]{2,1,0:T(8,128)(2,1)}, u32[]{:S(2)}, u32[]{:S(2)}) %all-to-all-start.2) | async-done | bytes 2097184 | tf_op jit(solution)/shard_map/all_to_all | solution.py:581
  122.9 35.0 %recurrence_forward.1 = (bf16[2,512,1536]{2,1,0:T(8,128)(2,1)}, f32[2,512,1536]{2,1,0:T(8,128)}, f32[2,512,1536]{2,1,0:T(8,128)}, f32[2,512,1536]{2,1,0:T(8,128)}, f32[2,512,1536]{2,1,0:T(8,128)}) custom-call(f32[2,512,1536]{2,1,0:T(8,128)} %copy-done.1, f32[2,8,1536]{2,1,0:T(8,128)} %pad_convert_fusion.rim_ref, s32[2,512,128]{2,1,0:T(8,128)} %broadcast_in_dim.34.dist_ref, ...), custom_call_target="tpu_custom_call" | custom-call | flops 2415919104 | bytes 37683200 | tf_op jit(solution)/shard_map/recurrence_forward/pallas_call | solution.py:371
  159.8 8.6 %all-gather = f32[8,2,1536]{2,1,0:T(2,128)S(1)} all-gather(f32[2,2,1536]{2,1,0:T(2,128)S(1)} %copy.157), channel_id=2, replica_groups=mesh['seq'=4,'zed'=4,'core'=2] {'seq'}, dimensions={0}, use_global_device_ids=true | all-gather | bytes 122880 | tf_op jit(solution)/shard_map/all_gather | solution.py:483
  191.0 9.2 %fusion.85 = f32[1024,3072]{1,0:T(8,128)} fusion(bf16[1024,1024]{1,0:T(8,128)(2,1)S(1)} %multiply_convert_fusion.3, bf16[1024,3072]{1,0:T(8,128)(2,1)S(1)} %bitcast.381), kind=kOutput, calls=%fused_computation.228 | convolution fusion | flops 6442450944 | bytes 20971520 | tf_op jit(solution)/shard_map/dot_general | solution.py:511
  200.2 9.2 %fusion.84 = f32[1024,3072]{1,0:T(8,128)} fusion(bf16[1024,1024]{1,0:T(8,128)(2,1)S(1)} %multiply_convert_fusion.3, bf16[1024,3072]{1,0:T(8,128)(2,1)S(1)} %bitcast.379), kind=kOutput, calls=%fused_computation.227 | convolution fusion | flops 6442450944 | bytes 20971520 | tf_op jit(solution)/shard_map/dot_general | solution.py:511
  209.4 26.3 %multiply_convert_fusion = (bf16[1024,3072]{1,0:T(8,128)(2,1)}, bf16[1024,3072]{1,0:T(8,128)(2,1)}, bf16[1024,3072]{1,0:T(8,128)(2,1)}) fusion(f32[1024,3072]{1,0:T(8,128)} %fusion.84, f32[1024,3072]{1,0:T(8,128)} %fusion.85, bf16[3072,1024]{1,0:T(8,128)(2,1)} %param.33, f32[128,8,8,128]{3,2,1,0:T(8,128)} %bitcast.316, pred[1024]{0:T(1024)(128)(4,1)S(1)} %lt.142), kind=kOutput, calls=%fused_computation.9 | convolution fusion | flops 6525288448 | bytes 54526976 | tf_op jit(solution)/shard_map/dot_general | solution.py:505
  235.7 12.1 %fusion.86 = f32[1024,1024]{1,0:T(8,128)} fusion(bf16[1024,3072]{1,0:T(8,128)(2,1)} %get-tuple-element.142, bf16[1024,3072]{1,0:T(8,128)(2,1)} %param.31), kind=kOutput, calls=%fused_computation.229 | convolution fusion | flops 6442450944 | bytes 16777216 | tf_op jit(solution)/shard_map/dot_general | solution.py:505
  247.9 9.1 %convolution_convert_fusion.2 = bf16[1024,3072]{1,0:T(8,128)(2,1)} fusion(bf16[1024,1024]{1,0:T(8,128)(2,1)S(1)} %copy-done.22, bf16[1024,3072]{1,0:T(8,128)(2,1)S(1)} %copy-done.51), kind=kOutput, calls=%fused_computation.32 | convolution fusion | flops 6445596672 | bytes 14680064 | tf_op jit(solution)/shard_map/dot_general | solution.py:499
  256.9 10.8 %convolution_convert_fusion = bf16[3072,1024]{1,0:T(8,128)(2,1)S(1)} fusion(bf16[1024,3072]{1,0:T(8,128)(2,1)} %get-tuple-element.143, f32[128,8,8,128]{3,2,1,0:T(8,128)S(1)} %bitcast.317, pred[1024]{0:T(1024)(128)(4,1)S(1)} %lt.142), kind=kOutput, calls=%fused_computation.30 | convolution fusion | flops 6446645248 | bytes 16778240 | tf_op jit(solution)/shard_map/dot_general | solution.py:499
  271.3 10.0 %convolution_convert_fusion.1 = bf16[1024,3072]{1,0:T(8,128)(2,1)S(1)} fusion(bf16[1024,1024]{1,0:T(8,128)(2,1)S(1)} %copy-done.22, bf16[1024,3072]{1,0:T(8,128)(2,1)} %get-tuple-element.141), kind=kOutput, calls=%fused_computation.31 | convolution fusion | flops 6445596672 | bytes 14680064 | tf_op jit(solution)/shard_map/dot_general | solution.py:499
  281.4 14.2 %multiply_reduce_fusion.1 = (f32[1024]{0:T(1024)S(1)}, f32[1024,1024]{1,0:T(8,128)S(1)}) fusion(f32[1024,1024]{1,0:T(8,128)S(1)} %copy-done.7, f32[1024]{0:T(1024)S(1)} %add_rsqrt_fusion, f32[1024]{0:T(1024)S(1)} %copy-done.42, f32[1024,1024]{1,0:T(8,128)} %fusion.86, bf16[1024,3072]{1,0:T(8,128)(2,1)} %get-tuple-element.141, bf16[1024,3072]{1,0:T(8,128)(2,1)} %param.32), kind=kOutput, calls=%fused_computation.43 | convolution fusion | flops 6447692800 | bytes 25178112 | tf_op jit(solution)/shard_map/dot_general | solution.py:505
  309.8 23.2 %recurrence_adjoint.1 = (bf16[2,512,1536]{2,1,0:T(8,128)(2,1)}, f32[2,512,1536]{2,1,0:T(8,128)}, f32[2,512,1536]{2,1,0:T(8,128)}, f32[2,1,1536]{2,1,0:T(1,128)}) custom-call(f32[2,512,1536]{2,1,0:T(8,128)} %bitcast.337, f32[2,512,1536]{2,1,0:T(8,128)} %bitcast.336, f32[2,512,1536]{2,1,0:T(8,128)} %get-tuple-element.29.state_ref, ...), custom_call_target="tpu_custom_call" | custom-call | bytes 47833088 | tf_op jit(solution)/shard_map/recurrence_adjoint/pallas_call | solution.py:371
  333.9 8.4 %all-gather.1 = f32[8,2,1536]{2,1,0:T(2,128)S(1)} all-gather(f32[2,2,1536]{2,1,0:T(2,128)S(1)} %copy.165), channel_id=3, replica_groups=mesh['seq'=4,'zed'=4,'core'=2] {'seq'}, dimensions={0}, use_global_device_ids=true | all-gather | bytes 122880 | tf_op jit(solution)/shard_map/all_gather | solution.py:483
  342.9 42.8 %recurrence_backward.1 = (bf16[2,512,1536]{2,1,0:T(8,128)(2,1)}, f32[2,8,1536]{2,1,0:T(8,128)}, f32[2,8,1536]{2,1,0:T(8,128)}, f32[8,1536]{1,0:T(8,128)}, f32[1536,256]{1,0:T(8,128)}) custom-call(f32[2,512,1536]{2,1,0:T(8,128)} %get-tuple-element.32.local_ref, f32[2,512,1536]{2,1,0:T(8,128)} %get-tuple-element.33.back_ref, f32[2,1,1536]{2,1,0:T(1,128)} %copy.166.out_ref, ...), custom_call_target="tpu_custom_call" | custom-call | flops 4831838208 | bytes 55255040 | tf_op jit(solution)/shard_map/recurrence_backward/pallas_call | solution.py:371
  396.6 10.1 %reshape.509 = bf16[16,32,3,1024]{3,2,1,0:T(4,128)(2,1)} reshape(bf16[16,32,3072]{2,1,0:T(8,128)(2,1)} %fusion.18) | data formatting | bytes 6291456 | tf_op jit(solution)/shard_map/reshape | solution.py:660
  417.7 10.1 %reshape.511 = bf16[16,32,3,1024]{3,2,1,0:T(4,128)(2,1)} reshape(bf16[16,32,3072]{2,1,0:T(8,128)(2,1)} %fusion.17) | data formatting | bytes 6291456 | tf_op jit(solution)/shard_map/reshape | solution.py:660
  440.1 12.6 %add_convert_fusion.1 = bf16[1024,1024]{1,0:T(8,128)(2,1)} fusion(f32[1024,1024]{1,0:T(8,128)} %copy-done.6, bf16[1024,3072]{1,0:T(8,128)(2,1)} %get-tuple-element.143, bf16[3072,1024]{1,0:T(8,128)(2,1)} %param.33), kind=kOutput, calls=%fused_computation.45 | convolution fusion | flops 6444548096 | bytes 18874368 | tf_op jit(solution)/shard_map/dot_general | solution.py:511
  504.8 8.9 %collective-permute-done.13 = f32[2,4,48,256]{3,2,1,0:T(8,128)S(1)} collective-permute-done((f32[2,4,48,256]{3,2,1,0:T(8,128)S(1)}, f32[2,4,48,256]{3,2,1,0:T(8,128)S(1)}, u32[]{:S(2)}, u32[]{:S(2)}) %collective-permute-start.13) | collective-permute-done | bytes 393248 | tf_op jit(solution)/shard_map/ppermute | solution.py:532
  561.5 19.4 %collective-permute-done.18 = bf16[2,4,48,1024]{3,2,1,0:T(8,128)(2,1)S(1)} collective-permute-done((bf16[2,4,48,1024]{3,2,1,0:T(8,128)(2,1)S(1)}, bf16[2,4,48,1024]{3,2,1,0:T(8,128)(2,1)S(1)}, u32[]{:S(2)}, u32[]{:S(2)}) %collective-permute-start.18) | collective-permute-done | bytes 786464 | tf_op jit(solution)/shard_map/ppermute | solution.py:532
  587.7 19.3 %collective-permute-done.3 = bf16[2,4,32,1536]{3,2,1,0:T(8,128)(2,1)S(1)} collective-permute-done((bf16[2,4,32,1536]{3,2,1,0:T(8,128)(2,1)S(1)}, bf16[2,4,32,1536]{3,2,1,0:T(8,128)(2,1)S(1)}, u32[]{:S(2)}, u32[]{:S(2)}) %collective-permute-start.3) | collective-permute-done | bytes 786464 | tf_op jit(solution)/shard_map/ppermute | solution.py:532
  609.3 9.5 %collective-permute-done.19 = bf16[1,4,48,1024]{3,2,1,0:T(8,128)(2,1)S(1)} collective-permute-done((bf16[1,4,48,1024]{3,2,1,0:T(8,128)(2,1)S(1)}, bf16[1,4,48,1024]{3,2,1,0:T(8,128)(2,1)S(1)}, u32[]{:S(2)}, u32[]{:S(2)}) %collective-permute-start.19) | collective-permute-done | bytes 393248 | tf_op jit(solution)/shard_map/ppermute | solution.py:532
  638.3 39.3 %collective-permute-done.10 = bf16[2,32,1536]{2,1,0:T(8,128)(2,1)S(1)} collective-permute-done((bf16[2,32,1536]{2,1,0:T(8,128)(2,1)S(1)}, bf16[2,32,1536]{2,1,0:T(8,128)(2,1)S(1)}, u32[]{:S(2)}, u32[]{:S(2)}) %collective-permute-start.10) | collective-permute-done | bytes 196640 | tf_op jit(solution)/shard_map/ppermute | solution.py:532
  677.7 8.9 %collective-permute-start.11 = (bf16[1,32,1536]{2,1,0:T(8,128)(2,1)S(1)}, bf16[1,32,1536]{2,1,0:T(8,128)(2,1)S(1)}, u32[]{:S(2)}, u32[]{:S(2)}) collective-permute-start(bf16[1,32,1536]{2,1,0:T(8,128)(2,1)S(1)} %constant_dynamic-slice_fusion.4), channel_id=1, source_target_pairs={{0,4},{2,6},{4,0},{6,2},{1,5},{3,7},{5,1},{7,3},{8,12},{10,14},{12... | collective-permute-start | bytes 294920 | tf_op jit(solution)/shard_map/ppermute | solution.py:532
  (299 shorter events, 291.9 us)
Async XLA Ops:
  7.2 55.8 %all-to-all-start = ((bf16[16,512,128]{2,1,0:T(8,128)(2,1)}), bf16[16,512,128]{2,1,0:T(8,128)(2,1)}, u32[]{:S(2)}, u32[]{:S(2)}) async-start(bf16[16,512,128]{2,1,0:T(8,128)(2,1)} %param.17), calls=%async_computation | async-start | bytes 4194304 | tf_op jit(solution)/shard_map/all_to_all | solution.py:580
  63.0 53.4 %all-to-all-start.2 = ((bf16[16,512,128]{2,1,0:T(8,128)(2,1)}), bf16[16,512,128]{2,1,0:T(8,128)(2,1)}, u32[]{:S(2)}, u32[]{:S(2)}) async-start(bf16[16,512,128]{2,1,0:T(8,128)(2,1)} %param.18), calls=%async_computation.2 | async-start | bytes 4194304 | tf_op jit(solution)/shard_map/all_to_all | solution.py:581
  67.4 648.3 %reduce-scatter.2.cloned.1.call-start = ((), (), s32[]{:S(2)}) async-start(), calls=%async_computation.5 | async-start | bytes 10027008 | tf_op jit(solution)/shard_map/reduce_scatter | solution.py:666
  95.9 25.3 %collective-permute-start = (bf16[2,3,1536]{2,1,0:T(4,128)(2,1)S(1)}, bf16[2,3,1536]{2,1,0:T(4,128)(2,1)S(1)}, u32[]{:S(2)}, u32[]{:S(2)}) collective-permute-start(bf16[2,3,1536]{2,1,0:T(4,128)(2,1)S(1)} %slice.207), channel_id=1, source_target_pairs={{0,8},{8,16},{16,24},{1,9},{9,17},{17,25},{2,10},{10,18},{18,26},{... | collective-permute-start | bytes 55304 | tf_op jit(solution)/shard_map/ppermute | solution.py:495
  269.9 161.5 %collective-permute-start.24 = (bf16[16,96,1024]{2,1,0:T(8,128)(2,1)}, bf16[16,96,1024]{2,1,0:T(8,128)(2,1)}, u32[]{:S(2)}, u32[]{:S(2)}) collective-permute-start(bf16[16,96,1024]{2,1,0:T(8,128)(2,1)} %dynamic-slice_bitcast_fusion), channel_id=1, source_target_pairs={{0,1},{1,0},{2,3},{3,2},{4,5},{5,4},{6,7},{7,6},{8,9},{9,8},{10,11... | collective-permute-start | bytes 9437192 | tf_op jit(solution)/shard_map/ppermute | solution.py:532
  301.4 89.5 %collective-permute-start.22 = (bf16[16,32,3072]{2,1,0:T(8,128)(2,1)}, bf16[16,32,3072]{2,1,0:T(8,128)(2,1)}, u32[]{:S(2)}, u32[]{:S(2)}) collective-permute-start(bf16[16,32,3072]{2,1,0:T(8,128)(2,1)} %dynamic-slice_bitcast_fusion.2), channel_id=1, source_target_pairs={{0,1},{1,0},{2,3},{3,2},{4,5},{5,4},{6,7},{7,6},{8,9},{9,8},{10,11... | collective-permute-start | bytes 9437192 | tf_op jit(solution)/shard_map/ppermute | solution.py:532
  301.4 110.6 %collective-permute-start.23 = (bf16[16,32,3072]{2,1,0:T(8,128)(2,1)}, bf16[16,32,3072]{2,1,0:T(8,128)(2,1)}, u32[]{:S(2)}, u32[]{:S(2)}) collective-permute-start(bf16[16,32,3072]{2,1,0:T(8,128)(2,1)} %dynamic-slice_bitcast_fusion.1), channel_id=1, source_target_pairs={{0,1},{1,0},{2,3},{3,2},{4,5},{5,4},{6,7},{7,6},{8,9},{9,8},{10,11... | collective-permute-start | bytes 9437192 | tf_op jit(solution)/shard_map/ppermute | solution.py:532
  458.9 160.8 %all-to-all-start.1 = ((bf16[2,512,1024]{1,0,2:T(2,128)(2,1)}), bf16[2,512,1024]{1,0,2:T(2,128)(2,1)}, u32[]{:S(2)}, u32[]{:S(2)}) async-start(bf16[2,512,1024]{1,0,2:T(2,128)(2,1)} %copy.159), calls=%async_computation.1 | async-start | bytes 4194304 | tf_op jit(solution)/shard_map/all_to_all | solution.py:642
  473.2 78.1 %collective-permute-start.17 = (bf16[16,48,1024]{2,1,0:T(8,128)(2,1)}, bf16[16,48,1024]{2,1,0:T(8,128)(2,1)}, u32[]{:S(2)}, u32[]{:S(2)}) collective-permute-start(bf16[16,48,1024]{2,1,0:T(8,128)(2,1)} %dynamic-slice_bitcast_fusion.3), channel_id=1, source_target_pairs={{0,1},{1,0},{2,3},{3,2},{4,5},{5,4},{6,7},{7,6},{8,9},{9,8},{10,11... | collective-permute-start | bytes 4718600 | tf_op jit(solution)/shard_map/ppermute | solution.py:532
  479.8 18.5 %collective-permute-start.12 = (f32[16,48,256]{2,1,0:T(8,128)S(1)}, f32[16,48,256]{2,1,0:T(8,128)S(1)}, u32[]{:S(2)}, u32[]{:S(2)}) collective-permute-start(f32[16,48,256]{2,1,0:T(8,128)S(1)} %dynamic-slice_bitcast_fusion.7), channel_id=1, source_target_pairs={{0,1},{1,0},{2,3},{3,2},{4,5},{5,4},{6,7},{7,6},{8,9},{9,8},{10,11... | collective-permute-start | bytes 2359304 | tf_op jit(solution)/shard_map/ppermute | solution.py:532
  485.9 69.6 %collective-permute-start.7 = (bf16[16,32,1536]{2,1,0:T(8,128)(2,1)}, bf16[16,32,1536]{2,1,0:T(8,128)(2,1)}, u32[]{:S(2)}, u32[]{:S(2)}) collective-permute-start(bf16[16,32,1536]{2,1,0:T(8,128)(2,1)} %dynamic-slice_bitcast_fusion.4), channel_id=1, source_target_pairs={{0,1},{1,0},{2,3},{3,2},{4,5},{5,4},{6,7},{7,6},{8,9},{9,8},{10,11... | collective-permute-start | bytes 4718600 | tf_op jit(solution)/shard_map/ppermute | solution.py:532
  530.4 16.8 %collective-permute-start.16 = (f32[1,48,256]{2,1,0:T(8,128)S(1)}, f32[1,48,256]{2,1,0:T(8,128)S(1)}, u32[]{:S(2)}, u32[]{:S(2)}) collective-permute-start(f32[1,48,256]{2,1,0:T(8,128)S(1)} %constant_dynamic-slice_fusion.2), channel_id=1, source_target_pairs={{0,4},{2,6},{4,0},{6,2},{1,5},{3,7},{5,1},{7,3},{8,12},{10,14},{12... | collective-permute-start | bytes 147464 | tf_op jit(solution)/shard_map/ppermute | solution.py:532
  540.3 18.5 %collective-permute-start.2 = (bf16[16,32,1536]{2,1,0:T(8,128)(2,1)}, bf16[16,32,1536]{2,1,0:T(8,128)(2,1)}, u32[]{:S(2)}, u32[]{:S(2)}) collective-permute-start(bf16[16,32,1536]{2,1,0:T(8,128)(2,1)} %dynamic-slice_bitcast_fusion.5), channel_id=1, source_target_pairs={{0,1},{1,0},{2,3},{3,2},{4,5},{5,4},{6,7},{7,6},{8,9},{9,8},{10,11... | collective-permute-start | bytes 4718600 | tf_op jit(solution)/shard_map/ppermute | solution.py:532
  554.0 26.9 %collective-permute-start.18 = (bf16[2,4,48,1024]{3,2,1,0:T(8,128)(2,1)S(1)}, bf16[2,4,48,1024]{3,2,1,0:T(8,128)(2,1)S(1)}, u32[]{:S(2)}, u32[]{:S(2)}) collective-permute-start(bf16[2,4,48,1024]{3,2,1,0:T(8,128)(2,1)S(1)} %dynamic-slice_bitcast_fusion.6), channel_id=1, source_target_pairs={{0,16},{8,24},{16,0},{24,8},{1,17},{9,25},{17,1},{25,9},{2,18},{10... | collective-permute-start | bytes 2359304 | tf_op jit(solution)/shard_map/ppermute | solution.py:532
  557.4 28.4 %collective-permute-start.8 = (bf16[2,4,32,1536]{3,2,1,0:T(8,128)(2,1)S(1)}, bf16[2,4,32,1536]{3,2,1,0:T(8,128)(2,1)S(1)}, u32[]{:S(2)}, u32[]{:S(2)}) collective-permute-start(bf16[2,4,32,1536]{3,2,1,0:T(8,128)(2,1)S(1)} %dynamic-slice_bitcast_fusion.8), channel_id=1, source_target_pairs={{0,8},{8,0},{16,24},{24,16},{1,9},{9,1},{17,25},{25,17},{2,10},{10... | collective-permute-start | bytes 2359304 | tf_op jit(solution)/shard_map/ppermute | solution.py:532
  560.8 46.3 %collective-permute-start.3 = (bf16[2,4,32,1536]{3,2,1,0:T(8,128)(2,1)S(1)}, bf16[2,4,32,1536]{3,2,1,0:T(8,128)(2,1)S(1)}, u32[]{:S(2)}, u32[]{:S(2)}) collective-permute-start(bf16[2,4,32,1536]{3,2,1,0:T(8,128)(2,1)S(1)} %dynamic-slice_bitcast_fusion.9), channel_id=1, source_target_pairs={{0,8},{8,0},{16,24},{24,16},{1,9},{9,1},{17,25},{25,17},{2,10},{10... | collective-permute-start | bytes 2359304 | tf_op jit(solution)/shard_map/ppermute | solution.py:532
  581.3 37.5 %collective-permute-start.19 = (bf16[1,4,48,1024]{3,2,1,0:T(8,128)(2,1)S(1)}, bf16[1,4,48,1024]{3,2,1,0:T(8,128)(2,1)S(1)}, u32[]{:S(2)}, u32[]{:S(2)}) collective-permute-start(bf16[1,4,48,1024]{3,2,1,0:T(8,128)(2,1)S(1)} %constant_dynamic-slice_fusion.1), channel_id=1, source_target_pairs={{0,8},{8,0},{16,24},{24,16},{1,9},{9,1},{17,25},{25,17},{2,10},{10... | collective-permute-start | bytes 1179656 | tf_op jit(solution)/shard_map/ppermute | solution.py:532
  586.8 37.4 %collective-permute-start.9 = (bf16[1,4,32,1536]{3,2,1,0:T(8,128)(2,1)}, bf16[1,4,32,1536]{3,2,1,0:T(8,128)(2,1)}, u32[]{:S(2)}, u32[]{:S(2)}) collective-permute-start(bf16[1,4,32,1536]{3,2,1,0:T(8,128)(2,1)} %constant_dynamic-slice_fusion.5), channel_id=1, source_target_pairs={{0,16},{8,24},{16,0},{24,8},{1,17},{9,25},{17,1},{25,9},{2,18},{10... | collective-permute-start | bytes 1179656 | tf_op jit(solution)/shard_map/ppermute | solution.py:532
  609.0 18.6 %collective-permute-start.4 = (bf16[1,4,32,1536]{3,2,1,0:T(8,128)(2,1)}, bf16[1,4,32,1536]{3,2,1,0:T(8,128)(2,1)}, u32[]{:S(2)}, u32[]{:S(2)}) collective-permute-start(bf16[1,4,32,1536]{3,2,1,0:T(8,128)(2,1)} %constant_dynamic-slice_fusion.7), channel_id=1, source_target_pairs={{0,16},{8,24},{16,0},{24,8},{1,17},{9,25},{17,1},{25,9},{2,18},{10... | collective-permute-start | bytes 1179656 | tf_op jit(solution)/shard_map/ppermute | solution.py:532
  619.7 89.8 %all-to-all-start.3 = ((bf16[2,512,1024]{1,0,2:T(2,128)(2,1)}), bf16[2,512,1024]{1,0,2:T(2,128)(2,1)}, u32[]{:S(2)}, u32[]{:S(2)}) async-start(bf16[2,512,1024]{1,0,2:T(2,128)(2,1)} %copy.167), calls=%async_computation.3 | async-start | bytes 4194304 | tf_op jit(solution)/shard_map/all_to_all | solution.py:731
  625.5 52.1 %collective-permute-start.10 = (bf16[2,32,1536]{2,1,0:T(8,128)(2,1)S(1)}, bf16[2,32,1536]{2,1,0:T(8,128)(2,1)S(1)}, u32[]{:S(2)}, u32[]{:S(2)}) collective-permute-start(bf16[2,32,1536]{2,1,0:T(8,128)(2,1)S(1)} %dynamic-slice_bitcast_fusion.12), channel_id=1, source_target_pairs={{0,2},{2,0},{4,6},{6,4},{1,3},{3,1},{5,7},{7,5},{8,10},{10,8},{12,... | collective-permute-start | bytes 589832 | tf_op jit(solution)/shard_map/ppermute | solution.py:532
  628.8 57.8 %collective-permute-start.5 = (bf16[2,32,1536]{2,1,0:T(8,128)(2,1)S(1)}, bf16[2,32,1536]{2,1,0:T(8,128)(2,1)S(1)}, u32[]{:S(2)}, u32[]{:S(2)}) collective-permute-start(bf16[2,32,1536]{2,1,0:T(8,128)(2,1)S(1)} %dynamic-slice_bitcast_fusion.13), channel_id=1, source_target_pairs={{0,2},{2,0},{4,6},{6,4},{1,3},{3,1},{5,7},{7,5},{8,10},{10,8},{12,... | collective-permute-start | bytes 589832 | tf_op jit(solution)/shard_map/ppermute | solution.py:532
  636.1 61.0 %collective-permute-start.21 = (bf16[1,48,1024]{2,1,0:T(8,128)(2,1)S(1)}, bf16[1,48,1024]{2,1,0:T(8,128)(2,1)S(1)}, u32[]{:S(2)}, u32[]{:S(2)}) collective-permute-start(bf16[1,48,1024]{2,1,0:T(8,128)(2,1)S(1)} %constant_dynamic-slice_fusion), channel_id=1, source_target_pairs={{0,4},{2,6},{4,0},{6,2},{1,5},{3,7},{5,1},{7,3},{8,12},{10,14},{12... | collective-permute-start | bytes 294920 | tf_op jit(solution)/shard_map/ppermute | solution.py:532
  677.7 21.5 %collective-permute-start.11 = (bf16[1,32,1536]{2,1,0:T(8,128)(2,1)S(1)}, bf16[1,32,1536]{2,1,0:T(8,128)(2,1)S(1)}, u32[]{:S(2)}, u32[]{:S(2)}) collective-permute-start(bf16[1,32,1536]{2,1,0:T(8,128)(2,1)S(1)} %constant_dynamic-slice_fusion.4), channel_id=1, source_target_pairs={{0,4},{2,6},{4,0},{6,2},{1,5},{3,7},{5,1},{7,3},{8,12},{10,14},{12... | collective-permute-start | bytes 294920 | tf_op jit(solution)/shard_map/ppermute | solution.py:532
  (62 other events, 765.4 us)
Sparse Core Ops, SparseCore 0:
  440.3 249.0 reduce-scatter.1

commit v3 on v2

--- a/solution.py
+++ b/solution.py
@@ -478,6 +478,364 @@
         )
 
 
+MESH = pl.DeviceIdType.MESH
+
+
+class Corners:
+    def __init__(self, seq, zed):
+        self.seq_bits, self.zed_bits = (seq.bit_length() - 1, zed.bit_length() - 1)
+        self.count = self.seq_bits + self.zed_bits
+        self.dims = (2,) * self.count
+        self.low = tuple(range(self.seq_bits))[::-1] + tuple(range(self.seq_bits, self.count))[::-1]
+        self.high = tuple(range(self.seq_bits)) + tuple(range(self.seq_bits, self.count))[::-1]
+
+    def place(self, dim):
+        if dim < self.seq_bits:
+            return ("seq", 2 ** (self.seq_bits - 1 - dim))
+        return ("zed", 2 ** (self.count - 1 - dim))
+
+    def bit(self, dim):
+        axis, weight = self.place(dim)
+        return lax.rem(lax.div(lax.axis_index(axis), weight), 2)
+
+    def partner(self, dim):
+        axis, weight = self.place(dim)
+        return {axis: lax.axis_index(axis) + weight * (1 - 2 * self.bit(dim))}
+
+
+def reduce_kernel(corners, orders, *refs):
+    streams = len(orders)
+    stages = corners.count + 1
+    given, outs, rest = (refs[:streams], refs[streams : 2 * streams], refs[2 * streams :])
+    owns, rest = (rest[:streams], rest[streams:])
+    slots, (send_sem, recv_sem, load_sem) = (rest[:-3], rest[-3:])
+    core = lax.axis_index("core")
+    partners = [{"core": 1 - core}] + [corners.partner(dim) for dim in range(corners.count)]
+    barrier = pltpu.get_barrier_semaphore()
+    for partner in partners:
+        pl.semaphore_signal(barrier, inc=1, device_id=partner, device_id_type=MESH)
+    pl.semaphore_wait(barrier, len(partners))
+
+    def indices(order, stage, last):
+        fixed = {dim: corners.bit(dim) for dim in order[: stage - 1]}
+        if last is not None:
+            fixed[order[stage - 1]] = last
+        return tuple(fixed.get(dim, slice(None)) for dim in range(corners.count))
+
+    def copy(stream, stage):
+        order = orders[stream]
+        if stage == 0:
+            source = given[stream].at[(slice(None),) * corners.count + (1 - core,)]
+            target = {"core": 1 - core}
+        else:
+            dim = order[stage - 1]
+            source = owns[stream].at[indices(order, stage, 1 - corners.bit(dim))]
+            target = corners.partner(dim)
+        return pltpu.make_async_remote_copy(
+            src_ref=source,
+            dst_ref=slots[stream * stages + stage],
+            send_sem=send_sem.at[stream, stage],
+            recv_sem=recv_sem.at[stream, stage],
+            device_id=target,
+            device_id_type=MESH,
+        )
+
+    def load(stream):
+        return pltpu.make_async_copy(
+            given[stream].at[(slice(None),) * corners.count + (core,)],
+            owns[stream],
+            load_sem.at[stream],
+        )
+
+    for stream in range(streams):
+        copy(stream, 0).start()
+        load(stream).start()
+    for stage in range(stages):
+        for stream in range(streams):
+            order = orders[stream]
+            own, slot = (owns[stream], slots[stream * stages + stage])
+            if stage == 0:
+                load(stream).wait()
+            copy(stream, stage).wait_recv()
+            left = [dim for dim in range(corners.count) if dim not in order[:stage]]
+            fixed = {dim: corners.bit(dim) for dim in order[:stage]}
+            if left:
+
+                def add(index, carry, own=own, slot=slot, left=left, fixed=fixed):
+                    part = {
+                        dim: lax.rem(lax.div(index, 2 ** (len(left) - 1 - place)), 2)
+                        for place, dim in enumerate(left)
+                    }
+                    mine = tuple({**fixed, **part}[dim] for dim in range(corners.count))
+                    come = tuple(part[dim] for dim in left)
+                    total = own[mine].astype(jnp.float32) + slot[come].astype(jnp.float32)
+                    own[mine] = total.astype(own.dtype)
+                    return carry
+
+                lax.fori_loop(0, 2 ** len(left), add, 0)
+                copy(stream, stage + 1).start()
+            else:
+                mine = tuple(fixed[dim] for dim in range(corners.count))
+                outs[stream][...] = own[mine].astype(jnp.float32) + slot[...].astype(jnp.float32)
+    for stage in range(stages):
+        for stream in range(streams):
+            copy(stream, stage).wait_send()
+
+
+def reduce_streams(gradients, highs):
+    corners = Corners(lax.axis_size("seq"), lax.axis_size("zed"))
+    devices = 2 ** (corners.count + 1)
+    orders = [corners.high if high else corners.low for high in highs]
+    blocks = [
+        g.reshape(corners.dims + (2, g.shape[0] // devices, g.shape[1])) for g in gradients
+    ]
+    outs = [jax.ShapeDtypeStruct(b.shape[-2:], jnp.float32) for b in blocks]
+    owns = [pltpu.VMEM(corners.dims + b.shape[-2:], b.dtype) for b in blocks]
+    slots = [
+        pltpu.VMEM((2,) * min(corners.count, corners.count - stage) + b.shape[-2:], b.dtype)
+        for b in blocks
+        for stage in range(corners.count + 1)
+    ]
+    grid = (len(blocks), corners.count + 1)
+    moved = sum(math.prod(g.shape) * g.dtype.itemsize for g in gradients)
+    return pl.pallas_call(
+        functools.partial(reduce_kernel, corners, orders),
+        name="reduce_streams",
+        in_specs=[pl.BlockSpec(memory_space=pl.ANY)] * len(blocks),
+        out_specs=[pl.BlockSpec(memory_space=pltpu.VMEM)] * len(blocks),
+        out_shape=outs,
+        scratch_shapes=owns
+        + slots
+        + [
+            pltpu.SemaphoreType.DMA(grid),
+            pltpu.SemaphoreType.DMA(grid),
+            pltpu.SemaphoreType.DMA((len(blocks),)),
+        ],
+        compiler_params=pltpu.CompilerParams(
+            collective_id=1, has_side_effects=True, vmem_limit_bytes=VMEM_BYTES
+        ),
+        cost_estimate=pl.CostEstimate(flops=0, bytes_accessed=20 * moved, transcendentals=0),
+    )(*blocks)
+
+
+def grads_kernel(
+    normed_ref,
+    dgate_ref,
+    dup_ref,
+    hidden_ref,
+    gout_ref,
+    mixed_ref,
+    dres_ref,
+    out_ref,
+    turned_ref,
+    made_wide,
+    made_down,
+    made_out,
+    come_wide,
+    come_down,
+    come_out,
+    send_sem,
+    recv_sem,
+    store_sem,
+):
+    step = pl.program_id(0)
+    core = lax.axis_index("core")
+    other = {"core": 1 - core}
+    wide_rows, down_rows, out_rows = (made_wide.shape[3], made_down.shape[3], made_out.shape[3])
+    wides, downs, lasts = (come_wide.shape[0], come_down.shape[0], come_out.shape[0])
+    total = wides + downs + lasts
+    down_at, out_at = (wides * wide_rows, wides * wide_rows + down_rows)
+
+    def exchange(made, come, index, slot):
+        return pltpu.make_async_remote_copy(
+            src_ref=made.at[lax.rem(index, 2), 1 - core],
+            dst_ref=come.at[index],
+            send_sem=send_sem.at[slot],
+            recv_sem=recv_sem.at[slot],
+            device_id=other,
+            device_id_type=MESH,
+        )
+
+    def store_wide(index):
+        return pltpu.make_async_copy(
+            come_wide.at[index],
+            out_ref.at[:, pl.ds(pl.multiple_of(index * wide_rows, wide_rows), wide_rows)],
+            store_sem.at[index],
+        )
+
+    def store_down(index):
+        chips = come_down.shape[1]
+        return pltpu.make_async_copy(
+            come_down.at[index],
+            out_ref.at[pl.ds(index * chips, chips), pl.ds(down_at, down_rows)],
+            store_sem.at[index + wides],
+        )
+
+    def store_out(index):
+        chips = come_out.shape[1]
+        return pltpu.make_async_copy(
+            come_out.at[index],
+            out_ref.at[pl.ds(index * chips, chips), pl.ds(out_at, out_rows)],
+            store_sem.at[index + wides + downs],
+        )
+
+    @pl.when(step == 0)
+    def _():
+        barrier = pltpu.get_barrier_semaphore()
+        pl.semaphore_signal(barrier, inc=1, device_id=other, device_id_type=MESH)
+        pl.semaphore_wait(barrier, 1)
+        turned_ref[...] = normed_ref[...].T
+
+    def product_wide(source, index):
+        made = made_wide.at[lax.rem(index, 2)]
+        chips, rows = (made.shape[1], made.shape[2])
+        tile = 256
+
+        def column(place, carry):
+            at = pl.ds(pl.multiple_of(place * tile, tile), tile)
+            part = jnp.dot(turned_ref[...], source[:, at], preferred_element_type=jnp.float32)
+            part = part.astype(jnp.bfloat16).reshape(chips, 2, rows, tile)
+            made[0, :, :, at] = part[:, 0]
+            made[1, :, :, at] = part[:, 1]
+            return carry
+
+        lax.fori_loop(0, source.shape[1] // tile, column, 0)
+
+    def product_tall(left, right, made_all, index):
+        made = made_all.at[lax.rem(index, 2)]
+        chips, rows = (made.shape[1], made.shape[2])
+        tile = 256
+
+        def column(place, carry):
+            at = pl.ds(pl.multiple_of(place * tile, tile), tile)
+            part = lax.dot_general(
+                left[...], right[:, at], (((0,), (0,)), ((), ())), preferred_element_type=jnp.float32
+            )
+            part = part.astype(jnp.bfloat16).reshape(chips, 2, rows, tile)
+            made[0, :, :, at] = part[:, 0]
+            made[1, :, :, at] = part[:, 1]
+            return carry
+
+        lax.fori_loop(0, right.shape[1] // tile, column, 0)
+
+    half = wides // 2
+
+    @pl.when(step < half)
+    def _():
+        product_wide(dgate_ref, step)
+
+    @pl.when((step >= half) & (step < wides))
+    def _():
+        product_wide(dup_ref, step)
+
+    @pl.when(step < wides)
+    def _():
+        exchange(made_wide, come_wide, step, step).start()
+
+    @pl.when((step >= wides) & (step < wides + downs))
+    def _():
+        product_tall(hidden_ref, gout_ref, made_down, step - wides)
+        exchange(made_down, come_down, step - wides, step).start()
+
+    @pl.when((step >= wides + downs) & (step < total))
+    def _():
+        product_tall(mixed_ref, dres_ref, made_out, step - wides - downs)
+        exchange(made_out, come_out, step - wides - downs, step).start()
+
+    def finish(made, come, index, slot, store):
+        exchange(made, come, index, slot).wait()
+        mine = made.at[lax.rem(index, 2), core]
+        arrived = come.at[index]
+
+        def add(chip, carry):
+            both = mine[chip].astype(jnp.float32) + arrived[chip].astype(jnp.float32)
+            arrived[chip] = both.astype(jnp.bfloat16)
+            return carry
+
+        lax.fori_loop(0, come.shape[1], add, 0)
+        store(index).start()
+
+    before = step - 1
+
+    @pl.when((before >= 0) & (before < wides))
+    def _():
+        finish(made_wide, come_wide, before, before, store_wide)
+
+    @pl.when((before >= wides) & (before < wides + downs))
+    def _():
+        finish(made_down, come_down, before - wides, before, store_down)
+
+    @pl.when(before >= wides + downs)
+    def _():
+        finish(made_out, come_out, before - wides - downs, before, store_out)
+
+    @pl.when(step == total)
+    def _():
+        for index in range(wides):
+            store_wide(index).wait()
+        for index in range(downs):
+            store_down(index).wait()
+        for index in range(lasts):
+            store_out(index).wait()
+
+
+def block_gradients(normed, dgate, dup, hidden, gout, mixed, dres):
+    tokens, model = normed.shape
+    ffn, rec = (hidden.shape[1], mixed.shape[1])
+    chips = lax.axis_size("seq") * lax.axis_size("zed")
+    devices = 2 * chips
+    wide_rows, down_rows, out_rows = (model // devices, ffn // devices, rec // devices)
+    chunk = 768
+    wides, downs, lasts = (2 * ffn // model, ffn // chunk, rec // chunk)
+    half = wides // 2
+    down_chips, out_chips = (chunk // (2 * down_rows), chunk // (2 * out_rows))
+    rows = wides * wide_rows + down_rows + out_rows
+    low = jnp.bfloat16
+
+    def whole(array):
+        return pl.BlockSpec(array.shape, lambda s: (0, 0), pipeline_mode=pl.Buffered(1))
+
+    def part(columns, first, count):
+        return pl.BlockSpec((tokens, columns), lambda s: (0, jnp.clip(s - first, 0, count - 1)))
+
+    total = wides + downs + lasts
+    flops = 2 * tokens * model * (3 * ffn + rec)
+    arrays = (normed, dgate, dup, hidden, gout, mixed, dres)
+    moved = sum(math.prod(a.shape) * 2 for a in arrays) + chips * rows * model * 2
+    return pl.pallas_call(
+        grads_kernel,
+        name="block_gradients",
+        grid=(total + 1,),
+        in_specs=[
+            whole(normed),
+            part(model, 0, half),
+            part(model, half, half),
+            part(chunk, wides, downs),
+            whole(gout),
+            part(chunk, wides + downs, lasts),
+            whole(dres),
+        ],
+        out_specs=pl.BlockSpec(memory_space=pl.ANY),
+        out_shape=jax.ShapeDtypeStruct((chips, rows, model), low),
+        scratch_shapes=[
+            pltpu.VMEM((model, tokens), low),
+            pltpu.VMEM((2, 2, chips, wide_rows, model), low),
+            pltpu.VMEM((2, 2, down_chips, down_rows, model), low),
+            pltpu.VMEM((2, 2, out_chips, out_rows, model), low),
+            pltpu.VMEM((wides, chips, wide_rows, model), low),
+            pltpu.VMEM((downs, down_chips, down_rows, model), low),
+            pltpu.VMEM((lasts, out_chips, out_rows, model), low),
+            pltpu.SemaphoreType.DMA((total,)),
+            pltpu.SemaphoreType.DMA((total,)),
+            pltpu.SemaphoreType.DMA((total,)),
+        ],
+        compiler_params=pltpu.CompilerParams(
+            collective_id=2, has_side_effects=True, vmem_limit_bytes=VMEM_BYTES
+        ),
+        cost_estimate=pl.CostEstimate(flops=flops, bytes_accessed=moved, transcendentals=0),
+    )(*arrays)
+
+
 def carried(factor, value, axis, backward):
     count, mine = (lax.axis_size(axis), lax.axis_index(axis))
     pieces = lax.all_gather(jnp.stack([factor, value]), axis)
@@ -521,40 +879,10 @@
     return inverse * (scaled - normed * mean_term)
 
 
-def halved(blocks, axis, bit, high, dtype):
-    count = lax.axis_size(axis)
-    mine = (lax.axis_index(axis) >> bit) & 1
-    half = blocks.shape[0] // 2
-    place = 0 if high else 1
-    pairs = blocks.reshape(((2, half) if high else (half, 2)) + blocks.shape[1:])
-    sent = lax.dynamic_index_in_dim(pairs, 1 - mine, place, keepdims=False)
-    kept = lax.dynamic_index_in_dim(pairs, mine, place, keepdims=False)
-    got = lax.ppermute(sent, axis, [(source, source ^ (1 << bit)) for source in range(count)])
-    return (kept.astype(jnp.float32) + got.astype(jnp.float32)).astype(dtype)
-
-
-def bits(axis):
-    return range(lax.axis_size(axis).bit_length() - 1)
-
-
-def core_summed(gradient):
-    devices = lax.axis_size(("seq", "zed", "core"))
-    blocks = gradient.reshape(devices, gradient.shape[0] // devices, gradient.shape[1])
-    return halved(blocks, "core", 0, False, gradient.dtype)
-
-
-def chips_summed(blocks, high):
-    seq, zed = (lax.axis_size("seq"), lax.axis_size("zed"))
-    low = blocks.dtype
-    seq_bits = reversed(bits("seq")) if high else bits("seq")
-    for bit in seq_bits:
-        outer = blocks.shape[0] // zed
-        blocks = blocks.reshape((outer, zed) + blocks.shape[1:])
-        blocks = halved(blocks, "seq", bit, high, low)
-        blocks = blocks.reshape((outer // 2 * zed,) + blocks.shape[2:])
-    for bit in bits("zed"):
-        blocks = halved(blocks, "zed", bit, False, jnp.float32 if bit == bits("zed")[-1] else low)
-    return blocks[0]
+def scattered(gradient):
+    return lax.psum_scatter(
+        gradient, ("seq", "zed", "core"), scatter_dimension=0, tiled=True
+    ).astype(jnp.float32)
 
 
 def body(
@@ -648,36 +976,23 @@
     )
     grad_out = jnp.where(is_valid, seq_g.reshape(tok_count, model_dim).astype(jnp.float32), 0.0)
     grad_low = grad_out.astype(jnp.bfloat16)
-    grad_down = core_summed(weight_grad(hidden_low, grad_low))
     grad_hidden = back_dot(grad_low, mlp_down)
     _, gelu_pull = jax.vjp(gelu_fn, mlp_gate_pre)
     mgate_low = gelu_pull(grad_hidden * mlp_up_pre)[0].astype(jnp.bfloat16)
     mup_low = (grad_hidden * gelu_gate).astype(jnp.bfloat16)
-    grad_mgate = core_summed(weight_grad(normed_low2, mgate_low))
-    grad_mup = core_summed(weight_grad(normed_low2, mup_low))
-    chips = grad_down.shape[0]
-    parts = [
-        jnp.swapaxes(part.reshape(chips, part.shape[1], -1, model_dim), 1, 2).reshape(
-            chips, -1, model_dim
-        )
-        for part in (grad_mgate, grad_mup)
-    ]
-    merged = jnp.concatenate([*parts, grad_down], axis=1)
-    own = lax.psum_scatter(merged, ("seq", "zed"), scatter_dimension=0, tiled=True)[0]
-    own = own.astype(jnp.float32)
-    own_rows = model_dim // (2 * chips)
-    count = parts[0].shape[1]
-
-    def unfolded(part):
-        return jnp.swapaxes(part.reshape(-1, own_rows, model_dim), 0, 1).reshape(own_rows, -1)
-
-    sum_mgate, sum_mup = (unfolded(own[:count]), unfolded(own[count : 2 * count]))
-    sum_down = own[2 * count :]
     grad_norm2 = back_dot(mgate_low, mlp_gate) + back_dot(mup_low, mlp_up)
     resid_part = norm_back(grad_norm2, normed_two, inv_two, norm2_gain)
     grad_resid = grad_out + resid_part
     resid_low = grad_resid.astype(jnp.bfloat16)
-    sum_rout = chips_summed(core_summed(weight_grad(mixed_low, resid_low)), True)
+    devices = lax.axis_size(("seq", "zed", "core"))
+    own_rows = model_dim // devices
+    tiled = own_rows % (2 * SUBLANES) == 0 and ffn_width % model_dim == 0
+    if tiled:
+        merged = block_gradients(
+            normed_low2, mgate_low, mup_low, hidden_low, grad_low, mixed_low, resid_low
+        )
+        merged, resid_low = lax.optimization_barrier((merged, resid_low))
+        merged = lax.psum_scatter(merged, "seq", scatter_dimension=0, tiled=True)
     grad_mixed = back_dot(resid_low, recur_out)
     gate_low, back_local, back_cum, first_term = core.adjoint(
         grad_mixed.reshape(row_count, block_len, rec_width),
@@ -711,11 +1026,6 @@
     small = jnp.concatenate(
         [gate_sums[:, :head_size], spare, gate_sums[:, head_size + SUBLANES :]], axis=1
     )
-    own_small = chips_summed(core_summed(small), True)
-    sum_lgates = jnp.concatenate(
-        [own_small[:, :head_size], own_small[:, LANES : LANES + head_size]], axis=1
-    )
-    own_sums = jnp.swapaxes(own_small[:, head_size : head_size + SUBLANES], 0, 1)
     from_next = passed_along(
         lead[:, SUBLANES - rim_size :, :].astype(jnp.bfloat16), "seq", -1
     )
@@ -723,12 +1033,45 @@
     branch_low = lax.dynamic_update_slice(
         branch_local, ending.astype(jnp.bfloat16), (0, block_len - SUBLANES, 0)
     ).reshape(tok_count, rec_width)
-    sum_rin = chips_summed(core_summed(weight_grad(normed_low, branch_low)), False)
-    sum_rgate = chips_summed(core_summed(weight_grad(normed_low, gate_low)), False)
+    grad_rin = weight_grad(normed_low, branch_low)
+    grad_rgate = weight_grad(normed_low, gate_low)
     grad_norm1 = back_dot(branch_low, recur_input) + back_dot(gate_low, recur_gate)
     input_part = norm_back(grad_norm1, normed_one, inv_one, norm1_gain)
     grad_x = (grad_resid + input_part).astype(jnp.bfloat16).reshape(row_count, block_len, model_dim)
+    if tiled:
+        merged, grad_x = lax.optimization_barrier((merged, grad_x))
+        merged = lax.psum_scatter(merged, "zed", scatter_dimension=0, tiled=True)
     grad_tokens = lax.all_to_all(grad_x, ("zed", "core"), split_axis=2, concat_axis=0, tiled=True)
+    if tiled:
+        sum_rgate, sum_rin, own_small = reduce_streams(
+            (grad_rgate, grad_rin, small.astype(jnp.bfloat16)), (False, True, False)
+        )
+        own = merged[0].astype(jnp.float32)
+        count = ffn_width // model_dim * own_rows
+
+        def unfolded(part):
+            return jnp.swapaxes(part.reshape(-1, own_rows, model_dim), 0, 1).reshape(own_rows, -1)
+
+        sum_mgate, sum_mup = (unfolded(own[:count]), unfolded(own[count : 2 * count]))
+        sum_down = own[2 * count : 2 * count + ffn_width // devices]
+        sum_rout = own[2 * count + ffn_width // devices :]
+    else:
+        sum_mgate, sum_mup, sum_down, sum_rout, sum_rgate, sum_rin = (
+            scattered(weight_grad(left, right))
+            for left, right in (
+                (normed_low2, mgate_low),
+                (normed_low2, mup_low),
+                (hidden_low, grad_low),
+                (mixed_low, resid_low),
+                (normed_low, gate_low),
+                (normed_low, branch_low),
+            )
+        )
+        own_small = scattered(small)
+    sum_lgates = jnp.concatenate(
+        [own_small[:, :head_size], own_small[:, LANES : LANES + head_size]], axis=1
+    )
+    own_sums = jnp.swapaxes(own_small[:, head_size : head_size + SUBLANES], 0, 1)
     device = lax.axis_index(("seq", "zed", "core"))
 
     def mine(array, size, axis=0):

time: 738 us -> 636 us (0.86)
  Pallas kernels: 101 us -> 208 us
  waiting for transfers between devices: 195 us -> 128 us
  local copies, waits for them, and re-layouts: 107 us -> 53.9 us
  starting transfers between devices: 58.4 us -> 25.9 us
  matrix products: 166 us -> 135 us
  other arithmetic: 68.6 us -> 44.1 us
    ppermute x23 -> x0, waiting for transfers between devices: 131 us -> none  [halved(): lax.ppermute(sent, axis, [(source, source ^ 1 << bit) for source in range...]
    pallas_call x0 -> x2, Pallas kernels: none -> 106 us  [the longest x1 59.3 us: reduce_streams(): pl.pallas_call(functools.partial(reduce_kernel, corners, orders), name='r...]
    all_to_all x1, waiting for transfers between devices: 0.01 us -> 63.1 us  [body(): lax.all_to_all(result.reshape(row_count, block_len, model_dim), ('zed', '...]
    ppermute x23 -> x0, starting transfers between devices: 33.8 us -> none  [halved(): lax.ppermute(sent, axis, [(source, source ^ 1 << bit) for source in range...]
    dot_general x6 -> x2, matrix products: 44.3 us -> 12.8 us  [weight_grad(): lax.dot_general(left, right, (((0,), (0,)), ((), ())), preferred_element_...]
    reshape x3 -> x0, local copies, waits for them, and re-layouts: 26.4 us -> none  [the longest x2 20.2 us: body(): part.reshape(chips, part.shape[1], -1, model_dim)]
    convert_element_type x16 -> x3, other arithmetic: 26.9 us -> 7 us  [the longest x1 3.64 us: body(): resid_low = grad_resid.astype(jnp.bfloat16)]
    squeeze x23 -> x0, local copies, waits for them, and re-layouts: 14.9 us -> none  [halved(): sent = lax.dynamic_index_in_dim(pairs, 1 - mine, place, keepdims=False)]
  transfers between devices with their start and end apart: 30 -> 8, of which waited for: 15 -> 3; matrix products, arithmetic and copies ran while one was open for 29% -> 20% of each run, Pallas kernels for 9% -> 20%
where the time goes in v3:
time: 636 us; the launch traced here: 627 us
  Pallas kernels  208 us (33%)
  matrix products  135 us (21%)
  waiting for transfers between devices  128 us (20%)
  local copies, waits for them, and re-layouts  53.9 us (8%)
  other arithmetic  44.1 us (7%)
  starting transfers between devices  25.9 us (4%)
  blocking collectives  17.5 us (3%)
  between operations  15 us (2%)
    pallas_call x3, Pallas kernels, channel_call(): pl.pallas_call(kernel, name=name, grid=(blocks,), in_specs=specs, out_spe...  103 us
    dot_general x6, matrix products, back_dot(): lax.dot_general(left, right, (((1,), (1,)), ((), ())), preferred_element_...  63.5 us
    all_to_all x1, waiting for transfers between devices, body(): lax.all_to_all(result.reshape(row_count, block_len, model_dim), ('zed', '...  63.1 us
    pallas_call x1, Pallas kernels, reduce_streams(): pl.pallas_call(functools.partial(reduce_kernel, corners, orders), name='r...  59.3 us
    dot_general x6, matrix products, fwd_dot(): return jnp.dot(left, right, preferred_element_type=jnp.float32)  54.8 us
    all_to_all x1, waiting for transfers between devices, body(): lax.all_to_all(tokens, ('zed', 'core'), split_axis=0, concat_axis=2, tile...  48.9 us
    pallas_call x1, Pallas kernels, block_gradients(): pl.pallas_call(grads_kernel, name='block_gradients', grid=(total + 1,), i...  46.3 us
    all_gather x2, blocking collectives, carried(): pieces = lax.all_gather(jnp.stack([factor, value]), axis)  17.5 us
  transfers between devices with their start and end apart: 8, of which 3 were waited for; matrix products, arithmetic and copies ran while one was open for 20% of the time, Pallas kernels for 20%

profile of v3, /device:TPU:0, one launch (start us, length us, event | category | flops | bytes accessed | tf_op | source)
XLA Modules:
  0.0 627.3 jit_solution(5481183720906597148)
XLA Ops:
  7.3 6.6 %all-to-all-start = ((bf16[16,512,128]{2,1,0:T(8,128)(2,1)}), bf16[16,512,128]{2,1,0:T(8,128)(2,1)}, u32[]{:S(2)}, u32[]{:S(2)}) async-start(bf16[16,512,128]{2,1,0:T(8,128)(2,1)} %param.17), calls=%async_computation | async-start | bytes 4194304 | tf_op jit(solution)/shard_map/all_to_all | solution.py:908
  14.1 48.9 %all-to-all-done = bf16[16,512,128]{2,1,0:T(8,128)(2,1)} async-done(((bf16[16,512,128]{2,1,0:T(8,128)(2,1)}), bf16[16,512,128]{2,1,0:T(8,128)(2,1)}, u32[]{:S(2)}, u32[]{:S(2)}) %all-to-all-start) | async-done | bytes 2097184 | tf_op jit(solution)/shard_map/all_to_all | solution.py:908
  76.6 6.7 %multiply_convert_fusion.2 = (bf16[8,2,512,128]{3,0,2,1:T(8,128)(2,1)}, f32[2,512,8,128]{3,2,1,0:T(8,128)}, f32[8,2,512,128]{3,0,2,1:T(8,128)}) fusion(f32[8,128]{1,0:T(8,128)S(1)} %bitcast.239, f32[2,512]{1,0:T(2,128)S(1)} %get-tuple-element.135, f32[8,2,512,128]{3,2,1,0:T(8,128)S(1)} %bitcast_convert_fusion), kind=kLoop, calls=%fused_computation.28 | loop fusion | flops 3145728 | bytes 14688256 | tf_op jit(solution)/shard_map/convert.23
  88.3 6.3 %fusion.18.branch_ref = f32[2,512,1536]{2,1,0:T(8,128)S(1)} fusion(bf16[1024,1536]{1,0:T(8,128)(2,1)} %param.22, f32[2,512,1024]{2,1,0:T(8,128)} %reshape.446, f32[1024]{0:T(1024)S(1)} %copy-done.28, f32[2,512]{1,0:T(2,128)S(1)} %get-tuple-element.135), kind=kOutput, calls=%fused_computation.44 | convolution fusion | flops 3224371200 | bytes 13639680 | tf_op jit(solution)/shard_map/dot_general | solution.py:869
  100.7 15.8 %all-to-all-done.2 = bf16[16,512,128]{2,1,0:T(8,128)(2,1)} async-done(((bf16[16,512,128]{2,1,0:T(8,128)(2,1)}), bf16[16,512,128]{2,1,0:T(8,128)(2,1)}, u32[]{:S(2)}, u32[]{:S(2)}) %all-to-all-start.2) | async-done | bytes 2097184 | tf_op jit(solution)/shard_map/all_to_all | solution.py:909
  123.1 35.2 %recurrence_forward.1 = (bf16[2,512,1536]{2,1,0:T(8,128)(2,1)}, f32[2,512,1536]{2,1,0:T(8,128)}, f32[2,512,1536]{2,1,0:T(8,128)}, f32[2,512,1536]{2,1,0:T(8,128)}, f32[2,512,1536]{2,1,0:T(8,128)}) custom-call(f32[2,512,1536]{2,1,0:T(8,128)} %copy-done.1, f32[2,8,1536]{2,1,0:T(8,128)} %pad_convert_fusion.rim_ref, s32[2,512,128]{2,1,0:T(8,128)} %broadcast_in_dim.34.dist_ref, ...), custom_call_target="tpu_custom_call" | custom-call | flops 2415919104 | bytes 37683200 | tf_op jit(solution)/shard_map/recurrence_forward/pallas_call | solution.py:371
  160.2 8.5 %all-gather = f32[8,2,1536]{2,1,0:T(2,128)S(1)} all-gather(f32[2,2,1536]{2,1,0:T(2,128)S(1)} %copy.94), channel_id=2, replica_groups=mesh['seq'=4,'zed'=4,'core'=2] {'seq'}, dimensions={0}, use_global_device_ids=true | all-gather | bytes 122880 | tf_op jit(solution)/shard_map/all_gather | solution.py:841
  170.0 6.2 multiply_add_fusion
  176.2 9.2 %fusion.15 = (bf16[1024,1536]{1,0:T(8,128)(2,1)S(1)}, f32[1024,1536]{1,0:T(8,128)}) fusion(f32[2,512,1536]{2,1,0:T(8,128)S(1)} %multiply_add_fusion, bf16[1024,1536]{1,0:T(8,128)(2,1)} %param.23, f32[128,8,8,128]{3,2,1,0:T(8,128)S(1)} %bitcast.202, f32[1024]{0:T(1024)S(1)} %copy-done.28, f32[1024]{0:T(1024)S(1)} %bitcast.233), kind=kOutput, calls=%fused_computation.21 | convolution fusion | flops 3240099840 | bytes 23076864 | tf_op jit(solution)/shard_map/dot_general | solution.py:869
  189.8 14.7 %fusion.67 = f32[1024,3072]{1,0:T(8,128)} fusion(bf16[1024,1024]{1,0:T(8,128)(2,1)S(1)} %multiply_convert_fusion.3.normed_ref, bf16[1024,3072]{1,0:T(8,128)(2,1)} %param.31), kind=kOutput, calls=%fused_computation.163 | convolution fusion | flops 6442450944 | bytes 20971520 | tf_op jit(solution)/shard_map/dot_general | solution.py:869
  204.6 9.1 %fusion.68 = f32[1024,3072]{1,0:T(8,128)} fusion(bf16[1024,1024]{1,0:T(8,128)(2,1)S(1)} %multiply_convert_fusion.3.normed_ref, bf16[1024,3072]{1,0:T(8,128)(2,1)S(1)} %bitcast.238), kind=kOutput, calls=%fused_computation.164 | convolution fusion | flops 6442450944 | bytes 20971520 | tf_op jit(solution)/shard_map/dot_general | solution.py:869
  213.7 23.9 %multiply_convert_fusion = (bf16[1024,3072]{1,0:T(8,128)(2,1)}, bf16[1024,3072]{1,0:T(8,128)(2,1)}, bf16[1024,3072]{1,0:T(8,128)(2,1)}) fusion(f32[1024,3072]{1,0:T(8,128)} %fusion.67, f32[1024,3072]{1,0:T(8,128)} %fusion.68, bf16[1024,1024]{1,0:T(8,128)(2,1)S(1)} %copy-done.9, bf16[3072,1024]{1,0:T(8,128)(2,1)} %param.33), kind=kOutput, calls=%fused_computation.9 | convolution fusion | flops 6524239872 | bytes 52428800 | tf_op jit(solution)/shard_map/dot_general | solution.py:863
  237.5 10.8 %fusion.69 = f32[1024,1024]{1,0:T(8,128)S(1)} fusion(bf16[1024,3072]{1,0:T(8,128)(2,1)} %get-tuple-element.124.dgate_ref, bf16[1024,3072]{1,0:T(8,128)(2,1)} %param.31), kind=kOutput, calls=%fused_computation.165 | convolution fusion | flops 6442450944 | bytes 16777216 | tf_op jit(solution)/shard_map/dot_general | solution.py:863
  248.3 11.4 %multiply_reduce_fusion.1 = (f32[1024]{0:T(1024)S(1)}, f32[1024,1024]{1,0:T(8,128)S(1)}) fusion(f32[1024,1024]{1,0:T(8,128)S(1)} %copy-done.6, f32[1024]{0:T(1024)S(1)} %add_rsqrt_fusion, f32[1024]{0:T(1024)S(1)} %copy-done.30, f32[1024,1024]{1,0:T(8,128)S(1)} %fusion.69, bf16[1024,3072]{1,0:T(8,128)(2,1)} %get-tuple-element.123.dup_ref, ...), kind=kOutput, calls=%fused_computation.33 | convolution fusion | flops 6447692800 | bytes 25178112 | tf_op jit(solution)/shard_map/dot_general | solution.py:863
  263.4 46.3 %block_gradients.1 = bf16[16,336,1024]{2,1,0:T(8,128)(2,1)} custom-call(bf16[1024,1024]{1,0:T(8,128)(2,1)} %copy-done.10, bf16[1024,3072]{1,0:T(8,128)(2,1)} %get-tuple-element.124.dgate_ref, bf16[1024,3072]{1,0:T(8,128)(2,1)} %get-tuple-element.123.dup_ref, bf16[1024,3072]{1,0:T(8,128)(2,1)} %get-tuple-element.125.hidden_ref, ...), custom_call_target="tpu_custom_call" | custom-call | flops 22548578304 | bytes 39321600 | tf_op jit(solution)/shard_map/block_gradients/pallas_call | solution.py:805
  311.1 6.9 %fusion.70 = f32[1024,1536]{1,0:T(8,128)} fusion(bf16[1024,1024]{1,0:T(8,128)(2,1)} %get-tuple-element.39.dres_ref, bf16[1536,1024]{1,0:T(8,128)(2,1)S(1)} %copy-done), kind=kOutput, calls=%fused_computation.166 | convolution fusion | flops 3221225472 | bytes 11534336 | tf_op jit(solution)/shard_map/dot_general | solution.py:863
  318.1 24.3 %recurrence_adjoint.1 = (bf16[2,512,1536]{2,1,0:T(8,128)(2,1)}, f32[2,512,1536]{2,1,0:T(8,128)}, f32[2,512,1536]{2,1,0:T(8,128)}, f32[2,1,1536]{2,1,0:T(1,128)}) custom-call(f32[2,512,1536]{2,1,0:T(8,128)} %bitcast.208, f32[2,512,1536]{2,1,0:T(8,128)} %bitcast.207, f32[2,512,1536]{2,1,0:T(8,128)} %get-tuple-element.36.state_ref, ...), custom_call_target="tpu_custom_call" | custom-call | bytes 47833088 | tf_op jit(solution)/shard_map/recurrence_adjoint/pallas_call | solution.py:371
  343.1 9.0 %all-gather.1 = f32[8,2,1536]{2,1,0:T(2,128)S(1)} all-gather(f32[2,2,1536]{2,1,0:T(2,128)S(1)} %copy.102), channel_id=3, replica_groups=mesh['seq'=4,'zed'=4,'core'=2] {'seq'}, dimensions={0}, use_global_device_ids=true | all-gather | bytes 122880 | tf_op jit(solution)/shard_map/all_gather | solution.py:841
  352.8 43.3 %recurrence_backward.1 = (bf16[2,512,1536]{2,1,0:T(8,128)(2,1)}, f32[2,8,1536]{2,1,0:T(8,128)}, f32[2,8,1536]{2,1,0:T(8,128)}, f32[8,1536]{1,0:T(8,128)}, f32[1536,256]{1,0:T(8,128)}) custom-call(f32[2,512,1536]{2,1,0:T(8,128)} %get-tuple-element.41.local_ref, f32[2,512,1536]{2,1,0:T(8,128)} %get-tuple-element.42.back_ref, f32[2,1,1536]{2,1,0:T(1,128)} %copy.103.out_ref, ...), custom_call_target="tpu_custom_call" | custom-call | flops 4831838208 | bytes 55255040 | tf_op jit(solution)/shard_map/recurrence_backward/pallas_call | solution.py:371
  398.3 11.6 %add_convert_fusion.1 = bf16[1024,1024]{1,0:T(8,128)(2,1)} fusion(f32[1024,1024]{1,0:T(8,128)S(1)} %copy-done.7, bf16[1024,3072]{1,0:T(8,128)(2,1)} %get-tuple-element.125.hidden_ref, bf16[3072,1024]{1,0:T(8,128)(2,1)} %param.33), kind=kOutput, calls=%fused_computation.35 | convolution fusion | flops 6444548096 | bytes 18874368 | tf_op jit(solution)/shard_map/dot_general | solution.py:869
  421.2 6.4 %fusion.71 = f32[1024,1024]{1,0:T(8,128)S(1)} fusion(bf16[1024,1536]{1,0:T(8,128)(2,1)} %bitcast.243, bf16[1024,1536]{1,0:T(8,128)(2,1)} %param.22), kind=kOutput, calls=%fused_computation.167 | convolution fusion | flops 3221225472 | bytes 10485760 | tf_op jit(solution)/shard_map/dot_general | solution.py:863
  440.3 63.1 %all-to-all-done.1 = bf16[2,512,1024]{1,0,2:T(2,128)(2,1)} async-done(((bf16[2,512,1024]{1,0,2:T(2,128)(2,1)}), bf16[2,512,1024]{1,0,2:T(2,128)(2,1)}, u32[]{:S(2)}, u32[]{:S(2)}) %all-to-all-start.1) | async-done | bytes 2097184 | tf_op jit(solution)/shard_map/all_to_all | solution.py:970
  518.0 7.9 %convolution_convert_fusion.1 = bf16[1024,1536]{1,0:T(8,128)(2,1)} fusion(bf16[1024,1536]{1,0:T(8,128)(2,1)} %bitcast.241, bf16[128,8,8,128]{3,2,1,0:T(8,128)(2,1)} %bitcast.212), kind=kOutput, calls=%fused_computation.42 | convolution fusion | flops 3222798336 | bytes 8388608 | tf_op jit(solution)/shard_map/dot_general | solution.py:857
  530.8 59.3 %reduce_streams.1 = (f32[32,1536]{1,0:T(8,128)}, f32[32,1536]{1,0:T(8,128)}, f32[48,256]{1,0:T(8,128)}) custom-call(bf16[2,2,2,2,2,32,1536]{6,5,4,3,2,1,0:T(8,128)(2,1)} %bitcast.209, bf16[2,2,2,2,2,32,1536]{6,5,4,3,2,1,0:T(8,128)(2,1)} %bitcast.210, bf16[2,2,2,2,2,48,256]{6,5,4,3,2,1,0:T(8,128)(2,1)} %pad_maximum_fusion.refs_2_), custom_call_target="tpu_custom_call" | custom-call | bytes 141557760 | tf_op jit(solution)/shard_map/reduce_streams/pallas_call | solution.py:601
  (176 shorter events, 120.8 us)
Async XLA Ops:
  7.2 178.2 %copy-start = (bf16[1536,1024]{1,0:T(8,128)(2,1)S(1)}, bf16[1536,1024]{1,0:T(8,128)(2,1)}, u32[]{:S(2)}) copy-start(bf16[1536,1024]{1,0:T(8,128)(2,1)} %param.29) | copy-start | bytes 9437188
  7.2 60.2 %copy-start.26 = (f32[1536]{0:T(1024)S(1)}, f32[1536]{0:T(1024)}, u32[]{:S(2)}) copy-start(f32[1536]{0:T(1024)} %param.28) | copy-start | bytes 18436
  7.2 60.3 %copy-start.27 = (f32[1536]{0:T(1024)S(1)}, f32[1536]{0:T(1024)}, u32[]{:S(2)}) copy-start(f32[1536]{0:T(1024)} %param.25) | copy-start | bytes 18436
  7.2 60.4 %copy-start.22 = (f32[4,1536]{1,0:T(4,128)S(1)}, f32[4,1536]{1,0:T(4,128)}, u32[]{:S(2)}) copy-start(f32[4,1536]{1,0:T(4,128)} %param.24) | copy-start | bytes 73732
  7.2 60.4 %copy-start.25 = (f32[2,1536]{1,0:T(2,128)S(1)}, f32[2,1536]{1,0:T(2,128)}, u32[]{:S(2)}) copy-start(f32[2,1536]{1,0:T(2,128)} %param.27) | copy-start | bytes 36868
  7.3 55.8 %all-to-all-start = ((bf16[16,512,128]{2,1,0:T(8,128)(2,1)}), bf16[16,512,128]{2,1,0:T(8,128)(2,1)}, u32[]{:S(2)}, u32[]{:S(2)}) async-start(bf16[16,512,128]{2,1,0:T(8,128)(2,1)} %param.17), calls=%async_computation | async-start | bytes 4194304 | tf_op jit(solution)/shard_map/all_to_all | solution.py:908
  63.0 53.4 %all-to-all-start.2 = ((bf16[16,512,128]{2,1,0:T(8,128)(2,1)}), bf16[16,512,128]{2,1,0:T(8,128)(2,1)}, u32[]{:S(2)}, u32[]{:S(2)}) async-start(bf16[16,512,128]{2,1,0:T(8,128)(2,1)} %param.18), calls=%async_computation.2 | async-start | bytes 4194304 | tf_op jit(solution)/shard_map/all_to_all | solution.py:909
  67.4 366.7 %reduce-scatter.3.cloned.1.call-start = ((), (), s32[]{:S(2)}) async-start(), calls=%async_computation.6 | async-start | bytes 13762560 | tf_op jit(solution)/shard_map/reduce_scatter | solution.py:995
  97.2 24.2 %collective-permute-start = (bf16[2,3,1536]{2,1,0:T(4,128)(2,1)S(1)}, bf16[2,3,1536]{2,1,0:T(4,128)(2,1)S(1)}, u32[]{:S(2)}, u32[]{:S(2)}) collective-permute-start(bf16[2,3,1536]{2,1,0:T(4,128)(2,1)S(1)} %slice.218), channel_id=1, source_target_pairs={{0,8},{8,16},{16,24},{1,9},{9,17},{17,25},{2,10},{10,18},{18,26},{... | collective-permute-start | bytes 55304 | tf_op jit(solution)/shard_map/ppermute | solution.py:853
  121.4 54.8 %copy-start.23 = (f32[1,4,2,128]{3,1,2,0:T(4,128)}, f32[1,4,2,128]{3,1,2,0:T(4,128)S(1)}, u32[]{:S(2)}) copy-start(f32[1,4,2,128]{3,1,2,0:T(4,128)S(1)} %copy.117) | copy-start | bytes 12292
  189.3 15.2 %copy-start.5 = (f32[1024,1024]{1,0:T(8,128)}, f32[1024,1024]{1,0:T(8,128)S(1)}, u32[]{:S(2)}) copy-start(f32[1024,1024]{1,0:T(8,128)S(1)} %get-tuple-element.140) | copy-start | bytes 12582916
  189.4 15.2 %slice-start = ((s8[6291456]{0:T(1024)(128)(4,1)}), s8[4194304]{0:T(1024)(128)(4,1)S(1)}, s32[]{:S(2)}) async-start(s8[6291456]{0:T(1024)(128)(4,1)} %bitcast.237), calls=%async_computation.8 | async-start | bytes 8388608
  189.8 14.7 %copy-start.10 = (bf16[1024,1024]{1,0:T(8,128)(2,1)}, bf16[1024,1024]{1,0:T(8,128)(2,1)S(1)}, u32[]{:S(2)}) copy-start(bf16[1024,1024]{1,0:T(8,128)(2,1)S(1)} %multiply_convert_fusion.3.normed_ref) | copy-start | bytes 6291460
  189.8 14.7 %slice-start.1 = ((s8[6291456]{0:T(1024)(128)(4,1)}), s8[2097152]{0:T(1024)(128)(4,1)S(1)}, s32[]{:S(2)}) async-start(s8[6291456]{0:T(1024)(128)(4,1)} %bitcast.237), calls=%async_computation.9 | async-start | bytes 4194304
  204.6 9.1 %copy-start.9 = (bf16[1024,1024]{1,0:T(8,128)(2,1)S(1)}, bf16[1024,1024]{1,0:T(8,128)(2,1)}, u32[]{:S(2)}) copy-start(bf16[1024,1024]{1,0:T(8,128)(2,1)} %fusion.17.gout_ref) | copy-start | bytes 6291460
  237.5 10.8 %copy-start.6 = (f32[1024,1024]{1,0:T(8,128)S(1)}, f32[1024,1024]{1,0:T(8,128)}, u32[]{:S(2)}) copy-start(f32[1024,1024]{1,0:T(8,128)} %copy-done.5) | copy-start | bytes 12582916
  318.1 24.3 %copy-start.19 = (f32[1,2,1536]{2,0,1:T(1,128)S(1)}, f32[1,2,1536]{2,0,1:T(1,128)}, u32[]{:S(2)}) copy-start(f32[1,2,1536]{2,0,1:T(1,128)} %copy-done.18) | copy-start | bytes 36868
  352.8 45.5 %copy-start.7 = (f32[1024,1024]{1,0:T(8,128)S(1)}, f32[1024,1024]{1,0:T(8,128)}, u32[]{:S(2)}) copy-start(f32[1024,1024]{1,0:T(8,128)} %copy-done.5) | copy-start | bytes 12582916
  397.0 23.5 %collective-permute-start.1 = (bf16[2,3,1536]{2,1,0:T(4,128)(2,1)S(1)}, bf16[2,3,1536]{2,1,0:T(4,128)(2,1)S(1)}, u32[]{:S(2)}, u32[]{:S(2)}) collective-permute-start(bf16[2,3,1536]{2,1,0:T(4,128)(2,1)S(1)} %slice.217), channel_id=1, source_target_pairs={{8,0},{16,8},{24,16},{9,1},{17,9},{25,17},{10,2},{18,10},{26,18},{... | collective-permute-start | bytes 55304 | tf_op jit(solution)/shard_map/ppermute | solution.py:853
  409.9 10.6 %copy-start.20 = (f32[2,8,1536]{2,1,0:T(8,128)S(1)}, f32[2,8,1536]{2,1,0:T(8,128)}, u32[]{:S(2)}) copy-start(f32[2,8,1536]{2,1,0:T(8,128)} %get-tuple-element.47) | copy-start | bytes 294916
  416.1 87.3 %all-to-all-start.1 = ((bf16[2,512,1024]{1,0,2:T(2,128)(2,1)}), bf16[2,512,1024]{1,0,2:T(2,128)(2,1)}, u32[]{:S(2)}, u32[]{:S(2)}) async-start(bf16[2,512,1024]{1,0,2:T(2,128)(2,1)} %copy.96), calls=%async_computation.1 | async-start | bytes 4194304 | tf_op jit(solution)/shard_map/all_to_all | solution.py:970
  420.4 190.4 %reduce-scatter.5.cloned.1.call-start = ((), (), s32[]{:S(2)}) async-start(), calls=%async_computation.7 | async-start | bytes 3440640 | tf_op jit(solution)/shard_map/reduce_scatter | solution.py:1043
  503.4 101.3 %all-to-all-start.3 = ((bf16[2,512,1024]{1,0,2:T(2,128)(2,1)}), bf16[2,512,1024]{1,0,2:T(2,128)(2,1)}, u32[]{:S(2)}, u32[]{:S(2)}) async-start(bf16[2,512,1024]{1,0,2:T(2,128)(2,1)} %copy.104), calls=%async_computation.4 | async-start | bytes 4194304 | tf_op jit(solution)/shard_map/all_to_all | solution.py:1044
  518.0 7.9 %copy-start.35 = (bf16[2,512,1536]{2,1,0:T(8,128)(2,1)S(1)}, bf16[2,512,1536]{2,1,0:T(8,128)(2,1)}, u32[]{:S(2)}) copy-start(bf16[2,512,1536]{2,1,0:T(8,128)(2,1)} %fusion.30) | copy-start | bytes 9437188
  (23 other events, 104.7 us)
Sparse Core Ops, SparseCore 0:
  309.9 106.9 reduce-scatter.2
  434.3 76.7 reduce-scatter.4

commit v4 on v3

--- a/solution.py
+++ b/solution.py
@@ -478,6 +478,155 @@
         )
 
 
+def gathered(parts_ref, at):
+    return jnp.concatenate([parts_ref[k, at, :] for k in range(parts_ref.shape[0])], axis=1)
+
+
+def front_kernel(
+    parts_ref, gain_ref, input_ref, gate_ref, x_ref, inverse_ref, normed_ref, branch_ref, pre_ref
+):
+    tokens = x_ref.shape[0]
+    piece = 64
+
+    @pl.when(pl.program_id(0) == 0)
+    def _():
+        def norm(index, carry):
+            at = pl.ds(pl.multiple_of(index * piece, piece), piece)
+            low = gathered(parts_ref, at)
+            x_ref[at, :] = low
+            value = low.astype(jnp.float32)
+            inverse = lax.rsqrt(jnp.mean(value * value, axis=1, keepdims=True) + EPS)
+            inverse_ref[at, :] = jnp.broadcast_to(inverse, (piece, LANES))
+            normed_ref[at, :] = (value * inverse * gain_ref[...]).astype(jnp.bfloat16)
+            return carry
+
+        lax.fori_loop(0, tokens // piece, norm, 0)
+
+    def multiply(index, carry):
+        at = pl.ds(pl.multiple_of(index * 256, 256), 256)
+        normed = normed_ref[at, :]
+        branch_ref[at, :] = jnp.dot(normed, input_ref[...], preferred_element_type=jnp.float32)
+        pre_ref[at, :] = jnp.dot(normed, gate_ref[...], preferred_element_type=jnp.float32)
+        return carry
+
+    lax.fori_loop(0, tokens // 256, multiply, 0)
+
+
+def front(parts, gain, recur_input, recur_gate):
+    count, tokens, width = parts.shape
+    model, rec = recur_input.shape
+    columns = 3 * LANES
+    low, f32 = (jnp.bfloat16, jnp.float32)
+    tall = pl.BlockSpec((model, columns), lambda j: (0, j))
+    wide = pl.BlockSpec((tokens, columns), lambda j: (0, j))
+
+    def whole(shape):
+        return pl.BlockSpec(shape, lambda j: (0,) * len(shape))
+
+    return pl.pallas_call(
+        front_kernel,
+        name="norm_and_project",
+        grid=(rec // columns,),
+        in_specs=[whole(parts.shape), whole((1, model)), tall, tall],
+        out_specs=[whole((tokens, model)), whole((tokens, LANES)), whole((tokens, model)), wide, wide],
+        out_shape=[
+            jax.ShapeDtypeStruct((tokens, model), low),
+            jax.ShapeDtypeStruct((tokens, LANES), f32),
+            jax.ShapeDtypeStruct((tokens, model), low),
+            jax.ShapeDtypeStruct((tokens, rec), f32),
+            jax.ShapeDtypeStruct((tokens, rec), f32),
+        ],
+        compiler_params=pltpu.CompilerParams(vmem_limit_bytes=VMEM_BYTES),
+        cost_estimate=pl.CostEstimate(
+            flops=4 * tokens * model * rec, bytes_accessed=20 * tokens * model, transcendentals=0
+        ),
+    )(parts, gain[None], recur_input, recur_gate)
+
+
+def collect_kernel(left_ref, parts_ref, out_ref):
+    rows, length = (left_ref.shape[0], out_ref.shape[0] // left_ref.shape[0])
+    piece = 64
+    for row in range(rows):
+
+        def step(index, carry, row=row):
+            base = pl.multiple_of(index * piece, piece)
+            at = pl.ds(row * length + base, piece)
+            low = gathered(parts_ref, at)
+            place = base + lax.broadcasted_iota(jnp.int32, low.shape, 0)
+            value = jnp.where(place < left_ref[row], low.astype(jnp.float32), 0.0)
+            out_ref[at, :] = value.astype(jnp.bfloat16)
+            return carry
+
+        lax.fori_loop(0, length // piece, step, 0)
+
+
+def collect(parts, left):
+    count, tokens, width = parts.shape
+    return pl.pallas_call(
+        collect_kernel,
+        name="collect_cotangent",
+        in_specs=[
+            pl.BlockSpec(memory_space=pltpu.SMEM),
+            pl.BlockSpec(memory_space=pltpu.VMEM),
+        ],
+        out_specs=pl.BlockSpec(memory_space=pltpu.VMEM),
+        out_shape=jax.ShapeDtypeStruct((tokens, count * width), parts.dtype),
+        compiler_params=pltpu.CompilerParams(vmem_limit_bytes=VMEM_BYTES),
+        cost_estimate=pl.CostEstimate(
+            flops=0, bytes_accessed=4 * count * tokens * width, transcendentals=0
+        ),
+    )(left, parts)
+
+
+def spread_kernel(whole_ref, out_ref):
+    out_ref[0] = whole_ref[...]
+
+
+def spread(whole, count):
+    tokens, width = (whole.shape[0], whole.shape[1] // count)
+    return pl.pallas_call(
+        spread_kernel,
+        name="spread_features",
+        grid=(count,),
+        in_specs=[pl.BlockSpec((tokens, width), lambda j: (0, j))],
+        out_specs=pl.BlockSpec((1, tokens, width), lambda j: (j, 0, 0)),
+        out_shape=jax.ShapeDtypeStruct((count, tokens, width), whole.dtype),
+        cost_estimate=pl.CostEstimate(
+            flops=0, bytes_accessed=4 * tokens * whole.shape[1], transcendentals=0
+        ),
+    )(whole)
+
+
+CHAN = ("zed", "core")
+
+
+def features_in(local):
+    count = lax.axis_size(CHAN)
+    rows, length, width = local.shape
+    if width % LANES == 0:
+        moved = lax.all_to_all(
+            local.reshape(count, rows // count, length, width), CHAN, 0, 0, tiled=True
+        )
+        return moved.reshape(count, -1, width)
+    moved = lax.all_to_all(local, CHAN, split_axis=0, concat_axis=2, tiled=True)
+    return moved.reshape(1, -1, count * width)
+
+
+def features_apart(whole, length):
+    count = lax.axis_size(CHAN)
+    width = whole.shape[1] // count
+    if width % LANES == 0:
+        return spread(whole, count).reshape(count, -1, length, width)
+    return whole.reshape(1, -1, length, count * width)
+
+
+def features_out(parts):
+    if parts.shape[0] > 1:
+        moved = lax.all_to_all(parts, CHAN, 0, 0, tiled=True)
+        return moved.reshape(-1, *parts.shape[2:])
+    return lax.all_to_all(parts[0], CHAN, split_axis=2, concat_axis=0, tiled=True)
+
+
 MESH = pl.DeviceIdType.MESH
 
 
@@ -904,11 +1053,9 @@
     mlp_up,
     mlp_down,
 ):
-    seq_x, seq_g = (
-        lax.all_to_all(tokens, ("zed", "core"), split_axis=0, concat_axis=2, tiled=True),
-        lax.all_to_all(cotangent, ("zed", "core"), split_axis=0, concat_axis=2, tiled=True),
-    )
-    row_count, block_len, model_dim = seq_x.shape
+    count = lax.axis_size(CHAN)
+    row_count, block_len = (tokens.shape[0] // count, tokens.shape[1])
+    model_dim = tokens.shape[2] * count
     tok_count = row_count * block_len
     rec_width = recur_input.shape[1]
     ffn_width = mlp_gate.shape[1]
@@ -921,13 +1068,9 @@
     bounds = jnp.concatenate([doc_starts, lengths[:, None]], axis=1)
     is_before = bounds[:, None, :] <= position[None, :, None]
     seg_start = jnp.max(jnp.where(is_before, bounds[:, None, :], 0), axis=2)
-    is_valid = (position[None, :] < lengths[:, None]).reshape(tok_count, 1)
-    flat_x = seq_x.reshape(tok_count, model_dim).astype(jnp.float32)
-    inv_one = lax.rsqrt(jnp.mean(flat_x * flat_x, axis=1, keepdims=True) + EPS)
-    normed_one = flat_x * inv_one
-    normed_low = (normed_one * norm1_gain).astype(jnp.bfloat16)
-    branch_pre = fwd_dot(normed_low, recur_input)
-    gate_pre = fwd_dot(normed_low, recur_gate)
+    low_x, inverse_lanes, normed_low, branch_pre, gate_pre = front(
+        features_in(tokens), norm1_gain, recur_input, recur_gate
+    )
     gate_act = gelu_fn(gate_pre)
     branch_rows = branch_pre.reshape(row_count, block_len, rec_width)
     core = Recurrence(row_count, block_len, rec_width, head_size)
@@ -953,12 +1096,13 @@
     lru_in, rate_gate, input_gate, local_state, cum_coef = core.forward(
         branch_rows, rim, dist, params, wide_gates
     )
+    cotangent, local_state = lax.optimization_barrier((features_in(cotangent), local_state))
     carry_in = carried(cum_coef[:, -1, :], local_state[:, -1, :], "seq", False)
     entering = carry_in[:, None, :]
     state_rows = local_state + cum_coef * entering
     state_flat = state_rows.reshape(tok_count, rec_width)
     mixed_low = (state_flat * gate_act).astype(jnp.bfloat16)
-    resid_one = flat_x + fwd_dot(mixed_low, recur_out)
+    resid_one = low_x.astype(jnp.float32) + fwd_dot(mixed_low, recur_out)
     inv_two = lax.rsqrt(jnp.mean(resid_one * resid_one, axis=1, keepdims=True) + EPS)
     normed_two = resid_one * inv_two
     normed_low2 = (normed_two * norm2_gain).astype(jnp.bfloat16)
@@ -967,22 +1111,18 @@
     gelu_gate = gelu_fn(mlp_gate_pre)
     hidden_low = (gelu_gate * mlp_up_pre).astype(jnp.bfloat16)
     result = (resid_one + fwd_dot(hidden_low, mlp_down)).astype(jnp.bfloat16)
-    output = lax.all_to_all(
-        result.reshape(row_count, block_len, model_dim),
-        ("zed", "core"),
-        split_axis=2,
-        concat_axis=0,
-        tiled=True,
-    )
-    grad_out = jnp.where(is_valid, seq_g.reshape(tok_count, model_dim).astype(jnp.float32), 0.0)
-    grad_low = grad_out.astype(jnp.bfloat16)
+    grad_low = collect(cotangent, lengths - seq_index * block_len)
     grad_hidden = back_dot(grad_low, mlp_down)
     _, gelu_pull = jax.vjp(gelu_fn, mlp_gate_pre)
     mgate_low = gelu_pull(grad_hidden * mlp_up_pre)[0].astype(jnp.bfloat16)
     mup_low = (grad_hidden * gelu_gate).astype(jnp.bfloat16)
+    result_parts, mgate_low, mup_low = lax.optimization_barrier(
+        (features_apart(result, block_len), mgate_low, mup_low)
+    )
+    output = features_out(result_parts)
     grad_norm2 = back_dot(mgate_low, mlp_gate) + back_dot(mup_low, mlp_up)
     resid_part = norm_back(grad_norm2, normed_two, inv_two, norm2_gain)
-    grad_resid = grad_out + resid_part
+    grad_resid = grad_low.astype(jnp.float32) + resid_part
     resid_low = grad_resid.astype(jnp.bfloat16)
     devices = lax.axis_size(("seq", "zed", "core"))
     own_rows = model_dim // devices
@@ -1005,6 +1145,7 @@
         params,
     )
     gate_low = gate_low.reshape(tok_count, rec_width)
+    output, back_local = lax.optimization_barrier((output, back_local))
     carry_out = carried(cum_coef[:, -1, :], first_term[:, 0, :], "seq", True)
     branch_local, tail, lead, channel_sums, gate_sums = core.backward(
         back_local,
@@ -1036,25 +1177,27 @@
     grad_rin = weight_grad(normed_low, branch_low)
     grad_rgate = weight_grad(normed_low, gate_low)
     grad_norm1 = back_dot(branch_low, recur_input) + back_dot(gate_low, recur_gate)
+    inv_one = inverse_lanes[:, :1]
+    normed_one = low_x.astype(jnp.float32) * inv_one
     input_part = norm_back(grad_norm1, normed_one, inv_one, norm1_gain)
-    grad_x = (grad_resid + input_part).astype(jnp.bfloat16).reshape(row_count, block_len, model_dim)
+    grad_x = (grad_resid + input_part).astype(jnp.bfloat16)
     if tiled:
         merged, grad_x = lax.optimization_barrier((merged, grad_x))
         merged = lax.psum_scatter(merged, "zed", scatter_dimension=0, tiled=True)
-    grad_tokens = lax.all_to_all(grad_x, ("zed", "core"), split_axis=2, concat_axis=0, tiled=True)
+    grad_tokens = features_out(features_apart(grad_x, block_len))
     if tiled:
         sum_rgate, sum_rin, own_small = reduce_streams(
             (grad_rgate, grad_rin, small.astype(jnp.bfloat16)), (False, True, False)
         )
         own = merged[0].astype(jnp.float32)
-        count = ffn_width // model_dim * own_rows
+        span = ffn_width // model_dim * own_rows
 
         def unfolded(part):
             return jnp.swapaxes(part.reshape(-1, own_rows, model_dim), 0, 1).reshape(own_rows, -1)
 
-        sum_mgate, sum_mup = (unfolded(own[:count]), unfolded(own[count : 2 * count]))
-        sum_down = own[2 * count : 2 * count + ffn_width // devices]
-        sum_rout = own[2 * count + ffn_width // devices :]
+        sum_mgate, sum_mup = (unfolded(own[:span]), unfolded(own[span : 2 * span]))
+        sum_down = own[2 * span : 2 * span + ffn_width // devices]
+        sum_rout = own[2 * span + ffn_width // devices :]
     else:
         sum_mgate, sum_mup, sum_down, sum_rout, sum_rgate, sum_rin = (
             scattered(weight_grad(left, right))

time: 636 us -> 563 us (0.89)
  waiting for transfers between devices: 128 us -> 11.2 us
  blocking collectives: 17.5 us -> 73.8 us
  Pallas kernels: 208 us -> 258 us
  local copies, waits for them, and re-layouts: 53.9 us -> 28.2 us
  matrix products: 135 us -> 121 us
  other arithmetic: 44.1 us -> 32.3 us
  starting transfers between devices: 25.9 us -> 18.3 us
    all_to_all x4 -> x3, waiting for transfers between devices: 128 us -> 6.46 us  [the longest x2 6.45 us: features_out(): moved = lax.all_to_all(parts, CHAN, 0, 0, tiled=True)]
    all_to_all x0 -> x1, blocking collectives: none -> 55.8 us  [features_in(): lax.all_to_all(local.reshape(count, rows // count, length, width), CHAN,...]
    pallas_call x0 -> x4, Pallas kernels: none -> 33.6 us  [the longest x1 18.9 us: front(): pl.pallas_call(front_kernel, name='norm_and_project', grid=(rec // column...]
    dot_general x6 -> x4, matrix products: 54.8 us -> 33.4 us  [fwd_dot(): return jnp.dot(left, right, preferred_element_type=jnp.float32)]
    pallas_call x1, Pallas kernels: 59.3 us -> 75 us  [reduce_streams(): pl.pallas_call(functools.partial(reduce_kernel, corners, orders), name='r...]
    all_to_all x2 -> x0, local copies, waits for them, and re-layouts: 12.3 us -> none  [the longest x1 6.17 us: body(): lax.all_to_all(grad_x, ('zed', 'core'), split_axis=2, concat_axis=0, tile...]
    another operation x2 -> x1, other arithmetic: 8.22 us -> 0.08 us
    convert_element_type x2 -> x0, local copies, waits for them, and re-layouts: 7.7 us -> none  [the longest x1 4.89 us: body(): flat_x = seq_x.reshape(tok_count, model_dim).astype(jnp.float32)]
  transfers between devices with their start and end apart: 8 -> 7, of which waited for: 3 -> 2; matrix products, arithmetic and copies ran while one was open for 20% -> 12% of each run, Pallas kernels for 20% -> 36%
where the time goes in v4:
time: 563 us; the launch traced here: 558 us
  Pallas kernels  258 us (46%)
  matrix products  121 us (21%)
  blocking collectives  73.8 us (13%)
  other arithmetic  32.3 us (6%)
  local copies, waits for them, and re-layouts  28.2 us (5%)
  starting transfers between devices  18.3 us (3%)
  between operations  15 us (3%)
  waiting for transfers between devices  11.2 us (2%)
    pallas_call x3, Pallas kernels, channel_call(): pl.pallas_call(kernel, name=name, grid=(blocks,), in_specs=specs, out_spe...  103 us
    pallas_call x1, Pallas kernels, reduce_streams(): pl.pallas_call(functools.partial(reduce_kernel, corners, orders), name='r...  75 us
    dot_general x6, matrix products, back_dot(): lax.dot_general(left, right, (((1,), (1,)), ((), ())), preferred_element_...  69 us
    all_to_all x1, blocking collectives, features_in(): lax.all_to_all(local.reshape(count, rows // count, length, width), CHAN,...  55.8 us
    pallas_call x1, Pallas kernels, block_gradients(): pl.pallas_call(grads_kernel, name='block_gradients', grid=(total + 1,), i...  46.2 us
    dot_general x4, matrix products, fwd_dot(): return jnp.dot(left, right, preferred_element_type=jnp.float32)  33.4 us
    pallas_call x1, Pallas kernels, front(): pl.pallas_call(front_kernel, name='norm_and_project', grid=(rec // column...  18.9 us
    all_gather x2, blocking collectives, carried(): pieces = lax.all_gather(jnp.stack([factor, value]), axis)  18 us
  transfers between devices with their start and end apart: 7, of which 2 were waited for; matrix products, arithmetic and copies ran while one was open for 12% of the time, Pallas kernels for 36%

profile of v4, /device:TPU:0, one launch (start us, length us, event | category | flops | bytes accessed | tf_op | source)
XLA Modules:
  0.0 558.0 jit_solution(6320343157049577291)
XLA Ops:
  7.2 55.8 %all_to_all.20 = bf16[8,2,512,128]{3,2,1,0:T(8,128)(2,1)} all-to-all(bf16[8,2,512,128]{3,2,1,0:T(8,128)(2,1)} %bitcast.167), channel_id=1, replica_groups=mesh['seq'=4,'zed'=4,'core'=2] {'zed','core'}, dimensions={0} | all-to-all | bytes 4194304 | tf_op jit(solution)/shard_map/all_to_all | solution.py:607
  71.3 18.9 %norm_and_project.1 = (bf16[1024,1024]{1,0:T(8,128)(2,1)}, f32[1024,128]{1,0:T(8,128)}, bf16[1024,1024]{1,0:T(8,128)(2,1)}, f32[1024,1536]{1,0:T(8,128)}, f32[1024,1536]{1,0:T(8,128)}) custom-call(bf16[8,1024,128]{2,1,0:T(8,128)(2,1)} %bitcast.169, f32[1,1024]{1,0:T(1,128)} %bitcast.189, bf16[1024,1536]{1,0:T(8,128)(2,1)} %input_ref.1, ...), custom_call_target="tpu_custom_call" | custom-call | flops 6442450944 | bytes 20971520 | tf_op jit(solution)/shard_map/norm_and_project/pallas_call | solution.py:526
  98.0 35.1 %recurrence_forward.1 = (bf16[2,512,1536]{2,1,0:T(8,128)(2,1)}, f32[2,512,1536]{2,1,0:T(8,128)}, f32[2,512,1536]{2,1,0:T(8,128)}, f32[2,512,1536]{2,1,0:T(8,128)}, f32[2,512,1536]{2,1,0:T(8,128)}) custom-call(f32[2,512,1536]{2,1,0:T(8,128)} %bitcast.154, f32[2,8,1536]{2,1,0:T(8,128)} %pad_convert_fusion.rim_ref, s32[2,512,128]{2,1,0:T(8,128)} %broadcast_in_dim.29.dist_ref, ...), custom_call_target="tpu_custom_call" | custom-call | flops 2415919104 | bytes 37683200 | tf_op jit(solution)/shard_map/recurrence_forward/pallas_call | solution.py:371
  135.1 10.3 %all-gather = f32[8,2,1536]{2,1,0:T(2,128)S(1)} all-gather(f32[2,2,1536]{2,1,0:T(2,128)S(1)} %copy.92), channel_id=2, replica_groups=mesh['seq'=4,'zed'=4,'core'=2] {'seq'}, dimensions={0}, use_global_device_ids=true | all-gather | bytes 122880 | tf_op jit(solution)/shard_map/all_gather | solution.py:990
  146.6 6.2 %multiply_add_fusion = f32[2,512,1536]{2,1,0:T(8,128)S(1)} fusion(f32[2,512,1536]{2,1,0:T(8,128)} %get-tuple-element.51.state_ref, f32[2,512,1536]{2,1,0:T(8,128)} %get-tuple-element.52.cum_ref, f32[2,1536]{1,0:T(2,128)S(1)} %fusion.36), kind=kLoop, calls=%fused_computation.22 | loop fusion | flops 3145728 | bytes 18886656 | tf_op jit(solution)/shard_map/add | solution.py:1102
  159.6 9.2 %fusion.62 = f32[1024,3072]{1,0:T(8,128)} fusion(bf16[1024,1024]{1,0:T(8,128)(2,1)S(1)} %multiply_convert_fusion.2.normed_ref, bf16[1024,3072]{1,0:T(8,128)(2,1)S(1)} %bitcast.188), kind=kOutput, calls=%fused_computation.149 | convolution fusion | flops 6442450944 | bytes 20971520 | tf_op jit(solution)/shard_map/dot_general | solution.py:1018
  168.8 9.2 %fusion.61 = f32[1024,3072]{1,0:T(8,128)} fusion(bf16[1024,1024]{1,0:T(8,128)(2,1)S(1)} %multiply_convert_fusion.2.normed_ref, bf16[1024,3072]{1,0:T(8,128)(2,1)S(1)} %bitcast.186), kind=kOutput, calls=%fused_computation.148 | convolution fusion | flops 6442450944 | bytes 20971520 | tf_op jit(solution)/shard_map/dot_general | solution.py:1018
  181.4 25.7 %multiply_convert_fusion = (bf16[1024,3072]{1,0:T(8,128)(2,1)}, bf16[1024,3072]{1,0:T(8,128)(2,1)}, bf16[1024,3072]{1,0:T(8,128)(2,1)}) fusion(f32[1024,3072]{1,0:T(8,128)} %fusion.61, f32[1024,3072]{1,0:T(8,128)} %fusion.62, bf16[1024,1024]{1,0:T(8,128)(2,1)} %collect_cotangent.1.gout_ref, bf16[3072,1024]{1,0:T(8,128)(2,1)} %param.33), kind=kOutput, calls=%fused_computation.9 | convolution fusion | flops 6524239872 | bytes 52428800 | tf_op jit(solution)/shard_map/dot_general | solution.py:1012
  207.1 11.6 %add_convert_fusion.whole_ref = bf16[1024,1024]{1,0:T(8,128)(2,1)} fusion(f32[1024,1024]{1,0:T(8,128)S(1)} %get-tuple-element.155, bf16[1024,3072]{1,0:T(8,128)(2,1)} %get-tuple-element.147.hidden_ref, bf16[3072,1024]{1,0:T(8,128)(2,1)} %param.33), kind=kOutput, calls=%fused_computation.38 | convolution fusion | flops 6444548096 | bytes 18874368 | tf_op jit(solution)/shard_map/dot_general | solution.py:1018
  218.6 5.6 %spread_features.2 = bf16[8,1024,128]{2,1,0:T(8,128)(2,1)} custom-call(bf16[1024,1024]{1,0:T(8,128)(2,1)} %add_convert_fusion.whole_ref), custom_call_target="tpu_custom_call" | custom-call | bytes 4194304 | tf_op jit(solution)/shard_map/spread_features/pallas_call | solution.py:587
  224.3 10.8 %fusion.63 = f32[1024,1024]{1,0:T(8,128)S(1)} fusion(bf16[1024,3072]{1,0:T(8,128)(2,1)} %get-tuple-element.56.dgate_ref, bf16[1024,3072]{1,0:T(8,128)(2,1)} %param.31), kind=kOutput, calls=%fused_computation.150 | convolution fusion | flops 6442450944 | bytes 16777216 | tf_op jit(solution)/shard_map/dot_general | solution.py:1012
  235.1 11.9 %multiply_reduce_fusion = (f32[1024]{0:T(1024)S(1)}, f32[1024,1024]{1,0:T(8,128)S(1)}) fusion(f32[1024,1024]{1,0:T(8,128)S(1)} %copy-done.2, f32[1024]{0:T(1024)S(1)} %add_rsqrt_fusion, f32[1024]{0:T(1024)S(1)} %copy-done.29, f32[1024,1024]{1,0:T(8,128)S(1)} %fusion.63, bf16[1024,3072]{1,0:T(8,128)(2,1)} %get-tuple-element.57.dup_ref, ...), kind=kOutput, calls=%fused_computation.36 | convolution fusion | flops 6447692800 | bytes 25178112 | tf_op jit(solution)/shard_map/dot_general | solution.py:1012
  251.3 46.2 %block_gradients.1 = bf16[16,336,1024]{2,1,0:T(8,128)(2,1)} custom-call(bf16[1024,1024]{1,0:T(8,128)(2,1)} %copy-done.9, bf16[1024,3072]{1,0:T(8,128)(2,1)} %get-tuple-element.56.dgate_ref, bf16[1024,3072]{1,0:T(8,128)(2,1)} %get-tuple-element.57.dup_ref, bf16[1024,3072]{1,0:T(8,128)(2,1)} %get-tuple-element.147.hidden_ref, ...), custom_call_target="tpu_custom_call" | custom-call | flops 22548578304 | bytes 39321600 | tf_op jit(solution)/shard_map/block_gradients/pallas_call | solution.py:954
  303.8 7.6 %fusion.64 = f32[1024,1536]{1,0:T(8,128)} fusion(bf16[1024,1024]{1,0:T(8,128)(2,1)} %fusion.57.dres_ref, bf16[1536,1024]{1,0:T(8,128)(2,1)S(1)} %copy-done), kind=kOutput, calls=%fused_computation.151 | convolution fusion | flops 3221225472 | bytes 11534336 | tf_op jit(solution)/shard_map/dot_general | solution.py:1012
  311.4 24.6 %recurrence_adjoint.1 = (bf16[2,512,1536]{2,1,0:T(8,128)(2,1)}, f32[2,512,1536]{2,1,0:T(8,128)}, f32[2,512,1536]{2,1,0:T(8,128)}, f32[2,1,1536]{2,1,0:T(1,128)}) custom-call(f32[2,512,1536]{2,1,0:T(8,128)} %bitcast.161, f32[2,512,1536]{2,1,0:T(8,128)} %bitcast.156, f32[2,512,1536]{2,1,0:T(8,128)} %get-tuple-element.51.state_ref, ...), custom_call_target="tpu_custom_call" | custom-call | bytes 47833088 | tf_op jit(solution)/shard_map/recurrence_adjoint/pallas_call | solution.py:371
  336.7 7.7 %all-gather.1 = f32[8,2,1536]{2,1,0:T(2,128)S(1)} all-gather(f32[2,2,1536]{2,1,0:T(2,128)S(1)} %copy.100), channel_id=3, replica_groups=mesh['seq'=4,'zed'=4,'core'=2] {'seq'}, dimensions={0}, use_global_device_ids=true | all-gather | bytes 122880 | tf_op jit(solution)/shard_map/all_gather | solution.py:990
  345.1 6.5 %all-to-all-done.2 = bf16[8,2,512,128]{3,2,1,0:T(8,128)(2,1)} async-done(((bf16[8,2,512,128]{3,2,1,0:T(8,128)(2,1)}), bf16[8,2,512,128]{3,2,1,0:T(8,128)(2,1)}, u32[]{:S(2)}, u32[]{:S(2)}) %all-to-all-start.2) | async-done | bytes 2097184 | tf_op jit(solution)/shard_map/all_to_all | solution.py:625
  351.6 43.3 %recurrence_backward.1 = (bf16[2,512,1536]{2,1,0:T(8,128)(2,1)}, f32[2,8,1536]{2,1,0:T(8,128)}, f32[2,8,1536]{2,1,0:T(8,128)}, f32[8,1536]{1,0:T(8,128)}, f32[1536,256]{1,0:T(8,128)}) custom-call(f32[2,512,1536]{2,1,0:T(8,128)} %get-tuple-element.64.local_ref, f32[2,512,1536]{2,1,0:T(8,128)} %get-tuple-element.65.back_ref, f32[2,1,1536]{2,1,0:T(1,128)} %copy.101.out_ref, ...), custom_call_target="tpu_custom_call" | custom-call | flops 4831838208 | bytes 55255040 | tf_op jit(solution)/shard_map/recurrence_backward/pallas_call | solution.py:371
  403.6 7.2 %fusion.65 = f32[1024,1024]{1,0:T(8,128)} fusion(bf16[1024,1536]{1,0:T(8,128)(2,1)} %bitcast.192, bf16[1024,1536]{1,0:T(8,128)(2,1)S(1)} %copy-done.30), kind=kOutput, calls=%fused_computation.152 | convolution fusion | flops 3221225472 | bytes 10485760 | tf_op jit(solution)/shard_map/dot_general | solution.py:1012
  410.9 5.8 %fusion.19 = (f32[1024]{0:T(1024)S(1)}, f32[1024,1024]{1,0:T(8,128)S(1)}) fusion(bf16[1024,1024]{1,0:T(8,128)(2,1)S(1)} %copy-done.11, f32[1024]{0:T(1024)S(1)} %slice_reduce_fusion, f32[1024]{0:T(1024)S(1)} %copy-done.33, f32[1024,1024]{1,0:T(8,128)} %fusion.65, bf16[1024,1536]{1,0:T(8,128)(2,1)S(1)} %bitcast.191, bf16[1024,1536]{1,0:T(8,128)(2,1)S(1)} %copy-done.31), kind=kOutput, calls=%fused_computation.29 | convolution fusion | flops 3227515904 | bytes 16789504 | tf_op jit(solution)/shard_map/dot_general | solution.py:1012
  419.8 5.8 %spread_features.3 = bf16[8,1024,128]{2,1,0:T(8,128)(2,1)} custom-call(bf16[1024,1024]{1,0:T(8,128)(2,1)} %fusion.23.whole_ref), custom_call_target="tpu_custom_call" | custom-call | bytes 4194304 | tf_op jit(solution)/shard_map/spread_features/pallas_call | solution.py:587
  430.0 7.8 %convolution_convert_fusion.1 = bf16[1024,1536]{1,0:T(8,128)(2,1)} fusion(bf16[1024,1024]{1,0:T(8,128)(2,1)} %get-tuple-element.74, bf16[1024,1536]{1,0:T(8,128)(2,1)} %bitcast.190), kind=kOutput, calls=%fused_computation.42 | convolution fusion | flops 3222798336 | bytes 8388608 | tf_op jit(solution)/shard_map/dot_general | solution.py:1006
  444.2 7.7 %convolution_convert_fusion = bf16[1024,1536]{1,0:T(8,128)(2,1)} fusion(bf16[1024,1024]{1,0:T(8,128)(2,1)} %get-tuple-element.74, bf16[1024,1536]{1,0:T(8,128)(2,1)} %bitcast.193), kind=kOutput, calls=%fused_computation.41 | convolution fusion | flops 3222798336 | bytes 8388608 | tf_op jit(solution)/shard_map/dot_general | solution.py:1006
  451.9 75.0 %reduce_streams.1 = (f32[32,1536]{1,0:T(8,128)}, f32[32,1536]{1,0:T(8,128)}, f32[48,256]{1,0:T(8,128)}) custom-call(bf16[2,2,2,2,2,32,1536]{6,5,4,3,2,1,0:T(8,128)(2,1)} %bitcast.162, bf16[2,2,2,2,2,32,1536]{6,5,4,3,2,1,0:T(8,128)(2,1)} %bitcast.163, bf16[2,2,2,2,2,48,256]{6,5,4,3,2,1,0:T(8,128)(2,1)} %pad_maximum_fusion.refs_2_), custom_call_target="tpu_custom_call" | custom-call | bytes 141557760 | tf_op jit(solution)/shard_map/reduce_streams/pallas_call | solution.py:750
  (176 shorter events, 87.7 us)
Async XLA Ops:
  7.2 148.4 %copy-start = (bf16[1536,1024]{1,0:T(8,128)(2,1)S(1)}, bf16[1536,1024]{1,0:T(8,128)(2,1)}, u32[]{:S(2)}) copy-start(bf16[1536,1024]{1,0:T(8,128)(2,1)} %param.29) | copy-start | bytes 9437188
  7.2 60.2 %copy-start.35 = (s32[2]{0:T(128)S(1)}, s32[2]{0:T(128)}, u32[]{:S(2)}) copy-start(s32[2]{0:T(128)} %param.20) | copy-start | bytes 28
  7.2 60.3 %copy-start.32 = (s32[2,8]{1,0:T(2,128)S(1)}, s32[2,8]{1,0:T(2,128)}, u32[]{:S(2)}) copy-start(s32[2,8]{1,0:T(2,128)} %param.19) | copy-start | bytes 196
  7.2 60.6 %copy-start.27 = (f32[1536]{0:T(1024)S(1)}, f32[1536]{0:T(1024)}, u32[]{:S(2)}) copy-start(f32[1536]{0:T(1024)} %param.28) | copy-start | bytes 18436
  63.0 70.2 %all-to-all-start.1 = ((bf16[8,2,512,128]{3,2,1,0:T(8,128)(2,1)}), bf16[8,2,512,128]{3,2,1,0:T(8,128)(2,1)}, u32[]{:S(2)}, u32[]{:S(2)}) async-start(bf16[8,2,512,128]{3,2,1,0:T(8,128)(2,1)} %bitcast.168), calls=%async_computation.1 | async-start | bytes 4194304 | tf_op jit(solution)/shard_map/all_to_all | solution.py:607
  67.4 352.4 %reduce-scatter.3.cloned.1.call-start = ((), (), s32[]{:S(2)}) async-start(), calls=%async_computation.6 | async-start | bytes 13762560 | tf_op jit(solution)/shard_map/reduce_scatter | solution.py:1135
  71.3 23.7 %copy-start.28 = (f32[1536]{0:T(1024)S(1)}, f32[1536]{0:T(1024)}, u32[]{:S(2)}) copy-start(f32[1536]{0:T(1024)} %param.25) | copy-start | bytes 18436
  71.3 23.8 %copy-start.25 = (f32[4,1536]{1,0:T(4,128)S(1)}, f32[4,1536]{1,0:T(4,128)}, u32[]{:S(2)}) copy-start(f32[4,1536]{1,0:T(4,128)} %param.24) | copy-start | bytes 73732
  71.3 23.8 %copy-start.26 = (f32[2,1536]{1,0:T(2,128)S(1)}, f32[2,1536]{1,0:T(2,128)}, u32[]{:S(2)}) copy-start(f32[2,1536]{1,0:T(2,128)} %param.27) | copy-start | bytes 36868
  91.1 5.3 collective-permute-start
  135.0 17.8 %slice-start = ((s8[6291456]{0:T(1024)(128)(4,1)}), s8[4194304]{0:T(1024)(128)(4,1)S(1)}, s32[]{:S(2)}) async-start(s8[6291456]{0:T(1024)(128)(4,1)} %bitcast.157), calls=%async_computation.8 | async-start | bytes 8388608
  159.1 47.9 %copy-start.1 = (f32[1024,1024]{1,0:T(8,128)}, f32[1024,1024]{1,0:T(8,128)S(1)}, u32[]{:S(2)}) copy-start(f32[1024,1024]{1,0:T(8,128)S(1)} %get-tuple-element.155) | copy-start | bytes 12582916
  159.2 9.7 %slice-start.2 = ((s8[6291456]{0:T(1024)(128)(4,1)}), s8[4194304]{0:T(1024)(128)(4,1)S(1)}, s32[]{:S(2)}) async-start(s8[6291456]{0:T(1024)(128)(4,1)} %bitcast.185), calls=%async_computation.10 | async-start | bytes 8388608
  159.6 9.2 %copy-start.9 = (bf16[1024,1024]{1,0:T(8,128)(2,1)}, bf16[1024,1024]{1,0:T(8,128)(2,1)S(1)}, u32[]{:S(2)}) copy-start(bf16[1024,1024]{1,0:T(8,128)(2,1)S(1)} %multiply_convert_fusion.2.normed_ref) | copy-start | bytes 6291460
  224.3 10.8 %copy-start.2 = (f32[1024,1024]{1,0:T(8,128)S(1)}, f32[1024,1024]{1,0:T(8,128)}, u32[]{:S(2)}) copy-start(f32[1024,1024]{1,0:T(8,128)} %copy-done.1) | copy-start | bytes 12582916
  235.1 14.0 %copy-start.4 = (bf16[1024,1024]{1,0:T(8,128)(2,1)S(1)}, bf16[1024,1024]{1,0:T(8,128)(2,1)}, u32[]{:S(2)}) copy-start(bf16[1024,1024]{1,0:T(8,128)(2,1)} %collect_cotangent.1.gout_ref) | copy-start | bytes 6291460
  297.5 54.0 %all-to-all-start.2 = ((bf16[8,2,512,128]{3,2,1,0:T(8,128)(2,1)}), bf16[8,2,512,128]{3,2,1,0:T(8,128)(2,1)}, u32[]{:S(2)}, u32[]{:S(2)}) async-start(bf16[8,2,512,128]{3,2,1,0:T(8,128)(2,1)} %bitcast.160), calls=%async_computation.2 | async-start | bytes 4194304 | tf_op jit(solution)/shard_map/all_to_all | solution.py:625
  302.4 233.0 %reduce-scatter.5.cloned.1.call-start = ((), (), s32[]{:S(2)}) async-start(), calls=%async_computation.7 | async-start | bytes 3440640 | tf_op jit(solution)/shard_map/reduce_scatter | solution.py:1186
  311.4 24.6 %copy-start.22 = (f32[1,2,1536]{2,0,1:T(1,128)S(1)}, f32[1,2,1536]{2,0,1:T(1,128)}, u32[]{:S(2)}) copy-start(f32[1,2,1536]{2,0,1:T(1,128)} %copy-done.21) | copy-start | bytes 36868
  351.6 45.5 %copy-start.17 = (f32[1024,128]{1,0:T(8,128)S(1)}, f32[1024,128]{1,0:T(8,128)}, u32[]{:S(2)}) copy-start(f32[1024,128]{1,0:T(8,128)} %get-tuple-element.63) | copy-start | bytes 1572868
  351.6 52.0 %copy-start.30 = (bf16[1024,1536]{1,0:T(8,128)(2,1)S(1)}, bf16[1024,1536]{1,0:T(8,128)(2,1)}, u32[]{:S(2)}) copy-start(bf16[1024,1536]{1,0:T(8,128)(2,1)} %input_ref.1) | copy-start | bytes 9437188
  395.8 6.2 %collective-permute-start.1 = (bf16[2,3,1536]{2,1,0:T(4,128)(2,1)S(1)}, bf16[2,3,1536]{2,1,0:T(4,128)(2,1)S(1)}, u32[]{:S(2)}, u32[]{:S(2)}) collective-permute-start(bf16[2,3,1536]{2,1,0:T(4,128)(2,1)S(1)} %slice.222), channel_id=1, source_target_pairs={{8,0},{16,8},{24,16},{9,1},{17,9},{25,17},{10,2},{18,10},{26,18},{... | collective-permute-start | bytes 55304 | tf_op jit(solution)/shard_map/ppermute | solution.py:1002
  425.6 109.8 %all-to-all-start.3 = ((bf16[8,2,512,128]{3,2,1,0:T(8,128)(2,1)}), bf16[8,2,512,128]{3,2,1,0:T(8,128)(2,1)}, u32[]{:S(2)}, u32[]{:S(2)}) async-start(bf16[8,2,512,128]{3,2,1,0:T(8,128)(2,1)} %bitcast.159), calls=%async_computation.4 | async-start | bytes 4194304 | tf_op jit(solution)/shard_map/all_to_all | solution.py:625
  539.8 9.9 %copy-start.13 = (f32[4,8,3,1024]{3,1,2,0:T(8,128)}, f32[4,8,3,1024]{3,1,2,0:T(8,128)S(1)}, u32[]{:S(2)}) copy-start(f32[4,8,3,1024]{3,1,2,0:T(8,128)S(1)} %copy.118) | copy-start | bytes 1179652
  (25 other events, 126.0 us)
Sparse Core Ops, SparseCore 0:
  297.6 109.2 reduce-scatter.2
  419.9 87.7 reduce-scatter.4

commit v5 on v4

--- a/solution.py
+++ b/solution.py
@@ -486,7 +486,7 @@
     parts_ref, gain_ref, input_ref, gate_ref, x_ref, inverse_ref, normed_ref, branch_ref, pre_ref
 ):
     tokens = x_ref.shape[0]
-    piece = 64
+    piece, tall = (64, min(tokens, 512))
 
     @pl.when(pl.program_id(0) == 0)
     def _():
@@ -503,19 +503,19 @@
         lax.fori_loop(0, tokens // piece, norm, 0)
 
     def multiply(index, carry):
-        at = pl.ds(pl.multiple_of(index * 256, 256), 256)
+        at = pl.ds(pl.multiple_of(index * tall, tall), tall)
         normed = normed_ref[at, :]
         branch_ref[at, :] = jnp.dot(normed, input_ref[...], preferred_element_type=jnp.float32)
         pre_ref[at, :] = jnp.dot(normed, gate_ref[...], preferred_element_type=jnp.float32)
         return carry
 
-    lax.fori_loop(0, tokens // 256, multiply, 0)
+    lax.fori_loop(0, tokens // tall, multiply, 0)
 
 
 def front(parts, gain, recur_input, recur_gate):
     count, tokens, width = parts.shape
     model, rec = recur_input.shape
-    columns = 3 * LANES
+    columns = 4 * LANES
     low, f32 = (jnp.bfloat16, jnp.float32)
     tall = pl.BlockSpec((model, columns), lambda j: (0, j))
     wide = pl.BlockSpec((tokens, columns), lambda j: (0, j))
@@ -543,39 +543,153 @@
     )(parts, gain[None], recur_input, recur_gate)
 
 
-def collect_kernel(left_ref, parts_ref, out_ref):
-    rows, length = (left_ref.shape[0], out_ref.shape[0] // left_ref.shape[0])
-    piece = 64
-    for row in range(rows):
-
-        def step(index, carry, row=row):
-            base = pl.multiple_of(index * piece, piece)
-            at = pl.ds(row * length + base, piece)
-            low = gathered(parts_ref, at)
-            place = base + lax.broadcasted_iota(jnp.int32, low.shape, 0)
-            value = jnp.where(place < left_ref[row], low.astype(jnp.float32), 0.0)
-            out_ref[at, :] = value.astype(jnp.bfloat16)
+def mlp_kernel(
+    left_ref,
+    parts_ref,
+    normed_ref,
+    resid_ref,
+    gain_ref,
+    gate_ref,
+    up_ref,
+    down_ref,
+    gout_ref,
+    hidden_ref,
+    dgate_ref,
+    dup_ref,
+    result_ref,
+    dres_ref,
+    total_ref,
+    back_ref,
+):
+    tokens, model = normed_ref.shape
+    chunk = down_ref.shape[0]
+    rows = left_ref.shape[0]
+    length = tokens // rows
+    step = pl.program_id(0)
+    slab = 32
+
+    @pl.when(step == 0)
+    def _():
+        for row in range(rows):
+
+            def collect(index, carry, row=row):
+                base = pl.multiple_of(index * slab, slab)
+                at = pl.ds(row * length + base, slab)
+                low = gathered(parts_ref, at)
+                place = base + lax.broadcasted_iota(jnp.int32, low.shape, 0)
+                value = jnp.where(place < left_ref[row], low.astype(jnp.float32), 0.0)
+                gout_ref[at, :] = value.astype(jnp.bfloat16)
+                total_ref[at, :] = resid_ref[at, :]
+                back_ref[at, :] = jnp.zeros((slab, model), jnp.float32)
+                return carry
+
+            lax.fori_loop(0, length // slab, collect, 0)
+
+    tall = min(tokens, 512)
+    wide = 256
+
+    def tile(index, carry):
+        at = pl.ds(pl.multiple_of(index * tall, tall), tall)
+        for column in range(chunk // wide):
+            own = slice(column * wide, (column + 1) * wide)
+            gate = jnp.dot(normed_ref[at, :], gate_ref[:, own], preferred_element_type=jnp.float32)
+            up = jnp.dot(normed_ref[at, :], up_ref[:, own], preferred_element_type=jnp.float32)
+            dhid = lax.dot_general(
+                gout_ref[at, :],
+                down_ref[own, :],
+                (((1,), (1,)), ((), ())),
+                preferred_element_type=jnp.float32,
+            )
+            act, slope = gelu_pair(gate)
+            hidden_ref[at, own] = (act * up).astype(jnp.bfloat16)
+            dgate_ref[at, own] = (dhid * up * slope).astype(jnp.bfloat16)
+            dup_ref[at, own] = (dhid * act).astype(jnp.bfloat16)
+        for column in range(model // (2 * wide)):
+            own = slice(column * 2 * wide, (column + 1) * 2 * wide)
+            total_ref[at, own] += jnp.dot(
+                hidden_ref[at, :], down_ref[:, own], preferred_element_type=jnp.float32
+            )
+            back_ref[at, own] += lax.dot_general(
+                dgate_ref[at, :],
+                gate_ref[own, :],
+                (((1,), (1,)), ((), ())),
+                preferred_element_type=jnp.float32,
+            ) + lax.dot_general(
+                dup_ref[at, :],
+                up_ref[own, :],
+                (((1,), (1,)), ((), ())),
+                preferred_element_type=jnp.float32,
+            )
+        return carry
+
+    lax.fori_loop(0, tokens // tall, tile, 0)
+
+    @pl.when(step == pl.num_programs(0) - 1)
+    def _():
+        parts, width = (result_ref.shape[0], result_ref.shape[2])
+        small = 16
+
+        def finish(index, carry):
+            at = pl.ds(pl.multiple_of(index * small, small), small)
+            result = total_ref[at, :].astype(jnp.bfloat16)
+            for part in range(parts):
+                result_ref[part, at, :] = result[:, part * width : (part + 1) * width]
+            resid = resid_ref[at, :]
+            inverse = lax.rsqrt(jnp.mean(resid * resid, axis=1, keepdims=True) + EPS)
+            normed = resid * inverse
+            scaled = back_ref[at, :] * gain_ref[...]
+            mean = jnp.mean(scaled * normed, axis=1, keepdims=True)
+            dres = gout_ref[at, :].astype(jnp.float32) + inverse * (scaled - normed * mean)
+            dres_ref[at, :] = dres.astype(jnp.bfloat16)
             return carry
 
-        lax.fori_loop(0, length // piece, step, 0)
-
-
-def collect(parts, left):
-    count, tokens, width = parts.shape
+        lax.fori_loop(0, tokens // small, finish, 0)
+
+
+def mlp(left, parts, normed, resid, gain, mlp_gate, mlp_up, mlp_down):
+    tokens, model = normed.shape
+    ffn = mlp_gate.shape[1]
+    chunk = 768
+    low, f32 = (jnp.bfloat16, jnp.float32)
+
+    def whole(shape):
+        return pl.BlockSpec(shape, lambda s: (0,) * len(shape), pipeline_mode=pl.Buffered(1))
+
+    columns = pl.BlockSpec((model, chunk), lambda s: (0, s))
+    made = pl.BlockSpec((tokens, chunk), lambda s: (0, s))
+    tall = jax.ShapeDtypeStruct((tokens, ffn), low)
+    square = jax.ShapeDtypeStruct((tokens, model), low)
     return pl.pallas_call(
-        collect_kernel,
-        name="collect_cotangent",
+        mlp_kernel,
+        name="mlp_forward_backward",
+        grid=(ffn // chunk,),
         in_specs=[
             pl.BlockSpec(memory_space=pltpu.SMEM),
-            pl.BlockSpec(memory_space=pltpu.VMEM),
+            whole(parts.shape),
+            whole(normed.shape),
+            whole(resid.shape),
+            whole((1, model)),
+            columns,
+            columns,
+            pl.BlockSpec((chunk, model), lambda s: (s, 0)),
         ],
-        out_specs=pl.BlockSpec(memory_space=pltpu.VMEM),
-        out_shape=jax.ShapeDtypeStruct((tokens, count * width), parts.dtype),
+        out_specs=[
+            whole((tokens, model)),
+            made,
+            made,
+            made,
+            whole(parts.shape),
+            whole((tokens, model)),
+        ],
+        out_shape=[square, tall, tall, tall, jax.ShapeDtypeStruct(parts.shape, low), square],
+        scratch_shapes=[pltpu.VMEM((tokens, model), f32), pltpu.VMEM((tokens, model), f32)],
         compiler_params=pltpu.CompilerParams(vmem_limit_bytes=VMEM_BYTES),
         cost_estimate=pl.CostEstimate(
-            flops=0, bytes_accessed=4 * count * tokens * width, transcendentals=0
+            flops=12 * tokens * model * ffn,
+            bytes_accessed=6 * (model + tokens) * ffn + 14 * tokens * model,
+            transcendentals=0,
         ),
-    )(left, parts)
+    )(left, parts, normed, resid, gain[None], mlp_gate, mlp_up, mlp_down)
 
 
 def spread_kernel(whole_ref, out_ref):
@@ -612,16 +726,17 @@
     return moved.reshape(1, -1, count * width)
 
 
-def features_apart(whole, length):
+def features_apart(whole):
     count = lax.axis_size(CHAN)
-    width = whole.shape[1] // count
-    if width % LANES == 0:
-        return spread(whole, count).reshape(count, -1, length, width)
-    return whole.reshape(1, -1, length, count * width)
-
-
-def features_out(parts):
-    if parts.shape[0] > 1:
+    if (whole.shape[1] // count) % LANES == 0:
+        return spread(whole, count)
+    return whole[None]
+
+
+def features_out(parts, rows):
+    blocks, tokens, width = parts.shape
+    parts = parts.reshape(blocks, rows, tokens // rows, width)
+    if blocks > 1:
         moved = lax.all_to_all(parts, CHAN, 0, 0, tiled=True)
         return moved.reshape(-1, *parts.shape[2:])
     return lax.all_to_all(parts[0], CHAN, split_axis=2, concat_axis=0, tiled=True)
@@ -1106,24 +1221,17 @@
     inv_two = lax.rsqrt(jnp.mean(resid_one * resid_one, axis=1, keepdims=True) + EPS)
     normed_two = resid_one * inv_two
     normed_low2 = (normed_two * norm2_gain).astype(jnp.bfloat16)
-    mlp_gate_pre = fwd_dot(normed_low2, mlp_gate)
-    mlp_up_pre = fwd_dot(normed_low2, mlp_up)
-    gelu_gate = gelu_fn(mlp_gate_pre)
-    hidden_low = (gelu_gate * mlp_up_pre).astype(jnp.bfloat16)
-    result = (resid_one + fwd_dot(hidden_low, mlp_down)).astype(jnp.bfloat16)
-    grad_low = collect(cotangent, lengths - seq_index * block_len)
-    grad_hidden = back_dot(grad_low, mlp_down)
-    _, gelu_pull = jax.vjp(gelu_fn, mlp_gate_pre)
-    mgate_low = gelu_pull(grad_hidden * mlp_up_pre)[0].astype(jnp.bfloat16)
-    mup_low = (grad_hidden * gelu_gate).astype(jnp.bfloat16)
-    result_parts, mgate_low, mup_low = lax.optimization_barrier(
-        (features_apart(result, block_len), mgate_low, mup_low)
-    )
-    output = features_out(result_parts)
-    grad_norm2 = back_dot(mgate_low, mlp_gate) + back_dot(mup_low, mlp_up)
-    resid_part = norm_back(grad_norm2, normed_two, inv_two, norm2_gain)
-    grad_resid = grad_low.astype(jnp.float32) + resid_part
-    resid_low = grad_resid.astype(jnp.bfloat16)
+    grad_low, hidden_low, mgate_low, mup_low, result_parts, resid_low = mlp(
+        lengths - seq_index * block_len,
+        cotangent,
+        normed_low2,
+        resid_one,
+        norm2_gain,
+        mlp_gate,
+        mlp_up,
+        mlp_down,
+    )
+    output = features_out(result_parts, row_count)
     devices = lax.axis_size(("seq", "zed", "core"))
     own_rows = model_dim // devices
     tiled = own_rows % (2 * SUBLANES) == 0 and ffn_width % model_dim == 0
@@ -1180,11 +1288,11 @@
     inv_one = inverse_lanes[:, :1]
     normed_one = low_x.astype(jnp.float32) * inv_one
     input_part = norm_back(grad_norm1, normed_one, inv_one, norm1_gain)
-    grad_x = (grad_resid + input_part).astype(jnp.bfloat16)
+    grad_x = (resid_low.astype(jnp.float32) + input_part).astype(jnp.bfloat16)
     if tiled:
         merged, grad_x = lax.optimization_barrier((merged, grad_x))
         merged = lax.psum_scatter(merged, "zed", scatter_dimension=0, tiled=True)
-    grad_tokens = features_out(features_apart(grad_x, block_len))
+    grad_tokens = features_out(features_apart(grad_x), row_count)
     if tiled:
         sum_rgate, sum_rin, own_small = reduce_streams(
             (grad_rgate, grad_rin, small.astype(jnp.bfloat16)), (False, True, False)

time: 563 us -> 530 us (0.941)
  matrix products: 121 us -> 39.2 us
  Pallas kernels: 258 us -> 315 us
  local copies, waits for them, and re-layouts: 28.2 us -> 21.2 us
    pallas_call x1, Pallas kernels: 3.37 us -> 65.5 us  [mlp(): pl.pallas_call(mlp_kernel, name='mlp_forward_backward', grid=(ffn // chun...]
    dot_general x6 -> x3, matrix products: 69 us -> 16.9 us  [back_dot(): lax.dot_general(left, right, (((1,), (1,)), ((), ())), preferred_element_...]
    dot_general x4 -> x1, matrix products: 33.4 us -> 3.53 us  [fwd_dot(): return jnp.dot(left, right, preferred_element_type=jnp.float32)]
    pallas_call x2 -> x1, Pallas kernels: 11.4 us -> 5.75 us  [spread(): pl.pallas_call(spread_kernel, name='spread_features', grid=(count,), in_s...]
    unnamed x92 -> x68, local copies, waits for them, and re-layouts: 12.2 us -> 8.39 us
  transfers between devices with their start and end apart: 7 -> 7, of which waited for: 2 -> 2; matrix products, arithmetic and copies ran while one was open for 12% -> 11% of each run, Pallas kernels for 36% -> 39%
where the time goes in v5:
time: 530 us; the launch traced here: 524 us
  Pallas kernels  315 us (59%)
  blocking collectives  73.4 us (14%)
  matrix products  39.2 us (7%)
  other arithmetic  31.1 us (6%)
  local copies, waits for them, and re-layouts  21.2 us (4%)
  starting transfers between devices  18.1 us (3%)
  between operations  15.1 us (3%)
  waiting for transfers between devices  11.5 us (2%)
    pallas_call x3, Pallas kernels, channel_call(): pl.pallas_call(kernel, name=name, grid=(blocks,), in_specs=specs, out_spe...  103 us
    pallas_call x1, Pallas kernels, reduce_streams(): pl.pallas_call(functools.partial(reduce_kernel, corners, orders), name='r...  77.6 us
    pallas_call x1, Pallas kernels, mlp(): pl.pallas_call(mlp_kernel, name='mlp_forward_backward', grid=(ffn // chun...  65.5 us
    all_to_all x1, blocking collectives, features_in(): lax.all_to_all(local.reshape(count, rows // count, length, width), CHAN,...  55.8 us
    pallas_call x1, Pallas kernels, block_gradients(): pl.pallas_call(grads_kernel, name='block_gradients', grid=(total + 1,), i...  46.2 us
    all_gather x2, blocking collectives, carried(): pieces = lax.all_gather(jnp.stack([factor, value]), axis)  17.6 us
    dot_general x3, matrix products, back_dot(): lax.dot_general(left, right, (((1,), (1,)), ((), ())), preferred_element_...  16.9 us
    pallas_call x1, Pallas kernels, front(): pl.pallas_call(front_kernel, name='norm_and_project', grid=(rec // column...  16.1 us
  transfers between devices with their start and end apart: 7, of which 2 were waited for; matrix products, arithmetic and copies ran while one was open for 11% of the time, Pallas kernels for 39%

profile of v5, /device:TPU:0, one launch (start us, length us, event | category | flops | bytes accessed | tf_op | source)
XLA Modules:
  0.0 524.1 jit_solution(5129419626775336106)
XLA Ops:
  7.2 55.8 %all_to_all.20 = bf16[8,2,512,128]{3,2,1,0:T(8,128)(2,1)} all-to-all(bf16[8,2,512,128]{3,2,1,0:T(8,128)(2,1)} %bitcast.156), channel_id=1, replica_groups=mesh['seq'=4,'zed'=4,'core'=2] {'zed','core'}, dimensions={0} | all-to-all | bytes 4194304 | tf_op jit(solution)/shard_map/all_to_all | solution.py:721
  63.0 4.5 all-to-all-start
  71.3 16.1 %norm_and_project.1 = (bf16[1024,1024]{1,0:T(8,128)(2,1)}, f32[1024,128]{1,0:T(8,128)}, bf16[1024,1024]{1,0:T(8,128)(2,1)}, f32[1024,1536]{1,0:T(8,128)}, f32[1024,1536]{1,0:T(8,128)}) custom-call(bf16[8,1024,128]{2,1,0:T(8,128)(2,1)} %bitcast.159, f32[1,1024]{1,0:T(1,128)} %bitcast.176, bf16[1024,1536]{1,0:T(8,128)(2,1)} %input_ref.1, ...), custom_call_target="tpu_custom_call" | custom-call | flops 6442450944 | bytes 20971520 | tf_op jit(solution)/shard_map/norm_and_project/pallas_call | solution.py:526
  88.3 3.4 collective-permute-start
  95.2 35.0 %recurrence_forward.1 = (bf16[2,512,1536]{2,1,0:T(8,128)(2,1)}, f32[2,512,1536]{2,1,0:T(8,128)}, f32[2,512,1536]{2,1,0:T(8,128)}, f32[2,512,1536]{2,1,0:T(8,128)}, f32[2,512,1536]{2,1,0:T(8,128)}) custom-call(f32[2,512,1536]{2,1,0:T(8,128)} %bitcast.143, f32[2,8,1536]{2,1,0:T(8,128)} %pad_convert_fusion.rim_ref, s32[2,512,128]{2,1,0:T(8,128)} %broadcast_in_dim.31.dist_ref, ...), custom_call_target="tpu_custom_call" | custom-call | flops 2415919104 | bytes 37683200 | tf_op jit(solution)/shard_map/recurrence_forward/pallas_call | solution.py:371
  132.2 10.1 %all-gather = f32[8,2,1536]{2,1,0:T(2,128)S(1)} all-gather(f32[2,2,1536]{2,1,0:T(2,128)S(1)} %copy.86), channel_id=2, replica_groups=mesh['seq'=4,'zed'=4,'core'=2] {'seq'}, dimensions={0}, use_global_device_ids=true | all-gather | bytes 122880 | tf_op jit(solution)/shard_map/all_gather | solution.py:1105
  142.3 6.2 %multiply_add_fusion = f32[2,512,1536]{2,1,0:T(8,128)S(1)} fusion(f32[2,512,1536]{2,1,0:T(8,128)} %get-tuple-element.55.state_ref, f32[2,512,1536]{2,1,0:T(8,128)} %get-tuple-element.56.cum_ref, f32[2,1536]{1,0:T(2,128)S(1)} %fusion.29), kind=kLoop, calls=%fused_computation.10 | loop fusion | flops 3145728 | bytes 18886656 | tf_op jit(solution)/shard_map/add | solution.py:1217
  151.4 3.5 multiply_reduce_fusion
  157.6 65.5 %mlp_forward_backward.1 = (bf16[1024,1024]{1,0:T(8,128)(2,1)}, bf16[1024,3072]{1,0:T(8,128)(2,1)}, bf16[1024,3072]{1,0:T(8,128)(2,1)}, bf16[1024,3072]{1,0:T(8,1...) custom-call(s32[2]{0:T(128)} %broadcast_subtract_fusion.1.left_ref, ...), custom_call_target="tpu_custom_call" | custom-call | flops 38654705664 | bytes 52428800 | tf_op jit(solution)/shard_map/mlp_forward_backward/pallas_call | solution.py:662
  223.1 46.2 %block_gradients.1 = bf16[16,336,1024]{2,1,0:T(8,128)(2,1)} custom-call(bf16[1024,1024]{1,0:T(8,128)(2,1)} %multiply_convert_fusion.normed_ref, bf16[1024,3072]{1,0:T(8,128)(2,1)} %get-tuple-element.59.dgate_ref, bf16[1024,3072]{1,0:T(8,128)(2,1)} %get-tuple-element.60.dup_ref, bf16[1024,3072]{1,0:T(8,128)(2,1)} %get-tuple-element.61.hidden_ref, ...), custom_call_target="tpu_custom_call" | custom-call | flops 22548578304 | bytes 39321600 | tf_op jit(solution)/shard_map/block_gradients/pallas_call | solution.py:1069
  269.3 5.0 all-to-all-start.2
  275.0 7.6 %fusion.53 = f32[1024,1536]{1,0:T(8,128)} fusion(bf16[1024,1024]{1,0:T(8,128)(2,1)} %get-tuple-element.64.dres_ref, bf16[1536,1024]{1,0:T(8,128)(2,1)S(1)} %copy-done), kind=kOutput, calls=%fused_computation.130 | convolution fusion | flops 3221225472 | bytes 11534336 | tf_op jit(solution)/shard_map/dot_general | solution.py:1127
  282.6 25.2 %recurrence_adjoint.1 = (bf16[2,512,1536]{2,1,0:T(8,128)(2,1)}, f32[2,512,1536]{2,1,0:T(8,128)}, f32[2,512,1536]{2,1,0:T(8,128)}, f32[2,1,1536]{2,1,0:T(1,128)}) custom-call(f32[2,512,1536]{2,1,0:T(8,128)} %bitcast.150, f32[2,512,1536]{2,1,0:T(8,128)} %bitcast.145, f32[2,512,1536]{2,1,0:T(8,128)} %get-tuple-element.55.state_ref, ...), custom_call_target="tpu_custom_call" | custom-call | bytes 47833088 | tf_op jit(solution)/shard_map/recurrence_adjoint/pallas_call | solution.py:371
  308.6 7.5 %all-gather.1 = f32[8,2,1536]{2,1,0:T(2,128)S(1)} all-gather(f32[2,2,1536]{2,1,0:T(2,128)S(1)} %copy.92), channel_id=3, replica_groups=mesh['seq'=4,'zed'=4,'core'=2] {'seq'}, dimensions={0}, use_global_device_ids=true | all-gather | bytes 122880 | tf_op jit(solution)/shard_map/all_gather | solution.py:1105
  316.7 6.7 %all-to-all-done.2 = bf16[8,2,512,128]{3,2,1,0:T(8,128)(2,1)} async-done(((bf16[8,2,512,128]{3,2,1,0:T(8,128)(2,1)}), bf16[8,2,512,128]{3,2,1,0:T(8,128)(2,1)}, u32[]{:S(2)}, u32[]{:S(2)}) %all-to-all-start.2) | async-done | bytes 2097184 | tf_op jit(solution)/shard_map/all_to_all | solution.py:740
  323.5 43.2 %recurrence_backward.1 = (bf16[2,512,1536]{2,1,0:T(8,128)(2,1)}, f32[2,8,1536]{2,1,0:T(8,128)}, f32[2,8,1536]{2,1,0:T(8,128)}, f32[8,1536]{1,0:T(8,128)}, f32[1536,256]{1,0:T(8,128)}) custom-call(f32[2,512,1536]{2,1,0:T(8,128)} %get-tuple-element.70.local_ref, f32[2,512,1536]{2,1,0:T(8,128)} %get-tuple-element.71.back_ref, f32[2,1,1536]{2,1,0:T(1,128)} %copy.93.out_ref, ...), custom_call_target="tpu_custom_call" | custom-call | flops 4831838208 | bytes 55255040 | tf_op jit(solution)/shard_map/recurrence_backward/pallas_call | solution.py:371
  369.1 4.7 collective-permute-done.1
  375.4 5.5 %fusion.54 = f32[1024,1024]{1,0:T(8,128)S(1)} fusion(bf16[1024,1536]{1,0:T(8,128)(2,1)} %bitcast.179, bf16[1024,1536]{1,0:T(8,128)(2,1)S(1)} %copy-done.22), kind=kOutput, calls=%fused_computation.131 | convolution fusion | flops 3221225472 | bytes 10485760 | tf_op jit(solution)/shard_map/dot_general | solution.py:1127
  380.9 3.8 fusion.12
  387.1 5.8 %spread_features.1 = bf16[8,1024,128]{2,1,0:T(8,128)(2,1)} custom-call(bf16[1024,1024]{1,0:T(8,128)(2,1)} %fusion.16.whole_ref), custom_call_target="tpu_custom_call" | custom-call | bytes 4194304 | tf_op jit(solution)/shard_map/spread_features/pallas_call | solution.py:701
  392.9 3.9 all-to-all-start.3
  396.8 7.8 %convolution_convert_fusion.1 = bf16[1024,1536]{1,0:T(8,128)(2,1)} fusion(bf16[1024,1024]{1,0:T(8,128)(2,1)} %get-tuple-element.80, bf16[1024,1536]{1,0:T(8,128)(2,1)} %bitcast.177), kind=kOutput, calls=%fused_computation.26 | convolution fusion | flops 3222798336 | bytes 8388608 | tf_op jit(solution)/shard_map/dot_general | solution.py:1121
  408.9 7.6 %convolution_convert_fusion = bf16[1024,1536]{1,0:T(8,128)(2,1)} fusion(bf16[1024,1024]{1,0:T(8,128)(2,1)} %get-tuple-element.80, bf16[1024,1536]{1,0:T(8,128)(2,1)} %bitcast.180), kind=kOutput, calls=%fused_computation.25 | convolution fusion | flops 3222798336 | bytes 8388608 | tf_op jit(solution)/shard_map/dot_general | solution.py:1121
  416.5 77.6 %reduce_streams.1 = (f32[32,1536]{1,0:T(8,128)}, f32[32,1536]{1,0:T(8,128)}, f32[48,256]{1,0:T(8,128)}) custom-call(bf16[2,2,2,2,2,32,1536]{6,5,4,3,2,1,0:T(8,128)(2,1)} %bitcast.151, bf16[2,2,2,2,2,32,1536]{6,5,4,3,2,1,0:T(8,128)(2,1)} %bitcast.152, bf16[2,2,2,2,2,48,256]{6,5,4,3,2,1,0:T(8,128)(2,1)} %pad_maximum_fusion.refs_2_), custom_call_target="tpu_custom_call" | custom-call | bytes 141557760 | tf_op jit(solution)/shard_map/reduce_streams/pallas_call | solution.py:865
  (141 shorter events, 50.9 us)
Async XLA Ops:
  7.2 144.2 %copy-start = (bf16[1536,1024]{1,0:T(8,128)(2,1)S(1)}, bf16[1536,1024]{1,0:T(8,128)(2,1)}, u32[]{:S(2)}) copy-start(bf16[1536,1024]{1,0:T(8,128)(2,1)} %param.29) | copy-start | bytes 9437188
  63.0 67.3 %all-to-all-start = ((bf16[8,2,512,128]{3,2,1,0:T(8,128)(2,1)}), bf16[8,2,512,128]{3,2,1,0:T(8,128)(2,1)}, u32[]{:S(2)}, u32[]{:S(2)}) async-start(bf16[8,2,512,128]{3,2,1,0:T(8,128)(2,1)} %bitcast.157), calls=%async_computation | async-start | bytes 4194304 | tf_op jit(solution)/shard_map/all_to_all | solution.py:721
  67.5 319.6 %reduce-scatter.3.cloned.1.call-start = ((), (), s32[]{:S(2)}) async-start(), calls=%async_computation.6 | async-start | bytes 13762560 | tf_op jit(solution)/shard_map/reduce_scatter | solution.py:1243
  71.3 20.9 %copy-start.20 = (f32[1536]{0:T(1024)S(1)}, f32[1536]{0:T(1024)}, u32[]{:S(2)}) copy-start(f32[1536]{0:T(1024)} %param.25) | copy-start | bytes 18436
  71.3 21.0 %copy-start.17 = (f32[4,1536]{1,0:T(4,128)S(1)}, f32[4,1536]{1,0:T(4,128)}, u32[]{:S(2)}) copy-start(f32[4,1536]{1,0:T(4,128)} %param.24) | copy-start | bytes 73732
  71.3 21.0 %copy-start.18 = (f32[2,1536]{1,0:T(2,128)S(1)}, f32[2,1536]{1,0:T(2,128)}, u32[]{:S(2)}) copy-start(f32[2,1536]{1,0:T(2,128)} %param.27) | copy-start | bytes 36868
  88.3 5.3 %collective-permute-start = (bf16[2,3,1536]{2,1,0:T(4,128)(2,1)S(1)}, bf16[2,3,1536]{2,1,0:T(4,128)(2,1)S(1)}, u32[]{:S(2)}, u32[]{:S(2)}) collective-permute-start(bf16[2,3,1536]{2,1,0:T(4,128)(2,1)S(1)} %slice.223), channel_id=1, source_target_pairs={{0,8},{8,16},{16,24},{1,9},{9,17},{17,25},{2,10},{10,18},{18,26},{... | collective-permute-start | bytes 55304 | tf_op jit(solution)/shard_map/ppermute | solution.py:1117
  132.1 16.4 %slice-start = ((s8[6291456]{0:T(1024)(128)(4,1)}), s8[4194304]{0:T(1024)(128)(4,1)S(1)}, s32[]{:S(2)}) async-start(s8[6291456]{0:T(1024)(128)(4,1)} %bitcast.146), calls=%async_computation.8 | async-start | bytes 8388608
  142.3 6.2 %slice-start.1 = ((s8[6291456]{0:T(1024)(128)(4,1)}), s8[2097152]{0:T(1024)(128)(4,1)S(1)}, s32[]{:S(2)}) async-start(s8[6291456]{0:T(1024)(128)(4,1)} %bitcast.146), calls=%async_computation.9 | async-start | bytes 4194304
  269.3 54.1 %all-to-all-start.2 = ((bf16[8,2,512,128]{3,2,1,0:T(8,128)(2,1)}), bf16[8,2,512,128]{3,2,1,0:T(8,128)(2,1)}, u32[]{:S(2)}, u32[]{:S(2)}) async-start(bf16[8,2,512,128]{3,2,1,0:T(8,128)(2,1)} %bitcast.158), calls=%async_computation.2 | async-start | bytes 4194304 | tf_op jit(solution)/shard_map/all_to_all | solution.py:740
  274.3 228.3 %reduce-scatter.5.cloned.1.call-start = ((), (), s32[]{:S(2)}) async-start(), calls=%async_computation.7 | async-start | bytes 3440640 | tf_op jit(solution)/shard_map/reduce_scatter | solution.py:1294
  323.5 45.5 %copy-start.15 = (f32[1024,128]{1,0:T(8,128)S(1)}, f32[1024,128]{1,0:T(8,128)}, u32[]{:S(2)}) copy-start(f32[1024,128]{1,0:T(8,128)} %get-tuple-element.69) | copy-start | bytes 1572868
  323.5 51.9 %copy-start.22 = (bf16[1024,1536]{1,0:T(8,128)(2,1)S(1)}, bf16[1024,1536]{1,0:T(8,128)(2,1)}, u32[]{:S(2)}) copy-start(bf16[1024,1536]{1,0:T(8,128)(2,1)} %input_ref.1) | copy-start | bytes 9437188
  367.6 6.2 %collective-permute-start.1 = (bf16[2,3,1536]{2,1,0:T(4,128)(2,1)S(1)}, bf16[2,3,1536]{2,1,0:T(4,128)(2,1)S(1)}, u32[]{:S(2)}, u32[]{:S(2)}) collective-permute-start(bf16[2,3,1536]{2,1,0:T(4,128)(2,1)S(1)} %slice.222), channel_id=1, source_target_pairs={{8,0},{16,8},{24,16},{9,1},{17,9},{25,17},{10,2},{18,10},{26,18},{... | collective-permute-start | bytes 55304 | tf_op jit(solution)/shard_map/ppermute | solution.py:1117
  375.4 5.5 %copy-start.8 = (bf16[1024,1024]{1,0:T(8,128)(2,1)S(1)}, bf16[1024,1024]{1,0:T(8,128)(2,1)}, u32[]{:S(2)}) copy-start(bf16[1024,1024]{1,0:T(8,128)(2,1)} %get-tuple-element.54) | copy-start | bytes 6291460
  375.4 5.5 %copy-start.23 = (bf16[1024,1536]{1,0:T(8,128)(2,1)S(1)}, bf16[1024,1536]{1,0:T(8,128)(2,1)}, u32[]{:S(2)}) copy-start(bf16[1024,1536]{1,0:T(8,128)(2,1)} %gate_ref.2) | copy-start | bytes 9437188
  375.4 5.5 %copy-start.25 = (f32[1024]{0:T(1024)S(1)}, f32[1024]{0:T(1024)}, u32[]{:S(2)}) copy-start(f32[1024]{0:T(1024)} %param.21) | copy-start | bytes 12292
  375.4 5.5 %copy-start.26 = (bf16[2,512,1536]{2,1,0:T(8,128)(2,1)S(1)}, bf16[2,512,1536]{2,1,0:T(8,128)(2,1)}, u32[]{:S(2)}) copy-start(bf16[2,512,1536]{2,1,0:T(8,128)(2,1)} %get-tuple-element.78) | copy-start | bytes 9437188
  392.9 109.7 %all-to-all-start.3 = ((bf16[8,2,512,128]{3,2,1,0:T(8,128)(2,1)}), bf16[8,2,512,128]{3,2,1,0:T(8,128)(2,1)S(1)}, u32[]{:S(2)}, u32[]{:S(2)}) async-start(bf16[8,2,512,128]{3,2,1,0:T(8,128)(2,1)} %bitcast.149), calls=%async_computation.4 | async-start | bytes 4194304 | tf_op jit(solution)/shard_map/all_to_all | solution.py:740
  396.8 7.8 %copy-start.10 = (f32[1536,256]{1,0:T(8,128)S(1)}, f32[1536,256]{1,0:T(8,128)}, u32[]{:S(2)}) copy-start(f32[1536,256]{1,0:T(8,128)} %get-tuple-element.81) | copy-start | bytes 4718596
  506.5 7.7 %copy-start.11 = (f32[4,8,3,1024]{3,1,2,0:T(8,128)}, f32[4,8,3,1024]{3,1,2,0:T(8,128)S(1)}, u32[]{:S(2)}) copy-start(f32[4,8,3,1024]{3,1,2,0:T(8,128)S(1)} %copy.108) | copy-start | bytes 1179652
  507.7 6.4 %copy-start.3 = (bf16[8,2,512,128]{3,2,1,0:T(8,128)(2,1)S(1)}, bf16[8,2,512,128]{3,2,1,0:T(8,128)(2,1)}, u32[]{:S(2)}) copy-start(bf16[8,2,512,128]{3,2,1,0:T(8,128)(2,1)} %copy-done.2) | copy-start | bytes 6291460
  508.3 7.2 %copy-start.12 = (f32[4,8,3,1024]{3,1,2,0:T(8,128)}, f32[4,8,3,1024]{3,1,2,0:T(8,128)S(1)}, u32[]{:S(2)}) copy-start(f32[4,8,3,1024]{3,1,2,0:T(8,128)S(1)} %copy.109) | copy-start | bytes 1179652
  510.9 6.0 %copy-start.1 = (bf16[1536,1024]{1,0:T(8,128)(2,1)S(1)}, bf16[1536,1024]{1,0:T(8,128)(2,1)}, u32[]{:S(2)}) copy-start(bf16[1536,1024]{1,0:T(8,128)(2,1)} %param.29) | copy-start | bytes 9437188
  (13 other events, 42.5 us)
Sparse Core Ops, SparseCore 0:
  269.4 109.3 reduce-scatter.2
  387.2 88.0 reduce-scatter.4

commit v6 on v5

--- a/solution.py
+++ b/solution.py
@@ -214,10 +214,10 @@
     dbranch_ref,
     tail_ref,
     head_ref,
-    sums_ref,
     dgates_ref,
     both_ref,
     dconv_ref,
+    sums_ref,
 ):
     rows, length, width = local_ref.shape
     taps = [par_ref[k : k + 1, :] for k in range(4)]
@@ -305,12 +305,13 @@
     row_head = lax.broadcasted_iota(jnp.int32, (width, width), 0) // head_size
     col_head = lax.broadcasted_iota(jnp.int32, (width, width), 1) // head_size
     own = row_head == col_head
+    folds = []
     for part in range(2):
         kept = jnp.where(own, wide[:, part * width : (part + 1) * width], 0.0)
         folded = kept
         for other in range(1, width // head_size):
             folded = folded + pltpu.roll(kept, width - other * head_size, 1)
-        dgates_ref[:, part * LANES : (part + 1) * LANES] = folded[:, :LANES]
+        folds.append(folded[:, :LANES])
 
     def conv_step(index, carry):
         sums, following = carry
@@ -364,6 +365,12 @@
         head_ref[row] = total
     for slot in range(5):
         sums_ref[slot : slot + 1, :] = jnp.sum(sums[slot], axis=0, keepdims=True)
+    above = jnp.zeros((head_size, width), jnp.float32)
+    below = jnp.zeros((LANES - head_size - SUBLANES, width), jnp.float32)
+    turned = jnp.concatenate([above, sums_ref[...], below], axis=0).T
+    lane = lax.broadcasted_iota(jnp.int32, (width, LANES), 1)
+    dgates_ref[:, :LANES] = jnp.where(lane < head_size, folds[0], turned).astype(dgates_ref.dtype)
+    dgates_ref[:, LANES:] = folds[1].astype(dgates_ref.dtype)
 
 
 def channel_call(kernel, name, arrays, specs, outs, out_specs, scratch, blocks, flops):
@@ -457,8 +464,7 @@
             self.shape(self.length, jnp.bfloat16),
             self.shape(SUBLANES, f32),
             self.shape(SUBLANES, f32),
-            jax.ShapeDtypeStruct((SUBLANES, self.channels), f32),
-            jax.ShapeDtypeStruct((self.channels, 2 * LANES), f32),
+            jax.ShapeDtypeStruct((self.channels, 2 * LANES), jnp.bfloat16),
         ]
         tall, one = (self.tall(), self.short(1))
         return channel_call(
@@ -468,10 +474,11 @@
             [tall, tall, one, tall, tall, one, tall, tall, tall, self.dist(), tall]
             + [self.short(SUBLANES), self.flat(16), self.gates(2 * self.width)],
             outs,
-            [tall, self.short(SUBLANES), self.short(SUBLANES), self.flat(SUBLANES), self.gates(2 * LANES)],
+            [tall, self.short(SUBLANES), self.short(SUBLANES), self.gates(2 * LANES)],
             [
                 pltpu.VMEM((self.rows, self.length, 2 * self.width), jnp.bfloat16),
                 pltpu.VMEM((self.rows, self.length, self.width), f32),
+                pltpu.VMEM((SUBLANES, self.width), f32),
             ],
             self.blocks,
             2 * self.flops,
@@ -767,119 +774,356 @@
         return {axis: lax.axis_index(axis) + weight * (1 - 2 * self.bit(dim))}
 
 
-def reduce_kernel(corners, orders, *refs):
-    streams = len(orders)
+def tail_kernel(
+    corners,
+    orders,
+    dgate_hbm,
+    dbranch_hbm,
+    ending_ref,
+    leading_ref,
+    mixed_hbm,
+    dres_hbm,
+    normed_hbm,
+    x_hbm,
+    inverse_hbm,
+    gain_ref,
+    input_hbm,
+    gate_hbm,
+    small_hbm,
+    tokens_ref,
+    sum_gate,
+    sum_out,
+    sum_in,
+    sum_small,
+    *refs,
+):
     stages = corners.count + 1
-    given, outs, rest = (refs[:streams], refs[streams : 2 * streams], refs[2 * streams :])
-    owns, rest = (rest[:streams], rest[streams:])
-    slots, (send_sem, recv_sem, load_sem) = (rest[:-3], rest[-3:])
-    core = lax.axis_index("core")
-    partners = [{"core": 1 - core}] + [corners.partner(dim) for dim in range(corners.count)]
+    dgate, dbranch, mixed, dres, normed, x, inverse, weight_in, weight_gate = refs[:9]
+    made_in, made_out, own_small, back, parts, rim = refs[9:15]
+    slots_in, slots_out, slots_small = (
+        refs[15 + k * stages : 15 + (k + 1) * stages] for k in range(3)
+    )
+    (
+        send_sem,
+        recv_sem,
+        load_sem,
+        move_send,
+        move_recv,
+        keep_sem,
+        rim_send,
+        rim_recv,
+    ) = refs[15 + 3 * stages :]
+    seq, zed, core = (lax.axis_index(axis) for axis in ("seq", "zed", "core"))
+    seqs, group = (lax.axis_size("seq"), 2 * lax.axis_size("zed"))
+    mine = zed * 2 + core
+    rows, length = (rim.shape[0], tokens_ref.shape[1])
+    model = x.shape[1]
+
+    def member(index):
+        return {"zed": lax.div(index, 2), "core": lax.rem(index, 2)}
+
+    loads = [
+        pltpu.make_async_copy(source, target, load_sem.at[place])
+        for place, (source, target) in enumerate(
+            (
+                (dbranch_hbm, dbranch),
+                (input_hbm, weight_in),
+                (dgate_hbm, dgate),
+                (gate_hbm, weight_gate),
+                (x_hbm, x),
+                (inverse_hbm, inverse),
+                (dres_hbm, dres),
+                (normed_hbm, normed),
+                (mixed_hbm, mixed),
+                (small_hbm.at[(slice(None),) * corners.count + (core,)], own_small),
+            )
+        )
+    ]
+    for load in loads:
+        load.start()
+
     barrier = pltpu.get_barrier_semaphore()
-    for partner in partners:
-        pl.semaphore_signal(barrier, inc=1, device_id=partner, device_id_type=MESH)
-    pl.semaphore_wait(barrier, len(partners))
-
-    def indices(order, stage, last):
-        fixed = {dim: corners.bit(dim) for dim in order[: stage - 1]}
-        if last is not None:
-            fixed[order[stage - 1]] = last
-        return tuple(fixed.get(dim, slice(None)) for dim in range(corners.count))
+    for other in range(1, group):
+        pl.semaphore_signal(
+            barrier, inc=1, device_id=member(lax.rem(mine + other, group)), device_id_type=MESH
+        )
+    for other in range(1, seqs):
+        pl.semaphore_signal(
+            barrier, inc=1, device_id={"seq": lax.rem(seq + other, seqs)}, device_id_type=MESH
+        )
+    pl.semaphore_wait(barrier, group - 1 + seqs - 1)
+
+    rim_copy = pltpu.make_async_remote_copy(
+        src_ref=leading_ref,
+        dst_ref=rim,
+        send_sem=rim_send,
+        recv_sem=rim_recv,
+        device_id={"seq": lax.rem(seq + seqs - 1, seqs)},
+        device_id_type=MESH,
+    )
+    rim_copy.start()
+
+    def own(stream, index):
+        if stream < 4:
+            return made_in.at[(stream,) + index + (core,)]
+        if stream < 6:
+            return made_out.at[(stream - 4,) + index + (core,)]
+        return own_small.at[index]
+
+    def slot(stream, stage):
+        if stream < 4:
+            return slots_in[stage].at[stream]
+        if stream < 6:
+            return slots_out[stage].at[stream - 4]
+        return slots_small[stage]
 
     def copy(stream, stage):
         order = orders[stream]
+        every = (slice(None),) * corners.count
         if stage == 0:
-            source = given[stream].at[(slice(None),) * corners.count + (1 - core,)]
+            if stream < 4:
+                source = made_in.at[(stream,) + every + (1 - core,)]
+            elif stream < 6:
+                source = made_out.at[(stream - 4,) + every + (1 - core,)]
+            else:
+                source = small_hbm.at[every + (1 - core,)]
             target = {"core": 1 - core}
         else:
             dim = order[stage - 1]
-            source = owns[stream].at[indices(order, stage, 1 - corners.bit(dim))]
+            fixed = {before: corners.bit(before) for before in order[: stage - 1]}
+            fixed[dim] = 1 - corners.bit(dim)
+            source = own(stream, tuple(fixed.get(d, slice(None)) for d in range(corners.count)))
             target = corners.partner(dim)
         return pltpu.make_async_remote_copy(
             src_ref=source,
-            dst_ref=slots[stream * stages + stage],
+            dst_ref=slot(stream, stage),
             send_sem=send_sem.at[stream, stage],
             recv_sem=recv_sem.at[stream, stage],
             device_id=target,
             device_id_type=MESH,
         )
 
-    def load(stream):
+    sums = [
+        sum_gate.at[:, : sum_gate.shape[1] // 2],
+        sum_gate.at[:, sum_gate.shape[1] // 2 :],
+        sum_in.at[:, : sum_in.shape[1] // 2],
+        sum_in.at[:, sum_in.shape[1] // 2 :],
+        sum_out.at[:, : sum_out.shape[1] // 2],
+        sum_out.at[:, sum_out.shape[1] // 2 :],
+        sum_small,
+    ]
+
+    def advance(stream, stage):
+        order = orders[stream]
+        copy(stream, stage).wait_recv()
+        left = [dim for dim in range(corners.count) if dim not in order[:stage]]
+        fixed = {dim: corners.bit(dim) for dim in order[:stage]}
+        arrived = slot(stream, stage)
+        if not left:
+            index = tuple(fixed[dim] for dim in range(corners.count))
+            sums[stream][...] = own(stream, index)[...].astype(jnp.float32) + arrived[...].astype(
+                jnp.float32
+            )
+            return
+
+        def add(index, carry):
+            part = {
+                dim: lax.rem(lax.div(index, 2 ** (len(left) - 1 - place)), 2)
+                for place, dim in enumerate(left)
+            }
+            kept = own(stream, tuple({**fixed, **part}[dim] for dim in range(corners.count)))
+            total = kept[...].astype(jnp.float32) + arrived[
+                tuple(part[dim] for dim in left)
+            ].astype(jnp.float32)
+            kept[...] = total.astype(jnp.bfloat16)
+            return carry
+
+        lax.fori_loop(0, 2 ** len(left), add, 0)
+        copy(stream, stage + 1).start()
+
+    def move(other, row):
+        to = lax.rem(mine + other, group)
+        return pltpu.make_async_remote_copy(
+            src_ref=parts.at[to, pl.ds(row * length, length)],
+            dst_ref=tokens_ref.at[mine * rows + row],
+            send_sem=move_send.at[other - 1, row],
+            recv_sem=move_recv.at[other - 1, row],
+            device_id=member(to),
+            device_id_type=MESH,
+        )
+
+    def keep(row):
         return pltpu.make_async_copy(
-            given[stream].at[(slice(None),) * corners.count + (core,)],
-            owns[stream],
-            load_sem.at[stream],
-        )
-
-    for stream in range(streams):
+            parts.at[mine, pl.ds(row * length, length)],
+            tokens_ref.at[mine * rows + row],
+            keep_sem.at[row],
+        )
+
+    tile = 256
+    width = parts.shape[2]
+
+    def back_row(row):
+        at_row = slice(row * length, (row + 1) * length)
+
+        def product(index, carry):
+            at = pl.ds(pl.multiple_of(index * tile, tile), tile)
+            contract = (((1,), (1,)), ((), ()))
+            back[:, at] = lax.dot_general(
+                dbranch[at_row, :], weight_in[at, :], contract, preferred_element_type=jnp.float32
+            ) + lax.dot_general(
+                dgate[at_row, :], weight_gate[at, :], contract, preferred_element_type=jnp.float32
+            )
+            return carry
+
+        lax.fori_loop(0, model // tile, product, 0)
+        slab = 16
+
+        def norm(index, carry):
+            base = pl.multiple_of(index * slab, slab)
+            at = pl.ds(row * length + base, slab)
+            inv = inverse[at, :1]
+            value = x[at, :].astype(jnp.float32) * inv
+            scaled = back[pl.ds(base, slab), :] * gain_ref[...]
+            mean = jnp.mean(scaled * value, axis=1, keepdims=True)
+            grad = dres[at, :].astype(jnp.float32) + inv * (scaled - value * mean)
+            grad = grad.astype(jnp.bfloat16)
+            for part in range(parts.shape[0]):
+                parts[part, at, :] = grad[:, part * width : (part + 1) * width]
+            return carry
+
+        lax.fori_loop(0, length // slab, norm, 0)
+        for other in range(1, group):
+            move(other, row).start()
+        keep(row).start()
+
+    def weight_product(left, right, made, stream, first):
+        columns = made.shape[-1]
+        shape = made.shape[1:-1]
+
+        def product(index, carry):
+            at = pl.ds(pl.multiple_of(index * tile, tile), tile)
+            source = pl.ds(pl.multiple_of(first + index * tile, tile), tile)
+            part = lax.dot_general(
+                left[...],
+                right[:, source],
+                (((0,), (0,)), ((), ())),
+                preferred_element_type=jnp.float32,
+            )
+            made[(stream,) + (slice(None),) * len(shape) + (at,)] = part.astype(
+                jnp.bfloat16
+            ).reshape(shape + (tile,))
+            return carry
+
+        lax.fori_loop(0, columns // tile, product, 0)
+
+    for load in loads[:2]:
+        load.wait()
+    rim_copy.wait()
+    live = jnp.where(seq < seqs - 1, 1.0, 0.0)
+    for row in range(rows):
+        at = slice((row + 1) * length - STEP, (row + 1) * length)
+        inside = dbranch[at, :].astype(jnp.float32)
+        last = ending_ref[row] + live * rim[row]
+        dbranch[at, :] = jnp.concatenate([inside[: STEP - SUBLANES], last], axis=0).astype(
+            jnp.bfloat16
+        )
+    for load in loads[2:7]:
+        load.wait()
+    copy(6, 0).start()
+    for row in range(rows):
+        back_row(row)
+    for load in loads[7:]:
+        load.wait()
+    half = made_in.shape[-1]
+    for stream in (0, 1):
+        weight_product(normed, dgate, made_in, stream, stream * half)
         copy(stream, 0).start()
-        load(stream).start()
+    half_out = made_out.shape[-1]
+    for stream in (4, 5):
+        weight_product(mixed, dres, made_out, stream - 4, (stream - 4) * half_out)
+        copy(stream, 0).start()
+    for stream in (0, 1, 6):
+        advance(stream, 0)
+    for stream in (2, 3):
+        weight_product(normed, dbranch, made_in, stream, (stream - 2) * half)
+        copy(stream, 0).start()
+    for stream in (4, 5, 2, 3):
+        advance(stream, 0)
+    for stage in range(1, stages):
+        for stream in (0, 1, 6, 4, 5, 2, 3):
+            advance(stream, stage)
     for stage in range(stages):
-        for stream in range(streams):
-            order = orders[stream]
-            own, slot = (owns[stream], slots[stream * stages + stage])
-            if stage == 0:
-                load(stream).wait()
-            copy(stream, stage).wait_recv()
-            left = [dim for dim in range(corners.count) if dim not in order[:stage]]
-            fixed = {dim: corners.bit(dim) for dim in order[:stage]}
-            if left:
-
-                def add(index, carry, own=own, slot=slot, left=left, fixed=fixed):
-                    part = {
-                        dim: lax.rem(lax.div(index, 2 ** (len(left) - 1 - place)), 2)
-                        for place, dim in enumerate(left)
-                    }
-                    mine = tuple({**fixed, **part}[dim] for dim in range(corners.count))
-                    come = tuple(part[dim] for dim in left)
-                    total = own[mine].astype(jnp.float32) + slot[come].astype(jnp.float32)
-                    own[mine] = total.astype(own.dtype)
-                    return carry
-
-                lax.fori_loop(0, 2 ** len(left), add, 0)
-                copy(stream, stage + 1).start()
-            else:
-                mine = tuple(fixed[dim] for dim in range(corners.count))
-                outs[stream][...] = own[mine].astype(jnp.float32) + slot[...].astype(jnp.float32)
-    for stage in range(stages):
-        for stream in range(streams):
+        for stream in range(7):
             copy(stream, stage).wait_send()
-
-
-def reduce_streams(gradients, highs):
+    for row in range(rows):
+        for other in range(1, group):
+            move(other, row).wait()
+        keep(row).wait()
+
+
+def tail(dgate, dbranch, ending, leading, mixed, dres, normed, x, inverse, gain, w_in, w_gate, small):
     corners = Corners(lax.axis_size("seq"), lax.axis_size("zed"))
-    devices = 2 ** (corners.count + 1)
-    orders = [corners.high if high else corners.low for high in highs]
-    blocks = [
-        g.reshape(corners.dims + (2, g.shape[0] // devices, g.shape[1])) for g in gradients
-    ]
-    outs = [jax.ShapeDtypeStruct(b.shape[-2:], jnp.float32) for b in blocks]
-    owns = [pltpu.VMEM(corners.dims + b.shape[-2:], b.dtype) for b in blocks]
-    slots = [
-        pltpu.VMEM((2,) * min(corners.count, corners.count - stage) + b.shape[-2:], b.dtype)
-        for b in blocks
-        for stage in range(corners.count + 1)
-    ]
-    grid = (len(blocks), corners.count + 1)
-    moved = sum(math.prod(g.shape) * g.dtype.itemsize for g in gradients)
+    group, devices = (lax.axis_size(CHAN), 2 ** (corners.count + 1))
+    tokens, model = x.shape
+    rec = dgate.shape[1]
+    rows = ending.shape[0]
+    length, width = (tokens // rows, model // group)
+    low, f32 = (jnp.bfloat16, jnp.float32)
+    stages = corners.count + 1
+    in_rows, out_rows = (model // devices, rec // devices)
+    small = small.reshape(corners.dims + (2, out_rows, small.shape[1]))
+    orders = [corners.low, corners.high] * 3 + [corners.low]
+
+    def slots(lead, shape):
+        return [pltpu.VMEM(lead + (2,) * (corners.count - k) + shape, low) for k in range(stages)]
+
+    in_shape, out_shape = ((in_rows, rec // 2), (out_rows, model // 2))
+    loaded = (dgate, dbranch, mixed, dres, normed, x, inverse, w_in, w_gate)
+    anyplace = pl.BlockSpec(memory_space=pl.ANY)
+    vmem = pl.BlockSpec(memory_space=pltpu.VMEM)
+    dma = pltpu.SemaphoreType.DMA
+    moved = sum(math.prod(a.shape) * a.dtype.itemsize for a in loaded)
     return pl.pallas_call(
-        functools.partial(reduce_kernel, corners, orders),
-        name="reduce_streams",
-        in_specs=[pl.BlockSpec(memory_space=pl.ANY)] * len(blocks),
-        out_specs=[pl.BlockSpec(memory_space=pltpu.VMEM)] * len(blocks),
-        out_shape=outs,
-        scratch_shapes=owns
-        + slots
+        functools.partial(tail_kernel, corners, orders),
+        name="tail",
+        in_specs=[anyplace, anyplace, vmem, vmem] + [anyplace] * 5 + [vmem] + [anyplace] * 3,
+        out_specs=[anyplace] + [vmem] * 4,
+        out_shape=[
+            jax.ShapeDtypeStruct((group * rows, length, width), low),
+            jax.ShapeDtypeStruct((in_rows, rec), f32),
+            jax.ShapeDtypeStruct((out_rows, model), f32),
+            jax.ShapeDtypeStruct((in_rows, rec), f32),
+            jax.ShapeDtypeStruct(small.shape[-2:], f32),
+        ],
+        scratch_shapes=[pltpu.VMEM(a.shape, a.dtype) for a in loaded]
         + [
-            pltpu.SemaphoreType.DMA(grid),
-            pltpu.SemaphoreType.DMA(grid),
-            pltpu.SemaphoreType.DMA((len(blocks),)),
+            pltpu.VMEM((4,) + corners.dims + (2,) + in_shape, low),
+            pltpu.VMEM((2,) + corners.dims + (2,) + out_shape, low),
+            pltpu.VMEM(corners.dims + small.shape[-2:], low),
+            pltpu.VMEM((length, model), f32),
+            pltpu.VMEM((group, tokens, width), low),
+            pltpu.VMEM(leading.shape, leading.dtype),
+        ]
+        + slots((4,), in_shape)
+        + slots((2,), out_shape)
+        + slots((), small.shape[-2:])
+        + [
+            dma((7, stages)),
+            dma((7, stages)),
+            dma((10,)),
+            dma((group - 1, rows)),
+            dma((group - 1, rows)),
+            dma((rows,)),
+            dma,
+            dma,
         ],
         compiler_params=pltpu.CompilerParams(
-            collective_id=1, has_side_effects=True, vmem_limit_bytes=VMEM_BYTES
+            collective_id=1, has_side_effects=True, vmem_limit_bytes=60 * 1024 * 1024
         ),
-        cost_estimate=pl.CostEstimate(flops=0, bytes_accessed=20 * moved, transcendentals=0),
-    )(*blocks)
+        cost_estimate=pl.CostEstimate(
+            flops=10 * tokens * model * rec, bytes_accessed=2 * moved, transcendentals=0
+        ),
+    )(dgate, dbranch, ending, leading, mixed, dres, normed, x, inverse, gain[None], w_in, w_gate, small)
 
 
 def grads_kernel(
@@ -888,16 +1132,12 @@
     dup_ref,
     hidden_ref,
     gout_ref,
-    mixed_ref,
-    dres_ref,
     out_ref,
     turned_ref,
     made_wide,
     made_down,
-    made_out,
     come_wide,
     come_down,
-    come_out,
     send_sem,
     recv_sem,
     store_sem,
@@ -905,10 +1145,10 @@
     step = pl.program_id(0)
     core = lax.axis_index("core")
     other = {"core": 1 - core}
-    wide_rows, down_rows, out_rows = (made_wide.shape[3], made_down.shape[3], made_out.shape[3])
-    wides, downs, lasts = (come_wide.shape[0], come_down.shape[0], come_out.shape[0])
-    total = wides + downs + lasts
-    down_at, out_at = (wides * wide_rows, wides * wide_rows + down_rows)
+    wide_rows, down_rows = (made_wide.shape[3], made_down.shape[3])
+    wides, downs = (come_wide.shape[0], come_down.shape[0])
+    total = wides + downs
+    down_at = wides * wide_rows
 
     def exchange(made, come, index, slot):
         return pltpu.make_async_remote_copy(
@@ -933,14 +1173,6 @@
             come_down.at[index],
             out_ref.at[pl.ds(index * chips, chips), pl.ds(down_at, down_rows)],
             store_sem.at[index + wides],
-        )
-
-    def store_out(index):
-        chips = come_out.shape[1]
-        return pltpu.make_async_copy(
-            come_out.at[index],
-            out_ref.at[pl.ds(index * chips, chips), pl.ds(out_at, out_rows)],
-            store_sem.at[index + wides + downs],
         )
 
     @pl.when(step == 0)
@@ -996,15 +1228,10 @@
     def _():
         exchange(made_wide, come_wide, step, step).start()
 
-    @pl.when((step >= wides) & (step < wides + downs))
+    @pl.when((step >= wides) & (step < total))
     def _():
         product_tall(hidden_ref, gout_ref, made_down, step - wides)
         exchange(made_down, come_down, step - wides, step).start()
-
-    @pl.when((step >= wides + downs) & (step < total))
-    def _():
-        product_tall(mixed_ref, dres_ref, made_out, step - wides - downs)
-        exchange(made_out, come_out, step - wides - downs, step).start()
 
     def finish(made, come, index, slot, store):
         exchange(made, come, index, slot).wait()
@@ -1025,13 +1252,9 @@
     def _():
         finish(made_wide, come_wide, before, before, store_wide)
 
-    @pl.when((before >= wides) & (before < wides + downs))
+    @pl.when(before >= wides)
     def _():
         finish(made_down, come_down, before - wides, before, store_down)
-
-    @pl.when(before >= wides + downs)
-    def _():
-        finish(made_out, come_out, before - wides - downs, before, store_out)
 
     @pl.when(step == total)
     def _():
@@ -1039,21 +1262,19 @@
             store_wide(index).wait()
         for index in range(downs):
             store_down(index).wait()
-        for index in range(lasts):
-            store_out(index).wait()
-
-
-def block_gradients(normed, dgate, dup, hidden, gout, mixed, dres):
+
+
+def block_gradients(normed, dgate, dup, hidden, gout):
     tokens, model = normed.shape
-    ffn, rec = (hidden.shape[1], mixed.shape[1])
+    ffn = hidden.shape[1]
     chips = lax.axis_size("seq") * lax.axis_size("zed")
     devices = 2 * chips
-    wide_rows, down_rows, out_rows = (model // devices, ffn // devices, rec // devices)
+    wide_rows, down_rows = (model // devices, ffn // devices)
     chunk = 768
-    wides, downs, lasts = (2 * ffn // model, ffn // chunk, rec // chunk)
+    wides, downs = (2 * ffn // model, ffn // chunk)
     half = wides // 2
-    down_chips, out_chips = (chunk // (2 * down_rows), chunk // (2 * out_rows))
-    rows = wides * wide_rows + down_rows + out_rows
+    down_chips = chunk // (2 * down_rows)
+    rows = wides * wide_rows + down_rows
     low = jnp.bfloat16
 
     def whole(array):
@@ -1062,9 +1283,9 @@
     def part(columns, first, count):
         return pl.BlockSpec((tokens, columns), lambda s: (0, jnp.clip(s - first, 0, count - 1)))
 
-    total = wides + downs + lasts
-    flops = 2 * tokens * model * (3 * ffn + rec)
-    arrays = (normed, dgate, dup, hidden, gout, mixed, dres)
+    total = wides + downs
+    flops = 6 * tokens * model * ffn
+    arrays = (normed, dgate, dup, hidden, gout)
     moved = sum(math.prod(a.shape) * 2 for a in arrays) + chips * rows * model * 2
     return pl.pallas_call(
         grads_kernel,
@@ -1076,8 +1297,6 @@
             part(model, half, half),
             part(chunk, wides, downs),
             whole(gout),
-            part(chunk, wides + downs, lasts),
-            whole(dres),
         ],
         out_specs=pl.BlockSpec(memory_space=pl.ANY),
         out_shape=jax.ShapeDtypeStruct((chips, rows, model), low),
@@ -1085,10 +1304,8 @@
             pltpu.VMEM((model, tokens), low),
             pltpu.VMEM((2, 2, chips, wide_rows, model), low),
             pltpu.VMEM((2, 2, down_chips, down_rows, model), low),
-            pltpu.VMEM((2, 2, out_chips, out_rows, model), low),
             pltpu.VMEM((wides, chips, wide_rows, model), low),
             pltpu.VMEM((downs, down_chips, down_rows, model), low),
-            pltpu.VMEM((lasts, out_chips, out_rows, model), low),
             pltpu.SemaphoreType.DMA((total,)),
             pltpu.SemaphoreType.DMA((total,)),
             pltpu.SemaphoreType.DMA((total,)),
@@ -1234,10 +1451,10 @@
     output = features_out(result_parts, row_count)
     devices = lax.axis_size(("seq", "zed", "core"))
     own_rows = model_dim // devices
-    tiled = own_rows % (2 * SUBLANES) == 0 and ffn_width % model_dim == 0
+    tiled = own_rows % (2 * SUBLANES) == 0 and tokens.shape[2] % LANES == 0
     if tiled:
         merged = block_gradients(
-            normed_low2, mgate_low, mup_low, hidden_low, grad_low, mixed_low, resid_low
+            normed_low2, mgate_low, mup_low, hidden_low, grad_low
         )
         merged, resid_low = lax.optimization_barrier((merged, resid_low))
         merged = lax.psum_scatter(merged, "seq", scatter_dimension=0, tiled=True)
@@ -1255,7 +1472,7 @@
     gate_low = gate_low.reshape(tok_count, rec_width)
     output, back_local = lax.optimization_barrier((output, back_local))
     carry_out = carried(cum_coef[:, -1, :], first_term[:, 0, :], "seq", True)
-    branch_local, tail, lead, channel_sums, gate_sums = core.backward(
+    branch_local, ending, leading, small = core.backward(
         back_local,
         back_cum,
         carry_out[:, None, :],
@@ -1271,31 +1488,24 @@
         params,
         wide_gates,
     )
-    spare = jnp.swapaxes(channel_sums, 0, 1)
-    small = jnp.concatenate(
-        [gate_sums[:, :head_size], spare, gate_sums[:, head_size + SUBLANES :]], axis=1
-    )
-    from_next = passed_along(
-        lead[:, SUBLANES - rim_size :, :].astype(jnp.bfloat16), "seq", -1
-    )
-    ending = tail + jnp.pad(from_next.astype(jnp.float32), ((0, 0), (SUBLANES - rim_size, 0), (0, 0)))
-    branch_low = lax.dynamic_update_slice(
-        branch_local, ending.astype(jnp.bfloat16), (0, block_len - SUBLANES, 0)
-    ).reshape(tok_count, rec_width)
-    grad_rin = weight_grad(normed_low, branch_low)
-    grad_rgate = weight_grad(normed_low, gate_low)
-    grad_norm1 = back_dot(branch_low, recur_input) + back_dot(gate_low, recur_gate)
-    inv_one = inverse_lanes[:, :1]
-    normed_one = low_x.astype(jnp.float32) * inv_one
-    input_part = norm_back(grad_norm1, normed_one, inv_one, norm1_gain)
-    grad_x = (resid_low.astype(jnp.float32) + input_part).astype(jnp.bfloat16)
+    branch_low = branch_local.reshape(tok_count, rec_width)
     if tiled:
-        merged, grad_x = lax.optimization_barrier((merged, grad_x))
+        merged, branch_low = lax.optimization_barrier((merged, branch_low))
         merged = lax.psum_scatter(merged, "zed", scatter_dimension=0, tiled=True)
-    grad_tokens = features_out(features_apart(grad_x), row_count)
-    if tiled:
-        sum_rgate, sum_rin, own_small = reduce_streams(
-            (grad_rgate, grad_rin, small.astype(jnp.bfloat16)), (False, True, False)
+        grad_tokens, sum_rgate, sum_rout, sum_rin, own_small = tail(
+            gate_low,
+            branch_low,
+            ending,
+            leading,
+            mixed_low,
+            resid_low,
+            normed_low,
+            low_x,
+            inverse_lanes,
+            norm1_gain,
+            recur_input,
+            recur_gate,
+            small,
         )
         own = merged[0].astype(jnp.float32)
         span = ffn_width // model_dim * own_rows
@@ -1304,9 +1514,23 @@
             return jnp.swapaxes(part.reshape(-1, own_rows, model_dim), 0, 1).reshape(own_rows, -1)
 
         sum_mgate, sum_mup = (unfolded(own[:span]), unfolded(own[span : 2 * span]))
-        sum_down = own[2 * span : 2 * span + ffn_width // devices]
-        sum_rout = own[2 * span + ffn_width // devices :]
+        sum_down = own[2 * span :]
     else:
+        from_next = passed_along(
+            leading[:, SUBLANES - rim_size :, :].astype(jnp.bfloat16), "seq", -1
+        )
+        ending = ending + jnp.pad(
+            from_next.astype(jnp.float32), ((0, 0), (SUBLANES - rim_size, 0), (0, 0))
+        )
+        branch_low = lax.dynamic_update_slice(
+            branch_local, ending.astype(jnp.bfloat16), (0, block_len - SUBLANES, 0)
+        ).reshape(tok_count, rec_width)
+        grad_norm1 = back_dot(branch_low, recur_input) + back_dot(gate_low, recur_gate)
+        inv_one = inverse_lanes[:, :1]
+        normed_one = low_x.astype(jnp.float32) * inv_one
+        input_part = norm_back(grad_norm1, normed_one, inv_one, norm1_gain)
+        grad_x = (resid_low.astype(jnp.float32) + input_part).astype(jnp.bfloat16)
+        grad_tokens = features_out(features_apart(grad_x), row_count)
         sum_mgate, sum_mup, sum_down, sum_rout, sum_rgate, sum_rin = (
             scattered(weight_grad(left, right))
             for left, right in (

time: 530 us -> 498 us (0.940)
  matrix products: 39.2 us -> 14.1 us
  Pallas kernels: 315 us -> 332 us
  other arithmetic: 31.1 us -> 22.8 us
    pallas_call x2 -> x1, Pallas kernels: 83.3 us -> 108 us  [tail(): pl.pallas_call(functools.partial(tail_kernel, corners, orders), name='tai...]
    dot_general x2 -> x0, matrix products: 15.4 us -> none  [weight_grad(): lax.dot_general(left, right, (((0,), (0,)), ((), ())), preferred_element_...]
    dot_general x3 -> x1, matrix products: 16.9 us -> 7.26 us  [back_dot(): lax.dot_general(left, right, (((1,), (1,)), ((), ())), preferred_element_...]
    pallas_call x1, Pallas kernels: 46.2 us -> 39.1 us  [block_gradients(): pl.pallas_call(grads_kernel, name='block_gradients', grid=(total + 1,), i...]
  transfers between devices with their start and end apart: 7 -> 5, of which waited for: 2 -> 1; matrix products, arithmetic and copies ran while one was open for 11% -> 5% of each run, Pallas kernels for 39% -> 46%
where the time goes in v6:
time: 498 us; the launch traced here: 497 us
  Pallas kernels  332 us (67%)
  blocking collectives  73.8 us (15%)
  other arithmetic  22.8 us (5%)
  local copies, waits for them, and re-layouts  19.5 us (4%)
  between operations  14.5 us (3%)
  matrix products  14.1 us (3%)
  starting transfers between devices  12.9 us (3%)
  waiting for transfers between devices  7.52 us (2%)
    pallas_call x1, Pallas kernels, tail(): pl.pallas_call(functools.partial(tail_kernel, corners, orders), name='tai...  108 us
    pallas_call x3, Pallas kernels, channel_call(): pl.pallas_call(kernel, name=name, grid=(blocks,), in_specs=specs, out_spe...  103 us
    pallas_call x1, Pallas kernels, mlp(): pl.pallas_call(mlp_kernel, name='mlp_forward_backward', grid=(ffn // chun...  65.4 us
    all_to_all x1, blocking collectives, features_in(): lax.all_to_all(local.reshape(count, rows // count, length, width), CHAN,...  55.8 us
    pallas_call x1, Pallas kernels, block_gradients(): pl.pallas_call(grads_kernel, name='block_gradients', grid=(total + 1,), i...  39.1 us
    all_gather x2, blocking collectives, carried(): pieces = lax.all_gather(jnp.stack([factor, value]), axis)  18 us
    pallas_call x1, Pallas kernels, front(): pl.pallas_call(front_kernel, name='norm_and_project', grid=(rec // column...  16.1 us
  transfers between devices with their start and end apart: 5, of which 1 were waited for; matrix products, arithmetic and copies ran while one was open for 5% of the time, Pallas kernels for 46%

profile of v6, /device:TPU:0, one launch (start us, length us, event | category | flops | bytes accessed | tf_op | source)
XLA Modules:
  0.0 497.0 jit_solution(16761788910435196902)
XLA Ops:
  7.2 55.8 %all_to_all.15 = bf16[8,2,512,128]{3,2,1,0:T(8,128)(2,1)} all-to-all(bf16[8,2,512,128]{3,2,1,0:T(8,128)(2,1)} %bitcast.133), channel_id=1, replica_groups=mesh['seq'=4,'zed'=4,'core'=2] {'zed','core'}, dimensions={0} | all-to-all | bytes 4194304 | tf_op jit(solution)/shard_map/all_to_all | solution.py:728
  63.0 4.4 all-to-all-start
  67.9 3.3 fusion.9.gates_ref
  71.2 16.1 %norm_and_project.1 = (bf16[1024,1024]{1,0:T(8,128)(2,1)}, f32[1024,128]{1,0:T(8,128)}, bf16[1024,1024]{1,0:T(8,128)(2,1)}, f32[1024,1536]{1,0:T(8,128)}, f32[1024,1536]{1,0:T(8,128)}) custom-call(bf16[8,1024,128]{2,1,0:T(8,128)(2,1)} %bitcast.136, f32[1,1024]{1,0:T(1,128)} %bitcast.151, bf16[1024,1536]{1,0:T(8,128)(2,1)} %input_hbm.1, ...), custom_call_target="tpu_custom_call" | custom-call | flops 6442450944 | bytes 20971520 | tf_op jit(solution)/shard_map/norm_and_project/pallas_call | solution.py:533
  88.2 3.4 collective-permute-start
  92.2 1.3 concatenate.10.par_ref
  95.1 35.0 %recurrence_forward.1 = (bf16[2,512,1536]{2,1,0:T(8,128)(2,1)}, f32[2,512,1536]{2,1,0:T(8,128)}, f32[2,512,1536]{2,1,0:T(8,128)}, f32[2,512,1536]{2,1,0:T(8,128)}, f32[2,512,1536]{2,1,0:T(8,128)}) custom-call(f32[2,512,1536]{2,1,0:T(8,128)} %bitcast.125, f32[2,8,1536]{2,1,0:T(8,128)} %pad_convert_fusion.rim_ref, s32[2,512,128]{2,1,0:T(8,128)} %broadcast_in_dim.31.dist_ref, ...), custom_call_target="tpu_custom_call" | custom-call | flops 2415919104 | bytes 37683200 | tf_op jit(solution)/shard_map/recurrence_forward/pallas_call | solution.py:378
  132.1 10.1 %all-gather = f32[8,2,1536]{2,1,0:T(2,128)S(1)} all-gather(f32[2,2,1536]{2,1,0:T(2,128)S(1)} %copy.77), channel_id=2, replica_groups=mesh['seq'=4,'zed'=4,'core'=2] {'seq'}, dimensions={0}, use_global_device_ids=true | all-gather | bytes 122880 | tf_op jit(solution)/shard_map/all_gather | solution.py:1322
  142.2 6.2 %multiply_add_fusion = f32[2,512,1536]{2,1,0:T(8,128)S(1)} fusion(f32[2,512,1536]{2,1,0:T(8,128)} %get-tuple-element.56.state_ref, f32[2,512,1536]{2,1,0:T(8,128)} %get-tuple-element.57.cum_ref, f32[2,1536]{1,0:T(2,128)S(1)} %fusion.21), kind=kLoop, calls=%fused_computation.10 | loop fusion | flops 3145728 | bytes 18886656 | tf_op jit(solution)/shard_map/add | solution.py:1434
  148.5 2.8 fusion.8.mixed_hbm
  151.3 3.5 multiply_reduce_fusion
  154.9 2.1 multiply_convert_fusion.normed_ref
  157.5 65.4 %mlp_forward_backward.1 = (bf16[1024,1024]{1,0:T(8,128)(2,1)}, bf16[1024,3072]{1,0:T(8,128)(2,1)}, bf16[1024,3072]{1,0:T(8,128)(2,1)}, bf16[1024,3072]{1,0:T(8,1...) custom-call(s32[2]{0:T(128)} %broadcast_subtract_fusion.1.left_ref, ...), custom_call_target="tpu_custom_call" | custom-call | flops 38654705664 | bytes 52428800 | tf_op jit(solution)/shard_map/mlp_forward_backward/pallas_call | solution.py:669
  222.9 39.1 %block_gradients.1 = bf16[16,288,1024]{2,1,0:T(8,128)(2,1)} custom-call(bf16[1024,1024]{1,0:T(8,128)(2,1)} %multiply_convert_fusion.normed_ref, bf16[1024,3072]{1,0:T(8,128)(2,1)} %get-tuple-element.60.dgate_ref, bf16[1024,3072]{1,0:T(8,128)(2,1)} %get-tuple-element.61.dup_ref, bf16[1024,3072]{1,0:T(8,128)(2,1)} %get-tuple-element.62.hidden_ref, ...), custom_call_target="tpu_custom_call" | custom-call | flops 19327352832 | bytes 32505856 | tf_op jit(solution)/shard_map/block_gradients/pallas_call | solution.py:1290
  262.0 5.0 %all-to-all-start.2 = ((bf16[8,2,512,128]{3,2,1,0:T(8,128)(2,1)}), bf16[8,2,512,128]{3,2,1,0:T(8,128)(2,1)}, u32[]{:S(2)}, u32[]{:S(2)}) async-start(bf16[8,2,512,128]{3,2,1,0:T(8,128)(2,1)} %bitcast.135), calls=%async_computation.2 | async-start | bytes 4194304 | tf_op jit(solution)/shard_map/all_to_all | solution.py:747
  267.7 7.3 %fusion.45 = f32[1024,1536]{1,0:T(8,128)} fusion(bf16[1024,1024]{1,0:T(8,128)(2,1)} %get-tuple-element.65.dres_hbm, bf16[1536,1024]{1,0:T(8,128)(2,1)S(1)} %copy-done), kind=kOutput, calls=%fused_computation.111 | convolution fusion | flops 3221225472 | bytes 11534336 | tf_op jit(solution)/shard_map/dot_general | solution.py:1344
  275.0 24.4 %recurrence_adjoint.1 = (bf16[2,512,1536]{2,1,0:T(8,128)(2,1)}, f32[2,512,1536]{2,1,0:T(8,128)}, f32[2,512,1536]{2,1,0:T(8,128)}, f32[2,1,1536]{2,1,0:T(1,128)}) custom-call(f32[2,512,1536]{2,1,0:T(8,128)} %bitcast.130, f32[2,512,1536]{2,1,0:T(8,128)} %bitcast.127, f32[2,512,1536]{2,1,0:T(8,128)} %get-tuple-element.56.state_ref, ...), custom_call_target="tpu_custom_call" | custom-call | bytes 47833088 | tf_op jit(solution)/shard_map/recurrence_adjoint/pallas_call | solution.py:378
  300.2 7.9 %all-gather.1 = f32[8,2,1536]{2,1,0:T(2,128)S(1)} all-gather(f32[2,2,1536]{2,1,0:T(2,128)S(1)} %copy.83), channel_id=3, replica_groups=mesh['seq'=4,'zed'=4,'core'=2] {'seq'}, dimensions={0}, use_global_device_ids=true | all-gather | bytes 122880 | tf_op jit(solution)/shard_map/all_gather | solution.py:1322
  308.7 7.5 %all-to-all-done.2 = bf16[8,2,512,128]{3,2,1,0:T(8,128)(2,1)} async-done(((bf16[8,2,512,128]{3,2,1,0:T(8,128)(2,1)}), bf16[8,2,512,128]{3,2,1,0:T(8,128)(2,1)}, u32[]{:S(2)}, u32[]{:S(2)}) %all-to-all-start.2) | async-done | bytes 2097184 | tf_op jit(solution)/shard_map/all_to_all | solution.py:747
  316.2 43.7 %recurrence_backward.1 = (bf16[2,512,1536]{2,1,0:T(8,128)(2,1)}, f32[2,8,1536]{2,1,0:T(8,128)}, f32[2,8,1536]{2,1,0:T(8,128)}, bf16[1536,256]{1,0:T(8,128)(2,1)}) custom-call(f32[2,512,1536]{2,1,0:T(8,128)} %get-tuple-element.71.local_ref, f32[2,512,1536]{2,1,0:T(8,128)} %get-tuple-element.72.back_ref, f32[2,1,1536]{2,1,0:T(1,128)} %copy.84.out_ref, ...), custom_call_target="tpu_custom_call" | custom-call | flops 4831838208 | bytes 54419456 | tf_op jit(solution)/shard_map/recurrence_backward/pallas_call | solution.py:378
  360.0 108.1 %tail.1 = (bf16[16,512,128]{2,1,0:T(8,128)(2,1)}, f32[32,1536]{1,0:T(8,128)}, f32[48,1024]{1,0:T(8,128)}, f32[32,1536]{1,0:T(8,128)}, f32[48,256]{1,0:T(8,128)}) custom-call(bf16[1024,1536]{1,0:T(8,128)(2,1)} %bitcast.153, bf16[1024,1536]{1,0:T(8,128)(2,1)} %bitcast.154, f32[2,8,1536]{2,1,0:T(8,128)} %get-tuple-element.78.ending_ref, ...), custom_call_target="tpu_custom_call" | custom-call | flops 16106127360 | bytes 45088768 | tf_op jit(solution)/shard_map/tail/pallas_call | solution.py:1086
  480.1 1.4 multiply_reduce_fusion.2
  483.6 3.2 copy.111
  486.8 1.3 copy.112
  (101 shorter events, 24.2 us)
Async XLA Ops:
  7.2 144.1 %copy-start = (bf16[1536,1024]{1,0:T(8,128)(2,1)S(1)}, bf16[1536,1024]{1,0:T(8,128)(2,1)}, u32[]{:S(2)}) copy-start(bf16[1536,1024]{1,0:T(8,128)(2,1)} %param.29) | copy-start | bytes 9437188
  7.2 60.2 %copy-start.16 = (s32[2]{0:T(128)S(1)}, s32[2]{0:T(128)}, u32[]{:S(2)}) copy-start(s32[2]{0:T(128)} %param.20) | copy-start | bytes 28
  7.2 60.3 %copy-start.15 = (s32[2,8]{1,0:T(2,128)S(1)}, s32[2,8]{1,0:T(2,128)}, u32[]{:S(2)}) copy-start(s32[2,8]{1,0:T(2,128)} %param.19) | copy-start | bytes 196
  7.2 60.7 %copy-start.12 = (f32[1536]{0:T(1024)S(1)}, f32[1536]{0:T(1024)}, u32[]{:S(2)}) copy-start(f32[1536]{0:T(1024)} %param.28) | copy-start | bytes 18436
  63.0 67.2 %all-to-all-start = ((bf16[8,2,512,128]{3,2,1,0:T(8,128)(2,1)}), bf16[8,2,512,128]{3,2,1,0:T(8,128)(2,1)}, u32[]{:S(2)}, u32[]{:S(2)}) async-start(bf16[8,2,512,128]{3,2,1,0:T(8,128)(2,1)} %bitcast.134), calls=%async_computation | async-start | bytes 4194304 | tf_op jit(solution)/shard_map/all_to_all | solution.py:728
  67.4 292.6 %reduce-scatter.3.cloned.1.call-start = ((), (), s32[]{:S(2)}) async-start(), calls=%async_computation.5 | async-start | bytes 11796480 | tf_op jit(solution)/shard_map/reduce_scatter | solution.py:1460
  71.2 20.9 %copy-start.13 = (f32[1536]{0:T(1024)S(1)}, f32[1536]{0:T(1024)}, u32[]{:S(2)}) copy-start(f32[1536]{0:T(1024)} %param.25) | copy-start | bytes 18436
  71.2 21.0 %copy-start.10 = (f32[4,1536]{1,0:T(4,128)S(1)}, f32[4,1536]{1,0:T(4,128)}, u32[]{:S(2)}) copy-start(f32[4,1536]{1,0:T(4,128)} %param.24) | copy-start | bytes 73732
  71.2 21.0 %copy-start.11 = (f32[2,1536]{1,0:T(2,128)S(1)}, f32[2,1536]{1,0:T(2,128)}, u32[]{:S(2)}) copy-start(f32[2,1536]{1,0:T(2,128)} %param.27) | copy-start | bytes 36868
  88.2 5.3 %collective-permute-start = (bf16[2,3,1536]{2,1,0:T(4,128)(2,1)S(1)}, bf16[2,3,1536]{2,1,0:T(4,128)(2,1)S(1)}, u32[]{:S(2)}, u32[]{:S(2)}) collective-permute-start(bf16[2,3,1536]{2,1,0:T(4,128)(2,1)S(1)} %slice.188), channel_id=1, source_target_pairs={{0,8},{8,16},{16,24},{1,9},{9,17},{17,25},{2,10},{10,18},{18,26},{... | collective-permute-start | bytes 55304 | tf_op jit(solution)/shard_map/ppermute | solution.py:1334
  132.0 16.4 %slice-start = ((s8[6291456]{0:T(1024)(128)(4,1)}), s8[4194304]{0:T(1024)(128)(4,1)S(1)}, s32[]{:S(2)}) async-start(s8[6291456]{0:T(1024)(128)(4,1)} %bitcast.128), calls=%async_computation.7 | async-start | bytes 8388608
  142.2 6.2 %slice-start.1 = ((s8[6291456]{0:T(1024)(128)(4,1)}), s8[2097152]{0:T(1024)(128)(4,1)S(1)}, s32[]{:S(2)}) async-start(s8[6291456]{0:T(1024)(128)(4,1)} %bitcast.128), calls=%async_computation.8 | async-start | bytes 4194304
  148.5 2.9 copy-start.17
  151.3 3.6 copy-start.3
  151.3 3.6 copy-start.14
  262.0 54.2 %all-to-all-start.2 = ((bf16[8,2,512,128]{3,2,1,0:T(8,128)(2,1)}), bf16[8,2,512,128]{3,2,1,0:T(8,128)(2,1)}, u32[]{:S(2)}, u32[]{:S(2)}) async-start(bf16[8,2,512,128]{3,2,1,0:T(8,128)(2,1)} %bitcast.135), calls=%async_computation.2 | async-start | bytes 4194304 | tf_op jit(solution)/shard_map/all_to_all | solution.py:747
  267.0 209.6 %reduce-scatter.5.cloned.1.call-start = ((), (), s32[]{:S(2)}) async-start(), calls=%async_computation.6 | async-start | bytes 2949120 | tf_op jit(solution)/shard_map/reduce_scatter | solution.py:1494
  476.6 4.8 copy-start.2
  478.3 8.5 %copy-start.5 = (f32[4,8,3,1024]{3,1,2,0:T(8,128)}, f32[4,8,3,1024]{3,1,2,0:T(8,128)S(1)}, u32[]{:S(2)}) copy-start(f32[4,8,3,1024]{3,1,2,0:T(8,128)S(1)} %copy.95) | copy-start | bytes 1179652
  479.8 7.0 %copy-start.4 = (bf16[16,512,128]{2,1,0:T(8,128)(2,1)S(1)}, bf16[16,512,128]{2,1,0:T(8,128)(2,1)}, u32[]{:S(2)}) copy-start(bf16[16,512,128]{2,1,0:T(8,128)(2,1)} %get-tuple-element.179) | copy-start | bytes 6291460
  480.0 8.1 %copy-start.6 = (f32[4,8,3,1024]{3,1,2,0:T(8,128)}, f32[4,8,3,1024]{3,1,2,0:T(8,128)S(1)}, u32[]{:S(2)}) copy-start(f32[4,8,3,1024]{3,1,2,0:T(8,128)S(1)} %copy.94) | copy-start | bytes 1179652
  483.6 4.5 copy-start.8
  483.6 5.2 %copy-start.7 = (f32[32,1536]{1,0:T(8,128)S(1)}, f32[32,1536]{1,0:T(8,128)}, u32[]{:S(2)}) copy-start(f32[32,1536]{1,0:T(8,128)} %get-tuple-element.182) | copy-start | bytes 589828
  483.6 5.9 %copy-start.9 = (f32[48,1024]{1,0:T(8,128)S(1)}, f32[48,1024]{1,0:T(8,128)}, u32[]{:S(2)}) copy-start(f32[48,1024]{1,0:T(8,128)} %get-tuple-element.188) | copy-start | bytes 589828
  (1 other events, 2.6 us)
Sparse Core Ops, SparseCore 0:
  262.1 96.1 reduce-scatter.2
  360.6 77.7 reduce-scatter.4

commit v7 on v6

--- a/solution.py
+++ b/solution.py
@@ -17,6 +17,7 @@
 SUBLANES = 8
 STEP = 16
 VMEM_BYTES = 56 * 1024 * 1024
+MESH = pl.DeviceIdType.MESH
 
 
 def sigmoid(value):
@@ -37,14 +38,31 @@
 
 def root_argument(log_decay, decay):
     y = 2.0 * log_decay
-    series = 1.0 + y * (1.0 / 7.0)
-    for divisor in (6.0, 5.0, 4.0, 3.0, 2.0):
-        series = 1.0 + (y * (1.0 / divisor)) * series
-    return jnp.where(y > -0.25, -y * series, 1.0 - decay * decay)
+    series = 1.0 + y * (0.5 + y * (1.0 / 6.0 + y * (1.0 / 24.0)))
+    return jnp.where(y > -0.05, -y * series, 1.0 - decay * decay)
 
 
 def across(column, width):
     return jnp.concatenate([column] * (width // LANES), axis=1)
+
+
+class Rows:
+    def __init__(self, refs):
+        self.refs = refs
+
+    def __getitem__(self, index):
+        if not isinstance(index, tuple):
+            return self.refs[index][0]
+        return self.refs[index[0]][(0,) + index[1:]]
+
+
+def by_rows(refs, rows, apart):
+    found = []
+    for split in apart:
+        count = rows if split else 1
+        found.append(Rows(refs[:count]) if split else refs[0])
+        refs = refs[count:]
+    return found, refs
 
 
 def forward_kernel(
@@ -58,9 +76,11 @@
     igate_ref,
     state_ref,
     cum_ref,
+    last_ref,
     both_ref,
 ):
     rows, length, width = branch_ref.shape
+    span = 2 * STEP if rows == 1 else STEP
     taps = [par_ref[k : k + 1, :] for k in range(4)]
     conv_bias, rate_bias, input_bias, soft = (par_ref[k : k + 1, :] for k in range(4, 8))
     place = lax.broadcasted_iota(jnp.int32, (SUBLANES, width), 0)
@@ -97,12 +117,12 @@
         lax.fori_loop(0, length // piece, dot_step, 0)
 
     def scan_step(index, carry):
-        base = pl.multiple_of(index * STEP, STEP)
+        base = pl.multiple_of(index * span, span)
         later = []
         for row in range(rows):
             run_cum, run_state = carry[row]
-            lru_both = lru_ref[row, pl.ds(base, STEP), :].astype(jnp.float32)
-            for half in range(STEP // SUBLANES):
+            lru_both = lru_ref[row, pl.ds(base, span), :].astype(jnp.float32)
+            for half in range(span // SUBLANES):
                 at = pl.ds(base + half * SUBLANES, SUBLANES)
                 lru = lru_both[half * SUBLANES : (half + 1) * SUBLANES]
                 start = across(dist_ref[row, at, :], width) == 0
@@ -130,24 +150,52 @@
         return tuple(later)
 
     one, zero = (jnp.ones((1, width), jnp.float32), jnp.zeros((1, width), jnp.float32))
-    lax.fori_loop(0, length // STEP, scan_step, tuple((one, zero) for _ in range(rows)))
-
-
-def adjoint_kernel(
-    dmix_ref,
-    pre_ref,
-    state_ref,
-    cum_ref,
-    carry_ref,
-    rate_ref,
-    dist_ref,
-    par_ref,
-    dgate_ref,
-    local_ref,
-    back_ref,
-    first_ref,
-):
-    rows, length, width = dmix_ref.shape
+    done = lax.fori_loop(0, length // span, scan_step, tuple((one, zero) for _ in range(rows)))
+    for row in range(rows):
+        for place in range(2):
+            last_ref[row, place : place + 1, :] = done[row][place]
+
+
+def carried(sent_ref, got_ref, out_ref, send_sem, recv_sem, backward):
+    seq, count = (lax.axis_index("seq"), lax.axis_size("seq"))
+
+    def other(step):
+        return {"seq": lax.rem(seq + step, count)}
+
+    barrier = pltpu.get_barrier_semaphore()
+    for step in range(1, count):
+        pl.semaphore_signal(barrier, inc=1, device_id=other(step), device_id_type=MESH)
+    pl.semaphore_wait(barrier, count - 1)
+    copies = [
+        pltpu.make_async_remote_copy(
+            src_ref=sent_ref,
+            dst_ref=got_ref.at[seq],
+            send_sem=send_sem.at[step - 1],
+            recv_sem=recv_sem.at[step - 1],
+            device_id=other(step),
+            device_id_type=MESH,
+        )
+        for step in range(1, count)
+    ]
+    for copy in copies:
+        copy.start()
+    got_ref[seq] = sent_ref[...]
+    for copy in copies:
+        copy.wait()
+    for row in range(sent_ref.shape[0]):
+        total = jnp.zeros(out_ref.shape[1:], jnp.float32)
+        for place in range(count - 1, 0, -1) if backward else range(count - 1):
+            longer = got_ref[place, row, 0:1, :] * total + got_ref[place, row, 1:2, :]
+            total = jnp.where(place > seq if backward else place < seq, longer, total)
+        out_ref[row] = total
+
+
+def adjoint_kernel(rows, *refs):
+    (dmix_ref, pre_ref, state_ref, cum_ref, carry_ref, rate_ref, dist_ref, par_ref), outs = by_rows(
+        refs, rows, (False, True, True, True, False, True, False, False)
+    )
+    dgate_ref, local_ref, back_ref, first_ref = outs
+    _, length, width = dmix_ref.shape
     soft = par_ref[7:8, :]
     place = lax.broadcasted_iota(jnp.int32, (SUBLANES, width), 0)
     last = length // STEP - 1
@@ -195,31 +243,38 @@
         first_ref[row] = done[row][1]
 
 
-def backward_kernel(
-    head_size,
-    local_ref,
-    back_ref,
-    out_ref,
-    state_ref,
-    cum_ref,
-    in_ref,
-    rate_ref,
-    igate_ref,
-    lru_ref,
-    dist_ref,
-    branch_ref,
-    rim_ref,
-    par_ref,
-    gates_ref,
-    dbranch_ref,
-    tail_ref,
-    head_ref,
-    dgates_ref,
-    both_ref,
-    dconv_ref,
-    sums_ref,
-):
-    rows, length, width = local_ref.shape
+def backward_kernel(head_size, rows, *refs):
+    (
+        local_ref,
+        back_ref,
+        first_ref,
+        last_ref,
+        state_ref,
+        cum_ref,
+        in_ref,
+        rate_ref,
+        igate_ref,
+        lru_ref,
+        dist_ref,
+        branch_ref,
+        rim_ref,
+        par_ref,
+        gates_ref,
+    ), others = by_rows(
+        refs, rows, (False,) * 3 + (True,) * 3 + (False,) + (True,) * 3 + (False,) + (True,) * 2 + (False,) * 2
+    )
+    dbranch_ref, tail_ref, head_ref, dgates_ref, both_ref, dconv_ref, sums_ref = others[:7]
+    leaving_ref, sent_ref, got_ref, send_sem, recv_sem = others[7:]
+    _, length, width = local_ref.shape
+
+    @pl.when(pl.program_id(0) == 0)
+    def _():
+        for row in range(rows):
+            sent_ref[row, 0:1, :] = last_ref[row, 0:1, :]
+            sent_ref[row, 1:2, :] = first_ref[row]
+        carried(sent_ref, got_ref, leaving_ref, send_sem, recv_sem, True)
+
+    block = pl.ds(pl.multiple_of(pl.program_id(0) * width, width), width)
     taps = [par_ref[k : k + 1, :] for k in range(4)]
     soft = par_ref[7:8, :]
     place = lax.broadcasted_iota(jnp.int32, (SUBLANES, width), 0)
@@ -233,7 +288,7 @@
         for row in range(rows):
             before = earlier[row]
             entering = in_ref[row]
-            leaving = out_ref[row]
+            leaving = leaving_ref[row, :, block]
             lru_both = lru_ref[row, pl.ds(base, STEP), :].astype(jnp.float32)
             drates, dinputs = ([], [])
             for half in range(STEP // SUBLANES):
@@ -373,7 +428,9 @@
     dgates_ref[:, LANES:] = folds[1].astype(dgates_ref.dtype)
 
 
-def channel_call(kernel, name, arrays, specs, outs, out_specs, scratch, blocks, flops):
+def channel_call(
+    kernel, name, arrays, specs, outs, out_specs, scratch, blocks, flops, params=()
+):
     moved = sum(math.prod(a.shape) * a.dtype.itemsize for a in (*arrays, *outs))
     return pl.pallas_call(
         kernel,
@@ -383,7 +440,7 @@
         out_specs=out_specs,
         out_shape=outs,
         scratch_shapes=scratch,
-        compiler_params=pltpu.CompilerParams(vmem_limit_bytes=VMEM_BYTES),
+        compiler_params=pltpu.CompilerParams(vmem_limit_bytes=VMEM_BYTES, **dict(params)),
         cost_estimate=pl.CostEstimate(flops=flops, bytes_accessed=moved, transcendentals=0),
     )(*arrays)
 
@@ -401,6 +458,12 @@
 
     def short(self, size):
         return pl.BlockSpec((self.rows, size, self.width), lambda j: (0, 0, j))
+
+    def apart(self, size):
+        return [pl.BlockSpec((1, size, self.width), lambda j: (0, 0, j))] * self.rows
+
+    def whole(self, rows, size):
+        return pl.BlockSpec((rows, size, self.channels), lambda j: (0, 0, 0))
 
     def flat(self, size):
         return pl.BlockSpec((size, self.width), lambda j: (0, j))
@@ -433,8 +496,8 @@
             "recurrence_forward",
             (branch, rim, dist, params, gates),
             [self.tall(), self.short(SUBLANES), self.dist(), self.flat(16), self.gates(2 * self.width)],
-            outs,
-            [self.tall()] * 5,
+            outs + [self.shape(2, f32)],
+            [self.tall()] * 5 + [self.short(2)],
             [pltpu.VMEM((self.rows, self.length, 2 * self.width), f32)],
             self.blocks,
             self.flops,
@@ -443,12 +506,12 @@
     def adjoint(self, dmix, pre, state, cum, entering, rate, dist, params):
         f32 = jnp.float32
         outs = [self.shape(self.length, d) for d in (jnp.bfloat16, f32, f32)] + [self.shape(1, f32)]
-        tall = self.tall()
+        tall, apart = (self.tall(), self.apart(self.length))
         return channel_call(
-            adjoint_kernel,
+            functools.partial(adjoint_kernel, self.rows),
             "recurrence_adjoint",
-            (dmix, pre, state, cum, entering, rate, dist, params),
-            [tall, tall, tall, tall, self.short(1), tall, self.dist(), self.flat(16)],
+            (dmix, *pre, *state, *cum, entering, *rate, dist, params),
+            [tall, *apart * 3, self.short(1), *apart, self.dist(), self.flat(16)],
             outs,
             [tall, tall, tall, self.short(1)],
             [],
@@ -457,7 +520,7 @@
         )
 
     def backward(
-        self, local, back, leaving, state, cum, entering, rate, igate, lru, dist, branch, rim, params, gates
+        self, local, back, first, last, state, cum, entering, rate, igate, lru, dist, branch, rim, params, gates
     ):
         f32 = jnp.float32
         outs = [
@@ -466,22 +529,32 @@
             self.shape(SUBLANES, f32),
             jax.ShapeDtypeStruct((self.channels, 2 * LANES), jnp.bfloat16),
         ]
-        tall, one = (self.tall(), self.short(1))
+        tall, apart = (self.tall(), self.apart(self.length))
+        seqs = lax.axis_size("seq")
+        summary = (self.rows, 2, self.channels)
         return channel_call(
-            functools.partial(backward_kernel, self.head_size),
+            functools.partial(backward_kernel, self.head_size, self.rows),
             "recurrence_backward",
-            (local, back, leaving, state, cum, entering, rate, igate, lru, dist, branch, rim, params, gates),
-            [tall, tall, one, tall, tall, one, tall, tall, tall, self.dist(), tall]
-            + [self.short(SUBLANES), self.flat(16), self.gates(2 * self.width)],
+            (local, back, first, *last, *state, *cum, entering, *rate, *igate, *lru, dist, *branch, *rim)
+            + (params, gates),
+            [tall, tall, self.whole(self.rows, 1), *[self.whole(1, 2)] * self.rows, *apart * 2]
+            + [self.short(1), *apart * 3, self.dist(), *apart, *self.apart(SUBLANES)]
+            + [self.flat(16), self.gates(2 * self.width)],
             outs,
             [tall, self.short(SUBLANES), self.short(SUBLANES), self.gates(2 * LANES)],
             [
                 pltpu.VMEM((self.rows, self.length, 2 * self.width), jnp.bfloat16),
                 pltpu.VMEM((self.rows, self.length, self.width), f32),
                 pltpu.VMEM((SUBLANES, self.width), f32),
+                pltpu.VMEM((self.rows, 1, self.channels), f32),
+                pltpu.VMEM(summary, f32),
+                pltpu.VMEM((seqs,) + summary, f32),
+                pltpu.SemaphoreType.DMA((seqs - 1,)),
+                pltpu.SemaphoreType.DMA((seqs - 1,)),
             ],
             self.blocks,
             2 * self.flops,
+            {"collective_id": 5, "has_side_effects": True},
         )
 
 
@@ -490,13 +563,32 @@
 
 
 def front_kernel(
-    parts_ref, gain_ref, input_ref, gate_ref, x_ref, inverse_ref, normed_ref, branch_ref, pre_ref
+    parts_ref,
+    gain_ref,
+    input_ref,
+    gate_ref,
+    x_ref,
+    inverse_ref,
+    normed_ref,
+    branch_ref,
+    pre_ref,
+    rim_ref,
+    edge_ref,
+    landed_ref,
+    send_sem,
+    recv_sem,
 ):
     tokens = x_ref.shape[0]
     piece, tall = (64, min(tokens, 512))
-
-    @pl.when(pl.program_id(0) == 0)
+    step, steps = (pl.program_id(0), edge_ref.shape[0])
+    seq, seqs = (lax.axis_index("seq"), lax.axis_size("seq"))
+    barrier = pltpu.get_barrier_semaphore()
+
+    @pl.when(step == 0)
     def _():
+        before = {"seq": lax.rem(seq + seqs - 1, seqs)}
+        pl.semaphore_signal(barrier, inc=1, device_id=before, device_id_type=MESH)
+
         def norm(index, carry):
             at = pl.ds(pl.multiple_of(index * piece, piece), piece)
             low = gathered(parts_ref, at)
@@ -517,12 +609,38 @@
         return carry
 
     lax.fori_loop(0, tokens // tall, multiply, 0)
+    edge_ref[step] = branch_ref[tokens - SUBLANES :, :]
+
+    def rim_copy(place):
+        return pltpu.make_async_remote_copy(
+            src_ref=edge_ref.at[place],
+            dst_ref=landed_ref.at[place],
+            send_sem=send_sem.at[place],
+            recv_sem=recv_sem.at[place],
+            device_id={"seq": lax.rem(seq + 1, seqs)},
+            device_id_type=MESH,
+        )
+
+    @pl.when(step == 0)
+    def _():
+        pl.semaphore_wait(barrier, 1)
+
+    rim_copy(step).start()
+
+    @pl.when(step == steps - 1)
+    def _():
+        columns = edge_ref.shape[2]
+        live = jnp.where(seq > 0, 1.0, 0.0)
+        for place in range(steps):
+            rim_copy(place).wait()
+            rim_ref[:, place * columns : (place + 1) * columns] = live * landed_ref[place]
 
 
 def front(parts, gain, recur_input, recur_gate):
     count, tokens, width = parts.shape
     model, rec = recur_input.shape
     columns = 4 * LANES
+    steps = rec // columns
     low, f32 = (jnp.bfloat16, jnp.float32)
     tall = pl.BlockSpec((model, columns), lambda j: (0, j))
     wide = pl.BlockSpec((tokens, columns), lambda j: (0, j))
@@ -533,21 +651,134 @@
     return pl.pallas_call(
         front_kernel,
         name="norm_and_project",
-        grid=(rec // columns,),
+        grid=(steps,),
         in_specs=[whole(parts.shape), whole((1, model)), tall, tall],
-        out_specs=[whole((tokens, model)), whole((tokens, LANES)), whole((tokens, model)), wide, wide],
+        out_specs=[whole((tokens, model)), whole((tokens, LANES)), whole((tokens, model)), wide, wide]
+        + [whole((SUBLANES, rec))],
         out_shape=[
             jax.ShapeDtypeStruct((tokens, model), low),
             jax.ShapeDtypeStruct((tokens, LANES), f32),
             jax.ShapeDtypeStruct((tokens, model), low),
             jax.ShapeDtypeStruct((tokens, rec), f32),
             jax.ShapeDtypeStruct((tokens, rec), f32),
+            jax.ShapeDtypeStruct((SUBLANES, rec), f32),
         ],
-        compiler_params=pltpu.CompilerParams(vmem_limit_bytes=VMEM_BYTES),
+        scratch_shapes=[
+            pltpu.VMEM((steps, SUBLANES, columns), f32),
+            pltpu.VMEM((steps, SUBLANES, columns), f32),
+            pltpu.SemaphoreType.DMA((steps,)),
+            pltpu.SemaphoreType.DMA((steps,)),
+        ],
+        compiler_params=pltpu.CompilerParams(
+            collective_id=3, has_side_effects=True, vmem_limit_bytes=VMEM_BYTES
+        ),
         cost_estimate=pl.CostEstimate(
             flops=4 * tokens * model * rec, bytes_accessed=20 * tokens * model, transcendentals=0
         ),
     )(parts, gain[None], recur_input, recur_gate)
+
+
+def middle_kernel(rows, *refs):
+    (last_ref, state_ref, cum_ref, pre_ref, x_ref, out_ref, gain_ref), others = by_rows(
+        refs, rows, (True,) * 5 + (False,) * 2
+    )
+    entering_ref, mixed_ref, resid_ref, normed_ref = others[:4]
+    sent_ref, got_ref, send_sem, recv_sem = others[4:]
+    tall, model = resid_ref.shape
+    step = pl.program_id(0)
+    tiles = pl.num_programs(0) // rows
+    slab = 16
+
+    @pl.when(step == 0)
+    def _():
+        for row in range(rows):
+            sent_ref[row] = last_ref[row]
+        carried(sent_ref, got_ref, entering_ref, send_sem, recv_sem, False)
+
+    for row in range(rows):
+
+        @pl.when(lax.div(step, tiles) == row)
+        def _(row=row):
+            def mix(index, carry):
+                at = pl.ds(pl.multiple_of(index * slab, slab), slab)
+                state = state_ref[row, at, :] + cum_ref[row, at, :] * entering_ref[row]
+                pre = pre_ref[row, at, :]
+                inner = jnp.tanh(pre * (GELU_C + (GELU_C * GELU_A) * (pre * pre)))
+                mixed_ref[at, :] = (state * (pre * (0.5 + 0.5 * inner))).astype(jnp.bfloat16)
+                return carry
+
+            lax.fori_loop(0, tall // slab, mix, 0)
+            tile = 512
+            for first in range(0, model, tile):
+                at = slice(first, first + tile)
+                resid_ref[:, at] = x_ref.refs[row][:, at].astype(jnp.float32) + jnp.dot(
+                    mixed_ref[...], out_ref[:, at], preferred_element_type=jnp.float32
+                )
+
+    def norm(index, carry):
+        at = pl.ds(pl.multiple_of(index * slab, slab), slab)
+        resid = resid_ref[at, :]
+        inverse = lax.rsqrt(jnp.mean(resid * resid, axis=1, keepdims=True) + EPS)
+        normed_ref[at, :] = (resid * inverse * gain_ref[...]).astype(jnp.bfloat16)
+        return carry
+
+    lax.fori_loop(0, tall // slab, norm, 0)
+
+
+def middle(last, state, cum, pre, x, recur_out, gain):
+    rows = len(state)
+    _, length, rec = state[0].shape
+    model = recur_out.shape[1]
+    tall = min(length, 256)
+    tiles = length // tall
+    tokens = rows * length
+    seqs = lax.axis_size("seq")
+    low, f32 = (jnp.bfloat16, jnp.float32)
+
+    def whole(shape):
+        return pl.BlockSpec(shape, lambda s: (0,) * len(shape), pipeline_mode=pl.Buffered(1))
+
+    def part(row):
+        return lambda s: (0, jnp.clip(s - row * tiles, 0, tiles - 1), 0)
+
+    def flat(row):
+        return lambda s: (jnp.clip(s - row * tiles, 0, tiles - 1), 0)
+
+    apart = [pl.BlockSpec((1, tall, rec), part(row)) for row in range(rows)]
+    summary = (rows, 2, rec)
+    return pl.pallas_call(
+        functools.partial(middle_kernel, rows),
+        name="mix_and_norm",
+        grid=(rows * tiles,),
+        in_specs=[whole((1, 2, rec))] * rows
+        + apart * 3
+        + [pl.BlockSpec((tall, model), flat(row)) for row in range(rows)]
+        + [whole(recur_out.shape), whole((1, model))],
+        out_specs=[
+            pl.BlockSpec((rows, 1, rec), lambda s: (0, 0, 0)),
+            pl.BlockSpec((tall, rec), lambda s: (s, 0)),
+            pl.BlockSpec((tall, model), lambda s: (s, 0)),
+            pl.BlockSpec((tall, model), lambda s: (s, 0)),
+        ],
+        out_shape=[
+            jax.ShapeDtypeStruct((rows, 1, rec), f32),
+            jax.ShapeDtypeStruct((tokens, rec), low),
+            jax.ShapeDtypeStruct((tokens, model), f32),
+            jax.ShapeDtypeStruct((tokens, model), low),
+        ],
+        scratch_shapes=[
+            pltpu.VMEM(summary, f32),
+            pltpu.VMEM((seqs,) + summary, f32),
+            pltpu.SemaphoreType.DMA((seqs - 1,)),
+            pltpu.SemaphoreType.DMA((seqs - 1,)),
+        ],
+        compiler_params=pltpu.CompilerParams(
+            collective_id=4, has_side_effects=True, vmem_limit_bytes=VMEM_BYTES
+        ),
+        cost_estimate=pl.CostEstimate(
+            flops=2 * tokens * rec * model, bytes_accessed=14 * tokens * rec, transcendentals=0
+        ),
+    )(*last, *state, *cum, *pre, *x, recur_out, gain[None])
 
 
 def mlp_kernel(
@@ -721,15 +952,15 @@
 CHAN = ("zed", "core")
 
 
-def features_in(local):
+def features_in(local, pick=slice(None)):
     count = lax.axis_size(CHAN)
     rows, length, width = local.shape
+    local = local.reshape(count, rows // count, length, width)[:, pick]
     if width % LANES == 0:
-        moved = lax.all_to_all(
-            local.reshape(count, rows // count, length, width), CHAN, 0, 0, tiled=True
-        )
-        return moved.reshape(count, -1, width)
-    moved = lax.all_to_all(local, CHAN, split_axis=0, concat_axis=2, tiled=True)
+        return lax.all_to_all(local, CHAN, 0, 0, tiled=True).reshape(count, -1, width)
+    moved = lax.all_to_all(
+        local.reshape(-1, length, width), CHAN, split_axis=0, concat_axis=2, tiled=True
+    )
     return moved.reshape(1, -1, count * width)
 
 
@@ -747,9 +978,6 @@
         moved = lax.all_to_all(parts, CHAN, 0, 0, tiled=True)
         return moved.reshape(-1, *parts.shape[2:])
     return lax.all_to_all(parts[0], CHAN, split_axis=2, concat_axis=0, tiled=True)
-
-
-MESH = pl.DeviceIdType.MESH
 
 
 class Corners:
@@ -783,20 +1011,16 @@
     leading_ref,
     mixed_hbm,
     dres_hbm,
-    normed_hbm,
-    x_hbm,
-    inverse_hbm,
     gain_ref,
     input_hbm,
     gate_hbm,
     small_hbm,
-    tokens_ref,
-    sum_gate,
-    sum_out,
-    sum_in,
-    sum_small,
     *refs,
 ):
+    rows = ending_ref.shape[0]
+    normed_hbms, x_hbms, inverse_hbms = (refs[k * rows : (k + 1) * rows] for k in range(3))
+    tokens_ref, sum_gate, sum_out, sum_in, sum_small = refs[3 * rows : 3 * rows + 5]
+    refs = refs[3 * rows + 5 :]
     stages = corners.count + 1
     dgate, dbranch, mixed, dres, normed, x, inverse, weight_in, weight_gate = refs[:9]
     made_in, made_out, own_small, back, parts, rim = refs[9:15]
@@ -816,28 +1040,34 @@
     seq, zed, core = (lax.axis_index(axis) for axis in ("seq", "zed", "core"))
     seqs, group = (lax.axis_size("seq"), 2 * lax.axis_size("zed"))
     mine = zed * 2 + core
-    rows, length = (rim.shape[0], tokens_ref.shape[1])
+    length = tokens_ref.shape[1]
     model = x.shape[1]
 
     def member(index):
         return {"zed": lax.div(index, 2), "core": lax.rem(index, 2)}
 
+    def by_row(sources, target):
+        return [
+            (source, target.at[pl.ds(row * length, length)]) for row, source in enumerate(sources)
+        ]
+
+    early = [
+        (dbranch_hbm, dbranch),
+        (input_hbm, weight_in),
+        (dgate_hbm, dgate),
+        (gate_hbm, weight_gate),
+        (dres_hbm, dres),
+        *by_row(x_hbms, x),
+        *by_row(inverse_hbms, inverse),
+    ]
+    late = [
+        *by_row(normed_hbms, normed),
+        (mixed_hbm, mixed),
+        (small_hbm.at[(slice(None),) * corners.count + (core,)], own_small),
+    ]
     loads = [
         pltpu.make_async_copy(source, target, load_sem.at[place])
-        for place, (source, target) in enumerate(
-            (
-                (dbranch_hbm, dbranch),
-                (input_hbm, weight_in),
-                (dgate_hbm, dgate),
-                (gate_hbm, weight_gate),
-                (x_hbm, x),
-                (inverse_hbm, inverse),
-                (dres_hbm, dres),
-                (normed_hbm, normed),
-                (mixed_hbm, mixed),
-                (small_hbm.at[(slice(None),) * corners.count + (core,)], own_small),
-            )
-        )
+        for place, (source, target) in enumerate(early + late)
     ]
     for load in loads:
         load.start()
@@ -1027,12 +1257,12 @@
         dbranch[at, :] = jnp.concatenate([inside[: STEP - SUBLANES], last], axis=0).astype(
             jnp.bfloat16
         )
-    for load in loads[2:7]:
+    for load in loads[2 : len(early)]:
         load.wait()
     copy(6, 0).start()
     for row in range(rows):
         back_row(row)
-    for load in loads[7:]:
+    for load in loads[len(early) :]:
         load.wait()
     half = made_in.shape[-1]
     for stream in (0, 1):
@@ -1061,10 +1291,10 @@
         keep(row).wait()
 
 
-def tail(dgate, dbranch, ending, leading, mixed, dres, normed, x, inverse, gain, w_in, w_gate, small):
+def tail(dgate, dbranch, ending, leading, mixed, dres, gain, w_in, w_gate, small, normed, x, inverse):
     corners = Corners(lax.axis_size("seq"), lax.axis_size("zed"))
     group, devices = (lax.axis_size(CHAN), 2 ** (corners.count + 1))
-    tokens, model = x.shape
+    tokens, model = dres.shape
     rec = dgate.shape[1]
     rows = ending.shape[0]
     length, width = (tokens // rows, model // group)
@@ -1078,7 +1308,8 @@
         return [pltpu.VMEM(lead + (2,) * (corners.count - k) + shape, low) for k in range(stages)]
 
     in_shape, out_shape = ((in_rows, rec // 2), (out_rows, model // 2))
-    loaded = (dgate, dbranch, mixed, dres, normed, x, inverse, w_in, w_gate)
+    loaded = (dgate, dbranch, mixed, dres, dres, dres)
+    loaded += (jax.ShapeDtypeStruct((tokens, LANES), f32), w_in, w_gate)
     anyplace = pl.BlockSpec(memory_space=pl.ANY)
     vmem = pl.BlockSpec(memory_space=pltpu.VMEM)
     dma = pltpu.SemaphoreType.DMA
@@ -1086,7 +1317,8 @@
     return pl.pallas_call(
         functools.partial(tail_kernel, corners, orders),
         name="tail",
-        in_specs=[anyplace, anyplace, vmem, vmem] + [anyplace] * 5 + [vmem] + [anyplace] * 3,
+        in_specs=[anyplace, anyplace, vmem, vmem, anyplace, anyplace, vmem]
+        + [anyplace] * (3 + 3 * rows),
         out_specs=[anyplace] + [vmem] * 4,
         out_shape=[
             jax.ShapeDtypeStruct((group * rows, length, width), low),
@@ -1110,7 +1342,7 @@
         + [
             dma((7, stages)),
             dma((7, stages)),
-            dma((10,)),
+            dma((7 + 3 * rows,)),
             dma((group - 1, rows)),
             dma((group - 1, rows)),
             dma((rows,)),
@@ -1123,7 +1355,7 @@
         cost_estimate=pl.CostEstimate(
             flops=10 * tokens * model * rec, bytes_accessed=2 * moved, transcendentals=0
         ),
-    )(dgate, dbranch, ending, leading, mixed, dres, normed, x, inverse, gain[None], w_in, w_gate, small)
+    )(dgate, dbranch, ending, leading, mixed, dres, gain[None], w_in, w_gate, small, *normed, *x, *inverse)
 
 
 def grads_kernel(
@@ -1185,7 +1417,7 @@
     def product_wide(source, index):
         made = made_wide.at[lax.rem(index, 2)]
         chips, rows = (made.shape[1], made.shape[2])
-        tile = 256
+        tile = 512
 
         def column(place, carry):
             at = pl.ds(pl.multiple_of(place * tile, tile), tile)
@@ -1200,7 +1432,7 @@
     def product_tall(left, right, made_all, index):
         made = made_all.at[lax.rem(index, 2)]
         chips, rows = (made.shape[1], made.shape[2])
-        tile = 256
+        tile = 512
 
         def column(place, carry):
             at = pl.ds(pl.multiple_of(place * tile, tile), tile)
@@ -1315,17 +1547,6 @@
         ),
         cost_estimate=pl.CostEstimate(flops=flops, bytes_accessed=moved, transcendentals=0),
     )(*arrays)
-
-
-def carried(factor, value, axis, backward):
-    count, mine = (lax.axis_size(axis), lax.axis_index(axis))
-    pieces = lax.all_gather(jnp.stack([factor, value]), axis)
-    order = range(count - 1, 0, -1) if backward else range(count - 1)
-    total = jnp.zeros_like(value)
-    for place in order:
-        longer = pieces[place, 0] * total + pieces[place, 1]
-        total = jnp.where(place > mine if backward else place < mine, longer, total)
-    return total
 
 
 def passed_along(value, axis, steps):
@@ -1400,16 +1621,6 @@
     bounds = jnp.concatenate([doc_starts, lengths[:, None]], axis=1)
     is_before = bounds[:, None, :] <= position[None, :, None]
     seg_start = jnp.max(jnp.where(is_before, bounds[:, None, :], 0), axis=2)
-    low_x, inverse_lanes, normed_low, branch_pre, gate_pre = front(
-        features_in(tokens), norm1_gain, recur_input, recur_gate
-    )
-    gate_act = gelu_fn(gate_pre)
-    branch_rows = branch_pre.reshape(row_count, block_len, rec_width)
-    core = Recurrence(row_count, block_len, rec_width, head_size)
-    prev_rim = passed_along(
-        branch_rows[:, block_len - rim_size :, :].astype(jnp.bfloat16), "seq", 1
-    ).astype(jnp.float32)
-    rim = jnp.pad(prev_rim, ((0, 0), (SUBLANES - rim_size, 0), (0, 0)))
     dist = jnp.broadcast_to(
         (position[None, :] - seg_start)[:, :, None], (row_count, block_len, LANES)
     )
@@ -1424,20 +1635,35 @@
         ],
         axis=0,
     )
+    core = Recurrence(row_count, block_len, rec_width, head_size)
     wide_gates = core.widen(lru_gates)
-    lru_in, rate_gate, input_gate, local_state, cum_coef = core.forward(
-        branch_rows, rim, dist, params, wide_gates
-    )
-    cotangent, local_state = lax.optimization_barrier((features_in(cotangent), local_state))
-    carry_in = carried(cum_coef[:, -1, :], local_state[:, -1, :], "seq", False)
-    entering = carry_in[:, None, :]
-    state_rows = local_state + cum_coef * entering
-    state_flat = state_rows.reshape(tok_count, rec_width)
-    mixed_low = (state_flat * gate_act).astype(jnp.bfloat16)
-    resid_one = low_x.astype(jnp.float32) + fwd_dot(mixed_low, recur_out)
-    inv_two = lax.rsqrt(jnp.mean(resid_one * resid_one, axis=1, keepdims=True) + EPS)
-    normed_two = resid_one * inv_two
-    normed_low2 = (normed_two * norm2_gain).astype(jnp.bfloat16)
+    if tokens.shape[2] % LANES == 0:
+        blocks = [features_in(tokens, slice(row, row + 1)) for row in range(row_count)]
+    else:
+        side = features_in(tokens)
+        blocks = [side[:, row * block_len : (row + 1) * block_len] for row in range(row_count)]
+    single = Recurrence(1, block_len, rec_width, head_size)
+    per_row = []
+    for row in range(row_count):
+        block = blocks[row]
+        if row:
+            block, _ = lax.optimization_barrier((block, per_row[-1][-1]))
+        else:
+            block, wide_gates, params, dist = lax.optimization_barrier(
+                (block, wide_gates, params, dist)
+            )
+        low_x, inverse, normed, branch, pre, rim = front(block, norm1_gain, recur_input, recur_gate)
+        branch, rim = (branch[None], rim[None])
+        scanned = single.forward(branch, rim, dist[row : row + 1], params, wide_gates)
+        per_row.append((low_x, inverse, normed, branch, pre[None], rim, *scanned))
+    low_x, inverse, normed_low, branch, gate_pre, rim, lru_in, rate, igate, state, cum, last = zip(
+        *per_row
+    )
+    entering, mixed_low, resid_one, normed_low2 = middle(
+        last, state, cum, gate_pre, low_x, recur_out, norm2_gain
+    )
+    cotangent, _ = lax.optimization_barrier((cotangent, low_x[-1]))
+    cotangent, resid_one = lax.optimization_barrier((features_in(cotangent), resid_one))
     grad_low, hidden_low, mgate_low, mup_low, result_parts, resid_low = mlp(
         lengths - seq_index * block_len,
         cotangent,
@@ -1461,29 +1687,29 @@
     grad_mixed = back_dot(resid_low, recur_out)
     gate_low, back_local, back_cum, first_term = core.adjoint(
         grad_mixed.reshape(row_count, block_len, rec_width),
-        gate_pre.reshape(row_count, block_len, rec_width),
-        local_state,
-        cum_coef,
+        gate_pre,
+        state,
+        cum,
         entering,
-        rate_gate,
+        rate,
         dist,
         params,
     )
     gate_low = gate_low.reshape(tok_count, rec_width)
     output, back_local = lax.optimization_barrier((output, back_local))
-    carry_out = carried(cum_coef[:, -1, :], first_term[:, 0, :], "seq", True)
     branch_local, ending, leading, small = core.backward(
         back_local,
         back_cum,
-        carry_out[:, None, :],
-        local_state,
-        cum_coef,
+        first_term,
+        last,
+        state,
+        cum,
         entering,
-        rate_gate,
-        input_gate,
+        rate,
+        igate,
         lru_in,
         dist,
-        branch_rows,
+        branch,
         rim,
         params,
         wide_gates,
@@ -1499,13 +1725,13 @@
             leading,
             mixed_low,
             resid_low,
-            normed_low,
-            low_x,
-            inverse_lanes,
             norm1_gain,
             recur_input,
             recur_gate,
             small,
+            normed_low,
+            low_x,
+            inverse,
         )
         own = merged[0].astype(jnp.float32)
         span = ffn_width // model_dim * own_rows
@@ -1526,8 +1752,9 @@
             branch_local, ending.astype(jnp.bfloat16), (0, block_len - SUBLANES, 0)
         ).reshape(tok_count, rec_width)
         grad_norm1 = back_dot(branch_low, recur_input) + back_dot(gate_low, recur_gate)
-        inv_one = inverse_lanes[:, :1]
-        normed_one = low_x.astype(jnp.float32) * inv_one
+        inv_one = jnp.concatenate(inverse)[:, :1]
+        normed_one = jnp.concatenate(low_x).astype(jnp.float32) * inv_one
+        normed_low = jnp.concatenate(normed_low)
         input_part = norm_back(grad_norm1, normed_one, inv_one, norm1_gain)
         grad_x = (resid_low.astype(jnp.float32) + input_part).astype(jnp.bfloat16)
         grad_tokens = features_out(features_apart(grad_x), row_count)

time: 498 us -> 485 us (0.974)
  blocking collectives: 73.8 us -> 0 us
  waiting for transfers between devices: 7.52 us -> 48.2 us
  Pallas kernels: 332 us -> 362 us
  other arithmetic: 22.8 us -> 9.41 us
  starting transfers between devices: 12.9 us -> 18.9 us
    all_to_all x1 -> x0, blocking collectives: 55.8 us -> none  [features_in(): lax.all_to_all(local.reshape(count, rows // count, length, width), CHAN,...]
    pallas_call x1 -> x3, Pallas kernels: 16.1 us -> 52.2 us  [the longest x2 27.1 us: front(): pl.pallas_call(front_kernel, name='norm_and_project', grid=(steps,), in_s...]
    all_to_all x1 -> x3, waiting for transfers between devices: 0.01 us -> 32.5 us  [features_in(): lax.all_to_all(local, CHAN, 0, 0, tiled=True).reshape(count, -1, width)]
    all_gather x2 -> x0, blocking collectives: 18 us -> none  [carried(): pieces = lax.all_gather(jnp.stack([factor, value]), axis)]
    all_to_all x1 -> x3, starting transfers between devices: 4.37 us -> 15.1 us  [features_in(): lax.all_to_all(local, CHAN, 0, 0, tiled=True).reshape(count, -1, width)]
    all_to_all x1, waiting for transfers between devices: 7.46 us -> 15.7 us  [features_out(): moved = lax.all_to_all(parts, CHAN, 0, 0, tiled=True)]
    add x2 -> x0, other arithmetic: 6.23 us -> none  [the longest x1 6.21 us: body(): state_rows = local_state + cum_coef * entering]
    pallas_call x3 -> x4, Pallas kernels: 103 us -> 103 us  [channel_call(): pl.pallas_call(kernel, name=name, grid=(blocks,), in_specs=specs, out_spe...]
  transfers between devices with their start and end apart: 5 -> 6, of which waited for: 1 -> 3; matrix products, arithmetic and copies ran while one was open for 5% -> 5% of each run, Pallas kernels for 46% -> 51%
where the time goes in v7:
time: 485 us; the launch traced here: 484 us
  Pallas kernels  362 us (75%)
  waiting for transfers between devices  48.2 us (10%)
  local copies, waits for them, and re-layouts  19.3 us (4%)
  starting transfers between devices  18.9 us (4%)
  between operations  14.4 us (3%)
  matrix products  11.7 us (2%)
  other arithmetic  9.41 us (2%)
    pallas_call x1, Pallas kernels, tail(): pl.pallas_call(functools.partial(tail_kernel, corners, orders), name='tai...  106 us
    pallas_call x4, Pallas kernels, channel_call(): pl.pallas_call(kernel, name=name, grid=(blocks,), in_specs=specs, out_spe...  103 us
    pallas_call x1, Pallas kernels, mlp(): pl.pallas_call(mlp_kernel, name='mlp_forward_backward', grid=(ffn // chun...  66.3 us
    pallas_call x1, Pallas kernels, block_gradients(): pl.pallas_call(grads_kernel, name='block_gradients', grid=(total + 1,), i...  34.8 us
    all_to_all x3, waiting for transfers between devices, features_in(): lax.all_to_all(local, CHAN, 0, 0, tiled=True).reshape(count, -1, width)  32.5 us
    pallas_call x2, Pallas kernels, front(): pl.pallas_call(front_kernel, name='norm_and_project', grid=(steps,), in_s...  27.1 us
    pallas_call x1, Pallas kernels, middle(): pl.pallas_call(functools.partial(middle_kernel, rows), name='mix_and_norm...  25.1 us
    all_to_all x1, waiting for transfers between devices, features_out(): moved = lax.all_to_all(parts, CHAN, 0, 0, tiled=True)  15.7 us
  transfers between devices with their start and end apart: 6, of which 3 were waited for; matrix products, arithmetic and copies ran while one was open for 5% of the time, Pallas kernels for 51%

profile of v7, /device:TPU:0, one launch (start us, length us, event | category | flops | bytes accessed | tf_op | source)
XLA Modules:
  0.0 484.0 jit_solution(3202557657899661801)
XLA Ops:
  7.2 3.1 fusion.21
  10.4 6.5 %all-to-all-start.1 = ((bf16[8,1,512,128]{3,2,1,0:T(8,128)(2,1)}), bf16[8,1,512,128]{3,2,1,0:T(8,128)(2,1)S(1)}, u32[]{:S(2)}, u32[]{:S(2)}) async-start(bf16[8,1,512,128]{3,2,1,0:T(8,128)(2,1)} %get-tuple-element.199), calls=%async_computation.1 | async-start | bytes 2097152 | tf_op jit(solution)/shard_map/all_to_all | solution.py:960
  17.1 26.3 %all-to-all-done.1 = bf16[8,1,512,128]{3,2,1,0:T(8,128)(2,1)S(1)} async-done(((bf16[8,1,512,128]{3,2,1,0:T(8,128)(2,1)}), bf16[8,1,512,128]{3,2,1,0:T(8,128)(2,1)S(1)}, u32[]{:S(2)}, u32[]{:S(2)}) %all-to-all-start.1) | async-done | bytes 1048608 | tf_op jit(solution)/shard_map/all_to_all | solution.py:960
  43.4 3.6 all-to-all-start
  47.1 1.3 concatenate.9.par_ref.refs_11_.refs_21_
  48.5 2.3 fusion.gates_ref.refs_22_
  51.9 14.5 %norm_and_project.2 = (bf16[512,1024]{1,0:T(8,128)(2,1)}, f32[512,128]{1,0:T(8,128)}, bf16[512,1024]{1,0:T(8,128)(2,1)}, f32[512,1536]{1,0:T(8,128)}, f32[512,1536]{1,0:T(8,128)}, /*index=5*/f32[8,1536]{1,0:T(8,128)}) custom-call(bf16[8,512,128]{2,1,0:T(8,128)(2,1)} %bitcast.61, f32[1,1024]{1,0:T(1,128)} %bitcast.70, bf16[1024,1536]{1,0:T(8,128)(2,1)} %input_hbm.1, ...), custom_call_target="tpu_custom_call" | custom-call | flops 3221225472 | bytes 10485760 | tf_op jit(solution)/shard_map/norm_and_project/pallas_call | solution.py:651
  66.4 17.0 %recurrence_forward.2 = (bf16[1,512,1536]{2,1,0:T(8,128)(2,1)}, f32[1,512,1536]{2,1,0:T(8,128)}, f32[1,512,1536]{2,1,0:T(8,128)}, f32[1,512,1536]{2,1,0:T(8,128)...) custom-call(f32[1,512,1536]{2,1,0:T(8,128)} %bitcast.40, f32[1,8,1536]{2,1,0:T(8,128)} %bitcast.64, ...), custom_call_target="tpu_custom_call" | custom-call | flops 1207959552 | bytes 20082688 | tf_op jit(solution)/shard_map/recurrence_forward/pallas_call | solution.py:435
  84.4 12.6 %norm_and_project.3 = (bf16[512,1024]{1,0:T(8,128)(2,1)}, f32[512,128]{1,0:T(8,128)}, bf16[512,1024]{1,0:T(8,128)(2,1)}, f32[512,1536]{1,0:T(8,128)}, f32[512,1536]{1,0:T(8,128)}, /*index=5*/f32[8,1536]{1,0:T(8,128)}) custom-call(bf16[8,512,128]{2,1,0:T(8,128)(2,1)} %bitcast.62, f32[1,1024]{1,0:T(1,128)} %bitcast.71, bf16[1024,1536]{1,0:T(8,128)(2,1)} %input_hbm.1, ...), custom_call_target="tpu_custom_call" | custom-call | flops 3221225472 | bytes 10485760 | tf_op jit(solution)/shard_map/norm_and_project/pallas_call | solution.py:651
  97.1 5.0 %all-to-all-start.2 = ((bf16[8,2,512,128]{3,2,1,0:T(8,128)(2,1)}), bf16[8,2,512,128]{3,2,1,0:T(8,128)(2,1)S(1)}, u32[]{:S(2)}, u32[]{:S(2)}) async-start(bf16[8,2,512,128]{3,2,1,0:T(8,128)(2,1)} %bitcast.8), calls=%async_computation.2 | async-start | bytes 4194304 | tf_op jit(solution)/shard_map/all_to_all | solution.py:960
  102.8 17.0 %recurrence_forward.3 = (bf16[1,512,1536]{2,1,0:T(8,128)(2,1)}, f32[1,512,1536]{2,1,0:T(8,128)}, f32[1,512,1536]{2,1,0:T(8,128)}, f32[1,512,1536]{2,1,0:T(8,128)...) custom-call(f32[1,512,1536]{2,1,0:T(8,128)} %bitcast.42, f32[1,8,1536]{2,1,0:T(8,128)} %bitcast.66, ...), custom_call_target="tpu_custom_call" | custom-call | flops 1207959552 | bytes 20082688 | tf_op jit(solution)/shard_map/recurrence_forward/pallas_call | solution.py:435
  119.9 25.1 %mix_and_norm.1 = (f32[2,1,1536]{2,1,0:T(1,128)}, bf16[1024,1536]{1,0:T(8,128)(2,1)}, f32[1024,1024]{1,0:T(8,128)}, bf16[1024,1024]{1,0:T(8,128)(2,1)}) custom-call(f32[1,2,1536]{2,1,0:T(2,128)} %get-tuple-element.82.refs_0_.refs_3_, f32[1,2,1536]{2,1,0:T(2,128)} %get-tuple-element.88.refs_1_.refs_4_, ...), custom_call_target="tpu_custom_call" | custom-call | flops 3221225472 | bytes 22020096 | tf_op jit(solution)/shard_map/mix_and_norm/pallas_call | solution.py:749
  145.0 6.1 %all-to-all-done.2 = bf16[8,2,512,128]{3,2,1,0:T(8,128)(2,1)S(1)} async-done(((bf16[8,2,512,128]{3,2,1,0:T(8,128)(2,1)}), bf16[8,2,512,128]{3,2,1,0:T(8,128)(2,1)S(1)}, u32[]{:S(2)}, u32[]{:S(2)}) %all-to-all-start.2) | async-done | bytes 2097184 | tf_op jit(solution)/shard_map/all_to_all | solution.py:960
  151.2 1.3 copy-done.5
  152.5 66.3 %mlp_forward_backward.1 = (bf16[1024,1024]{1,0:T(8,128)(2,1)}, bf16[1024,3072]{1,0:T(8,128)(2,1)}, bf16[1024,3072]{1,0:T(8,128)(2,1)}, bf16[1024,3072]{1,0:T(8,1...) custom-call(s32[2]{0:T(128)} %broadcast_subtract_fusion.1.left_ref, bf16[8,1024,128]{2,1,0:T(8,128)(2,1)} %bitcast.54, ...), custom_call_target="tpu_custom_call" | custom-call | flops 38654705664 | bytes 52428800 | tf_op jit(solution)/shard_map/mlp_forward_backward/pallas_call | solution.py:900
  218.7 34.8 %block_gradients.1 = bf16[16,288,1024]{2,1,0:T(8,128)(2,1)} custom-call(bf16[1024,1024]{1,0:T(8,128)(2,1)} %get-tuple-element.98.normed_ref, bf16[1024,3072]{1,0:T(8,128)(2,1)} %get-tuple-element.101.dgate_ref, bf16[1024,3072]{1,0:T(8,128)(2,1)} %get-tuple-element.102.dup_ref, bf16[1024,3072]{1,0:T(8,128)(2,1)} %get-tuple-element.103.hidden_ref, ...), custom_call_target="tpu_custom_call" | custom-call | flops 19327352832 | bytes 32505856 | tf_op jit(solution)/shard_map/block_gradients/pallas_call | solution.py:1522
  253.6 3.6 all-to-all-start.3
  257.3 9.4 %fusion.25 = f32[1024,1536]{1,0:T(8,128)} fusion(bf16[1024,1024]{1,0:T(8,128)(2,1)} %get-tuple-element.106.dres_hbm, bf16[1536,1024]{1,0:T(8,128)(2,1)} %refs_10_.1), kind=kOutput, calls=%fused_computation.61 | convolution fusion | flops 3221225472 | bytes 11534336 | tf_op jit(solution)/shard_map/dot_general | solution.py:1565
  266.6 23.9 %recurrence_adjoint.1 = (bf16[2,512,1536]{2,1,0:T(8,128)(2,1)}, f32[2,512,1536]{2,1,0:T(8,128)}, f32[2,512,1536]{2,1,0:T(8,128)}, f32[2,1,1536]{2,1,0:T(1,128)}) custom-call(f32[2,512,1536]{2,1,0:T(8,128)} %bitcast.49, f32[1,512,1536]{2,1,0:T(8,128)} %bitcast.45, f32[1,512,1536]{2,1,0:T(8,128)} %bitcast.47, ...), custom_call_target="tpu_custom_call" | custom-call | bytes 47833088 | tf_op jit(solution)/shard_map/recurrence_adjoint/pallas_call | solution.py:435
  290.5 15.7 %all-to-all-done.3 = bf16[8,2,512,128]{3,2,1,0:T(8,128)(2,1)S(1)} async-done(((bf16[8,2,512,128]{3,2,1,0:T(8,128)(2,1)}), bf16[8,2,512,128]{3,2,1,0:T(8,128)(2,1)S(1)}, u32[]{:S(2)}, u32[]{:S(2)}) %all-to-all-start.3) | async-done | bytes 2097184 | tf_op jit(solution)/shard_map/all_to_all | solution.py:978
  306.2 45.3 %recurrence_backward.1 = (bf16[2,512,1536]{2,1,0:T(8,128)(2,1)}, f32[2,8,1536]{2,1,0:T(8,128)}, f32[2,8,1536]{2,1,0:T(8,128)}, bf16[1536,256]{1,0:T(8,128)(2,1)}) custom-call(f32[2,512,1536]{2,1,0:T(8,128)} %get-tuple-element.114.refs_0_, f32[2,512,1536]{2,1,0:T(8,128)} %get-tuple-element.115.refs_1_, f32[2,1,1536]{2,1,0:T(1,128)} %get-tuple-element.116.refs_2_, ...), custom_call_target="tpu_custom_call" | custom-call | flops 4831838208 | bytes 54444032 | tf_op jit(solution)/shard_map/recurrence_backward/pallas_call | solution.py:435
  351.6 105.5 %tail.1 = (bf16[16,512,128]{2,1,0:T(8,128)(2,1)}, f32[32,1536]{1,0:T(8,128)}, f32[48,1024]{1,0:T(8,128)}, f32[32,1536]{1,0:T(8,128)}, f32[48,256]{1,0:T(8,128)}) custom-call(bf16[1024,1536]{1,0:T(8,128)(2,1)} %bitcast.73, bf16[1024,1536]{1,0:T(8,128)(2,1)} %bitcast.74, f32[2,8,1536]{2,1,0:T(8,128)} %get-tuple-element.123.ending_ref, ...), custom_call_target="tpu_custom_call" | custom-call | flops 16106127360 | bytes 45088768 | tf_op jit(solution)/shard_map/tail/pallas_call | solution.py:1317
  472.4 1.3 copy.67
  473.8 1.3 copy.68
  (83 shorter events, 20.7 us)
Async XLA Ops:
  7.2 41.3 %copy-start = (bf16[1536,192]{0,1:T(8,128)(2,1)S(1)}, bf16[1536,192]{0,1:T(8,128)(2,1)}, u32[]{:S(2)}) copy-start(bf16[1536,192]{0,1:T(8,128)(2,1)} %param.26) | copy-start | bytes 1769476
  7.2 9.6 %copy-start.18 = (s32[2]{0:T(128)S(1)}, s32[2]{0:T(128)}, u32[]{:S(2)}) copy-start(s32[2]{0:T(128)} %param.20) | copy-start | bytes 28
  7.2 9.7 %copy-start.16 = (f32[1536]{0:T(1024)S(1)}, f32[1536]{0:T(1024)}, u32[]{:S(2)}) copy-start(f32[1536]{0:T(1024)} %param.25) | copy-start | bytes 18436
  7.2 9.7 %copy-start.17 = (s32[2,8]{1,0:T(2,128)S(1)}, s32[2,8]{1,0:T(2,128)}, u32[]{:S(2)}) copy-start(s32[2,8]{1,0:T(2,128)} %param.19) | copy-start | bytes 196
  10.3 36.6 %copy-start.15 = (f32[1536]{0:T(1024)S(1)}, f32[1536]{0:T(1024)}, u32[]{:S(2)}) copy-start(f32[1536]{0:T(1024)} %param.28) | copy-start | bytes 18436
  10.3 36.7 %copy-start.13 = (f32[4,1536]{1,0:T(4,128)S(1)}, f32[4,1536]{1,0:T(4,128)}, u32[]{:S(2)}) copy-start(f32[4,1536]{1,0:T(4,128)} %param.24) | copy-start | bytes 73732
  10.3 36.7 %copy-start.14 = (f32[2,1536]{1,0:T(2,128)S(1)}, f32[2,1536]{1,0:T(2,128)}, u32[]{:S(2)}) copy-start(f32[2,1536]{1,0:T(2,128)} %param.27) | copy-start | bytes 36868
  10.4 33.1 %all-to-all-start.1 = ((bf16[8,1,512,128]{3,2,1,0:T(8,128)(2,1)}), bf16[8,1,512,128]{3,2,1,0:T(8,128)(2,1)S(1)}, u32[]{:S(2)}, u32[]{:S(2)}) async-start(bf16[8,1,512,128]{3,2,1,0:T(8,128)(2,1)} %get-tuple-element.199), calls=%async_computation.1 | async-start | bytes 2097152 | tf_op jit(solution)/shard_map/all_to_all | solution.py:960
  43.4 7.4 %copy-start.8 = (bf16[8,1,512,128]{3,2,1,0:T(8,128)(2,1)}, bf16[8,1,512,128]{3,2,1,0:T(8,128)(2,1)S(1)}, u32[]{:S(2)}) copy-start(bf16[8,1,512,128]{3,2,1,0:T(8,128)(2,1)S(1)} %all-to-all-done.1) | copy-start | bytes 3145732
  43.4 40.0 %all-to-all-start = ((bf16[8,1,512,128]{3,2,1,0:T(8,128)(2,1)}), bf16[8,1,512,128]{3,2,1,0:T(8,128)(2,1)S(1)}, u32[]{:S(2)}, u32[]{:S(2)}) async-start(bf16[8,1,512,128]{3,2,1,0:T(8,128)(2,1)} %get-tuple-element.200), calls=%async_computation | async-start | bytes 2097152 | tf_op jit(solution)/shard_map/all_to_all | solution.py:960
  51.0 15.4 %copy-start.2 = (s32[2,512,128]{2,1,0:T(8,128)}, s32[2,512,128]{2,1,0:T(8,128)S(1)}, u32[]{:S(2)}) copy-start(s32[2,512,128]{2,1,0:T(8,128)S(1)} %broadcast_in_dim.73.refs_10_.refs_16_) | copy-start | bytes 1572868
  97.1 54.1 %all-to-all-start.2 = ((bf16[8,2,512,128]{3,2,1,0:T(8,128)(2,1)}), bf16[8,2,512,128]{3,2,1,0:T(8,128)(2,1)S(1)}, u32[]{:S(2)}, u32[]{:S(2)}) async-start(bf16[8,2,512,128]{3,2,1,0:T(8,128)(2,1)} %bitcast.8), calls=%async_computation.2 | async-start | bytes 4194304 | tf_op jit(solution)/shard_map/all_to_all | solution.py:960
  102.1 249.4 %reduce-scatter.3.cloned.1.call-start = ((), (), s32[]{:S(2)}) async-start(), calls=%async_computation.6 | async-start | bytes 11796480 | tf_op jit(solution)/shard_map/reduce_scatter | solution.py:1686
  151.2 1.3 copy-start.5
  253.6 52.6 %all-to-all-start.3 = ((bf16[8,2,512,128]{3,2,1,0:T(8,128)(2,1)}), bf16[8,2,512,128]{3,2,1,0:T(8,128)(2,1)S(1)}, u32[]{:S(2)}, u32[]{:S(2)}) async-start(bf16[8,2,512,128]{3,2,1,0:T(8,128)(2,1)} %bitcast.53), calls=%async_computation.3 | async-start | bytes 4194304 | tf_op jit(solution)/shard_map/all_to_all | solution.py:978
  257.2 208.4 %reduce-scatter.5.cloned.1.call-start = ((), (), s32[]{:S(2)}) async-start(), calls=%async_computation.7 | async-start | bytes 2949120 | tf_op jit(solution)/shard_map/reduce_scatter | solution.py:1720
  465.6 4.7 copy-start.3
  467.2 6.5 %copy-start.6 = (f32[4,8,3,1024]{3,1,2,0:T(8,128)}, f32[4,8,3,1024]{3,1,2,0:T(8,128)S(1)}, u32[]{:S(2)}) copy-start(f32[4,8,3,1024]{3,1,2,0:T(8,128)S(1)} %copy.60) | copy-start | bytes 1179652
  469.0 4.8 copy-start.7
  470.2 3.5 copy-start.4
  472.4 4.7 copy-start.1
  473.8 1.3 copy-start.11
  473.8 2.0 copy-start.10
  473.8 2.7 copy-start.12
  (1 other events, 1.0 us)
Sparse Core Ops, SparseCore 0:
  253.7 92.8 reduce-scatter.2
  351.7 74.0 reduce-scatter.4

commit v8 on v7

--- a/solution.py
+++ b/solution.py
@@ -191,11 +191,26 @@
 
 
 def adjoint_kernel(rows, *refs):
-    (dmix_ref, pre_ref, state_ref, cum_ref, carry_ref, rate_ref, dist_ref, par_ref), outs = by_rows(
-        refs, rows, (False, True, True, True, False, True, False, False)
-    )
-    dgate_ref, local_ref, back_ref, first_ref = outs
+    (
+        dres_ref,
+        weight_ref,
+        pre_ref,
+        state_ref,
+        cum_ref,
+        carry_ref,
+        rate_ref,
+        dist_ref,
+        par_ref,
+    ), outs = by_rows(refs, rows, (False, False, True, True, True, False, True, False, False))
+    dgate_ref, local_ref, back_ref, first_ref, dmix_ref = outs
     _, length, width = dmix_ref.shape
+    for row in range(rows):
+        dmix_ref[row] = lax.dot_general(
+            dres_ref[row * length : (row + 1) * length, :],
+            weight_ref[...],
+            (((1,), (1,)), ((), ())),
+            preferred_element_type=jnp.float32,
+        )
     soft = par_ref[7:8, :]
     place = lax.broadcasted_iota(jnp.int32, (SUBLANES, width), 0)
     last = length // STEP - 1
@@ -503,20 +518,28 @@
             self.flops,
         )
 
-    def adjoint(self, dmix, pre, state, cum, entering, rate, dist, params):
+    def adjoint(self, dres, weight, pre, state, cum, entering, rate, dist, params):
         f32 = jnp.float32
         outs = [self.shape(self.length, d) for d in (jnp.bfloat16, f32, f32)] + [self.shape(1, f32)]
         tall, apart = (self.tall(), self.apart(self.length))
         return channel_call(
             functools.partial(adjoint_kernel, self.rows),
             "recurrence_adjoint",
-            (dmix, *pre, *state, *cum, entering, *rate, dist, params),
-            [tall, *apart * 3, self.short(1), *apart, self.dist(), self.flat(16)],
+            (dres, weight, *pre, *state, *cum, entering, *rate, dist, params),
+            [
+                pl.BlockSpec(dres.shape, lambda j: (0, 0)),
+                self.gates(weight.shape[1]),
+                *apart * 3,
+                self.short(1),
+                *apart,
+                self.dist(),
+                self.flat(16),
+            ],
             outs,
             [tall, tall, tall, self.short(1)],
-            [],
+            [pltpu.VMEM((self.rows, self.length, self.width), f32)],
             self.blocks,
-            0,
+            2 * self.rows * self.length * weight.size,
         )
 
     def backward(
@@ -599,7 +622,7 @@
             normed_ref[at, :] = (value * inverse * gain_ref[...]).astype(jnp.bfloat16)
             return carry
 
-        lax.fori_loop(0, tokens // piece, norm, 0)
+        lax.fori_loop(0, tokens // piece, norm, 0, unroll=2)
 
     def multiply(index, carry):
         at = pl.ds(pl.multiple_of(index * tall, tall), tall)
@@ -707,7 +730,7 @@
                 mixed_ref[at, :] = (state * (pre * (0.5 + 0.5 * inner))).astype(jnp.bfloat16)
                 return carry
 
-            lax.fori_loop(0, tall // slab, mix, 0)
+            lax.fori_loop(0, tall // slab, mix, 0, unroll=2)
             tile = 512
             for first in range(0, model, tile):
                 at = slice(first, first + tile)
@@ -722,7 +745,7 @@
         normed_ref[at, :] = (resid * inverse * gain_ref[...]).astype(jnp.bfloat16)
         return carry
 
-    lax.fori_loop(0, tall // slab, norm, 0)
+    lax.fori_loop(0, tall // slab, norm, 0, unroll=4)
 
 
 def middle(last, state, cum, pre, x, recur_out, gain):
@@ -881,7 +904,7 @@
             dres_ref[at, :] = dres.astype(jnp.bfloat16)
             return carry
 
-        lax.fori_loop(0, tokens // small, finish, 0)
+        lax.fori_loop(0, tokens // small, finish, 0, unroll=4)
 
 
 def mlp(left, parts, normed, resid, gain, mlp_gate, mlp_up, mlp_down):
@@ -1051,23 +1074,24 @@
             (source, target.at[pl.ds(row * length, length)]) for row, source in enumerate(sources)
         ]
 
-    early = [
+    pairs = [
         (dbranch_hbm, dbranch),
         (input_hbm, weight_in),
         (dgate_hbm, dgate),
         (gate_hbm, weight_gate),
-        (dres_hbm, dres),
         *by_row(x_hbms, x),
         *by_row(inverse_hbms, inverse),
-    ]
-    late = [
+        (dres_hbm, dres),
         *by_row(normed_hbms, normed),
         (mixed_hbm, mixed),
         (small_hbm.at[(slice(None),) * corners.count + (core,)], own_small),
     ]
+    kinds = []
+    for name in ('dbranch', 'win', 'dgate', 'wgate', 'x', 'inverse', 'dres', 'normed', 'mixed', 'small'):
+        kinds += [name] * (rows if name in ("normed", "x", "inverse") else 1)
     loads = [
         pltpu.make_async_copy(source, target, load_sem.at[place])
-        for place, (source, target) in enumerate(early + late)
+        for place, (source, target) in enumerate(pairs)
     ]
     for load in loads:
         load.start()
@@ -1221,7 +1245,7 @@
                 parts[part, at, :] = grad[:, part * width : (part + 1) * width]
             return carry
 
-        lax.fori_loop(0, length // slab, norm, 0)
+        lax.fori_loop(0, length // slab, norm, 0, unroll=4)
         for other in range(1, group):
             move(other, row).start()
         keep(row).start()
@@ -1246,42 +1270,73 @@
 
         lax.fori_loop(0, columns // tile, product, 0)
 
-    for load in loads[:2]:
-        load.wait()
-    rim_copy.wait()
-    live = jnp.where(seq < seqs - 1, 1.0, 0.0)
-    for row in range(rows):
-        at = slice((row + 1) * length - STEP, (row + 1) * length)
-        inside = dbranch[at, :].astype(jnp.float32)
-        last = ending_ref[row] + live * rim[row]
-        dbranch[at, :] = jnp.concatenate([inside[: STEP - SUBLANES], last], axis=0).astype(
-            jnp.bfloat16
-        )
-    for load in loads[2 : len(early)]:
-        load.wait()
-    copy(6, 0).start()
-    for row in range(rows):
-        back_row(row)
-    for load in loads[len(early) :]:
-        load.wait()
-    half = made_in.shape[-1]
-    for stream in (0, 1):
-        weight_product(normed, dgate, made_in, stream, stream * half)
+    half, half_out = (made_in.shape[-1], made_out.shape[-1])
+    waited, reached = (set(), {})
+
+    def need(*names):
+        for place, name in enumerate(kinds):
+            if name in names and place not in waited:
+                waited.add(place)
+                loads[place].wait()
+
+    def fix_rim():
+        need("dbranch")
+        rim_copy.wait()
+        live = jnp.where(seq < seqs - 1, 1.0, 0.0)
+        for row in range(rows):
+            at = slice((row + 1) * length - STEP, (row + 1) * length)
+            inside = dbranch[at, :].astype(jnp.float32)
+            last = ending_ref[row] + live * rim[row]
+            dbranch[at, :] = jnp.concatenate([inside[: STEP - SUBLANES], last], axis=0).astype(
+                jnp.bfloat16
+            )
+
+    def begin(stream):
         copy(stream, 0).start()
-    half_out = made_out.shape[-1]
-    for stream in (4, 5):
-        weight_product(mixed, dres, made_out, stream - 4, (stream - 4) * half_out)
-        copy(stream, 0).start()
-    for stream in (0, 1, 6):
-        advance(stream, 0)
-    for stream in (2, 3):
-        weight_product(normed, dbranch, made_in, stream, (stream - 2) * half)
-        copy(stream, 0).start()
-    for stream in (4, 5, 2, 3):
-        advance(stream, 0)
-    for stage in range(1, stages):
-        for stream in (0, 1, 6, 4, 5, 2, 3):
-            advance(stream, stage)
+        reached[stream] = 0
+
+    def progress(streams):
+        for stream in streams:
+            if stream in reached and reached[stream] < stages:
+                if stream == 6:
+                    need("small")
+                advance(stream, reached[stream])
+                reached[stream] += 1
+
+    def compute(item):
+        if item == "gate":
+            need("normed", "dgate")
+            for stream in (0, 1):
+                weight_product(normed, dgate, made_in, stream, stream * half)
+                begin(stream)
+        elif item == "out":
+            need("mixed", "dres")
+            for stream in (4, 5):
+                weight_product(mixed, dres, made_out, stream - 4, (stream - 4) * half_out)
+                begin(stream)
+        elif item == "in":
+            need("normed", "dbranch")
+            for stream in (2, 3):
+                weight_product(normed, dbranch, made_in, stream, (stream - 2) * half)
+                begin(stream)
+        else:
+            need("dbranch", "dgate", "win", "wgate", "x", "inverse", "dres")
+            back_row(item)
+
+    begin(6)
+    fix_rim()
+    compute(0)
+    compute(1)
+    compute('gate')
+    progress((6,))
+    compute('out')
+    progress((0, 1))
+    compute('in')
+    progress((0, 1))
+    progress((4, 5))
+    progress((6,))
+    while any(reached[stream] < stages for stream in range(7)):
+        progress((0, 1, 4, 5, 2, 3, 6))
     for stage in range(stages):
         for stream in range(7):
             copy(stream, stage).wait_send()
@@ -1684,9 +1739,9 @@
         )
         merged, resid_low = lax.optimization_barrier((merged, resid_low))
         merged = lax.psum_scatter(merged, "seq", scatter_dimension=0, tiled=True)
-    grad_mixed = back_dot(resid_low, recur_out)
     gate_low, back_local, back_cum, first_term = core.adjoint(
-        grad_mixed.reshape(row_count, block_len, rec_width),
+        resid_low,
+        recur_out,
         gate_pre,
         state,
         cum,
@@ -1696,7 +1751,6 @@
         params,
     )
     gate_low = gate_low.reshape(tok_count, rec_width)
-    output, back_local = lax.optimization_barrier((output, back_local))
     branch_local, ending, leading, small = core.backward(
         back_local,
         back_cum,
@@ -1716,7 +1770,7 @@
     )
     branch_low = branch_local.reshape(tok_count, rec_width)
     if tiled:
-        merged, branch_low = lax.optimization_barrier((merged, branch_low))
+        output, merged, branch_low = lax.optimization_barrier((output, merged, branch_low))
         merged = lax.psum_scatter(merged, "zed", scatter_dimension=0, tiled=True)
         grad_tokens, sum_rgate, sum_rout, sum_rin, own_small = tail(
             gate_low,

time: 485 us -> 483 us (level)
  matrix products: 11.7 us -> 2.27 us
    reduce_scatter x1, waiting for transfers between devices: 0.02 us -> 16.9 us  [body(): merged = lax.psum_scatter(merged, 'seq', scatter_dimension=0, tiled=True)]
    all_to_all x1, waiting for transfers between devices: 15.7 us -> 0.01 us  [features_out(): moved = lax.all_to_all(parts, CHAN, 0, 0, tiled=True)]
    pallas_call x1, Pallas kernels: 106 us -> 117 us  [tail(): pl.pallas_call(functools.partial(tail_kernel, corners, orders), name='tai...]
    dot_general x1 -> x0, matrix products: 9.38 us -> none  [back_dot(): lax.dot_general(left, right, (((1,), (1,)), ((), ())), preferred_element_...]
    pallas_call x1, Pallas kernels: 66.3 us -> 57.9 us  [mlp(): pl.pallas_call(mlp_kernel, name='mlp_forward_backward', grid=(ffn // chun...]
  transfers between devices with their start and end apart: 6 -> 6, of which waited for: 3 -> 3; matrix products, arithmetic and copies ran while one was open for 5% -> 3% of each run, Pallas kernels for 51% -> 54%
where the time goes in v8:
time: 483 us; the launch traced here: 482 us
  Pallas kernels  365 us (76%)
  waiting for transfers between devices  52.9 us (11%)
  local copies, waits for them, and re-layouts  19.3 us (4%)
  starting transfers between devices  19.1 us (4%)
  between operations  14.4 us (3%)
  other arithmetic  9.41 us (2%)
    pallas_call x1, Pallas kernels, tail(): pl.pallas_call(functools.partial(tail_kernel, corners, orders), name='tai...  117 us
    pallas_call x4, Pallas kernels, channel_call(): pl.pallas_call(kernel, name=name, grid=(blocks,), in_specs=specs, out_spe...  107 us
    pallas_call x1, Pallas kernels, mlp(): pl.pallas_call(mlp_kernel, name='mlp_forward_backward', grid=(ffn // chun...  57.9 us
    all_to_all x3, waiting for transfers between devices, features_in(): lax.all_to_all(local, CHAN, 0, 0, tiled=True).reshape(count, -1, width)  35.9 us
    pallas_call x1, Pallas kernels, block_gradients(): pl.pallas_call(grads_kernel, name='block_gradients', grid=(total + 1,), i...  34.8 us
    pallas_call x2, Pallas kernels, front(): pl.pallas_call(front_kernel, name='norm_and_project', grid=(steps,), in_s...  26.6 us
    pallas_call x1, Pallas kernels, middle(): pl.pallas_call(functools.partial(middle_kernel, rows), name='mix_and_norm...  21.6 us
    reduce_scatter x1, waiting for transfers between devices, body(): merged = lax.psum_scatter(merged, 'seq', scatter_dimension=0, tiled=True)  16.9 us
  transfers between devices with their start and end apart: 6, of which 3 were waited for; matrix products, arithmetic and copies ran while one was open for 3% of the time, Pallas kernels for 54%

profile of v8, /device:TPU:0, one launch (start us, length us, event | category | flops | bytes accessed | tf_op | source)
XLA Modules:
  0.0 482.2 jit_solution(5564668734467471069)
XLA Ops:
  7.2 3.1 fusion.21
  10.4 6.5 %all-to-all-start.1 = ((bf16[8,1,512,128]{3,2,1,0:T(8,128)(2,1)}), bf16[8,1,512,128]{3,2,1,0:T(8,128)(2,1)S(1)}, u32[]{:S(2)}, u32[]{:S(2)}) async-start(bf16[8,1,512,128]{3,2,1,0:T(8,128)(2,1)} %get-tuple-element.197), calls=%async_computation.1 | async-start | bytes 2097152 | tf_op jit(solution)/shard_map/all_to_all | solution.py:983
  17.1 26.3 %all-to-all-done.1 = bf16[8,1,512,128]{3,2,1,0:T(8,128)(2,1)S(1)} async-done(((bf16[8,1,512,128]{3,2,1,0:T(8,128)(2,1)}), bf16[8,1,512,128]{3,2,1,0:T(8,128)(2,1)S(1)}, u32[]{:S(2)}, u32[]{:S(2)}) %all-to-all-start.1) | async-done | bytes 1048608 | tf_op jit(solution)/shard_map/all_to_all | solution.py:983
  43.4 3.6 all-to-all-start
  47.1 1.3 concatenate.9.par_ref.refs_12_.refs_21_
  48.5 2.3 fusion.gates_ref.refs_22_
  51.9 13.9 %norm_and_project.2 = (bf16[512,1024]{1,0:T(8,128)(2,1)}, f32[512,128]{1,0:T(8,128)}, bf16[512,1024]{1,0:T(8,128)(2,1)}, f32[512,1536]{1,0:T(8,128)}, f32[512,1536]{1,0:T(8,128)}, /*index=5*/f32[8,1536]{1,0:T(8,128)}) custom-call(bf16[8,512,128]{2,1,0:T(8,128)(2,1)} %bitcast.57, f32[1,1024]{1,0:T(1,128)} %bitcast.66, bf16[1024,1536]{1,0:T(8,128)(2,1)} %input_hbm.1, ...), custom_call_target="tpu_custom_call" | custom-call | flops 3221225472 | bytes 10485760 | tf_op jit(solution)/shard_map/norm_and_project/pallas_call | solution.py:674
  65.8 17.0 %recurrence_forward.2 = (bf16[1,512,1536]{2,1,0:T(8,128)(2,1)}, f32[1,512,1536]{2,1,0:T(8,128)}, f32[1,512,1536]{2,1,0:T(8,128)}, f32[1,512,1536]{2,1,0:T(8,128)...) custom-call(f32[1,512,1536]{2,1,0:T(8,128)} %bitcast.37, f32[1,8,1536]{2,1,0:T(8,128)} %bitcast.60, ...), custom_call_target="tpu_custom_call" | custom-call | flops 1207959552 | bytes 20082688 | tf_op jit(solution)/shard_map/recurrence_forward/pallas_call | solution.py:450
  83.8 12.7 %norm_and_project.3 = (bf16[512,1024]{1,0:T(8,128)(2,1)}, f32[512,128]{1,0:T(8,128)}, bf16[512,1024]{1,0:T(8,128)(2,1)}, f32[512,1536]{1,0:T(8,128)}, f32[512,1536]{1,0:T(8,128)}, /*index=5*/f32[8,1536]{1,0:T(8,128)}) custom-call(bf16[8,512,128]{2,1,0:T(8,128)(2,1)} %bitcast.58, f32[1,1024]{1,0:T(1,128)} %bitcast.67, bf16[1024,1536]{1,0:T(8,128)(2,1)} %input_hbm.1, ...), custom_call_target="tpu_custom_call" | custom-call | flops 3221225472 | bytes 10485760 | tf_op jit(solution)/shard_map/norm_and_project/pallas_call | solution.py:674
  96.5 5.0 %all-to-all-start.2 = ((bf16[8,2,512,128]{3,2,1,0:T(8,128)(2,1)}), bf16[8,2,512,128]{3,2,1,0:T(8,128)(2,1)S(1)}, u32[]{:S(2)}, u32[]{:S(2)}) async-start(bf16[8,2,512,128]{3,2,1,0:T(8,128)(2,1)} %bitcast.8), calls=%async_computation.2 | async-start | bytes 4194304 | tf_op jit(solution)/shard_map/all_to_all | solution.py:983
  102.2 17.2 %recurrence_forward.3 = (bf16[1,512,1536]{2,1,0:T(8,128)(2,1)}, f32[1,512,1536]{2,1,0:T(8,128)}, f32[1,512,1536]{2,1,0:T(8,128)}, f32[1,512,1536]{2,1,0:T(8,128)...) custom-call(f32[1,512,1536]{2,1,0:T(8,128)} %bitcast.39, f32[1,8,1536]{2,1,0:T(8,128)} %bitcast.62, ...), custom_call_target="tpu_custom_call" | custom-call | flops 1207959552 | bytes 20082688 | tf_op jit(solution)/shard_map/recurrence_forward/pallas_call | solution.py:450
  119.4 21.6 %mix_and_norm.1 = (f32[2,1,1536]{2,1,0:T(1,128)}, bf16[1024,1536]{1,0:T(8,128)(2,1)}, f32[1024,1024]{1,0:T(8,128)}, bf16[1024,1024]{1,0:T(8,128)(2,1)}) custom-call(f32[1,2,1536]{2,1,0:T(2,128)} %get-tuple-element.81.refs_0_.refs_3_, f32[1,2,1536]{2,1,0:T(2,128)} %get-tuple-element.87.refs_1_.refs_4_, ...), custom_call_target="tpu_custom_call" | custom-call | flops 3221225472 | bytes 22020096 | tf_op jit(solution)/shard_map/mix_and_norm/pallas_call | solution.py:772
  141.0 9.6 %all-to-all-done.2 = bf16[8,2,512,128]{3,2,1,0:T(8,128)(2,1)S(1)} async-done(((bf16[8,2,512,128]{3,2,1,0:T(8,128)(2,1)}), bf16[8,2,512,128]{3,2,1,0:T(8,128)(2,1)S(1)}, u32[]{:S(2)}, u32[]{:S(2)}) %all-to-all-start.2) | async-done | bytes 2097184 | tf_op jit(solution)/shard_map/all_to_all | solution.py:983
  150.6 1.3 copy-done.5
  151.9 57.9 %mlp_forward_backward.1 = (bf16[1024,1024]{1,0:T(8,128)(2,1)}, bf16[1024,3072]{1,0:T(8,128)(2,1)}, bf16[1024,3072]{1,0:T(8,128)(2,1)}, bf16[1024,3072]{1,0:T(8,1...) custom-call(s32[2]{0:T(128)} %broadcast_subtract_fusion.1.left_ref, bf16[8,1024,128]{2,1,0:T(8,128)(2,1)} %bitcast.50, ...), custom_call_target="tpu_custom_call" | custom-call | flops 38654705664 | bytes 52428800 | tf_op jit(solution)/shard_map/mlp_forward_backward/pallas_call | solution.py:923
  209.8 34.8 %block_gradients.1 = bf16[16,288,1024]{2,1,0:T(8,128)(2,1)} custom-call(bf16[1024,1024]{1,0:T(8,128)(2,1)} %get-tuple-element.97.normed_ref, bf16[1024,3072]{1,0:T(8,128)(2,1)} %get-tuple-element.100.dgate_ref, bf16[1024,3072]{1,0:T(8,128)(2,1)} %get-tuple-element.101.dup_ref, bf16[1024,3072]{1,0:T(8,128)(2,1)} %get-tuple-element.102.hidden_ref, ...), custom_call_target="tpu_custom_call" | custom-call | flops 19327352832 | bytes 32505856 | tf_op jit(solution)/shard_map/block_gradients/pallas_call | solution.py:1577
  244.6 3.6 all-to-all-start.3
  248.5 26.3 %recurrence_adjoint.1 = (bf16[2,512,1536]{2,1,0:T(8,128)(2,1)}, f32[2,512,1536]{2,1,0:T(8,128)}, f32[2,512,1536]{2,1,0:T(8,128)}, f32[2,1,1536]{2,1,0:T(1,128)}) custom-call(bf16[1024,1024]{1,0:T(8,128)(2,1)} %get-tuple-element.106.refs_0_.dres_hbm, bf16[1536,1024]{1,0:T(8,128)(2,1)} %refs_1_.1, f32[1,512,1536]{2,1,0:T(8,128)} %bitcast.42, ...), custom_call_target="tpu_custom_call" | custom-call | flops 3221225472 | bytes 46784512 | tf_op jit(solution)/shard_map/recurrence_adjoint/pallas_call | solution.py:450
  274.9 46.5 %recurrence_backward.1 = (bf16[2,512,1536]{2,1,0:T(8,128)(2,1)}, f32[2,8,1536]{2,1,0:T(8,128)}, f32[2,8,1536]{2,1,0:T(8,128)}, bf16[1536,256]{1,0:T(8,128)(2,1)}) custom-call(f32[2,512,1536]{2,1,0:T(8,128)} %get-tuple-element.110.refs_0_, f32[2,512,1536]{2,1,0:T(8,128)} %get-tuple-element.111.refs_1_, f32[2,1,1536]{2,1,0:T(1,128)} %get-tuple-element.112.refs_2_, ...), custom_call_target="tpu_custom_call" | custom-call | flops 4831838208 | bytes 54444032 | tf_op jit(solution)/shard_map/recurrence_backward/pallas_call | solution.py:450
  321.4 16.9 %reduce-scatter.3.cloned.1.call-done = bf16[4,288,1024]{2,1,0:T(8,128)(2,1)} async-done(((bf16[16,288,1024]{2,1,0:T(8,128)(2,1)}), bf16[4,288,1024]{2,1,0:T(8,128)(2,1)}) %reduce-scatter.3.cloned.1.call-update) | async-done | bytes 2359312 | tf_op jit(solution)/shard_map/reduce_scatter | solution.py:1741
  338.4 117.0 %tail.1 = (bf16[16,512,128]{2,1,0:T(8,128)(2,1)}, f32[32,1536]{1,0:T(8,128)}, f32[48,1024]{1,0:T(8,128)}, f32[32,1536]{1,0:T(8,128)}, f32[48,256]{1,0:T(8,128)}) custom-call(bf16[1024,1536]{1,0:T(8,128)(2,1)} %bitcast.69, bf16[1024,1536]{1,0:T(8,128)(2,1)} %bitcast.70, f32[2,8,1536]{2,1,0:T(8,128)} %get-tuple-element.121.ending_ref, ...), custom_call_target="tpu_custom_call" | custom-call | flops 16106127360 | bytes 45088768 | tf_op jit(solution)/shard_map/tail/pallas_call | solution.py:1372
  462.5 1.3 dynamic-slice_divide_fusion.1
  470.7 1.3 copy.67
  472.0 1.3 copy.68
  (82 shorter events, 19.6 us)
Async XLA Ops:
  7.2 41.3 %copy-start = (bf16[1536,192]{0,1:T(8,128)(2,1)S(1)}, bf16[1536,192]{0,1:T(8,128)(2,1)}, u32[]{:S(2)}) copy-start(bf16[1536,192]{0,1:T(8,128)(2,1)} %param.26) | copy-start | bytes 1769476
  7.2 9.6 %copy-start.18 = (s32[2]{0:T(128)S(1)}, s32[2]{0:T(128)}, u32[]{:S(2)}) copy-start(s32[2]{0:T(128)} %param.20) | copy-start | bytes 28
  7.2 9.7 %copy-start.16 = (f32[1536]{0:T(1024)S(1)}, f32[1536]{0:T(1024)}, u32[]{:S(2)}) copy-start(f32[1536]{0:T(1024)} %param.25) | copy-start | bytes 18436
  7.2 9.7 %copy-start.17 = (s32[2,8]{1,0:T(2,128)S(1)}, s32[2,8]{1,0:T(2,128)}, u32[]{:S(2)}) copy-start(s32[2,8]{1,0:T(2,128)} %param.19) | copy-start | bytes 196
  10.3 36.6 %copy-start.15 = (f32[1536]{0:T(1024)S(1)}, f32[1536]{0:T(1024)}, u32[]{:S(2)}) copy-start(f32[1536]{0:T(1024)} %param.28) | copy-start | bytes 18436
  10.3 36.7 %copy-start.13 = (f32[4,1536]{1,0:T(4,128)S(1)}, f32[4,1536]{1,0:T(4,128)}, u32[]{:S(2)}) copy-start(f32[4,1536]{1,0:T(4,128)} %param.24) | copy-start | bytes 73732
  10.3 36.7 %copy-start.14 = (f32[2,1536]{1,0:T(2,128)S(1)}, f32[2,1536]{1,0:T(2,128)}, u32[]{:S(2)}) copy-start(f32[2,1536]{1,0:T(2,128)} %param.27) | copy-start | bytes 36868
  10.4 33.1 %all-to-all-start.1 = ((bf16[8,1,512,128]{3,2,1,0:T(8,128)(2,1)}), bf16[8,1,512,128]{3,2,1,0:T(8,128)(2,1)S(1)}, u32[]{:S(2)}, u32[]{:S(2)}) async-start(bf16[8,1,512,128]{3,2,1,0:T(8,128)(2,1)} %get-tuple-element.197), calls=%async_computation.1 | async-start | bytes 2097152 | tf_op jit(solution)/shard_map/all_to_all | solution.py:983
  43.4 7.4 %copy-start.8 = (bf16[8,1,512,128]{3,2,1,0:T(8,128)(2,1)}, bf16[8,1,512,128]{3,2,1,0:T(8,128)(2,1)S(1)}, u32[]{:S(2)}) copy-start(bf16[8,1,512,128]{3,2,1,0:T(8,128)(2,1)S(1)} %all-to-all-done.1) | copy-start | bytes 3145732
  43.4 39.4 %all-to-all-start = ((bf16[8,1,512,128]{3,2,1,0:T(8,128)(2,1)}), bf16[8,1,512,128]{3,2,1,0:T(8,128)(2,1)S(1)}, u32[]{:S(2)}, u32[]{:S(2)}) async-start(bf16[8,1,512,128]{3,2,1,0:T(8,128)(2,1)} %get-tuple-element.198), calls=%async_computation | async-start | bytes 2097152 | tf_op jit(solution)/shard_map/all_to_all | solution.py:983
  51.0 14.8 %copy-start.2 = (s32[2,512,128]{2,1,0:T(8,128)}, s32[2,512,128]{2,1,0:T(8,128)S(1)}, u32[]{:S(2)}) copy-start(s32[2,512,128]{2,1,0:T(8,128)S(1)} %broadcast_in_dim.73.refs_11_.refs_16_) | copy-start | bytes 1572868
  96.5 54.1 %all-to-all-start.2 = ((bf16[8,2,512,128]{3,2,1,0:T(8,128)(2,1)}), bf16[8,2,512,128]{3,2,1,0:T(8,128)(2,1)S(1)}, u32[]{:S(2)}, u32[]{:S(2)}) async-start(bf16[8,2,512,128]{3,2,1,0:T(8,128)(2,1)} %bitcast.8), calls=%async_computation.2 | async-start | bytes 4194304 | tf_op jit(solution)/shard_map/all_to_all | solution.py:983
  101.5 236.8 %reduce-scatter.3.cloned.1.call-start = ((), (), s32[]{:S(2)}) async-start(), calls=%async_computation.6 | async-start | bytes 11796480 | tf_op jit(solution)/shard_map/reduce_scatter | solution.py:1741
  150.6 1.3 copy-start.5
  244.6 76.7 %all-to-all-start.3 = ((bf16[8,2,512,128]{3,2,1,0:T(8,128)(2,1)}), bf16[8,2,512,128]{3,2,1,0:T(8,128)(2,1)S(1)}, u32[]{:S(2)}, u32[]{:S(2)}) async-start(bf16[8,2,512,128]{3,2,1,0:T(8,128)(2,1)} %bitcast.49), calls=%async_computation.3 | async-start | bytes 4194304 | tf_op jit(solution)/shard_map/all_to_all | solution.py:1001
  248.3 215.5 %reduce-scatter.5.cloned.1.call-start = ((), (), s32[]{:S(2)}) async-start(), calls=%async_computation.7 | async-start | bytes 2949120 | tf_op jit(solution)/shard_map/reduce_scatter | solution.py:1774
  463.8 4.7 copy-start.3
  465.5 6.5 %copy-start.6 = (f32[4,8,3,1024]{3,1,2,0:T(8,128)}, f32[4,8,3,1024]{3,1,2,0:T(8,128)S(1)}, u32[]{:S(2)}) copy-start(f32[4,8,3,1024]{3,1,2,0:T(8,128)S(1)} %copy.60) | copy-start | bytes 1179652
  467.2 4.8 copy-start.7
  468.5 3.5 copy-start.4
  470.7 4.7 copy-start.1
  472.0 1.3 copy-start.11
  472.0 2.0 copy-start.10
  472.0 2.7 copy-start.12
  (1 other events, 1.0 us)
Sparse Core Ops, SparseCore 0:
  244.8 93.5 reduce-scatter.2
  340.6 82.9 reduce-scatter.4

commit v9 on v8

--- a/solution.py
+++ b/solution.py
@@ -350,7 +350,7 @@
         gate_step,
         ((zeros, zeros, zeros), tuple(in_ref[row] for row in range(rows))),
     )
-    for slot, total in zip((5, 6, 7), (sums[1], sums[2], sums[0])):
+    for slot, total in zip((5, 6, 7), (sums[1], sums[2], sums[0] * par_ref[8:9, :])):
         sums_ref[slot : slot + 1, :] = jnp.sum(total, axis=0, keepdims=True)
 
     piece = min(length, 256)
@@ -804,12 +804,10 @@
     )(*last, *state, *cum, *pre, *x, recur_out, gain[None])
 
 
-def mlp_kernel(
+def hidden_kernel(
     left_ref,
     parts_ref,
     normed_ref,
-    resid_ref,
-    gain_ref,
     gate_ref,
     up_ref,
     down_ref,
@@ -817,19 +815,14 @@
     hidden_ref,
     dgate_ref,
     dup_ref,
-    result_ref,
-    dres_ref,
-    total_ref,
-    back_ref,
 ):
     tokens, model = normed_ref.shape
     chunk = down_ref.shape[0]
     rows = left_ref.shape[0]
     length = tokens // rows
-    step = pl.program_id(0)
     slab = 32
 
-    @pl.when(step == 0)
+    @pl.when(pl.program_id(0) == 0)
     def _():
         for row in range(rows):
 
@@ -840,8 +833,6 @@
                 place = base + lax.broadcasted_iota(jnp.int32, low.shape, 0)
                 value = jnp.where(place < left_ref[row], low.astype(jnp.float32), 0.0)
                 gout_ref[at, :] = value.astype(jnp.bfloat16)
-                total_ref[at, :] = resid_ref[at, :]
-                back_ref[at, :] = jnp.zeros((slab, model), jnp.float32)
                 return carry
 
             lax.fori_loop(0, length // slab, collect, 0)
@@ -865,21 +856,49 @@
             hidden_ref[at, own] = (act * up).astype(jnp.bfloat16)
             dgate_ref[at, own] = (dhid * up * slope).astype(jnp.bfloat16)
             dup_ref[at, own] = (dhid * act).astype(jnp.bfloat16)
-        for column in range(model // (2 * wide)):
-            own = slice(column * 2 * wide, (column + 1) * 2 * wide)
+        return carry
+
+    lax.fori_loop(0, tokens // tall, tile, 0)
+
+
+def back_kernel(
+    hidden_ref,
+    dgate_ref,
+    dup_ref,
+    gout_ref,
+    resid_ref,
+    gain_ref,
+    gate_ref,
+    up_ref,
+    down_ref,
+    result_ref,
+    dres_ref,
+    total_ref,
+    back_ref,
+):
+    tokens, model = resid_ref.shape
+    step = pl.program_id(0)
+
+    @pl.when(step == 0)
+    def _():
+        total_ref[...] = resid_ref[...]
+        back_ref[...] = jnp.zeros_like(back_ref)
+
+    tall = min(tokens, 512)
+    wide = 512
+
+    def tile(index, carry):
+        at = pl.ds(pl.multiple_of(index * tall, tall), tall)
+        contract = (((1,), (1,)), ((), ()))
+        for column in range(model // wide):
+            own = slice(column * wide, (column + 1) * wide)
             total_ref[at, own] += jnp.dot(
                 hidden_ref[at, :], down_ref[:, own], preferred_element_type=jnp.float32
             )
             back_ref[at, own] += lax.dot_general(
-                dgate_ref[at, :],
-                gate_ref[own, :],
-                (((1,), (1,)), ((), ())),
-                preferred_element_type=jnp.float32,
+                dgate_ref[at, :], gate_ref[own, :], contract, preferred_element_type=jnp.float32
             ) + lax.dot_general(
-                dup_ref[at, :],
-                up_ref[own, :],
-                (((1,), (1,)), ((), ())),
-                preferred_element_type=jnp.float32,
+                dup_ref[at, :], up_ref[own, :], contract, preferred_element_type=jnp.float32
             )
         return carry
 
@@ -907,50 +926,184 @@
         lax.fori_loop(0, tokens // small, finish, 0, unroll=4)
 
 
-def mlp(left, parts, normed, resid, gain, mlp_gate, mlp_up, mlp_down):
+MLP_CHUNK = 768
+
+
+def resident(shape):
+    return pl.BlockSpec(shape, lambda s: (0,) * len(shape), pipeline_mode=pl.Buffered(1))
+
+
+def mlp_specs(tokens, model):
+    columns = pl.BlockSpec((model, MLP_CHUNK), lambda s: (0, s))
+    down = pl.BlockSpec((MLP_CHUNK, model), lambda s: (s, 0))
+    made = pl.BlockSpec((tokens, MLP_CHUNK), lambda s: (0, s))
+    return ([columns, columns, down], [made] * 3)
+
+
+def mlp_hidden(left, parts, normed, mlp_gate, mlp_up, mlp_down):
     tokens, model = normed.shape
     ffn = mlp_gate.shape[1]
-    chunk = 768
-    low, f32 = (jnp.bfloat16, jnp.float32)
-
-    def whole(shape):
-        return pl.BlockSpec(shape, lambda s: (0,) * len(shape), pipeline_mode=pl.Buffered(1))
-
-    columns = pl.BlockSpec((model, chunk), lambda s: (0, s))
-    made = pl.BlockSpec((tokens, chunk), lambda s: (0, s))
+    low = jnp.bfloat16
+    weights, made = mlp_specs(tokens, model)
     tall = jax.ShapeDtypeStruct((tokens, ffn), low)
-    square = jax.ShapeDtypeStruct((tokens, model), low)
     return pl.pallas_call(
-        mlp_kernel,
-        name="mlp_forward_backward",
-        grid=(ffn // chunk,),
+        hidden_kernel,
+        name="mlp_hidden",
+        grid=(ffn // MLP_CHUNK,),
         in_specs=[
             pl.BlockSpec(memory_space=pltpu.SMEM),
-            whole(parts.shape),
-            whole(normed.shape),
-            whole(resid.shape),
-            whole((1, model)),
-            columns,
-            columns,
-            pl.BlockSpec((chunk, model), lambda s: (s, 0)),
+            resident(parts.shape),
+            resident(normed.shape),
+            *weights,
         ],
-        out_specs=[
-            whole((tokens, model)),
-            made,
-            made,
-            made,
-            whole(parts.shape),
-            whole((tokens, model)),
+        out_specs=[resident((tokens, model)), *made],
+        out_shape=[jax.ShapeDtypeStruct((tokens, model), low), tall, tall, tall],
+        compiler_params=pltpu.CompilerParams(vmem_limit_bytes=VMEM_BYTES),
+        cost_estimate=pl.CostEstimate(
+            flops=6 * tokens * model * ffn,
+            bytes_accessed=6 * (model + tokens) * ffn + 6 * tokens * model,
+            transcendentals=0,
+        ),
+    )(left, parts, normed, mlp_gate, mlp_up, mlp_down)
+
+
+def mlp_back(hidden, dgate, dup, gout, resid, gain, mlp_gate, mlp_up, mlp_down, parts_shape):
+    tokens, model = resid.shape
+    ffn = mlp_gate.shape[1]
+    low, f32 = (jnp.bfloat16, jnp.float32)
+    weights, made = mlp_specs(tokens, model)
+    return pl.pallas_call(
+        back_kernel,
+        name="mlp_back",
+        grid=(ffn // MLP_CHUNK,),
+        in_specs=[
+            *made,
+            resident((tokens, model)),
+            resident((tokens, model)),
+            resident((1, model)),
+            *weights,
         ],
-        out_shape=[square, tall, tall, tall, jax.ShapeDtypeStruct(parts.shape, low), square],
+        out_specs=[resident(parts_shape), resident((tokens, model))],
+        out_shape=[
+            jax.ShapeDtypeStruct(parts_shape, low),
+            jax.ShapeDtypeStruct((tokens, model), low),
+        ],
         scratch_shapes=[pltpu.VMEM((tokens, model), f32), pltpu.VMEM((tokens, model), f32)],
         compiler_params=pltpu.CompilerParams(vmem_limit_bytes=VMEM_BYTES),
         cost_estimate=pl.CostEstimate(
-            flops=12 * tokens * model * ffn,
-            bytes_accessed=6 * (model + tokens) * ffn + 14 * tokens * model,
+            flops=6 * tokens * model * ffn,
+            bytes_accessed=6 * (model + tokens) * ffn + 10 * tokens * model,
             transcendentals=0,
         ),
-    )(left, parts, normed, resid, gain[None], mlp_gate, mlp_up, mlp_down)
+    )(hidden, dgate, dup, gout, resid, gain[None], mlp_gate, mlp_up, mlp_down)
+
+
+def outputs_kernel(
+    device_ref,
+    own_ref,
+    gate_sum,
+    in_sum,
+    out_sum,
+    small_ref,
+    input_ref,
+    gate_ref,
+    mlp_gate_ref,
+    mlp_up_ref,
+    gain1_ref,
+    gain2_ref,
+    sum_gain1,
+    sum_in,
+    sum_gate,
+    sum_taps,
+    sum_bias,
+    sum_lgates,
+    sum_lbias,
+    sum_decay,
+    sum_out,
+    sum_gain2,
+    sum_mgate,
+    sum_mup,
+    sum_down,
+):
+    rows = sum_mgate.shape[0]
+    model = own_ref.shape[1]
+    parts = sum_mgate.shape[1] // model
+    for part in range(parts):
+        at = slice(part * model, (part + 1) * model)
+        sum_mgate[:, at] = own_ref[part * rows : (part + 1) * rows, :].astype(jnp.float32)
+        sum_mup[:, at] = own_ref[(parts + part) * rows : (parts + part + 1) * rows, :].astype(
+            jnp.float32
+        )
+    sum_down[...] = own_ref[2 * parts * rows :, :].astype(jnp.float32)
+
+    def weighed(*pairs):
+        return sum(
+            jnp.sum(weight[...].astype(jnp.float32) * gradient[...], axis=1, keepdims=True)
+            for weight, gradient in pairs
+        )
+
+    sum_gain1[...] = weighed((input_ref, in_sum), (gate_ref, gate_sum)) / gain1_ref[...]
+    sum_gain2[...] = weighed((mlp_gate_ref, sum_mgate), (mlp_up_ref, sum_mup)) / gain2_ref[...]
+    sum_in[...] = in_sum[...]
+    sum_gate[...] = gate_sum[...]
+    sum_out[...] = out_sum[...]
+    channels = small_ref.shape[0]
+    size = sum_lgates.shape[1] // 2
+    first, second = (small_ref[:, :LANES], small_ref[:, LANES:])
+    lane = lax.broadcasted_iota(jnp.int32, (channels, LANES), 1)
+    moved = pltpu.roll(second, size, 1)
+    sum_lgates[:, :LANES] = jnp.where(lane < size, first, moved)
+    sum_lgates[:, LANES:] = moved[:, : 2 * size - LANES]
+    filled = jnp.concatenate([first, jnp.zeros((LANES - channels, LANES), jnp.float32)], axis=0)
+    turned = filled.T
+    sum_taps[...] = turned[size : size + 4, :channels]
+    sum_bias[...] = turned[size + 4 : size + 5, :channels]
+    sum_lbias[...] = turned[size + 5 : size + 7, :channels]
+    sum_decay[...] = turned[size + 7 : size + 8, :channels]
+
+
+def outputs(
+    device, own, gate_sum, in_sum, out_sum, small, recur_input, recur_gate, mlp_gate, mlp_up, gain1, gain2, size
+):
+    rows, rec = in_sum.shape
+    model, ffn = mlp_gate.shape
+    channels = small.shape[0]
+    f32 = jnp.float32
+
+    def whole(shape):
+        return pl.BlockSpec(shape, lambda s, device: (0,) * len(shape))
+
+    def mine(shape):
+        return pl.BlockSpec(shape, lambda s, device: (device[0], 0))
+
+    given = (own, gate_sum, in_sum, out_sum, small)
+    shapes = [(rows, 1), (rows, rec), (rows, rec), (4, channels), (1, channels)]
+    shapes += [(channels, 2 * size), (2, channels), (1, channels), out_sum.shape, (rows, 1)]
+    shapes += [(rows, ffn), (rows, ffn), (own.shape[0] - 2 * ffn // model * rows, model)]
+    return pl.pallas_call(
+        outputs_kernel,
+        name="outputs",
+        grid_spec=pltpu.PrefetchScalarGridSpec(
+            num_scalar_prefetch=1,
+            grid=(1,),
+            in_specs=[whole(a.shape) for a in given]
+            + [mine((rows, rec))] * 2
+            + [mine((rows, ffn))] * 2
+            + [mine((rows, 1))] * 2,
+            out_specs=[whole(shape) for shape in shapes],
+        ),
+        out_shape=[jax.ShapeDtypeStruct(shape, f32) for shape in shapes],
+        compiler_params=pltpu.CompilerParams(vmem_limit_bytes=VMEM_BYTES),
+    )(
+        device[None],
+        *given,
+        recur_input,
+        recur_gate,
+        mlp_gate,
+        mlp_up,
+        gain1[:, None],
+        gain2[:, None],
+    )
 
 
 def spread_kernel(whole_ref, out_ref):
@@ -1686,7 +1839,8 @@
             conv_bias[None],
             lru_bias,
             (-8.0 * soft_decay)[None],
-            jnp.zeros((SUBLANES, rec_width), jnp.float32),
+            (8.0 * jax.nn.sigmoid(-lru_decay))[None],
+            jnp.zeros((SUBLANES - 1, rec_width), jnp.float32),
         ],
         axis=0,
     )
@@ -1717,28 +1871,31 @@
     entering, mixed_low, resid_one, normed_low2 = middle(
         last, state, cum, gate_pre, low_x, recur_out, norm2_gain
     )
-    cotangent, _ = lax.optimization_barrier((cotangent, low_x[-1]))
+    cotangent, _ = lax.optimization_barrier((cotangent, block))
     cotangent, resid_one = lax.optimization_barrier((features_in(cotangent), resid_one))
-    grad_low, hidden_low, mgate_low, mup_low, result_parts, resid_low = mlp(
-        lengths - seq_index * block_len,
-        cotangent,
-        normed_low2,
+    grad_low, hidden_low, mgate_low, mup_low = mlp_hidden(
+        lengths - seq_index * block_len, cotangent, normed_low2, mlp_gate, mlp_up, mlp_down
+    )
+    devices = lax.axis_size(("seq", "zed", "core"))
+    own_rows = model_dim // devices
+    tiled = own_rows % (2 * SUBLANES) == 0 and tokens.shape[2] % LANES == 0
+    if tiled:
+        merged = block_gradients(normed_low2, mgate_low, mup_low, hidden_low, grad_low)
+        merged, hidden_low = lax.optimization_barrier((merged, hidden_low))
+        merged = lax.psum_scatter(merged, "seq", scatter_dimension=0, tiled=True)
+    result_parts, resid_low = mlp_back(
+        hidden_low,
+        mgate_low,
+        mup_low,
+        grad_low,
         resid_one,
         norm2_gain,
         mlp_gate,
         mlp_up,
         mlp_down,
+        cotangent.shape,
     )
     output = features_out(result_parts, row_count)
-    devices = lax.axis_size(("seq", "zed", "core"))
-    own_rows = model_dim // devices
-    tiled = own_rows % (2 * SUBLANES) == 0 and tokens.shape[2] % LANES == 0
-    if tiled:
-        merged = block_gradients(
-            normed_low2, mgate_low, mup_low, hidden_low, grad_low
-        )
-        merged, resid_low = lax.optimization_barrier((merged, resid_low))
-        merged = lax.psum_scatter(merged, "seq", scatter_dimension=0, tiled=True)
     gate_low, back_local, back_cum, first_term = core.adjoint(
         resid_low,
         recur_out,
@@ -1787,14 +1944,25 @@
             low_x,
             inverse,
         )
-        own = merged[0].astype(jnp.float32)
-        span = ffn_width // model_dim * own_rows
-
-        def unfolded(part):
-            return jnp.swapaxes(part.reshape(-1, own_rows, model_dim), 0, 1).reshape(own_rows, -1)
-
-        sum_mgate, sum_mup = (unfolded(own[:span]), unfolded(own[span : 2 * span]))
-        sum_down = own[2 * span :]
+        device = lax.axis_index(("seq", "zed", "core"))
+        sums = outputs(
+            device,
+            merged[0],
+            sum_rgate,
+            sum_rin,
+            sum_rout,
+            own_small,
+            recur_input,
+            recur_gate,
+            mlp_gate,
+            mlp_up,
+            norm1_gain,
+            norm2_gain,
+            head_size,
+        )
+        flat = (0, 4, 7, 9)
+        sums = [part.reshape(-1) if place in flat else part for place, part in enumerate(sums)]
+        return (output, grad_tokens, *sums)
     else:
         from_next = passed_along(
             leading[:, SUBLANES - rim_size :, :].astype(jnp.bfloat16), "seq", -1
@@ -1842,8 +2010,7 @@
     sum_gain2 = (weighed(mlp_gate, sum_mgate) + weighed(mlp_up, sum_mup)) / mine(
         norm2_gain, own_rows
     )
-    own_channels = own_sums.shape[1]
-    sum_decay = 8.0 * jax.nn.sigmoid(-mine(lru_decay, own_channels)) * own_sums[7]
+    sum_decay = own_sums[7]
     return (
         output,
         grad_tokens,

time: 483 us -> 452 us (0.936)
  waiting for transfers between devices: 52.9 us -> 26.4 us
  Pallas kernels: 365 us -> 371 us
  other arithmetic: 9.41 us -> 3.44 us
  local copies, waits for them, and re-layouts: 19.3 us -> 13.8 us
    reduce_scatter x1, waiting for transfers between devices: 16.9 us -> 0.02 us  [body(): merged = lax.psum_scatter(merged, 'seq', scatter_dimension=0, tiled=True)]
    pallas_call x1 -> x3, Pallas kernels: 57.9 us -> 68 us  [the longest x1 34.2 us: mlp_back(): pl.pallas_call(back_kernel, name='mlp_back', grid=(ffn // MLP_CHUNK,), in...]
    all_to_all x3, waiting for transfers between devices: 35.9 us -> 26.3 us  [features_in(): lax.all_to_all(local, CHAN, 0, 0, tiled=True).reshape(count, -1, width)]
  transfers between devices with their start and end apart: 6 -> 6, of which waited for: 3 -> 1; matrix products, arithmetic and copies ran while one was open for 3% -> 2% of each run, Pallas kernels for 54% -> 67%
where the time goes in v9:
time: 452 us
  Pallas kernels  371 us (82%)
  waiting for transfers between devices  26.4 us (6%)
  starting transfers between devices  20.4 us (5%)
  between operations  14.4 us (3%)
  local copies, waits for them, and re-layouts  13.8 us (3%)
    pallas_call x1, Pallas kernels, tail(): pl.pallas_call(functools.partial(tail_kernel, corners, orders), name='tai...  113 us
    pallas_call x4, Pallas kernels, channel_call(): pl.pallas_call(kernel, name=name, grid=(blocks,), in_specs=specs, out_spe...  107 us
    pallas_call x1, Pallas kernels, block_gradients(): pl.pallas_call(grads_kernel, name='block_gradients', grid=(total + 1,), i...  34.7 us
    pallas_call x1, Pallas kernels, mlp_back(): pl.pallas_call(back_kernel, name='mlp_back', grid=(ffn // MLP_CHUNK,), in...  34.2 us
    pallas_call x1, Pallas kernels, mlp_hidden(): pl.pallas_call(hidden_kernel, name='mlp_hidden', grid=(ffn // MLP_CHUNK,)...  30.8 us
    pallas_call x2, Pallas kernels, front(): pl.pallas_call(front_kernel, name='norm_and_project', grid=(steps,), in_s...  26.5 us
    all_to_all x3, waiting for transfers between devices, features_in(): lax.all_to_all(local, CHAN, 0, 0, tiled=True).reshape(count, -1, width)  26.3 us
    pallas_call x1, Pallas kernels, middle(): pl.pallas_call(functools.partial(middle_kernel, rows), name='mix_and_norm...  21.6 us
  transfers between devices with their start and end apart: 6, of which 1 were waited for; matrix products, arithmetic and copies ran while one was open for 2% of the time, Pallas kernels for 67%

profile of v9, /device:TPU:0, one launch (start us, length us, event | category | flops | bytes accessed | tf_op | source)
XLA Modules:
  0.0 451.5 jit_solution(14338946987700940706)
XLA Ops:
  7.2 3.1 fusion.21
  10.4 6.5 %all-to-all-start = ((bf16[8,1,512,128]{3,2,1,0:T(8,128)(2,1)}), bf16[8,1,512,128]{3,2,1,0:T(8,128)(2,1)S(1)}, u32[]{:S(2)}, u32[]{:S(2)}) async-start(bf16[8,1,512,128]{3,2,1,0:T(8,128)(2,1)} %get-tuple-element.162), calls=%async_computation | async-start | bytes 2097152 | tf_op jit(solution)/shard_map/all_to_all | solution.py:1136
  17.1 26.3 %all-to-all-done = bf16[8,1,512,128]{3,2,1,0:T(8,128)(2,1)S(1)} async-done(((bf16[8,1,512,128]{3,2,1,0:T(8,128)(2,1)}), bf16[8,1,512,128]{3,2,1,0:T(8,128)(2,1)S(1)}, u32[]{:S(2)}, u32[]{:S(2)}) %all-to-all-start) | async-done | bytes 1048608 | tf_op jit(solution)/shard_map/all_to_all | solution.py:1136
  43.4 3.6 all-to-all-start.1
  48.6 2.2 fusion.gates_ref.refs_22_
  51.9 13.9 %norm_and_project.2 = (bf16[512,1024]{1,0:T(8,128)(2,1)}, f32[512,128]{1,0:T(8,128)}, bf16[512,1024]{1,0:T(8,128)(2,1)}, f32[512,1536]{1,0:T(8,128)}, f32[512,1536]{1,0:T(8,128)}, /*index=5*/f32[8,1536]{1,0:T(8,128)}) custom-call(bf16[8,512,128]{2,1,0:T(8,128)(2,1)} %bitcast.43, f32[1,1024]{1,0:T(1,128)} %bitcast.52, bf16[1024,1536]{1,0:T(8,128)(2,1)} %input_ref.5, ...), custom_call_target="tpu_custom_call" | custom-call | flops 3221225472 | bytes 10485760 | tf_op jit(solution)/shard_map/norm_and_project/pallas_call | solution.py:674
  65.9 17.0 %recurrence_forward.2 = (bf16[1,512,1536]{2,1,0:T(8,128)(2,1)}, f32[1,512,1536]{2,1,0:T(8,128)}, f32[1,512,1536]{2,1,0:T(8,128)}, f32[1,512,1536]{2,1,0:T(8,128)...) custom-call(f32[1,512,1536]{2,1,0:T(8,128)} %bitcast.30, f32[1,8,1536]{2,1,0:T(8,128)} %bitcast.45, ...), custom_call_target="tpu_custom_call" | custom-call | flops 1207959552 | bytes 20082688 | tf_op jit(solution)/shard_map/recurrence_forward/pallas_call | solution.py:450
  83.9 5.0 %all-to-all-start.2 = ((bf16[8,2,512,128]{3,2,1,0:T(8,128)(2,1)}), bf16[8,2,512,128]{3,2,1,0:T(8,128)(2,1)S(1)}, u32[]{:S(2)}, u32[]{:S(2)}) async-start(bf16[8,2,512,128]{3,2,1,0:T(8,128)(2,1)} %bitcast.13), calls=%async_computation.2 | async-start | bytes 4194304 | tf_op jit(solution)/shard_map/all_to_all | solution.py:1136
  89.6 12.5 %norm_and_project.3 = (bf16[512,1024]{1,0:T(8,128)(2,1)}, f32[512,128]{1,0:T(8,128)}, bf16[512,1024]{1,0:T(8,128)(2,1)}, f32[512,1536]{1,0:T(8,128)}, f32[512,1536]{1,0:T(8,128)}, /*index=5*/f32[8,1536]{1,0:T(8,128)}) custom-call(bf16[8,512,128]{2,1,0:T(8,128)(2,1)} %bitcast.42, f32[1,1024]{1,0:T(1,128)} %bitcast.53, bf16[1024,1536]{1,0:T(8,128)(2,1)} %input_ref.5, ...), custom_call_target="tpu_custom_call" | custom-call | flops 3221225472 | bytes 10485760 | tf_op jit(solution)/shard_map/norm_and_project/pallas_call | solution.py:674
  102.2 17.0 %recurrence_forward.3 = (bf16[1,512,1536]{2,1,0:T(8,128)(2,1)}, f32[1,512,1536]{2,1,0:T(8,128)}, f32[1,512,1536]{2,1,0:T(8,128)}, f32[1,512,1536]{2,1,0:T(8,128)...) custom-call(f32[1,512,1536]{2,1,0:T(8,128)} %bitcast.32, f32[1,8,1536]{2,1,0:T(8,128)} %bitcast.47, ...), custom_call_target="tpu_custom_call" | custom-call | flops 1207959552 | bytes 20082688 | tf_op jit(solution)/shard_map/recurrence_forward/pallas_call | solution.py:450
  119.2 21.6 %mix_and_norm.1 = (f32[2,1,1536]{2,1,0:T(1,128)}, bf16[1024,1536]{1,0:T(8,128)(2,1)}, f32[1024,1024]{1,0:T(8,128)}, bf16[1024,1024]{1,0:T(8,128)(2,1)}) custom-call(f32[1,2,1536]{2,1,0:T(2,128)} %get-tuple-element.94.refs_0_.refs_3_, f32[1,2,1536]{2,1,0:T(2,128)} %get-tuple-element.98.refs_1_.refs_4_, ...), custom_call_target="tpu_custom_call" | custom-call | flops 3221225472 | bytes 22020096 | tf_op jit(solution)/shard_map/mix_and_norm/pallas_call | solution.py:772
  140.9 1.3 copy-done.4
  142.2 30.8 %mlp_hidden.1 = (bf16[1024,1024]{1,0:T(8,128)(2,1)}, bf16[1024,3072]{1,0:T(8,128)(2,1)}, bf16[1024,3072]{1,0:T(8,128)(2,1)}, bf16[1024,3072]{1,0:T(8,128)(2,1)}) custom-call(s32[2]{0:T(128)} %broadcast_subtract_fusion.1.left_ref, bf16[8,1024,128]{2,1,0:T(8,128)(2,1)} %bitcast.41, bf16[1024,1024]{1,0:T(8,128)(2,1)} %get-tuple-element.107.normed_ref, ...), custom_call_target="tpu_custom_call" | custom-call | flops 19327352832 | bytes 44040192 | tf_op jit(solution)/shard_map/mlp_hidden/pallas_call | solution.py:949
  173.0 34.7 %block_gradients.1 = bf16[16,288,1024]{2,1,0:T(8,128)(2,1)} custom-call(bf16[1024,1024]{1,0:T(8,128)(2,1)} %get-tuple-element.107.normed_ref, bf16[1024,3072]{1,0:T(8,128)(2,1)} %get-tuple-element.111.dgate_ref, bf16[1024,3072]{1,0:T(8,128)(2,1)} %get-tuple-element.112.dup_ref, bf16[1024,3072]{1,0:T(8,128)(2,1)} %get-tuple-element.115.hidden_ref, ...), custom_call_target="tpu_custom_call" | custom-call | flops 19327352832 | bytes 32505856 | tf_op jit(solution)/shard_map/block_gradients/pallas_call | solution.py:1730
  207.7 34.2 %mlp_back.1 = (bf16[8,1024,128]{2,1,0:T(8,128)(2,1)}, bf16[1024,1024]{1,0:T(8,128)(2,1)}) custom-call(bf16[1024,3072]{1,0:T(8,128)(2,1)} %get-tuple-element.115.hidden_ref, bf16[1024,3072]{1,0:T(8,128)(2,1)} %get-tuple-element.111.dgate_ref, bf16[1024,3072]{1,0:T(8,128)(2,1)} %get-tuple-element.112.dup_ref, bf16[1024,1024]{1,0:T(8,128)(2,1)} %get-tuple-element.114.gout_ref, ...), custom_call_target="tpu_custom_call" | custom-call | flops 19327352832 | bytes 48234496 | tf_op jit(solution)/shard_map/mlp_back/pallas_call | solution.py:975
  241.9 4.9 %all-to-all-start.3 = ((bf16[8,2,512,128]{3,2,1,0:T(8,128)(2,1)}), bf16[8,2,512,128]{3,2,1,0:T(8,128)(2,1)S(1)}, u32[]{:S(2)}, u32[]{:S(2)}) async-start(bf16[8,2,512,128]{3,2,1,0:T(8,128)(2,1)} %bitcast.40), calls=%async_computation.3 | async-start | bytes 4194304 | tf_op jit(solution)/shard_map/all_to_all | solution.py:1154
  247.0 26.4 %recurrence_adjoint.1 = (bf16[2,512,1536]{2,1,0:T(8,128)(2,1)}, f32[2,512,1536]{2,1,0:T(8,128)}, f32[2,512,1536]{2,1,0:T(8,128)}, f32[2,1,1536]{2,1,0:T(1,128)}) custom-call(bf16[1024,1024]{1,0:T(8,128)(2,1)} %get-tuple-element.119.refs_0_.dres_hbm, bf16[1536,1024]{1,0:T(8,128)(2,1)} %refs_1_.1, f32[1,512,1536]{2,1,0:T(8,128)} %bitcast.35, ...), custom_call_target="tpu_custom_call" | custom-call | flops 3221225472 | bytes 46784512 | tf_op jit(solution)/shard_map/recurrence_adjoint/pallas_call | solution.py:450
  273.5 46.7 %recurrence_backward.1 = (bf16[2,512,1536]{2,1,0:T(8,128)(2,1)}, f32[2,8,1536]{2,1,0:T(8,128)}, f32[2,8,1536]{2,1,0:T(8,128)}, bf16[1536,256]{1,0:T(8,128)(2,1)}) custom-call(f32[2,512,1536]{2,1,0:T(8,128)} %get-tuple-element.123.refs_0_, f32[2,512,1536]{2,1,0:T(8,128)} %get-tuple-element.124.refs_1_, f32[2,1,1536]{2,1,0:T(1,128)} %get-tuple-element.125.refs_2_, ...), custom_call_target="tpu_custom_call" | custom-call | flops 4831838208 | bytes 54444032 | tf_op jit(solution)/shard_map/recurrence_backward/pallas_call | solution.py:450
  322.4 112.9 %tail.1 = (bf16[16,512,128]{2,1,0:T(8,128)(2,1)}, f32[32,1536]{1,0:T(8,128)}, f32[48,1024]{1,0:T(8,128)}, f32[32,1536]{1,0:T(8,128)}, f32[48,256]{1,0:T(8,128)}) custom-call(bf16[1024,1536]{1,0:T(8,128)(2,1)} %bitcast.56, bf16[1024,1536]{1,0:T(8,128)(2,1)} %bitcast.57, f32[2,8,1536]{2,1,0:T(8,128)} %get-tuple-element.134.ending_ref, ...), custom_call_target="tpu_custom_call" | custom-call | flops 16106127360 | bytes 45088768 | tf_op jit(solution)/shard_map/tail/pallas_call | solution.py:1525
  435.3 3.0 outputs.1
  438.3 1.3 reduce
  439.6 1.3 reduce.1
  441.0 1.3 copy.52
  443.3 1.3 copy.53
  (57 shorter events, 8.0 us)
Async XLA Ops:
  7.2 41.4 %copy-start = (bf16[1536,192]{0,1:T(8,128)(2,1)S(1)}, bf16[1536,192]{0,1:T(8,128)(2,1)}, u32[]{:S(2)}) copy-start(bf16[1536,192]{0,1:T(8,128)(2,1)} %param.26) | copy-start | bytes 1769476
  7.2 9.6 %copy-start.14 = (s32[2]{0:T(128)S(1)}, s32[2]{0:T(128)}, u32[]{:S(2)}) copy-start(s32[2]{0:T(128)} %param.20) | copy-start | bytes 28
  7.2 9.7 %copy-start.13 = (s32[2,8]{1,0:T(2,128)S(1)}, s32[2,8]{1,0:T(2,128)}, u32[]{:S(2)}) copy-start(s32[2,8]{1,0:T(2,128)} %param.19) | copy-start | bytes 196
  10.3 36.7 %copy-start.10 = (f32[1536]{0:T(1024)S(1)}, f32[1536]{0:T(1024)}, u32[]{:S(2)}) copy-start(f32[1536]{0:T(1024)} %param.28) | copy-start | bytes 18436
  10.3 36.7 %copy-start.11 = (f32[1536]{0:T(1024)S(1)}, f32[1536]{0:T(1024)}, u32[]{:S(2)}) copy-start(f32[1536]{0:T(1024)} %param.25) | copy-start | bytes 18436
  10.3 36.8 %copy-start.7 = (f32[4,1536]{1,0:T(4,128)S(1)}, f32[4,1536]{1,0:T(4,128)}, u32[]{:S(2)}) copy-start(f32[4,1536]{1,0:T(4,128)} %param.24) | copy-start | bytes 73732
  10.3 36.8 %copy-start.9 = (f32[2,1536]{1,0:T(2,128)S(1)}, f32[2,1536]{1,0:T(2,128)}, u32[]{:S(2)}) copy-start(f32[2,1536]{1,0:T(2,128)} %param.27) | copy-start | bytes 36868
  10.4 33.1 %all-to-all-start = ((bf16[8,1,512,128]{3,2,1,0:T(8,128)(2,1)}), bf16[8,1,512,128]{3,2,1,0:T(8,128)(2,1)S(1)}, u32[]{:S(2)}, u32[]{:S(2)}) async-start(bf16[8,1,512,128]{3,2,1,0:T(8,128)(2,1)} %get-tuple-element.162), calls=%async_computation | async-start | bytes 2097152 | tf_op jit(solution)/shard_map/all_to_all | solution.py:1136
  43.4 7.4 %copy-start.6 = (bf16[8,1,512,128]{3,2,1,0:T(8,128)(2,1)}, bf16[8,1,512,128]{3,2,1,0:T(8,128)(2,1)S(1)}, u32[]{:S(2)}) copy-start(bf16[8,1,512,128]{3,2,1,0:T(8,128)(2,1)S(1)} %all-to-all-done) | copy-start | bytes 3145732
  43.4 39.5 %all-to-all-start.1 = ((bf16[8,1,512,128]{3,2,1,0:T(8,128)(2,1)}), bf16[8,1,512,128]{3,2,1,0:T(8,128)(2,1)S(1)}, u32[]{:S(2)}, u32[]{:S(2)}) async-start(bf16[8,1,512,128]{3,2,1,0:T(8,128)(2,1)} %get-tuple-element.161), calls=%async_computation.1 | async-start | bytes 2097152 | tf_op jit(solution)/shard_map/all_to_all | solution.py:1136
  51.0 14.9 %copy-start.2 = (s32[2,512,128]{2,1,0:T(8,128)}, s32[2,512,128]{2,1,0:T(8,128)S(1)}, u32[]{:S(2)}) copy-start(s32[2,512,128]{2,1,0:T(8,128)S(1)} %broadcast_in_dim.86.refs_11_.refs_16_) | copy-start | bytes 1572868
  82.9 1.0 copy-start.5
  83.9 57.0 %all-to-all-start.2 = ((bf16[8,2,512,128]{3,2,1,0:T(8,128)(2,1)}), bf16[8,2,512,128]{3,2,1,0:T(8,128)(2,1)S(1)}, u32[]{:S(2)}, u32[]{:S(2)}) async-start(bf16[8,2,512,128]{3,2,1,0:T(8,128)(2,1)} %bitcast.13), calls=%async_computation.2 | async-start | bytes 4194304 | tf_op jit(solution)/shard_map/all_to_all | solution.py:1136
  88.9 231.4 %reduce-scatter.3.cloned.1.call-start = ((), (), s32[]{:S(2)}) async-start(), calls=%async_computation.6 | async-start | bytes 11796480 | tf_op jit(solution)/shard_map/reduce_scatter | solution.py:1885
  140.9 1.3 copy-start.4
  241.9 78.3 %all-to-all-start.3 = ((bf16[8,2,512,128]{3,2,1,0:T(8,128)(2,1)}), bf16[8,2,512,128]{3,2,1,0:T(8,128)(2,1)S(1)}, u32[]{:S(2)}, u32[]{:S(2)}) async-start(bf16[8,2,512,128]{3,2,1,0:T(8,128)(2,1)} %bitcast.40), calls=%async_computation.3 | async-start | bytes 4194304 | tf_op jit(solution)/shard_map/all_to_all | solution.py:1154
  246.8 188.6 %reduce-scatter.5.cloned.1.call-start = ((), (), s32[]{:S(2)}) async-start(), calls=%async_computation.7 | async-start | bytes 2949120 | tf_op jit(solution)/shard_map/reduce_scatter | solution.py:1931
  273.5 46.8 %copy-start.12 = (f32[1024]{0:T(1024)S(1)}, f32[1024]{0:T(1024)}, u32[]{:S(2)}) copy-start(f32[1024]{0:T(1024)} %param.21) | copy-start | bytes 12292
  273.5 47.9 %copy-start.8 = (f32[1024]{0:T(1024)S(1)}, f32[1024]{0:T(1024)}, u32[]{:S(2)}) copy-start(f32[1024]{0:T(1024)} %param.30) | copy-start | bytes 12292
  441.0 2.3 copy-start.3
  441.0 3.7 copy-start.1
Sparse Core Ops, SparseCore 0:
  207.9 96.1 reduce-scatter.2
  320.4 78.3 reduce-scatter.4

commit v10 on v9

--- a/solution.py
+++ b/solution.py
@@ -259,6 +259,27 @@
 
 
 def backward_kernel(head_size, rows, *refs):
+    first_at = 2
+    sent_ref, got_ref, send_sem, recv_sem = refs[-4:]
+    leaving_ref = refs[-8]
+    lasts = Rows(refs[first_at + 1 : first_at + 1 + rows])
+
+    @pl.when(pl.program_id(0) == 0)
+    def _():
+        for row in range(rows):
+            sent_ref[row, 0:1, :] = lasts[row, 0:1, :]
+            sent_ref[row, 1:2, :] = refs[first_at][row]
+        carried(sent_ref, got_ref, leaving_ref, send_sem, recv_sem, True)
+
+    block_backward(head_size, rows, 0, leaving_ref, *refs[:-8], *refs[-7:-4])
+
+
+def later_backward_kernel(head_size, rows, first, *refs):
+    held = 4
+    block_backward(head_size, rows, first, refs[0], *refs[1 + held :])
+
+
+def block_backward(head_size, rows, first_block, leaving_ref, *refs):
     (
         local_ref,
         back_ref,
@@ -278,18 +299,11 @@
     ), others = by_rows(
         refs, rows, (False,) * 3 + (True,) * 3 + (False,) + (True,) * 3 + (False,) + (True,) * 2 + (False,) * 2
     )
-    dbranch_ref, tail_ref, head_ref, dgates_ref, both_ref, dconv_ref, sums_ref = others[:7]
-    leaving_ref, sent_ref, got_ref, send_sem, recv_sem = others[7:]
+    dbranch_ref, tail_ref, head_ref, dgates_ref = others[:4]
+    both_ref, dconv_ref, sums_ref = others[-3:]
     _, length, width = local_ref.shape
-
-    @pl.when(pl.program_id(0) == 0)
-    def _():
-        for row in range(rows):
-            sent_ref[row, 0:1, :] = last_ref[row, 0:1, :]
-            sent_ref[row, 1:2, :] = first_ref[row]
-        carried(sent_ref, got_ref, leaving_ref, send_sem, recv_sem, True)
-
-    block = pl.ds(pl.multiple_of(pl.program_id(0) * width, width), width)
+    here = pl.program_id(0) + first_block
+    block = pl.ds(pl.multiple_of(here * width, width), width)
     taps = [par_ref[k : k + 1, :] for k in range(4)]
     soft = par_ref[7:8, :]
     place = lax.broadcasted_iota(jnp.int32, (SUBLANES, width), 0)
@@ -543,7 +557,7 @@
         )
 
     def backward(
-        self, local, back, first, last, state, cum, entering, rate, igate, lru, dist, branch, rim, params, gates
+        self, local, back, first, last, state, cum, entering, rate, igate, lru, dist, branch, rim, params, gates, between_calls
     ):
         f32 = jnp.float32
         outs = [
@@ -552,33 +566,72 @@
             self.shape(SUBLANES, f32),
             jax.ShapeDtypeStruct((self.channels, 2 * LANES), jnp.bfloat16),
         ]
-        tall, apart = (self.tall(), self.apart(self.length))
         seqs = lax.axis_size("seq")
         summary = (self.rows, 2, self.channels)
-        return channel_call(
+        arrays = (local, back, first, *last, *state, *cum, entering, *rate, *igate, *lru, dist, *branch, *rim)
+        arrays += (params, gates)
+        early = self.blocks - 1
+        scratch = [
+            pltpu.VMEM((self.rows, self.length, 2 * self.width), jnp.bfloat16),
+            pltpu.VMEM((self.rows, self.length, self.width), f32),
+            pltpu.VMEM((SUBLANES, self.width), f32),
+        ]
+
+        def specs(offset):
+            rows, width = (self.rows, self.width)
+
+            def wide(rows, size):
+                return pl.BlockSpec((rows, size, width), lambda j: (0, 0, j + offset))
+
+            def flat(size):
+                return pl.BlockSpec((size, width), lambda j: (0, j + offset))
+
+            def tall(columns):
+                return pl.BlockSpec((width, columns), lambda j: (j + offset, 0))
+
+            whole, apart = (wide(rows, self.length), [wide(1, self.length)] * rows)
+            given = [whole, whole, self.whole(rows, 1), *[self.whole(1, 2)] * rows, *apart * 2]
+            given += [wide(rows, 1), *apart * 3, self.dist(), *apart, *[wide(1, SUBLANES)] * rows]
+            given += [flat(16), tall(2 * width)]
+            made = [whole, wide(rows, SUBLANES), wide(rows, SUBLANES), tall(2 * LANES)]
+            return (given, made)
+
+        given, made = specs(0)
+        *found, leaving = channel_call(
             functools.partial(backward_kernel, self.head_size, self.rows),
             "recurrence_backward",
-            (local, back, first, *last, *state, *cum, entering, *rate, *igate, *lru, dist, *branch, *rim)
-            + (params, gates),
-            [tall, tall, self.whole(self.rows, 1), *[self.whole(1, 2)] * self.rows, *apart * 2]
-            + [self.short(1), *apart * 3, self.dist(), *apart, *self.apart(SUBLANES)]
-            + [self.flat(16), self.gates(2 * self.width)],
-            outs,
-            [tall, self.short(SUBLANES), self.short(SUBLANES), self.gates(2 * LANES)],
-            [
-                pltpu.VMEM((self.rows, self.length, 2 * self.width), jnp.bfloat16),
-                pltpu.VMEM((self.rows, self.length, self.width), f32),
-                pltpu.VMEM((SUBLANES, self.width), f32),
-                pltpu.VMEM((self.rows, 1, self.channels), f32),
+            arrays,
+            given,
+            outs + [self.shape(1, f32)],
+            made + [self.whole(self.rows, 1)],
+            scratch
+            + [
                 pltpu.VMEM(summary, f32),
                 pltpu.VMEM((seqs,) + summary, f32),
                 pltpu.SemaphoreType.DMA((seqs - 1,)),
                 pltpu.SemaphoreType.DMA((seqs - 1,)),
             ],
-            self.blocks,
+            early,
             2 * self.flops,
             {"collective_id": 5, "has_side_effects": True},
         )
+        between, leaving = between_calls(leaving)
+        given, made = specs(early)
+        done = pl.pallas_call(
+            functools.partial(later_backward_kernel, self.head_size, self.rows, early),
+            name="recurrence_backward_end",
+            grid=(self.blocks - early,),
+            in_specs=[self.whole(self.rows, 1)] + [pl.BlockSpec(memory_space=pl.ANY)] * 4 + given,
+            out_specs=made,
+            out_shape=outs,
+            scratch_shapes=scratch,
+            input_output_aliases={1 + k: k for k in range(4)},
+            compiler_params=pltpu.CompilerParams(vmem_limit_bytes=VMEM_BYTES),
+            cost_estimate=pl.CostEstimate(
+                flops=self.flops // 2, bytes_accessed=16 * self.flops // self.width, transcendentals=0
+            ),
+        )(leaving, *found, *arrays)
+        return (*done, between)
 
 
 def gathered(parts_ref, at):
@@ -702,35 +755,58 @@
 
 
 def middle_kernel(rows, *refs):
-    (last_ref, state_ref, cum_ref, pre_ref, x_ref, out_ref, gain_ref), others = by_rows(
+    (last_ref, state_hbm, cum_hbm, pre_hbm, x_ref, out_ref, gain_ref), others = by_rows(
         refs, rows, (True,) * 5 + (False,) * 2
     )
     entering_ref, mixed_ref, resid_ref, normed_ref = others[:4]
-    sent_ref, got_ref, send_sem, recv_sem = others[4:]
+    sent_ref, got_ref, held_ref, send_sem, recv_sem, load_sem = others[4:]
     tall, model = resid_ref.shape
-    step = pl.program_id(0)
-    tiles = pl.num_programs(0) // rows
+    step, steps = (pl.program_id(0), pl.num_programs(0))
+    tiles = steps // rows
     slab = 16
+
+    def on_row(place, act):
+        for row in range(rows):
+
+            @pl.when(lax.div(place, tiles) == row)
+            def _(row=row):
+                at = pl.ds(pl.multiple_of(lax.rem(place, tiles) * tall, tall), tall)
+                slot = lax.rem(place, 2)
+                for kind, source in enumerate((state_hbm, cum_hbm, pre_hbm)):
+                    act(
+                        pltpu.make_async_copy(
+                            source.refs[row].at[0, at], held_ref.at[slot, kind], load_sem.at[slot, kind]
+                        )
+                    )
 
     @pl.when(step == 0)
     def _():
+        on_row(step, lambda copy: copy.start())
         for row in range(rows):
             sent_ref[row] = last_ref[row]
         carried(sent_ref, got_ref, entering_ref, send_sem, recv_sem, False)
 
+    @pl.when(step + 1 < steps)
+    def _():
+        on_row(step + 1, lambda copy: copy.start())
+
+    on_row(step, lambda copy: copy.wait())
+    slot = lax.rem(step, 2)
+    mine = lax.div(step, tiles)
+
+    def mix(index, carry):
+        at = pl.ds(pl.multiple_of(index * slab, slab), slab)
+        state = held_ref[slot, 0, at, :] + held_ref[slot, 1, at, :] * entering_ref[mine]
+        pre = held_ref[slot, 2, at, :]
+        inner = jnp.tanh(pre * (GELU_C + (GELU_C * GELU_A) * (pre * pre)))
+        mixed_ref[at, :] = (state * (pre * (0.5 + 0.5 * inner))).astype(jnp.bfloat16)
+        return carry
+
+    lax.fori_loop(0, tall // slab, mix, 0, unroll=2)
     for row in range(rows):
 
-        @pl.when(lax.div(step, tiles) == row)
+        @pl.when(mine == row)
         def _(row=row):
-            def mix(index, carry):
-                at = pl.ds(pl.multiple_of(index * slab, slab), slab)
-                state = state_ref[row, at, :] + cum_ref[row, at, :] * entering_ref[row]
-                pre = pre_ref[row, at, :]
-                inner = jnp.tanh(pre * (GELU_C + (GELU_C * GELU_A) * (pre * pre)))
-                mixed_ref[at, :] = (state * (pre * (0.5 + 0.5 * inner))).astype(jnp.bfloat16)
-                return carry
-
-            lax.fori_loop(0, tall // slab, mix, 0, unroll=2)
             tile = 512
             for first in range(0, model, tile):
                 at = slice(first, first + tile)
@@ -761,20 +837,16 @@
     def whole(shape):
         return pl.BlockSpec(shape, lambda s: (0,) * len(shape), pipeline_mode=pl.Buffered(1))
 
-    def part(row):
-        return lambda s: (0, jnp.clip(s - row * tiles, 0, tiles - 1), 0)
-
     def flat(row):
         return lambda s: (jnp.clip(s - row * tiles, 0, tiles - 1), 0)
 
-    apart = [pl.BlockSpec((1, tall, rec), part(row)) for row in range(rows)]
     summary = (rows, 2, rec)
     return pl.pallas_call(
         functools.partial(middle_kernel, rows),
         name="mix_and_norm",
         grid=(rows * tiles,),
         in_specs=[whole((1, 2, rec))] * rows
-        + apart * 3
+        + [pl.BlockSpec(memory_space=pl.ANY)] * (3 * rows)
         + [pl.BlockSpec((tall, model), flat(row)) for row in range(rows)]
         + [whole(recur_out.shape), whole((1, model))],
         out_specs=[
@@ -792,8 +864,10 @@
         scratch_shapes=[
             pltpu.VMEM(summary, f32),
             pltpu.VMEM((seqs,) + summary, f32),
+            pltpu.VMEM((2, 3, tall, rec), f32),
             pltpu.SemaphoreType.DMA((seqs - 1,)),
             pltpu.SemaphoreType.DMA((seqs - 1,)),
+            pltpu.SemaphoreType.DMA((2, 3)),
         ],
         compiler_params=pltpu.CompilerParams(
             collective_id=4, has_side_effects=True, vmem_limit_bytes=VMEM_BYTES
@@ -876,33 +950,36 @@
     total_ref,
     back_ref,
 ):
-    tokens, model = resid_ref.shape
-    step = pl.program_id(0)
+    tall, model = hidden_ref.shape[0], gout_ref.shape[1]
+    step, tile = (pl.program_id(0), pl.program_id(1))
+    wide = 512
+    contract = (((1,), (1,)), ((), ()))
+    rows = pl.ds(pl.multiple_of(tile * tall, tall), tall)
+
+    def products(own):
+        forth = jnp.dot(hidden_ref[...], down_ref[:, own], preferred_element_type=jnp.float32)
+        back = lax.dot_general(
+            dgate_ref[...], gate_ref[own, :], contract, preferred_element_type=jnp.float32
+        ) + lax.dot_general(
+            dup_ref[...], up_ref[own, :], contract, preferred_element_type=jnp.float32
+        )
+        return (forth, back)
 
     @pl.when(step == 0)
     def _():
-        total_ref[...] = resid_ref[...]
-        back_ref[...] = jnp.zeros_like(back_ref)
-
-    tall = min(tokens, 512)
-    wide = 512
-
-    def tile(index, carry):
-        at = pl.ds(pl.multiple_of(index * tall, tall), tall)
-        contract = (((1,), (1,)), ((), ()))
-        for column in range(model // wide):
-            own = slice(column * wide, (column + 1) * wide)
-            total_ref[at, own] += jnp.dot(
-                hidden_ref[at, :], down_ref[:, own], preferred_element_type=jnp.float32
-            )
-            back_ref[at, own] += lax.dot_general(
-                dgate_ref[at, :], gate_ref[own, :], contract, preferred_element_type=jnp.float32
-            ) + lax.dot_general(
-                dup_ref[at, :], up_ref[own, :], contract, preferred_element_type=jnp.float32
-            )
-        return carry
-
-    lax.fori_loop(0, tokens // tall, tile, 0)
+        for first in range(0, model, wide):
+            own = slice(first, first + wide)
+            forth, back = products(own)
+            total_ref[rows, own] = resid_ref[rows, own] + forth
+            back_ref[rows, own] = back
+
+    @pl.when(step > 0)
+    def _():
+        for first in range(0, model, wide):
+            own = slice(first, first + wide)
+            forth, back = products(own)
+            total_ref[rows, own] += forth
+            back_ref[rows, own] += back
 
     @pl.when(step == pl.num_programs(0) - 1)
     def _():
@@ -910,7 +987,7 @@
         small = 16
 
         def finish(index, carry):
-            at = pl.ds(pl.multiple_of(index * small, small), small)
+            at = pl.ds(pl.multiple_of(tile * tall + index * small, small), small)
             result = total_ref[at, :].astype(jnp.bfloat16)
             for part in range(parts):
                 result_ref[part, at, :] = result[:, part * width : (part + 1) * width]
@@ -923,7 +1000,7 @@
             dres_ref[at, :] = dres.astype(jnp.bfloat16)
             return carry
 
-        lax.fori_loop(0, tokens // small, finish, 0, unroll=4)
+        lax.fori_loop(0, tall // small, finish, 0, unroll=4)
 
 
 MLP_CHUNK = 768
@@ -971,17 +1048,28 @@
     tokens, model = resid.shape
     ffn = mlp_gate.shape[1]
     low, f32 = (jnp.bfloat16, jnp.float32)
-    weights, made = mlp_specs(tokens, model)
+    chunk, tall = (2 * MLP_CHUNK, min(tokens, 512))
+
+    def resident(shape):
+        return pl.BlockSpec(shape, lambda s, t: (0,) * len(shape), pipeline_mode=pl.Buffered(1))
+
+    columns = pl.BlockSpec((model, chunk), lambda s, t: (0, s))
+    down = pl.BlockSpec((chunk, model), lambda s, t: (s, 0))
+    made = pl.BlockSpec((tall, chunk), lambda s, t: (t, s))
     return pl.pallas_call(
         back_kernel,
         name="mlp_back",
-        grid=(ffn // MLP_CHUNK,),
+        grid=(ffn // chunk, tokens // tall),
         in_specs=[
-            *made,
+            made,
+            made,
+            made,
             resident((tokens, model)),
             resident((tokens, model)),
             resident((1, model)),
-            *weights,
+            columns,
+            columns,
+            down,
         ],
         out_specs=[resident(parts_shape), resident((tokens, model))],
         out_shape=[
@@ -1042,8 +1130,18 @@
             for weight, gradient in pairs
         )
 
-    sum_gain1[...] = weighed((input_ref, in_sum), (gate_ref, gate_sum)) / gain1_ref[...]
-    sum_gain2[...] = weighed((mlp_gate_ref, sum_mgate), (mlp_up_ref, sum_mup)) / gain2_ref[...]
+    def as_row(column, gain):
+        lane = lax.broadcasted_iota(jnp.int32, (rows, LANES), 1)
+        place = lax.broadcasted_iota(jnp.int32, (rows, LANES), 0)
+        whole = lax.broadcasted_iota(jnp.int32, (rows, model), 1)
+        own = device_ref[0] * rows + lax.broadcasted_iota(jnp.int32, (rows, model), 0)
+        own_gain = jnp.sum(jnp.where(whole == own, gain[...], 0.0), axis=1, keepdims=True)
+        return jnp.sum(jnp.where(lane == place, column / own_gain, 0.0), axis=0, keepdims=True)
+
+    row1 = as_row(weighed((input_ref, in_sum), (gate_ref, gate_sum)), gain1_ref)
+    row2 = as_row(weighed((mlp_gate_ref, sum_mgate), (mlp_up_ref, sum_mup)), gain2_ref)
+    sum_gain1[...] = row1[:, :rows]
+    sum_gain2[...] = row2[:, :rows]
     sum_in[...] = in_sum[...]
     sum_gate[...] = gate_sum[...]
     sum_out[...] = out_sum[...]
@@ -1077,8 +1175,8 @@
         return pl.BlockSpec(shape, lambda s, device: (device[0], 0))
 
     given = (own, gate_sum, in_sum, out_sum, small)
-    shapes = [(rows, 1), (rows, rec), (rows, rec), (4, channels), (1, channels)]
-    shapes += [(channels, 2 * size), (2, channels), (1, channels), out_sum.shape, (rows, 1)]
+    shapes = [(1, rows), (rows, rec), (rows, rec), (4, channels), (1, channels)]
+    shapes += [(channels, 2 * size), (2, channels), (1, channels), out_sum.shape, (1, rows)]
     shapes += [(rows, ffn), (rows, ffn), (own.shape[0] - 2 * ffn // model * rows, model)]
     return pl.pallas_call(
         outputs_kernel,
@@ -1089,7 +1187,7 @@
             in_specs=[whole(a.shape) for a in given]
             + [mine((rows, rec))] * 2
             + [mine((rows, ffn))] * 2
-            + [mine((rows, 1))] * 2,
+            + [whole((1, model))] * 2,
             out_specs=[whole(shape) for shape in shapes],
         ),
         out_shape=[jax.ShapeDtypeStruct(shape, f32) for shape in shapes],
@@ -1101,8 +1199,8 @@
         recur_gate,
         mlp_gate,
         mlp_up,
-        gain1[:, None],
-        gain2[:, None],
+        gain1[None],
+        gain2[None],
     )
 
 
@@ -1908,7 +2006,14 @@
         params,
     )
     gate_low = gate_low.reshape(tok_count, rec_width)
-    branch_local, ending, leading, small = core.backward(
+
+    def zed_stage(leaving):
+        if not tiled:
+            return ((), leaving)
+        done, leaving = lax.optimization_barrier((merged, leaving))
+        return (lax.psum_scatter(done, "zed", scatter_dimension=0, tiled=True), leaving)
+
+    branch_local, ending, leading, small, merged_own = core.backward(
         back_local,
         back_cum,
         first_term,
@@ -1924,11 +2029,11 @@
         rim,
         params,
         wide_gates,
+        zed_stage,
     )
     branch_low = branch_local.reshape(tok_count, rec_width)
     if tiled:
-        output, merged, branch_low = lax.optimization_barrier((output, merged, branch_low))
-        merged = lax.psum_scatter(merged, "zed", scatter_dimension=0, tiled=True)
+        output, branch_low = lax.optimization_barrier((output, branch_low))
         grad_tokens, sum_rgate, sum_rout, sum_rin, own_small = tail(
             gate_low,
             branch_low,
@@ -1947,7 +2052,7 @@
         device = lax.axis_index(("seq", "zed", "core"))
         sums = outputs(
             device,
-            merged[0],
+            merged_own[0],
             sum_rgate,
             sum_rin,
             sum_rout,

time: 452 us -> 439 us (0.971)
  Pallas kernels: 371 us -> 363 us
    pallas_call x1 -> x2, Pallas kernels: 34.2 us -> 49.5 us  [the longest x1 35 us: mlp_back(): pl.pallas_call(back_kernel, name='mlp_back', grid=(ffn // chunk, tokens /...]
    pallas_call x1, Pallas kernels: 113 us -> 101 us  [tail(): pl.pallas_call(functools.partial(tail_kernel, corners, orders), name='tai...]
    pallas_call x4, Pallas kernels: 107 us -> 98.4 us  [channel_call(): pl.pallas_call(kernel, name=name, grid=(blocks,), in_specs=specs, out_spe...]
  transfers between devices with their start and end apart: 6 -> 6, of which waited for: 1 -> 1; matrix products, arithmetic and copies ran while one was open for 2% -> 1% of each run, Pallas kernels for 67% -> 67%
where the time goes in v10:
time: 439 us; the launch traced here: 438 us
  Pallas kernels  363 us (83%)
  waiting for transfers between devices  26.4 us (6%)
  starting transfers between devices  20.1 us (5%)
  between operations  14.4 us (3%)
  local copies, waits for them, and re-layouts  11.7 us (3%)
    pallas_call x1, Pallas kernels, tail(): pl.pallas_call(functools.partial(tail_kernel, corners, orders), name='tai...  101 us
    pallas_call x4, Pallas kernels, channel_call(): pl.pallas_call(kernel, name=name, grid=(blocks,), in_specs=specs, out_spe...  98.4 us
    pallas_call x1, Pallas kernels, mlp_back(): pl.pallas_call(back_kernel, name='mlp_back', grid=(ffn // chunk, tokens /...  35 us
    pallas_call x1, Pallas kernels, block_gradients(): pl.pallas_call(grads_kernel, name='block_gradients', grid=(total + 1,), i...  34.7 us
    pallas_call x1, Pallas kernels, mlp_hidden(): pl.pallas_call(hidden_kernel, name='mlp_hidden', grid=(ffn // MLP_CHUNK,)...  30.8 us
    pallas_call x2, Pallas kernels, front(): pl.pallas_call(front_kernel, name='norm_and_project', grid=(steps,), in_s...  26.6 us
    all_to_all x3, waiting for transfers between devices, features_in(): lax.all_to_all(local, CHAN, 0, 0, tiled=True).reshape(count, -1, width)  26.3 us
    pallas_call x1, Pallas kernels, middle(): pl.pallas_call(functools.partial(middle_kernel, rows), name='mix_and_norm...  18.9 us
  transfers between devices with their start and end apart: 6, of which 1 were waited for; matrix products, arithmetic and copies ran while one was open for 1% of the time, Pallas kernels for 67%

profile of v10, /device:TPU:0, one launch (start us, length us, event | category | flops | bytes accessed | tf_op | source)
XLA Modules:
  0.0 438.1 jit_solution(16989469511744356800)
XLA Ops:
  7.2 3.1 fusion.21
  10.4 6.5 %all-to-all-start = ((bf16[8,1,512,128]{3,2,1,0:T(8,128)(2,1)}), bf16[8,1,512,128]{3,2,1,0:T(8,128)(2,1)S(1)}, u32[]{:S(2)}, u32[]{:S(2)}) async-start(bf16[8,1,512,128]{3,2,1,0:T(8,128)(2,1)} %get-tuple-element.174), calls=%async_computation | async-start | bytes 2097152 | tf_op jit(solution)/shard_map/all_to_all | solution.py:1234
  17.1 26.3 %all-to-all-done = bf16[8,1,512,128]{3,2,1,0:T(8,128)(2,1)S(1)} async-done(((bf16[8,1,512,128]{3,2,1,0:T(8,128)(2,1)}), bf16[8,1,512,128]{3,2,1,0:T(8,128)(2,1)S(1)}, u32[]{:S(2)}, u32[]{:S(2)}) %all-to-all-start) | async-done | bytes 1048608 | tf_op jit(solution)/shard_map/all_to_all | solution.py:1234
  43.4 3.6 all-to-all-start.1
  47.1 1.3 concatenate.6.par_ref.refs_12_.refs_21_.refs_26_
  48.6 2.2 fusion.gates_ref.refs_22_.refs_27_
  51.9 14.0 %norm_and_project.2 = (bf16[512,1024]{1,0:T(8,128)(2,1)}, f32[512,128]{1,0:T(8,128)}, bf16[512,1024]{1,0:T(8,128)(2,1)}, f32[512,1536]{1,0:T(8,128)}, f32[512,1536]{1,0:T(8,128)}, /*index=5*/f32[8,1536]{1,0:T(8,128)}) custom-call(bf16[8,512,128]{2,1,0:T(8,128)(2,1)} %bitcast.46, f32[1,1024]{1,0:T(1,128)} %bitcast.58, bf16[1024,1536]{1,0:T(8,128)(2,1)} %input_ref.5, ...), custom_call_target="tpu_custom_call" | custom-call | flops 3221225472 | bytes 10485760 | tf_op jit(solution)/shard_map/norm_and_project/pallas_call | solution.py:727
  65.9 17.2 %recurrence_forward.2 = (bf16[1,512,1536]{2,1,0:T(8,128)(2,1)}, f32[1,512,1536]{2,1,0:T(8,128)}, f32[1,512,1536]{2,1,0:T(8,128)}, f32[1,512,1536]{2,1,0:T(8,128)...) custom-call(f32[1,512,1536]{2,1,0:T(8,128)} %bitcast.30, f32[1,8,1536]{2,1,0:T(8,128)} %bitcast.49, ...), custom_call_target="tpu_custom_call" | custom-call | flops 1207959552 | bytes 20082688 | tf_op jit(solution)/shard_map/recurrence_forward/pallas_call | solution.py:464
  84.0 5.0 %all-to-all-start.2 = ((bf16[8,2,512,128]{3,2,1,0:T(8,128)(2,1)}), bf16[8,2,512,128]{3,2,1,0:T(8,128)(2,1)S(1)}, u32[]{:S(2)}, u32[]{:S(2)}) async-start(bf16[8,2,512,128]{3,2,1,0:T(8,128)(2,1)} %bitcast.13), calls=%async_computation.2 | async-start | bytes 4194304 | tf_op jit(solution)/shard_map/all_to_all | solution.py:1234
  89.8 12.6 %norm_and_project.3 = (bf16[512,1024]{1,0:T(8,128)(2,1)}, f32[512,128]{1,0:T(8,128)}, bf16[512,1024]{1,0:T(8,128)(2,1)}, f32[512,1536]{1,0:T(8,128)}, f32[512,1536]{1,0:T(8,128)}, /*index=5*/f32[8,1536]{1,0:T(8,128)}) custom-call(bf16[8,512,128]{2,1,0:T(8,128)(2,1)} %bitcast.45, f32[1,1024]{1,0:T(1,128)} %bitcast.59, bf16[1024,1536]{1,0:T(8,128)(2,1)} %input_ref.5, ...), custom_call_target="tpu_custom_call" | custom-call | flops 3221225472 | bytes 10485760 | tf_op jit(solution)/shard_map/norm_and_project/pallas_call | solution.py:727
  102.4 17.0 %recurrence_forward.3 = (bf16[1,512,1536]{2,1,0:T(8,128)(2,1)}, f32[1,512,1536]{2,1,0:T(8,128)}, f32[1,512,1536]{2,1,0:T(8,128)}, f32[1,512,1536]{2,1,0:T(8,128)...) custom-call(f32[1,512,1536]{2,1,0:T(8,128)} %bitcast.33, f32[1,8,1536]{2,1,0:T(8,128)} %bitcast.52, ...), custom_call_target="tpu_custom_call" | custom-call | flops 1207959552 | bytes 20082688 | tf_op jit(solution)/shard_map/recurrence_forward/pallas_call | solution.py:464
  119.4 18.9 %mix_and_norm.1 = (f32[2,1,1536]{2,1,0:T(1,128)}, bf16[1024,1536]{1,0:T(8,128)(2,1)}, f32[1024,1024]{1,0:T(8,128)}, bf16[1024,1024]{1,0:T(8,128)(2,1)}) custom-call(f32[1,2,1536]{2,1,0:T(2,128)} %get-tuple-element.100.refs_0_.refs_3_.refs_8_, f32[1,2,1536]{2,1,0:T(2,128)} %get-tuple-element.104.refs_1_.refs_4_.refs_9_, ...), custom_call_target="tpu_custom_call" | custom-call | flops 3221225472 | bytes 22020096 | tf_op jit(solution)/shard_map/mix_and_norm/pallas_call | solution.py:844
  138.3 1.3 copy-done.4
  139.6 30.8 %mlp_hidden.1 = (bf16[1024,1024]{1,0:T(8,128)(2,1)}, bf16[1024,3072]{1,0:T(8,128)(2,1)}, bf16[1024,3072]{1,0:T(8,128)(2,1)}, bf16[1024,3072]{1,0:T(8,128)(2,1)}) custom-call(s32[2]{0:T(128)} %broadcast_subtract_fusion.1.left_ref, bf16[8,1024,128]{2,1,0:T(8,128)(2,1)} %bitcast.44, bf16[1024,1024]{1,0:T(8,128)(2,1)} %get-tuple-element.113.normed_ref, ...), custom_call_target="tpu_custom_call" | custom-call | flops 19327352832 | bytes 44040192 | tf_op jit(solution)/shard_map/mlp_hidden/pallas_call | solution.py:1026
  170.5 34.7 %block_gradients.1 = bf16[16,288,1024]{2,1,0:T(8,128)(2,1)} custom-call(bf16[1024,1024]{1,0:T(8,128)(2,1)} %get-tuple-element.113.normed_ref, bf16[1024,3072]{1,0:T(8,128)(2,1)} %get-tuple-element.117.dgate_ref, bf16[1024,3072]{1,0:T(8,128)(2,1)} %get-tuple-element.118.dup_ref, bf16[1024,3072]{1,0:T(8,128)(2,1)} %get-tuple-element.121.hidden_ref, ...), custom_call_target="tpu_custom_call" | custom-call | flops 19327352832 | bytes 32505856 | tf_op jit(solution)/shard_map/block_gradients/pallas_call | solution.py:1828
  205.2 35.0 %mlp_back.1 = (bf16[8,1024,128]{2,1,0:T(8,128)(2,1)}, bf16[1024,1024]{1,0:T(8,128)(2,1)}) custom-call(bf16[1024,3072]{1,0:T(8,128)(2,1)} %get-tuple-element.121.hidden_ref, bf16[1024,3072]{1,0:T(8,128)(2,1)} %get-tuple-element.117.dgate_ref, bf16[1024,3072]{1,0:T(8,128)(2,1)} %get-tuple-element.118.dup_ref, bf16[1024,1024]{1,0:T(8,128)(2,1)} %get-tuple-element.120.gout_ref, ...), custom_call_target="tpu_custom_call" | custom-call | flops 19327352832 | bytes 48234496 | tf_op jit(solution)/shard_map/mlp_back/pallas_call | solution.py:1059
  240.1 4.8 %all-to-all-start.3 = ((bf16[8,2,512,128]{3,2,1,0:T(8,128)(2,1)}), bf16[8,2,512,128]{3,2,1,0:T(8,128)(2,1)S(1)}, u32[]{:S(2)}, u32[]{:S(2)}) async-start(bf16[8,2,512,128]{3,2,1,0:T(8,128)(2,1)} %bitcast.43), calls=%async_computation.3 | async-start | bytes 4194304 | tf_op jit(solution)/shard_map/all_to_all | solution.py:1252
  245.0 26.4 %recurrence_adjoint.1 = (bf16[2,512,1536]{2,1,0:T(8,128)(2,1)}, f32[2,512,1536]{2,1,0:T(8,128)}, f32[2,512,1536]{2,1,0:T(8,128)}, f32[2,1,1536]{2,1,0:T(1,128)}) custom-call(bf16[1024,1024]{1,0:T(8,128)(2,1)} %get-tuple-element.125.refs_0_.dres_hbm, bf16[1536,1024]{1,0:T(8,128)(2,1)} %refs_1_.1, f32[1,512,1536]{2,1,0:T(8,128)} %bitcast.37, ...), custom_call_target="tpu_custom_call" | custom-call | flops 3221225472 | bytes 46784512 | tf_op jit(solution)/shard_map/recurrence_adjoint/pallas_call | solution.py:464
  271.4 37.8 %recurrence_backward.1 = (bf16[2,512,1536]{2,1,0:T(8,128)(2,1)}, f32[2,8,1536]{2,1,0:T(8,128)}, f32[2,8,1536]{2,1,0:T(8,128)}, bf16[1536,256]{1,0:T(8,128)(2,1)}, f32[2,1,1536]{2,1,0:T(1,128)}) custom-call(f32[2,512,1536]{2,1,0:T(8,128)} %get-tuple-element.129.refs_0_.refs_5_, f32[2,512,1536]{2,1,0:T(8,128)} %get-tuple-element.130.refs_1_.refs_6_, ...), custom_call_target="tpu_custom_call" | custom-call | flops 4831838208 | bytes 54456320 | tf_op jit(solution)/shard_map/recurrence_backward/pallas_call | solution.py:464
  309.2 14.5 %recurrence_backward_end.1 = (bf16[2,512,1536]{2,1,0:T(8,128)(2,1)}, f32[2,8,1536]{2,1,0:T(8,128)}, f32[2,8,1536]{2,1,0:T(8,128)}, bf16[1536,256]{1,0:T(8,128)(2,1)}) custom-call(f32[2,1,1536]{2,1,0:T(1,128)} %get-tuple-element.137.refs_0_, ...), custom_call_target="tpu_custom_call", output_to_operand_aliasing={{0}: (1, {}), {1}: (2, {}), {2}: (3, {}), {3}: (4, {})} | custom-call | flops 1207959552 | bytes 100663296 | tf_op jit(solution)/shard_map/recurrence_backward_end/pallas_call | solution.py:620
  323.8 100.7 %tail.1 = (bf16[16,512,128]{2,1,0:T(8,128)(2,1)}, f32[32,1536]{1,0:T(8,128)}, f32[48,1024]{1,0:T(8,128)}, f32[32,1536]{1,0:T(8,128)}, f32[48,256]{1,0:T(8,128)}) custom-call(bf16[1024,1536]{1,0:T(8,128)(2,1)} %bitcast.62, bf16[1024,1536]{1,0:T(8,128)(2,1)} %bitcast.41, f32[2,8,1536]{2,1,0:T(8,128)} %get-tuple-element.146.ending_ref, ...), custom_call_target="tpu_custom_call" | custom-call | flops 16106127360 | bytes 45088768 | tf_op jit(solution)/shard_map/tail/pallas_call | solution.py:1623
  424.5 3.0 outputs.1
  427.6 1.3 copy.54
  429.9 1.3 copy.55
  (50 shorter events, 4.4 us)
Async XLA Ops:
  7.2 41.4 %copy-start = (bf16[1536,192]{0,1:T(8,128)(2,1)S(1)}, bf16[1536,192]{0,1:T(8,128)(2,1)}, u32[]{:S(2)}) copy-start(bf16[1536,192]{0,1:T(8,128)(2,1)} %param.26) | copy-start | bytes 1769476
  7.2 9.6 %copy-start.12 = (s32[2]{0:T(128)S(1)}, s32[2]{0:T(128)}, u32[]{:S(2)}) copy-start(s32[2]{0:T(128)} %param.20) | copy-start | bytes 28
  7.2 9.7 %copy-start.10 = (f32[1536]{0:T(1024)S(1)}, f32[1536]{0:T(1024)}, u32[]{:S(2)}) copy-start(f32[1536]{0:T(1024)} %param.25) | copy-start | bytes 18436
  7.2 9.7 %copy-start.11 = (s32[2,8]{1,0:T(2,128)S(1)}, s32[2,8]{1,0:T(2,128)}, u32[]{:S(2)}) copy-start(s32[2,8]{1,0:T(2,128)} %param.19) | copy-start | bytes 196
  10.3 36.6 %copy-start.9 = (f32[1536]{0:T(1024)S(1)}, f32[1536]{0:T(1024)}, u32[]{:S(2)}) copy-start(f32[1536]{0:T(1024)} %param.28) | copy-start | bytes 18436
  10.3 36.7 %copy-start.7 = (f32[4,1536]{1,0:T(4,128)S(1)}, f32[4,1536]{1,0:T(4,128)}, u32[]{:S(2)}) copy-start(f32[4,1536]{1,0:T(4,128)} %param.24) | copy-start | bytes 73732
  10.3 36.7 %copy-start.8 = (f32[2,1536]{1,0:T(2,128)S(1)}, f32[2,1536]{1,0:T(2,128)}, u32[]{:S(2)}) copy-start(f32[2,1536]{1,0:T(2,128)} %param.27) | copy-start | bytes 36868
  10.4 33.1 %all-to-all-start = ((bf16[8,1,512,128]{3,2,1,0:T(8,128)(2,1)}), bf16[8,1,512,128]{3,2,1,0:T(8,128)(2,1)S(1)}, u32[]{:S(2)}, u32[]{:S(2)}) async-start(bf16[8,1,512,128]{3,2,1,0:T(8,128)(2,1)} %get-tuple-element.174), calls=%async_computation | async-start | bytes 2097152 | tf_op jit(solution)/shard_map/all_to_all | solution.py:1234
  43.4 7.4 %copy-start.6 = (bf16[8,1,512,128]{3,2,1,0:T(8,128)(2,1)}, bf16[8,1,512,128]{3,2,1,0:T(8,128)(2,1)S(1)}, u32[]{:S(2)}) copy-start(bf16[8,1,512,128]{3,2,1,0:T(8,128)(2,1)S(1)} %all-to-all-done) | copy-start | bytes 3145732
  43.4 39.6 %all-to-all-start.1 = ((bf16[8,1,512,128]{3,2,1,0:T(8,128)(2,1)}), bf16[8,1,512,128]{3,2,1,0:T(8,128)(2,1)S(1)}, u32[]{:S(2)}, u32[]{:S(2)}) async-start(bf16[8,1,512,128]{3,2,1,0:T(8,128)(2,1)} %get-tuple-element.173), calls=%async_computation.1 | async-start | bytes 2097152 | tf_op jit(solution)/shard_map/all_to_all | solution.py:1234
  51.0 14.9 %copy-start.2 = (s32[2,512,128]{2,1,0:T(8,128)}, s32[2,512,128]{2,1,0:T(8,128)S(1)}, u32[]{:S(2)}) copy-start(s32[2,512,128]{2,1,0:T(8,128)S(1)} %broadcast_in_dim.82.refs_11_.refs_16_.refs_21_) | copy-start | bytes 1572868
  83.1 1.0 copy-start.5
  84.0 54.3 %all-to-all-start.2 = ((bf16[8,2,512,128]{3,2,1,0:T(8,128)(2,1)}), bf16[8,2,512,128]{3,2,1,0:T(8,128)(2,1)S(1)}, u32[]{:S(2)}, u32[]{:S(2)}) async-start(bf16[8,2,512,128]{3,2,1,0:T(8,128)(2,1)} %bitcast.13), calls=%async_computation.2 | async-start | bytes 4194304 | tf_op jit(solution)/shard_map/all_to_all | solution.py:1234
  89.1 220.1 %reduce-scatter.3.cloned.1.call-start = ((), (), s32[]{:S(2)}) async-start(), calls=%async_computation.6 | async-start | bytes 11796480 | tf_op jit(solution)/shard_map/reduce_scatter | solution.py:1983
  138.3 1.3 copy-start.4
  240.1 83.6 %all-to-all-start.3 = ((bf16[8,2,512,128]{3,2,1,0:T(8,128)(2,1)}), bf16[8,2,512,128]{3,2,1,0:T(8,128)(2,1)S(1)}, u32[]{:S(2)}, u32[]{:S(2)}) async-start(bf16[8,2,512,128]{3,2,1,0:T(8,128)(2,1)} %bitcast.43), calls=%async_computation.3 | async-start | bytes 4194304 | tf_op jit(solution)/shard_map/all_to_all | solution.py:1252
  244.9 179.6 %reduce-scatter.5.cloned.1.call-start = ((), (), s32[]{:S(2)}) async-start(), calls=%async_computation.7 | async-start | bytes 2949120 | tf_op jit(solution)/shard_map/reduce_scatter | solution.py:2014
  427.5 2.3 copy-start.3
  427.5 3.7 copy-start.1
Sparse Core Ops, SparseCore 0:
  205.3 96.0 reduce-scatter.2
  309.4 66.3 reduce-scatter.4

commit v11 on v10

--- a/solution.py
+++ b/solution.py
@@ -677,15 +677,10 @@
 
         lax.fori_loop(0, tokens // piece, norm, 0, unroll=2)
 
-    def multiply(index, carry):
-        at = pl.ds(pl.multiple_of(index * tall, tall), tall)
-        normed = normed_ref[at, :]
-        branch_ref[at, :] = jnp.dot(normed, input_ref[...], preferred_element_type=jnp.float32)
-        pre_ref[at, :] = jnp.dot(normed, gate_ref[...], preferred_element_type=jnp.float32)
-        return carry
-
-    lax.fori_loop(0, tokens // tall, multiply, 0)
-    edge_ref[step] = branch_ref[tokens - SUBLANES :, :]
+    ending = jnp.dot(
+        normed_ref[tokens - STEP :, :], input_ref[...], preferred_element_type=jnp.float32
+    )
+    edge_ref[step] = ending[STEP - SUBLANES :, :]
 
     def rim_copy(place):
         return pltpu.make_async_remote_copy(
@@ -702,6 +697,15 @@
         pl.semaphore_wait(barrier, 1)
 
     rim_copy(step).start()
+
+    def multiply(index, carry):
+        at = pl.ds(pl.multiple_of(index * tall, tall), tall)
+        normed = normed_ref[at, :]
+        branch_ref[at, :] = jnp.dot(normed, input_ref[...], preferred_element_type=jnp.float32)
+        pre_ref[at, :] = jnp.dot(normed, gate_ref[...], preferred_element_type=jnp.float32)
+        return carry
+
+    lax.fori_loop(0, tokens // tall, multiply, 0)
 
     @pl.when(step == steps - 1)
     def _():
@@ -939,8 +943,8 @@
     hidden_ref,
     dgate_ref,
     dup_ref,
-    gout_ref,
-    resid_ref,
+    gout_hbm,
+    resid_hbm,
     gain_ref,
     gate_ref,
     up_ref,
@@ -949,12 +953,26 @@
     dres_ref,
     total_ref,
     back_ref,
+    gout_ref,
+    resid_ref,
+    load_sem,
 ):
-    tall, model = hidden_ref.shape[0], gout_ref.shape[1]
+    tall, model = (hidden_ref.shape[0], gout_ref.shape[1])
     step, tile = (pl.program_id(0), pl.program_id(1))
     wide = 512
     contract = (((1,), (1,)), ((), ()))
     rows = pl.ds(pl.multiple_of(tile * tall, tall), tall)
+
+    def loads():
+        return (
+            pltpu.make_async_copy(gout_hbm, gout_ref, load_sem.at[0]),
+            pltpu.make_async_copy(resid_hbm, resid_ref, load_sem.at[1]),
+        )
+
+    @pl.when((step == 0) & (tile == 0))
+    def _():
+        for load in loads():
+            load.start()
 
     def products(own):
         forth = jnp.dot(hidden_ref[...], down_ref[:, own], preferred_element_type=jnp.float32)
@@ -970,7 +988,7 @@
         for first in range(0, model, wide):
             own = slice(first, first + wide)
             forth, back = products(own)
-            total_ref[rows, own] = resid_ref[rows, own] + forth
+            total_ref[rows, own] = forth
             back_ref[rows, own] = back
 
     @pl.when(step > 0)
@@ -981,6 +999,11 @@
             total_ref[rows, own] += forth
             back_ref[rows, own] += back
 
+    @pl.when((step == pl.num_programs(0) - 1) & (tile == 0))
+    def _():
+        for load in loads():
+            load.wait()
+
     @pl.when(step == pl.num_programs(0) - 1)
     def _():
         parts, width = (result_ref.shape[0], result_ref.shape[2])
@@ -988,10 +1011,10 @@
 
         def finish(index, carry):
             at = pl.ds(pl.multiple_of(tile * tall + index * small, small), small)
-            result = total_ref[at, :].astype(jnp.bfloat16)
+            resid = resid_ref[at, :]
+            result = (resid + total_ref[at, :]).astype(jnp.bfloat16)
             for part in range(parts):
                 result_ref[part, at, :] = result[:, part * width : (part + 1) * width]
-            resid = resid_ref[at, :]
             inverse = lax.rsqrt(jnp.mean(resid * resid, axis=1, keepdims=True) + EPS)
             normed = resid * inverse
             scaled = back_ref[at, :] * gain_ref[...]
@@ -1048,7 +1071,7 @@
     tokens, model = resid.shape
     ffn = mlp_gate.shape[1]
     low, f32 = (jnp.bfloat16, jnp.float32)
-    chunk, tall = (2 * MLP_CHUNK, min(tokens, 512))
+    chunk, tall = (1024, min(tokens, 512))
 
     def resident(shape):
         return pl.BlockSpec(shape, lambda s, t: (0,) * len(shape), pipeline_mode=pl.Buffered(1))
@@ -1064,8 +1087,8 @@
             made,
             made,
             made,
-            resident((tokens, model)),
-            resident((tokens, model)),
+            pl.BlockSpec(memory_space=pl.ANY),
+            pl.BlockSpec(memory_space=pl.ANY),
             resident((1, model)),
             columns,
             columns,
@@ -1076,7 +1099,13 @@
             jax.ShapeDtypeStruct(parts_shape, low),
             jax.ShapeDtypeStruct((tokens, model), low),
         ],
-        scratch_shapes=[pltpu.VMEM((tokens, model), f32), pltpu.VMEM((tokens, model), f32)],
+        scratch_shapes=[
+            pltpu.VMEM((tokens, model), f32),
+            pltpu.VMEM((tokens, model), f32),
+            pltpu.VMEM((tokens, model), low),
+            pltpu.VMEM((tokens, model), f32),
+            pltpu.SemaphoreType.DMA((2,)),
+        ],
         compiler_params=pltpu.CompilerParams(vmem_limit_bytes=VMEM_BYTES),
         cost_estimate=pl.CostEstimate(
             flops=6 * tokens * model * ffn,
@@ -1945,7 +1974,11 @@
     core = Recurrence(row_count, block_len, rec_width, head_size)
     wide_gates = core.widen(lru_gates)
     if tokens.shape[2] % LANES == 0:
-        blocks = [features_in(tokens, slice(row, row + 1)) for row in range(row_count)]
+        blocks = [features_in(tokens, slice(0, 1))]
+        later, wide_gates, params, dist = lax.optimization_barrier(
+            (tokens, wide_gates, params, dist)
+        )
+        blocks += [features_in(later, slice(row, row + 1)) for row in range(1, row_count)]
     else:
         side = features_in(tokens)
         blocks = [side[:, row * block_len : (row + 1) * block_len] for row in range(row_count)]
@@ -1955,10 +1988,6 @@
         block = blocks[row]
         if row:
             block, _ = lax.optimization_barrier((block, per_row[-1][-1]))
-        else:
-            block, wide_gates, params, dist = lax.optimization_barrier(
-                (block, wide_gates, params, dist)
-            )
         low_x, inverse, normed, branch, pre, rim = front(block, norm1_gain, recur_input, recur_gate)
         branch, rim = (branch[None], rim[None])
         scanned = single.forward(branch, rim, dist[row : row + 1], params, wide_gates)

time: 439 us -> 431 us (0.982)
  waiting for transfers between devices: 26.4 us -> 21.4 us
    all_to_all x3, waiting for transfers between devices: 26.3 us -> 21.3 us  [features_in(): lax.all_to_all(local, CHAN, 0, 0, tiled=True).reshape(count, -1, width)]
  transfers between devices with their start and end apart: 6 -> 6, of which waited for: 1 -> 1; matrix products, arithmetic and copies ran while one was open for 1% -> 2% of each run, Pallas kernels for 67% -> 68%
where the time goes in v11:
time: 431 us; the launch traced here: 430 us
  Pallas kernels  359 us (83%)
  waiting for transfers between devices  21.4 us (5%)
  starting transfers between devices  20.1 us (5%)
  between operations  14.4 us (3%)
  local copies, waits for them, and re-layouts  12 us (3%)
    pallas_call x1, Pallas kernels, tail(): pl.pallas_call(functools.partial(tail_kernel, corners, orders), name='tai...  101 us
    pallas_call x4, Pallas kernels, channel_call(): pl.pallas_call(kernel, name=name, grid=(blocks,), in_specs=specs, out_spe...  98.9 us
    pallas_call x1, Pallas kernels, block_gradients(): pl.pallas_call(grads_kernel, name='block_gradients', grid=(total + 1,), i...  34.6 us
    pallas_call x1, Pallas kernels, mlp_back(): pl.pallas_call(back_kernel, name='mlp_back', grid=(ffn // chunk, tokens /...  31.7 us
    pallas_call x1, Pallas kernels, mlp_hidden(): pl.pallas_call(hidden_kernel, name='mlp_hidden', grid=(ffn // MLP_CHUNK,)...  30.9 us
    pallas_call x2, Pallas kernels, front(): pl.pallas_call(front_kernel, name='norm_and_project', grid=(steps,), in_s...  25.6 us
    all_to_all x3, waiting for transfers between devices, features_in(): lax.all_to_all(local, CHAN, 0, 0, tiled=True).reshape(count, -1, width)  21.3 us
    pallas_call x1, Pallas kernels, middle(): pl.pallas_call(functools.partial(middle_kernel, rows), name='mix_and_norm...  18.9 us
  transfers between devices with their start and end apart: 6, of which 1 were waited for; matrix products, arithmetic and copies ran while one was open for 2% of the time, Pallas kernels for 68%

profile of v11, /device:TPU:0, one launch (start us, length us, event | category | flops | bytes accessed | tf_op | source)
XLA Modules:
  0.0 430.2 jit_solution(4451347302695850186)
XLA Ops:
  7.3 2.4 slice.16
  9.6 6.3 %all-to-all-start = ((bf16[8,1,512,128]{3,2,1,0:T(8,128)(2,1)}), bf16[8,1,512,128]{3,2,1,0:T(8,128)(2,1)}, u32[]{:S(2)}, u32[]{:S(2)}) async-start(bf16[8,1,512,128]{3,2,1,0:T(8,128)(2,1)} %slice.16), calls=%async_computation | async-start | bytes 2097152 | tf_op jit(solution)/shard_map/all_to_all | solution.py:1263
  16.3 1.3 concatenate.6.par_ref.refs_12_.refs_21_.refs_26_
  17.8 2.2 fusion.gates_ref.refs_22_.refs_27_
  21.4 21.3 %all-to-all-done = bf16[8,1,512,128]{3,2,1,0:T(8,128)(2,1)} async-done(((bf16[8,1,512,128]{3,2,1,0:T(8,128)(2,1)}), bf16[8,1,512,128]{3,2,1,0:T(8,128)(2,1)}, u32[]{:S(2)}, u32[]{:S(2)}) %all-to-all-start) | async-done | bytes 1048608 | tf_op jit(solution)/shard_map/all_to_all | solution.py:1263
  42.7 3.6 all-to-all-start.1
  47.0 13.1 %norm_and_project.2 = (bf16[512,1024]{1,0:T(8,128)(2,1)}, f32[512,128]{1,0:T(8,128)}, bf16[512,1024]{1,0:T(8,128)(2,1)}, f32[512,1536]{1,0:T(8,128)}, f32[512,1536]{1,0:T(8,128)}, /*index=5*/f32[8,1536]{1,0:T(8,128)}) custom-call(bf16[8,512,128]{2,1,0:T(8,128)(2,1)} %bitcast.1.parts_ref, f32[1,1024]{1,0:T(1,128)} %bitcast.59, bf16[1024,1536]{1,0:T(8,128)(2,1)} %input_ref.5, ...), custom_call_target="tpu_custom_call" | custom-call | flops 3221225472 | bytes 10485760 | tf_op jit(solution)/shard_map/norm_and_project/pallas_call | solution.py:731
  60.1 17.1 %recurrence_forward.2 = (bf16[1,512,1536]{2,1,0:T(8,128)(2,1)}, f32[1,512,1536]{2,1,0:T(8,128)}, f32[1,512,1536]{2,1,0:T(8,128)}, f32[1,512,1536]{2,1,0:T(8,128)...) custom-call(f32[1,512,1536]{2,1,0:T(8,128)} %bitcast.31, f32[1,8,1536]{2,1,0:T(8,128)} %bitcast.50, ...), custom_call_target="tpu_custom_call" | custom-call | flops 1207959552 | bytes 20082688 | tf_op jit(solution)/shard_map/recurrence_forward/pallas_call | solution.py:464
  78.2 5.0 %all-to-all-start.2 = ((bf16[8,2,512,128]{3,2,1,0:T(8,128)(2,1)}), bf16[8,2,512,128]{3,2,1,0:T(8,128)(2,1)S(1)}, u32[]{:S(2)}, u32[]{:S(2)}) async-start(bf16[8,2,512,128]{3,2,1,0:T(8,128)(2,1)} %bitcast.14), calls=%async_computation.2 | async-start | bytes 4194304 | tf_op jit(solution)/shard_map/all_to_all | solution.py:1263
  84.0 12.6 %norm_and_project.3 = (bf16[512,1024]{1,0:T(8,128)(2,1)}, f32[512,128]{1,0:T(8,128)}, bf16[512,1024]{1,0:T(8,128)(2,1)}, f32[512,1536]{1,0:T(8,128)}, f32[512,1536]{1,0:T(8,128)}, /*index=5*/f32[8,1536]{1,0:T(8,128)}) custom-call(bf16[8,512,128]{2,1,0:T(8,128)(2,1)} %bitcast.47, f32[1,1024]{1,0:T(1,128)} %bitcast.60, bf16[1024,1536]{1,0:T(8,128)(2,1)} %input_ref.5, ...), custom_call_target="tpu_custom_call" | custom-call | flops 3221225472 | bytes 10485760 | tf_op jit(solution)/shard_map/norm_and_project/pallas_call | solution.py:731
  96.6 17.0 %recurrence_forward.3 = (bf16[1,512,1536]{2,1,0:T(8,128)(2,1)}, f32[1,512,1536]{2,1,0:T(8,128)}, f32[1,512,1536]{2,1,0:T(8,128)}, f32[1,512,1536]{2,1,0:T(8,128)...) custom-call(f32[1,512,1536]{2,1,0:T(8,128)} %bitcast.34, f32[1,8,1536]{2,1,0:T(8,128)} %bitcast.53, ...), custom_call_target="tpu_custom_call" | custom-call | flops 1207959552 | bytes 20082688 | tf_op jit(solution)/shard_map/recurrence_forward/pallas_call | solution.py:464
  113.6 18.9 %mix_and_norm.1 = (f32[2,1,1536]{2,1,0:T(1,128)}, bf16[1024,1536]{1,0:T(8,128)(2,1)}, f32[1024,1024]{1,0:T(8,128)}, bf16[1024,1024]{1,0:T(8,128)(2,1)}) custom-call(f32[1,2,1536]{2,1,0:T(2,128)} %get-tuple-element.99.refs_0_.refs_3_.refs_8_, f32[1,2,1536]{2,1,0:T(2,128)} %get-tuple-element.104.refs_1_.refs_4_.refs_9_, ...), custom_call_target="tpu_custom_call" | custom-call | flops 3221225472 | bytes 22020096 | tf_op jit(solution)/shard_map/mix_and_norm/pallas_call | solution.py:848
  132.5 1.3 copy-done.5
  133.8 30.9 %mlp_hidden.1 = (bf16[1024,1024]{1,0:T(8,128)(2,1)}, bf16[1024,3072]{1,0:T(8,128)(2,1)}, bf16[1024,3072]{1,0:T(8,128)(2,1)}, bf16[1024,3072]{1,0:T(8,128)(2,1)}) custom-call(s32[2]{0:T(128)} %broadcast_subtract_fusion.1.left_ref, bf16[8,1024,128]{2,1,0:T(8,128)(2,1)} %bitcast.46, bf16[1024,1024]{1,0:T(8,128)(2,1)} %get-tuple-element.113.normed_ref, ...), custom_call_target="tpu_custom_call" | custom-call | flops 19327352832 | bytes 44040192 | tf_op jit(solution)/shard_map/mlp_hidden/pallas_call | solution.py:1049
  164.7 34.6 %block_gradients.1 = bf16[16,288,1024]{2,1,0:T(8,128)(2,1)} custom-call(bf16[1024,1024]{1,0:T(8,128)(2,1)} %get-tuple-element.113.normed_ref, bf16[1024,3072]{1,0:T(8,128)(2,1)} %get-tuple-element.117.dgate_ref, bf16[1024,3072]{1,0:T(8,128)(2,1)} %get-tuple-element.118.dup_ref, bf16[1024,3072]{1,0:T(8,128)(2,1)} %get-tuple-element.121.hidden_ref, ...), custom_call_target="tpu_custom_call" | custom-call | flops 19327352832 | bytes 32505856 | tf_op jit(solution)/shard_map/block_gradients/pallas_call | solution.py:1857
  199.4 31.7 %mlp_back.1 = (bf16[8,1024,128]{2,1,0:T(8,128)(2,1)}, bf16[1024,1024]{1,0:T(8,128)(2,1)}) custom-call(bf16[1024,3072]{1,0:T(8,128)(2,1)} %get-tuple-element.121.hidden_ref, bf16[1024,3072]{1,0:T(8,128)(2,1)} %get-tuple-element.117.dgate_ref, bf16[1024,3072]{1,0:T(8,128)(2,1)} %get-tuple-element.118.dup_ref, ...), custom_call_target="tpu_custom_call" | custom-call | flops 19327352832 | bytes 48234496 | tf_op jit(solution)/shard_map/mlp_back/pallas_call | solution.py:1082
  231.1 4.9 %all-to-all-start.3 = ((bf16[8,2,512,128]{3,2,1,0:T(8,128)(2,1)}), bf16[8,2,512,128]{3,2,1,0:T(8,128)(2,1)S(1)}, u32[]{:S(2)}, u32[]{:S(2)}) async-start(bf16[8,2,512,128]{3,2,1,0:T(8,128)(2,1)} %bitcast.45), calls=%async_computation.3 | async-start | bytes 4194304 | tf_op jit(solution)/shard_map/all_to_all | solution.py:1281
  236.0 26.4 %recurrence_adjoint.1 = (bf16[2,512,1536]{2,1,0:T(8,128)(2,1)}, f32[2,512,1536]{2,1,0:T(8,128)}, f32[2,512,1536]{2,1,0:T(8,128)}, f32[2,1,1536]{2,1,0:T(1,128)}) custom-call(bf16[1024,1024]{1,0:T(8,128)(2,1)} %get-tuple-element.125.refs_0_.dres_hbm, bf16[1536,1024]{1,0:T(8,128)(2,1)} %refs_1_.1, f32[1,512,1536]{2,1,0:T(8,128)} %bitcast.38, ...), custom_call_target="tpu_custom_call" | custom-call | flops 3221225472 | bytes 46784512 | tf_op jit(solution)/shard_map/recurrence_adjoint/pallas_call | solution.py:464
  262.4 38.3 %recurrence_backward.1 = (bf16[2,512,1536]{2,1,0:T(8,128)(2,1)}, f32[2,8,1536]{2,1,0:T(8,128)}, f32[2,8,1536]{2,1,0:T(8,128)}, bf16[1536,256]{1,0:T(8,128)(2,1)}, f32[2,1,1536]{2,1,0:T(1,128)}) custom-call(f32[2,512,1536]{2,1,0:T(8,128)} %get-tuple-element.129.refs_0_.refs_5_, f32[2,512,1536]{2,1,0:T(8,128)} %get-tuple-element.130.refs_1_.refs_6_, ...), custom_call_target="tpu_custom_call" | custom-call | flops 4831838208 | bytes 54456320 | tf_op jit(solution)/shard_map/recurrence_backward/pallas_call | solution.py:464
  300.8 14.5 %recurrence_backward_end.1 = (bf16[2,512,1536]{2,1,0:T(8,128)(2,1)}, f32[2,8,1536]{2,1,0:T(8,128)}, f32[2,8,1536]{2,1,0:T(8,128)}, bf16[1536,256]{1,0:T(8,128)(2,1)}) custom-call(f32[2,1,1536]{2,1,0:T(1,128)} %get-tuple-element.137.refs_0_, ...), custom_call_target="tpu_custom_call", output_to_operand_aliasing={{0}: (1, {}), {1}: (2, {}), {2}: (3, {}), {3}: (4, {})} | custom-call | flops 1207959552 | bytes 100663296 | tf_op jit(solution)/shard_map/recurrence_backward_end/pallas_call | solution.py:620
  315.3 101.4 %tail.1 = (bf16[16,512,128]{2,1,0:T(8,128)(2,1)}, f32[32,1536]{1,0:T(8,128)}, f32[48,1024]{1,0:T(8,128)}, f32[32,1536]{1,0:T(8,128)}, f32[48,256]{1,0:T(8,128)}) custom-call(bf16[1024,1536]{1,0:T(8,128)(2,1)} %bitcast.63, bf16[1024,1536]{1,0:T(8,128)(2,1)} %bitcast.42, f32[2,8,1536]{2,1,0:T(8,128)} %get-tuple-element.146.ending_ref, ...), custom_call_target="tpu_custom_call" | custom-call | flops 16106127360 | bytes 45088768 | tf_op jit(solution)/shard_map/tail/pallas_call | solution.py:1652
  416.7 3.0 outputs.1
  419.7 1.3 copy.54
  422.1 1.3 copy.55
  (51 shorter events, 5.5 us)
Async XLA Ops:
  7.2 10.6 %copy-start = (bf16[1536,192]{0,1:T(8,128)(2,1)S(1)}, bf16[1536,192]{0,1:T(8,128)(2,1)}, u32[]{:S(2)}) copy-start(bf16[1536,192]{0,1:T(8,128)(2,1)} %param.26) | copy-start | bytes 1769476
  7.2 8.8 %copy-start.12 = (s32[2]{0:T(128)S(1)}, s32[2]{0:T(128)}, u32[]{:S(2)}) copy-start(s32[2]{0:T(128)} %param.20) | copy-start | bytes 28
  7.2 8.8 %copy-start.10 = (f32[1536]{0:T(1024)S(1)}, f32[1536]{0:T(1024)}, u32[]{:S(2)}) copy-start(f32[1536]{0:T(1024)} %param.25) | copy-start | bytes 18436
  7.2 8.8 %copy-start.11 = (s32[2,8]{1,0:T(2,128)S(1)}, s32[2,8]{1,0:T(2,128)}, u32[]{:S(2)}) copy-start(s32[2,8]{1,0:T(2,128)} %param.19) | copy-start | bytes 196
  7.2 9.0 %copy-start.9 = (f32[1536]{0:T(1024)S(1)}, f32[1536]{0:T(1024)}, u32[]{:S(2)}) copy-start(f32[1536]{0:T(1024)} %param.28) | copy-start | bytes 18436
  7.2 9.1 %copy-start.8 = (f32[2,1536]{1,0:T(2,128)S(1)}, f32[2,1536]{1,0:T(2,128)}, u32[]{:S(2)}) copy-start(f32[2,1536]{1,0:T(2,128)} %param.27) | copy-start | bytes 36868
  7.2 9.1 %copy-start.7 = (f32[4,1536]{1,0:T(4,128)S(1)}, f32[4,1536]{1,0:T(4,128)}, u32[]{:S(2)}) copy-start(f32[4,1536]{1,0:T(4,128)} %param.24) | copy-start | bytes 73732
  9.6 33.0 %all-to-all-start = ((bf16[8,1,512,128]{3,2,1,0:T(8,128)(2,1)}), bf16[8,1,512,128]{3,2,1,0:T(8,128)(2,1)}, u32[]{:S(2)}, u32[]{:S(2)}) async-start(bf16[8,1,512,128]{3,2,1,0:T(8,128)(2,1)} %slice.16), calls=%async_computation | async-start | bytes 2097152 | tf_op jit(solution)/shard_map/all_to_all | solution.py:1263
  16.3 3.9 copy-start.3
  20.2 39.9 %copy-start.2 = (s32[2,512,128]{2,1,0:T(8,128)}, s32[2,512,128]{2,1,0:T(8,128)S(1)}, u32[]{:S(2)}) copy-start(s32[2,512,128]{2,1,0:T(8,128)S(1)} %broadcast_in_dim.85.refs_11_.refs_16_.refs_21_) | copy-start | bytes 1572868
  42.7 34.6 %all-to-all-start.1 = ((bf16[8,1,512,128]{3,2,1,0:T(8,128)(2,1)}), bf16[8,1,512,128]{3,2,1,0:T(8,128)(2,1)S(1)}, u32[]{:S(2)}, u32[]{:S(2)}) async-start(bf16[8,1,512,128]{3,2,1,0:T(8,128)(2,1)} %slice.17), calls=%async_computation.1 | async-start | bytes 2097152 | tf_op jit(solution)/shard_map/all_to_all | solution.py:1263
  77.2 1.0 copy-start.6
  78.2 54.3 %all-to-all-start.2 = ((bf16[8,2,512,128]{3,2,1,0:T(8,128)(2,1)}), bf16[8,2,512,128]{3,2,1,0:T(8,128)(2,1)S(1)}, u32[]{:S(2)}, u32[]{:S(2)}) async-start(bf16[8,2,512,128]{3,2,1,0:T(8,128)(2,1)} %bitcast.14), calls=%async_computation.2 | async-start | bytes 4194304 | tf_op jit(solution)/shard_map/all_to_all | solution.py:1263
  83.2 217.5 %reduce-scatter.3.cloned.1.call-start = ((), (), s32[]{:S(2)}) async-start(), calls=%async_computation.6 | async-start | bytes 11796480 | tf_op jit(solution)/shard_map/reduce_scatter | solution.py:2012
  132.5 1.3 copy-start.5
  231.1 84.2 %all-to-all-start.3 = ((bf16[8,2,512,128]{3,2,1,0:T(8,128)(2,1)}), bf16[8,2,512,128]{3,2,1,0:T(8,128)(2,1)S(1)}, u32[]{:S(2)}, u32[]{:S(2)}) async-start(bf16[8,2,512,128]{3,2,1,0:T(8,128)(2,1)} %bitcast.45), calls=%async_computation.3 | async-start | bytes 4194304 | tf_op jit(solution)/shard_map/all_to_all | solution.py:1281
  236.0 180.7 %reduce-scatter.5.cloned.1.call-start = ((), (), s32[]{:S(2)}) async-start(), calls=%async_computation.7 | async-start | bytes 2949120 | tf_op jit(solution)/shard_map/reduce_scatter | solution.py:2043
  419.7 2.3 copy-start.4
  419.7 3.7 copy-start.1
Sparse Core Ops, SparseCore 0:
  199.5 96.2 reduce-scatter.2
  300.9 66.9 reduce-scatter.4

commit v12 on v11

--- a/solution.py
+++ b/solution.py
@@ -65,7 +65,7 @@
     return found, refs
 
 
-def forward_kernel(
+def scan_block(
     branch_ref,
     rim_ref,
     dist_ref,
@@ -103,7 +103,7 @@
             lru_ref[row, pl.ds(base, STEP), :] = jnp.concatenate(pieces, axis=0).astype(jnp.bfloat16)
             return before
 
-        lax.fori_loop(0, length // STEP, conv_step, rim_ref[row])
+        lax.fori_loop(0, length // STEP, conv_step, rim_ref[row], unroll=2)
 
         piece = min(length, 256)
 
@@ -150,7 +150,9 @@
         return tuple(later)
 
     one, zero = (jnp.ones((1, width), jnp.float32), jnp.zeros((1, width), jnp.float32))
-    done = lax.fori_loop(0, length // span, scan_step, tuple((one, zero) for _ in range(rows)))
+    done = lax.fori_loop(
+        0, length // span, scan_step, tuple((one, zero) for _ in range(rows)), unroll=2
+    )
     for row in range(rows):
         for place in range(2):
             last_ref[row, place : place + 1, :] = done[row][place]
@@ -253,7 +255,7 @@
         return tuple(later)
 
     one, zero = (jnp.ones((1, width), jnp.float32), jnp.zeros((1, width), jnp.float32))
-    done = lax.fori_loop(0, last + 1, step, tuple((one, zero) for _ in range(rows)))
+    done = lax.fori_loop(0, last + 1, step, tuple((one, zero) for _ in range(rows)), unroll=2)
     for row in range(rows):
         first_ref[row] = done[row][1]
 
@@ -363,6 +365,7 @@
         length // STEP,
         gate_step,
         ((zeros, zeros, zeros), tuple(in_ref[row] for row in range(rows))),
+        unroll=2,
     )
     for slot, total in zip((5, 6, 7), (sums[1], sums[2], sums[0] * par_ref[8:9, :])):
         sums_ref[slot : slot + 1, :] = jnp.sum(total, axis=0, keepdims=True)
@@ -437,6 +440,7 @@
         length // STEP,
         conv_step,
         ((zeros,) * 5, tuple((zeros,) * 3 for _ in range(rows))),
+        unroll=2,
     )
     sums = list(sums)
     for row in range(rows):
@@ -516,21 +520,6 @@
         mine = (jnp.arange(self.channels) // size) % heads
         wide = jnp.dot(lru_gates, spread, preferred_element_type=jnp.float32)
         return jnp.where(mine[:, None] == owner[None, :], wide, 0.0).astype(jnp.bfloat16)
-
-    def forward(self, branch, rim, dist, params, gates):
-        f32 = jnp.float32
-        outs = [self.shape(self.length, d) for d in (jnp.bfloat16, f32, f32, f32, f32)]
-        return channel_call(
-            forward_kernel,
-            "recurrence_forward",
-            (branch, rim, dist, params, gates),
-            [self.tall(), self.short(SUBLANES), self.dist(), self.flat(16), self.gates(2 * self.width)],
-            outs + [self.shape(2, f32)],
-            [self.tall()] * 5 + [self.short(2)],
-            [pltpu.VMEM((self.rows, self.length, 2 * self.width), f32)],
-            self.blocks,
-            self.flops,
-        )
 
     def adjoint(self, dres, weight, pre, state, cum, entering, rate, dist, params):
         f32 = jnp.float32
@@ -643,20 +632,30 @@
     gain_ref,
     input_ref,
     gate_ref,
+    dist_ref,
+    par_ref,
+    gates_ref,
     x_ref,
     inverse_ref,
     normed_ref,
     branch_ref,
     pre_ref,
     rim_ref,
+    lru_ref,
+    rate_ref,
+    igate_ref,
+    state_ref,
+    cum_ref,
+    last_ref,
     edge_ref,
     landed_ref,
+    both_ref,
     send_sem,
     recv_sem,
 ):
     tokens = x_ref.shape[0]
     piece, tall = (64, min(tokens, 512))
-    step, steps = (pl.program_id(0), edge_ref.shape[0])
+    step = pl.program_id(0)
     seq, seqs = (lax.axis_index("seq"), lax.axis_size("seq"))
     barrier = pltpu.get_barrier_semaphore()
 
@@ -681,71 +680,89 @@
         normed_ref[tokens - STEP :, :], input_ref[...], preferred_element_type=jnp.float32
     )
     edge_ref[step] = ending[STEP - SUBLANES :, :]
-
-    def rim_copy(place):
-        return pltpu.make_async_remote_copy(
-            src_ref=edge_ref.at[place],
-            dst_ref=landed_ref.at[place],
-            send_sem=send_sem.at[place],
-            recv_sem=recv_sem.at[place],
-            device_id={"seq": lax.rem(seq + 1, seqs)},
-            device_id_type=MESH,
-        )
+    rim_copy = pltpu.make_async_remote_copy(
+        src_ref=edge_ref.at[step],
+        dst_ref=landed_ref.at[step],
+        send_sem=send_sem.at[step],
+        recv_sem=recv_sem.at[step],
+        device_id={"seq": lax.rem(seq + 1, seqs)},
+        device_id_type=MESH,
+    )
 
     @pl.when(step == 0)
     def _():
         pl.semaphore_wait(barrier, 1)
 
-    rim_copy(step).start()
+    rim_copy.start()
 
     def multiply(index, carry):
         at = pl.ds(pl.multiple_of(index * tall, tall), tall)
         normed = normed_ref[at, :]
-        branch_ref[at, :] = jnp.dot(normed, input_ref[...], preferred_element_type=jnp.float32)
-        pre_ref[at, :] = jnp.dot(normed, gate_ref[...], preferred_element_type=jnp.float32)
+        branch_ref[0, at, :] = jnp.dot(normed, input_ref[...], preferred_element_type=jnp.float32)
+        pre_ref[0, at, :] = jnp.dot(normed, gate_ref[...], preferred_element_type=jnp.float32)
         return carry
 
     lax.fori_loop(0, tokens // tall, multiply, 0)
-
-    @pl.when(step == steps - 1)
-    def _():
-        columns = edge_ref.shape[2]
-        live = jnp.where(seq > 0, 1.0, 0.0)
-        for place in range(steps):
-            rim_copy(place).wait()
-            rim_ref[:, place * columns : (place + 1) * columns] = live * landed_ref[place]
-
-
-def front(parts, gain, recur_input, recur_gate):
+    rim_copy.wait()
+    rim_ref[0] = jnp.where(seq > 0, 1.0, 0.0) * landed_ref[step]
+    scan_block(
+        branch_ref,
+        rim_ref,
+        dist_ref,
+        par_ref,
+        gates_ref,
+        lru_ref,
+        rate_ref,
+        igate_ref,
+        state_ref,
+        cum_ref,
+        last_ref,
+        both_ref,
+    )
+
+
+def front(parts, gain, recur_input, recur_gate, dist, params, gates):
     count, tokens, width = parts.shape
     model, rec = recur_input.shape
-    columns = 4 * LANES
+    columns = gates.shape[1] // 2
     steps = rec // columns
     low, f32 = (jnp.bfloat16, jnp.float32)
     tall = pl.BlockSpec((model, columns), lambda j: (0, j))
-    wide = pl.BlockSpec((tokens, columns), lambda j: (0, j))
 
     def whole(shape):
         return pl.BlockSpec(shape, lambda j: (0,) * len(shape))
 
+    def wide(size, dtype):
+        spec = pl.BlockSpec((1, size, columns), lambda j: (0, 0, j))
+        return (spec, jax.ShapeDtypeStruct((1, size, rec), dtype))
+
+    made = [wide(tokens, f32), wide(tokens, f32), wide(SUBLANES, f32), wide(tokens, low)]
+    made += [wide(tokens, f32)] * 4 + [wide(2, f32)]
     return pl.pallas_call(
         front_kernel,
-        name="norm_and_project",
+        name="project_and_scan",
         grid=(steps,),
-        in_specs=[whole(parts.shape), whole((1, model)), tall, tall],
-        out_specs=[whole((tokens, model)), whole((tokens, LANES)), whole((tokens, model)), wide, wide]
-        + [whole((SUBLANES, rec))],
+        in_specs=[
+            whole(parts.shape),
+            whole((1, model)),
+            tall,
+            tall,
+            whole(dist.shape),
+            pl.BlockSpec((16, columns), lambda j: (0, j)),
+            pl.BlockSpec((columns, 2 * columns), lambda j: (j, 0)),
+        ],
+        out_specs=[whole((tokens, model)), whole((tokens, LANES)), whole((tokens, model))]
+        + [spec for spec, _ in made],
         out_shape=[
             jax.ShapeDtypeStruct((tokens, model), low),
             jax.ShapeDtypeStruct((tokens, LANES), f32),
             jax.ShapeDtypeStruct((tokens, model), low),
-            jax.ShapeDtypeStruct((tokens, rec), f32),
-            jax.ShapeDtypeStruct((tokens, rec), f32),
-            jax.ShapeDtypeStruct((SUBLANES, rec), f32),
-        ],
+        ]
+        + [shape for _, shape in made],
         scratch_shapes=[
             pltpu.VMEM((steps, SUBLANES, columns), f32),
             pltpu.VMEM((steps, SUBLANES, columns), f32),
+            pltpu.VMEM((1, tokens, 2 * columns), f32),
             pltpu.SemaphoreType.DMA((steps,)),
             pltpu.SemaphoreType.DMA((steps,)),
         ],
@@ -753,9 +770,9 @@
             collective_id=3, has_side_effects=True, vmem_limit_bytes=VMEM_BYTES
         ),
         cost_estimate=pl.CostEstimate(
-            flops=4 * tokens * model * rec, bytes_accessed=20 * tokens * model, transcendentals=0
+            flops=5 * tokens * model * rec, bytes_accessed=40 * tokens * model, transcendentals=0
         ),
-    )(parts, gain[None], recur_input, recur_gate)
+    )(parts, gain[None], recur_input, recur_gate, dist, params, gates)
 
 
 def middle_kernel(rows, *refs):
@@ -1982,16 +1999,22 @@
     else:
         side = features_in(tokens)
         blocks = [side[:, row * block_len : (row + 1) * block_len] for row in range(row_count)]
-    single = Recurrence(1, block_len, rec_width, head_size)
     per_row = []
     for row in range(row_count):
         block = blocks[row]
         if row:
             block, _ = lax.optimization_barrier((block, per_row[-1][-1]))
-        low_x, inverse, normed, branch, pre, rim = front(block, norm1_gain, recur_input, recur_gate)
-        branch, rim = (branch[None], rim[None])
-        scanned = single.forward(branch, rim, dist[row : row + 1], params, wide_gates)
-        per_row.append((low_x, inverse, normed, branch, pre[None], rim, *scanned))
+        per_row.append(
+            front(
+                block,
+                norm1_gain,
+                recur_input,
+                recur_gate,
+                dist[row : row + 1],
+                params,
+                wide_gates,
+            )
+        )
     low_x, inverse, normed_low, branch, gate_pre, rim, lru_in, rate, igate, state, cum, last = zip(
         *per_row
     )

time: 431 us -> 434 us (level)
    pallas_call x2, Pallas kernels: 25.6 us -> 63.8 us  [front(): pl.pallas_call(front_kernel, name='project_and_scan', grid=(steps,), in_s...]
    pallas_call x4 -> x2, Pallas kernels: 98.9 us -> 63.1 us  [channel_call(): pl.pallas_call(kernel, name=name, grid=(blocks,), in_specs=specs, out_spe...]
where the time goes in v12:
time: 434 us; the launch traced here: 433 us
  Pallas kernels  362 us (83%)
  waiting for transfers between devices  21.4 us (5%)
  starting transfers between devices  20.1 us (5%)
  between operations  14.4 us (3%)
  local copies, waits for them, and re-layouts  12 us (3%)
    pallas_call x1, Pallas kernels, tail(): pl.pallas_call(functools.partial(tail_kernel, corners, orders), name='tai...  102 us
    pallas_call x2, Pallas kernels, front(): pl.pallas_call(front_kernel, name='project_and_scan', grid=(steps,), in_s...  63.8 us
    pallas_call x2, Pallas kernels, channel_call(): pl.pallas_call(kernel, name=name, grid=(blocks,), in_specs=specs, out_spe...  63.1 us
    pallas_call x1, Pallas kernels, block_gradients(): pl.pallas_call(grads_kernel, name='block_gradients', grid=(total + 1,), i...  34.7 us
    pallas_call x1, Pallas kernels, mlp_back(): pl.pallas_call(back_kernel, name='mlp_back', grid=(ffn // chunk, tokens /...  31.6 us
    pallas_call x1, Pallas kernels, mlp_hidden(): pl.pallas_call(hidden_kernel, name='mlp_hidden', grid=(ffn // MLP_CHUNK,)...  30.8 us
    all_to_all x3, waiting for transfers between devices, features_in(): lax.all_to_all(local, CHAN, 0, 0, tiled=True).reshape(count, -1, width)  21.3 us
    pallas_call x1, Pallas kernels, middle(): pl.pallas_call(functools.partial(middle_kernel, rows), name='mix_and_norm...  19.1 us
  transfers between devices with their start and end apart: 6, of which 1 were waited for; matrix products, arithmetic and copies ran while one was open for 2% of the time, Pallas kernels for 68%

profile of v12, /device:TPU:0, one launch (start us, length us, event | category | flops | bytes accessed | tf_op | source)
XLA Modules:
  0.0 433.2 jit_solution(1227641807178447799)
XLA Ops:
  7.3 2.4 slice.16
  9.6 6.3 %all-to-all-start = ((bf16[8,1,512,128]{3,2,1,0:T(8,128)(2,1)}), bf16[8,1,512,128]{3,2,1,0:T(8,128)(2,1)}, u32[]{:S(2)}, u32[]{:S(2)}) async-start(bf16[8,1,512,128]{3,2,1,0:T(8,128)(2,1)} %slice.16), calls=%async_computation | async-start | bytes 2097152 | tf_op jit(solution)/shard_map/all_to_all | solution.py:1280
  16.3 1.3 concatenate.6.par_ref.refs_12_.refs_21_.refs_26_
  17.8 2.2 fusion.gates_ref.refs_22_.refs_27_
  20.3 1.1 slice.17
  21.4 21.3 %all-to-all-done = bf16[8,1,512,128]{3,2,1,0:T(8,128)(2,1)} async-done(((bf16[8,1,512,128]{3,2,1,0:T(8,128)(2,1)}), bf16[8,1,512,128]{3,2,1,0:T(8,128)(2,1)}, u32[]{:S(2)}, u32[]{:S(2)}) %all-to-all-start) | async-done | bytes 1048608 | tf_op jit(solution)/shard_map/all_to_all | solution.py:1280
  42.7 3.6 all-to-all-start.1
  47.0 31.9 %project_and_scan.2 = (bf16[512,1024]{1,0:T(8,128)(2,1)}, f32[512,128]{1,0:T(8,128)}, bf16[512,1024]{1,0:T(8,128)(2,1)}, f32[1,512,1536]{2,1,0:T(8,128)}, f32[1,...) custom-call(bf16[8,512,128]{2,1,0:T(8,128)(2,1)} %bitcast.1.parts_re, ...), custom_call_target="tpu_custom_call" | custom-call | flops 4026531840 | bytes 20971520 | tf_op jit(solution)/shard_map/project_and_scan/pallas_call | solution.py:741
  80.0 5.0 %all-to-all-start.2 = ((bf16[8,2,512,128]{3,2,1,0:T(8,128)(2,1)}), bf16[8,2,512,128]{3,2,1,0:T(8,128)(2,1)S(1)}, u32[]{:S(2)}, u32[]{:S(2)}) async-start(bf16[8,2,512,128]{3,2,1,0:T(8,128)(2,1)} %bitcast.8), calls=%async_computation.2 | async-start | bytes 4194304 | tf_op jit(solution)/shard_map/all_to_all | solution.py:1280
  85.8 31.8 %project_and_scan.3 = (bf16[512,1024]{1,0:T(8,128)(2,1)}, f32[512,128]{1,0:T(8,128)}, bf16[512,1024]{1,0:T(8,128)(2,1)}, f32[1,512,1536]{2,1,0:T(8,128)}, f32[1,...) custom-call(bf16[8,512,128]{2,1,0:T(8,128)(2,1)} %bitcast.31, ...), custom_call_target="tpu_custom_call" | custom-call | flops 4026531840 | bytes 20971520 | tf_op jit(solution)/shard_map/project_and_scan/pallas_call | solution.py:741
  117.6 19.1 %mix_and_norm.1 = (f32[2,1,1536]{2,1,0:T(1,128)}, bf16[1024,1536]{1,0:T(8,128)(2,1)}, f32[1024,1024]{1,0:T(8,128)}, bf16[1024,1024]{1,0:T(8,128)(2,1)}) custom-call(f32[1,2,1536]{2,1,0:T(2,128)} %get-tuple-element.97.refs_0_.refs_3_.refs_8_, f32[1,2,1536]{2,1,0:T(2,128)} %get-tuple-element.100.refs_1_.refs_4_.refs_9_, ...), custom_call_target="tpu_custom_call" | custom-call | flops 3221225472 | bytes 22020096 | tf_op jit(solution)/shard_map/mix_and_norm/pallas_call | solution.py:865
  136.8 1.3 copy-done.5
  138.1 30.8 %mlp_hidden.1 = (bf16[1024,1024]{1,0:T(8,128)(2,1)}, bf16[1024,3072]{1,0:T(8,128)(2,1)}, bf16[1024,3072]{1,0:T(8,128)(2,1)}, bf16[1024,3072]{1,0:T(8,128)(2,1)}) custom-call(s32[2]{0:T(128)} %broadcast_subtract_fusion.1.left_ref, bf16[8,1024,128]{2,1,0:T(8,128)(2,1)} %bitcast.30, bf16[1024,1024]{1,0:T(8,128)(2,1)} %get-tuple-element.109.normed_ref, ...), custom_call_target="tpu_custom_call" | custom-call | flops 19327352832 | bytes 44040192 | tf_op jit(solution)/shard_map/mlp_hidden/pallas_call | solution.py:1066
  168.9 34.7 %block_gradients.1 = bf16[16,288,1024]{2,1,0:T(8,128)(2,1)} custom-call(bf16[1024,1024]{1,0:T(8,128)(2,1)} %get-tuple-element.109.normed_ref, bf16[1024,3072]{1,0:T(8,128)(2,1)} %get-tuple-element.113.dgate_ref, bf16[1024,3072]{1,0:T(8,128)(2,1)} %get-tuple-element.114.dup_ref, bf16[1024,3072]{1,0:T(8,128)(2,1)} %get-tuple-element.117.hidden_ref, ...), custom_call_target="tpu_custom_call" | custom-call | flops 19327352832 | bytes 32505856 | tf_op jit(solution)/shard_map/block_gradients/pallas_call | solution.py:1874
  203.6 31.6 %mlp_back.1 = (bf16[8,1024,128]{2,1,0:T(8,128)(2,1)}, bf16[1024,1024]{1,0:T(8,128)(2,1)}) custom-call(bf16[1024,3072]{1,0:T(8,128)(2,1)} %get-tuple-element.117.hidden_ref, bf16[1024,3072]{1,0:T(8,128)(2,1)} %get-tuple-element.113.dgate_ref, bf16[1024,3072]{1,0:T(8,128)(2,1)} %get-tuple-element.114.dup_ref, ...), custom_call_target="tpu_custom_call" | custom-call | flops 19327352832 | bytes 48234496 | tf_op jit(solution)/shard_map/mlp_back/pallas_call | solution.py:1099
  235.2 4.9 %all-to-all-start.3 = ((bf16[8,2,512,128]{3,2,1,0:T(8,128)(2,1)}), bf16[8,2,512,128]{3,2,1,0:T(8,128)(2,1)S(1)}, u32[]{:S(2)}, u32[]{:S(2)}) async-start(bf16[8,2,512,128]{3,2,1,0:T(8,128)(2,1)} %bitcast.29), calls=%async_computation.3 | async-start | bytes 4194304 | tf_op jit(solution)/shard_map/all_to_all | solution.py:1298
  240.2 25.7 %recurrence_adjoint.1 = (bf16[2,512,1536]{2,1,0:T(8,128)(2,1)}, f32[2,512,1536]{2,1,0:T(8,128)}, f32[2,512,1536]{2,1,0:T(8,128)}, f32[2,1,1536]{2,1,0:T(1,128)}) custom-call(bf16[1024,1024]{1,0:T(8,128)(2,1)} %get-tuple-element.121.refs_0_.dres_hbm, bf16[1536,1024]{1,0:T(8,128)(2,1)} %refs_1_.1, f32[1,512,1536]{2,1,0:T(8,128)} %get-tuple-element.105.refs_6_.refs_2_, ...), custom_call_target="tpu_custom_call" | custom-call | flops 3221225472 | bytes 46784512 | tf_op jit(solution)/shard_map/recurrence_adjoint/pallas_call | solution.py:468
  265.9 37.4 %recurrence_backward.1 = (bf16[2,512,1536]{2,1,0:T(8,128)(2,1)}, f32[2,8,1536]{2,1,0:T(8,128)}, f32[2,8,1536]{2,1,0:T(8,128)}, bf16[1536,256]{1,0:T(8,128)(2,1)}, f32[2,1,1536]{2,1,0:T(1,128)}) custom-call(f32[2,512,1536]{2,1,0:T(8,128)} %get-tuple-element.125.refs_0_.refs_5_, f32[2,512,1536]{2,1,0:T(8,128)} %get-tuple-element.126.refs_1_.refs_6_, ...), custom_call_target="tpu_custom_call" | custom-call | flops 4831838208 | bytes 54456320 | tf_op jit(solution)/shard_map/recurrence_backward/pallas_call | solution.py:468
  303.3 14.3 %recurrence_backward_end.1 = (bf16[2,512,1536]{2,1,0:T(8,128)(2,1)}, f32[2,8,1536]{2,1,0:T(8,128)}, f32[2,8,1536]{2,1,0:T(8,128)}, bf16[1536,256]{1,0:T(8,128)(2,1)}) custom-call(f32[2,1,1536]{2,1,0:T(1,128)} %get-tuple-element.137.refs_0_, ...), custom_call_target="tpu_custom_call", output_to_operand_aliasing={{0}: (1, {}), {1}: (2, {}), {2}: (3, {}), {3}: (4, {})} | custom-call | flops 1207959552 | bytes 100663296 | tf_op jit(solution)/shard_map/recurrence_backward_end/pallas_call | solution.py:609
  317.6 102.0 %tail.1 = (bf16[16,512,128]{2,1,0:T(8,128)(2,1)}, f32[32,1536]{1,0:T(8,128)}, f32[48,1024]{1,0:T(8,128)}, f32[32,1536]{1,0:T(8,128)}, f32[48,256]{1,0:T(8,128)}) custom-call(bf16[1024,1536]{1,0:T(8,128)(2,1)} %bitcast.41, bf16[1024,1536]{1,0:T(8,128)(2,1)} %bitcast.26, f32[2,8,1536]{2,1,0:T(8,128)} %get-tuple-element.146.ending_ref, ...), custom_call_target="tpu_custom_call" | custom-call | flops 16106127360 | bytes 45088768 | tf_op jit(solution)/shard_map/tail/pallas_call | solution.py:1669
  419.7 3.0 outputs.1
  422.7 1.3 copy.54
  424.0 1.0 copy-done.4
  425.0 1.3 copy.55
  (49 shorter events, 3.3 us)
Async XLA Ops:
  7.2 10.6 %copy-start = (bf16[1536,192]{0,1:T(8,128)(2,1)S(1)}, bf16[1536,192]{0,1:T(8,128)(2,1)}, u32[]{:S(2)}) copy-start(bf16[1536,192]{0,1:T(8,128)(2,1)} %param.26) | copy-start | bytes 1769476
  7.2 8.8 %copy-start.12 = (s32[2]{0:T(128)S(1)}, s32[2]{0:T(128)}, u32[]{:S(2)}) copy-start(s32[2]{0:T(128)} %param.20) | copy-start | bytes 28
  7.2 8.8 %copy-start.10 = (f32[1536]{0:T(1024)S(1)}, f32[1536]{0:T(1024)}, u32[]{:S(2)}) copy-start(f32[1536]{0:T(1024)} %param.25) | copy-start | bytes 18436
  7.2 8.8 %copy-start.11 = (s32[2,8]{1,0:T(2,128)S(1)}, s32[2,8]{1,0:T(2,128)}, u32[]{:S(2)}) copy-start(s32[2,8]{1,0:T(2,128)} %param.19) | copy-start | bytes 196
  7.2 9.0 %copy-start.9 = (f32[1536]{0:T(1024)S(1)}, f32[1536]{0:T(1024)}, u32[]{:S(2)}) copy-start(f32[1536]{0:T(1024)} %param.28) | copy-start | bytes 18436
  7.2 9.1 %copy-start.8 = (f32[2,1536]{1,0:T(2,128)S(1)}, f32[2,1536]{1,0:T(2,128)}, u32[]{:S(2)}) copy-start(f32[2,1536]{1,0:T(2,128)} %param.27) | copy-start | bytes 36868
  7.2 9.1 %copy-start.7 = (f32[4,1536]{1,0:T(4,128)S(1)}, f32[4,1536]{1,0:T(4,128)}, u32[]{:S(2)}) copy-start(f32[4,1536]{1,0:T(4,128)} %param.24) | copy-start | bytes 73732
  9.6 33.0 %all-to-all-start = ((bf16[8,1,512,128]{3,2,1,0:T(8,128)(2,1)}), bf16[8,1,512,128]{3,2,1,0:T(8,128)(2,1)}, u32[]{:S(2)}, u32[]{:S(2)}) async-start(bf16[8,1,512,128]{3,2,1,0:T(8,128)(2,1)} %slice.16), calls=%async_computation | async-start | bytes 2097152 | tf_op jit(solution)/shard_map/all_to_all | solution.py:1280
  16.3 3.9 copy-start.3
  20.2 58.8 %copy-start.2 = (s32[2,512,128]{2,1,0:T(8,128)}, s32[2,512,128]{2,1,0:T(8,128)S(1)}, u32[]{:S(2)}) copy-start(s32[2,512,128]{2,1,0:T(8,128)S(1)} %broadcast_in_dim.65.refs_11_.refs_16_.refs_21_) | copy-start | bytes 1572868
  42.7 36.4 %all-to-all-start.1 = ((bf16[8,1,512,128]{3,2,1,0:T(8,128)(2,1)}), bf16[8,1,512,128]{3,2,1,0:T(8,128)(2,1)S(1)}, u32[]{:S(2)}, u32[]{:S(2)}) async-start(bf16[8,1,512,128]{3,2,1,0:T(8,128)(2,1)} %slice.17), calls=%async_computation.1 | async-start | bytes 2097152 | tf_op jit(solution)/shard_map/all_to_all | solution.py:1280
  79.0 1.0 copy-start.6
  80.0 56.8 %all-to-all-start.2 = ((bf16[8,2,512,128]{3,2,1,0:T(8,128)(2,1)}), bf16[8,2,512,128]{3,2,1,0:T(8,128)(2,1)S(1)}, u32[]{:S(2)}, u32[]{:S(2)}) async-start(bf16[8,2,512,128]{3,2,1,0:T(8,128)(2,1)} %bitcast.8), calls=%async_computation.2 | async-start | bytes 4194304 | tf_op jit(solution)/shard_map/all_to_all | solution.py:1280
  85.0 218.3 %reduce-scatter.3.cloned.1.call-start = ((), (), s32[]{:S(2)}) async-start(), calls=%async_computation.6 | async-start | bytes 11796480 | tf_op jit(solution)/shard_map/reduce_scatter | solution.py:2035
  136.8 1.3 copy-start.5
  235.2 82.4 %all-to-all-start.3 = ((bf16[8,2,512,128]{3,2,1,0:T(8,128)(2,1)}), bf16[8,2,512,128]{3,2,1,0:T(8,128)(2,1)S(1)}, u32[]{:S(2)}, u32[]{:S(2)}) async-start(bf16[8,2,512,128]{3,2,1,0:T(8,128)(2,1)} %bitcast.29), calls=%async_computation.3 | async-start | bytes 4194304 | tf_op jit(solution)/shard_map/all_to_all | solution.py:1298
  240.1 179.6 %reduce-scatter.5.cloned.1.call-start = ((), (), s32[]{:S(2)}) async-start(), calls=%async_computation.7 | async-start | bytes 2949120 | tf_op jit(solution)/shard_map/reduce_scatter | solution.py:2066
  422.7 2.3 copy-start.4
  422.7 3.7 copy-start.1
Sparse Core Ops, SparseCore 0:
  203.7 96.3 reduce-scatter.2
  303.4 67.0 reduce-scatter.4

commit v13 on v12

--- a/solution.py
+++ b/solution.py
@@ -647,7 +647,6 @@
     state_ref,
     cum_ref,
     last_ref,
-    edge_ref,
     landed_ref,
     both_ref,
     send_sem,
@@ -676,15 +675,11 @@
 
         lax.fori_loop(0, tokens // piece, norm, 0, unroll=2)
 
-    ending = jnp.dot(
-        normed_ref[tokens - STEP :, :], input_ref[...], preferred_element_type=jnp.float32
-    )
-    edge_ref[step] = ending[STEP - SUBLANES :, :]
     rim_copy = pltpu.make_async_remote_copy(
-        src_ref=edge_ref.at[step],
-        dst_ref=landed_ref.at[step],
-        send_sem=send_sem.at[step],
-        recv_sem=recv_sem.at[step],
+        src_ref=normed_ref.at[tokens - STEP :],
+        dst_ref=landed_ref,
+        send_sem=send_sem,
+        recv_sem=recv_sem,
         device_id={"seq": lax.rem(seq + 1, seqs)},
         device_id_type=MESH,
     )
@@ -692,8 +687,7 @@
     @pl.when(step == 0)
     def _():
         pl.semaphore_wait(barrier, 1)
-
-    rim_copy.start()
+        rim_copy.start()
 
     def multiply(index, carry):
         at = pl.ds(pl.multiple_of(index * tall, tall), tall)
@@ -703,8 +697,13 @@
         return carry
 
     lax.fori_loop(0, tokens // tall, multiply, 0)
-    rim_copy.wait()
-    rim_ref[0] = jnp.where(seq > 0, 1.0, 0.0) * landed_ref[step]
+
+    @pl.when(step == 0)
+    def _():
+        rim_copy.wait()
+
+    before = jnp.dot(landed_ref[...], input_ref[...], preferred_element_type=jnp.float32)
+    rim_ref[0] = jnp.where(seq > 0, 1.0, 0.0) * before[STEP - SUBLANES :]
     scan_block(
         branch_ref,
         rim_ref,
@@ -760,11 +759,10 @@
         ]
         + [shape for _, shape in made],
         scratch_shapes=[
-            pltpu.VMEM((steps, SUBLANES, columns), f32),
-            pltpu.VMEM((steps, SUBLANES, columns), f32),
+            pltpu.VMEM((STEP, model), low),
             pltpu.VMEM((1, tokens, 2 * columns), f32),
-            pltpu.SemaphoreType.DMA((steps,)),
-            pltpu.SemaphoreType.DMA((steps,)),
+            pltpu.SemaphoreType.DMA,
+            pltpu.SemaphoreType.DMA,
         ],
         compiler_params=pltpu.CompilerParams(
             collective_id=3, has_side_effects=True, vmem_limit_bytes=VMEM_BYTES

time: 434 us -> 425 us (0.979)
  Pallas kernels: 362 us -> 354 us
    pallas_call x2, Pallas kernels: 63.8 us -> 55.3 us  [front(): pl.pallas_call(front_kernel, name='project_and_scan', grid=(steps,), in_s...]
  transfers between devices with their start and end apart: 6 -> 6, of which waited for: 1 -> 2; matrix products, arithmetic and copies ran while one was open for 2% -> 2% of each run, Pallas kernels for 68% -> 67%
where the time goes in v13:
time: 425 us
  Pallas kernels  354 us (83%)
  waiting for transfers between devices  23.2 us (5%)
  starting transfers between devices  18.7 us (4%)
  between operations  14.4 us (3%)
  local copies, waits for them, and re-layouts  12 us (3%)
    pallas_call x1, Pallas kernels, tail(): pl.pallas_call(functools.partial(tail_kernel, corners, orders), name='tai...  101 us
    pallas_call x2, Pallas kernels, channel_call(): pl.pallas_call(kernel, name=name, grid=(blocks,), in_specs=specs, out_spe...  63.8 us
    pallas_call x2, Pallas kernels, front(): pl.pallas_call(front_kernel, name='project_and_scan', grid=(steps,), in_s...  55.3 us
    pallas_call x1, Pallas kernels, block_gradients(): pl.pallas_call(grads_kernel, name='block_gradients', grid=(total + 1,), i...  34.7 us
    pallas_call x1, Pallas kernels, mlp_back(): pl.pallas_call(back_kernel, name='mlp_back', grid=(ffn // chunk, tokens /...  31.5 us
    pallas_call x1, Pallas kernels, mlp_hidden(): pl.pallas_call(hidden_kernel, name='mlp_hidden', grid=(ffn // MLP_CHUNK,)...  30.8 us
    all_to_all x3, waiting for transfers between devices, features_in(): lax.all_to_all(local, CHAN, 0, 0, tiled=True).reshape(count, -1, width)  23.2 us
    pallas_call x1, Pallas kernels, middle(): pl.pallas_call(functools.partial(middle_kernel, rows), name='mix_and_norm...  19 us
  transfers between devices with their start and end apart: 6, of which 2 were waited for; matrix products, arithmetic and copies ran while one was open for 2% of the time, Pallas kernels for 67%

profile of v13, /device:TPU:0, one launch (start us, length us, event | category | flops | bytes accessed | tf_op | source)
XLA Modules:
  0.0 424.9 jit_solution(14602855861580694642)
XLA Ops:
  7.3 2.4 slice.16
  9.6 6.3 %all-to-all-start = ((bf16[8,1,512,128]{3,2,1,0:T(8,128)(2,1)}), bf16[8,1,512,128]{3,2,1,0:T(8,128)(2,1)}, u32[]{:S(2)}, u32[]{:S(2)}) async-start(bf16[8,1,512,128]{3,2,1,0:T(8,128)(2,1)} %slice.16), calls=%async_computation | async-start | bytes 2097152 | tf_op jit(solution)/shard_map/all_to_all | solution.py:1278
  16.3 1.3 concatenate.6.par_ref.refs_12_.refs_21_.refs_26_
  17.8 2.2 fusion.gates_ref.refs_22_.refs_27_
  20.3 1.1 slice.17
  21.4 21.3 %all-to-all-done = bf16[8,1,512,128]{3,2,1,0:T(8,128)(2,1)} async-done(((bf16[8,1,512,128]{3,2,1,0:T(8,128)(2,1)}), bf16[8,1,512,128]{3,2,1,0:T(8,128)(2,1)}, u32[]{:S(2)}, u32[]{:S(2)}) %all-to-all-start) | async-done | bytes 1048608 | tf_op jit(solution)/shard_map/all_to_all | solution.py:1278
  42.7 3.6 all-to-all-start.1
  47.0 27.8 %project_and_scan.2 = (bf16[512,1024]{1,0:T(8,128)(2,1)}, f32[512,128]{1,0:T(8,128)}, bf16[512,1024]{1,0:T(8,128)(2,1)}, f32[1,512,1536]{2,1,0:T(8,128)}, f32[1,...) custom-call(bf16[8,512,128]{2,1,0:T(8,128)(2,1)} %bitcast.1.parts_re, ...), custom_call_target="tpu_custom_call" | custom-call | flops 4026531840 | bytes 20971520 | tf_op jit(solution)/shard_map/project_and_scan/pallas_call | solution.py:740
  75.9 5.0 %all-to-all-start.2 = ((bf16[8,2,512,128]{3,2,1,0:T(8,128)(2,1)}), bf16[8,2,512,128]{3,2,1,0:T(8,128)(2,1)S(1)}, u32[]{:S(2)}, u32[]{:S(2)}) async-start(bf16[8,2,512,128]{3,2,1,0:T(8,128)(2,1)} %bitcast.8), calls=%async_computation.2 | async-start | bytes 4194304 | tf_op jit(solution)/shard_map/all_to_all | solution.py:1278
  81.6 27.5 %project_and_scan.3 = (bf16[512,1024]{1,0:T(8,128)(2,1)}, f32[512,128]{1,0:T(8,128)}, bf16[512,1024]{1,0:T(8,128)(2,1)}, f32[1,512,1536]{2,1,0:T(8,128)}, f32[1,...) custom-call(bf16[8,512,128]{2,1,0:T(8,128)(2,1)} %bitcast.31, ...), custom_call_target="tpu_custom_call" | custom-call | flops 4026531840 | bytes 20971520 | tf_op jit(solution)/shard_map/project_and_scan/pallas_call | solution.py:740
  109.0 19.0 %mix_and_norm.1 = (f32[2,1,1536]{2,1,0:T(1,128)}, bf16[1024,1536]{1,0:T(8,128)(2,1)}, f32[1024,1024]{1,0:T(8,128)}, bf16[1024,1024]{1,0:T(8,128)(2,1)}) custom-call(f32[1,2,1536]{2,1,0:T(2,128)} %get-tuple-element.97.refs_0_.refs_3_.refs_8_, f32[1,2,1536]{2,1,0:T(2,128)} %get-tuple-element.100.refs_1_.refs_4_.refs_9_, ...), custom_call_target="tpu_custom_call" | custom-call | flops 3221225472 | bytes 22020096 | tf_op jit(solution)/shard_map/mix_and_norm/pallas_call | solution.py:863
  128.0 1.9 all-to-all-done.2
  129.9 1.3 copy-done.5
  131.2 30.8 %mlp_hidden.1 = (bf16[1024,1024]{1,0:T(8,128)(2,1)}, bf16[1024,3072]{1,0:T(8,128)(2,1)}, bf16[1024,3072]{1,0:T(8,128)(2,1)}, bf16[1024,3072]{1,0:T(8,128)(2,1)}) custom-call(s32[2]{0:T(128)} %broadcast_subtract_fusion.1.left_ref, bf16[8,1024,128]{2,1,0:T(8,128)(2,1)} %bitcast.30, bf16[1024,1024]{1,0:T(8,128)(2,1)} %get-tuple-element.109.normed_ref, ...), custom_call_target="tpu_custom_call" | custom-call | flops 19327352832 | bytes 44040192 | tf_op jit(solution)/shard_map/mlp_hidden/pallas_call | solution.py:1064
  162.0 34.7 %block_gradients.1 = bf16[16,288,1024]{2,1,0:T(8,128)(2,1)} custom-call(bf16[1024,1024]{1,0:T(8,128)(2,1)} %get-tuple-element.109.normed_ref, bf16[1024,3072]{1,0:T(8,128)(2,1)} %get-tuple-element.113.dgate_ref, bf16[1024,3072]{1,0:T(8,128)(2,1)} %get-tuple-element.114.dup_ref, bf16[1024,3072]{1,0:T(8,128)(2,1)} %get-tuple-element.117.hidden_ref, ...), custom_call_target="tpu_custom_call" | custom-call | flops 19327352832 | bytes 32505856 | tf_op jit(solution)/shard_map/block_gradients/pallas_call | solution.py:1872
  196.7 31.5 %mlp_back.1 = (bf16[8,1024,128]{2,1,0:T(8,128)(2,1)}, bf16[1024,1024]{1,0:T(8,128)(2,1)}) custom-call(bf16[1024,3072]{1,0:T(8,128)(2,1)} %get-tuple-element.117.hidden_ref, bf16[1024,3072]{1,0:T(8,128)(2,1)} %get-tuple-element.113.dgate_ref, bf16[1024,3072]{1,0:T(8,128)(2,1)} %get-tuple-element.114.dup_ref, ...), custom_call_target="tpu_custom_call" | custom-call | flops 19327352832 | bytes 48234496 | tf_op jit(solution)/shard_map/mlp_back/pallas_call | solution.py:1097
  228.3 3.6 all-to-all-start.3
  232.0 25.7 %recurrence_adjoint.1 = (bf16[2,512,1536]{2,1,0:T(8,128)(2,1)}, f32[2,512,1536]{2,1,0:T(8,128)}, f32[2,512,1536]{2,1,0:T(8,128)}, f32[2,1,1536]{2,1,0:T(1,128)}) custom-call(bf16[1024,1024]{1,0:T(8,128)(2,1)} %get-tuple-element.121.refs_0_.dres_hbm, bf16[1536,1024]{1,0:T(8,128)(2,1)} %refs_1_.1, f32[1,512,1536]{2,1,0:T(8,128)} %get-tuple-element.105.refs_6_.refs_2_, ...), custom_call_target="tpu_custom_call" | custom-call | flops 3221225472 | bytes 46784512 | tf_op jit(solution)/shard_map/recurrence_adjoint/pallas_call | solution.py:468
  257.7 38.1 %recurrence_backward.1 = (bf16[2,512,1536]{2,1,0:T(8,128)(2,1)}, f32[2,8,1536]{2,1,0:T(8,128)}, f32[2,8,1536]{2,1,0:T(8,128)}, bf16[1536,256]{1,0:T(8,128)(2,1)}, f32[2,1,1536]{2,1,0:T(1,128)}) custom-call(f32[2,512,1536]{2,1,0:T(8,128)} %get-tuple-element.125.refs_0_.refs_5_, f32[2,512,1536]{2,1,0:T(8,128)} %get-tuple-element.126.refs_1_.refs_6_, ...), custom_call_target="tpu_custom_call" | custom-call | flops 4831838208 | bytes 54456320 | tf_op jit(solution)/shard_map/recurrence_backward/pallas_call | solution.py:468
  295.8 14.3 %recurrence_backward_end.1 = (bf16[2,512,1536]{2,1,0:T(8,128)(2,1)}, f32[2,8,1536]{2,1,0:T(8,128)}, f32[2,8,1536]{2,1,0:T(8,128)}, bf16[1536,256]{1,0:T(8,128)(2,1)}) custom-call(f32[2,1,1536]{2,1,0:T(1,128)} %get-tuple-element.137.refs_0_, ...), custom_call_target="tpu_custom_call", output_to_operand_aliasing={{0}: (1, {}), {1}: (2, {}), {2}: (3, {}), {3}: (4, {})} | custom-call | flops 1207959552 | bytes 100663296 | tf_op jit(solution)/shard_map/recurrence_backward_end/pallas_call | solution.py:609
  310.1 101.2 %tail.1 = (bf16[16,512,128]{2,1,0:T(8,128)(2,1)}, f32[32,1536]{1,0:T(8,128)}, f32[48,1024]{1,0:T(8,128)}, f32[32,1536]{1,0:T(8,128)}, f32[48,256]{1,0:T(8,128)}) custom-call(bf16[1024,1536]{1,0:T(8,128)(2,1)} %bitcast.41, bf16[1024,1536]{1,0:T(8,128)(2,1)} %bitcast.26, f32[2,8,1536]{2,1,0:T(8,128)} %get-tuple-element.146.ending_ref, ...), custom_call_target="tpu_custom_call" | custom-call | flops 16106127360 | bytes 45088768 | tf_op jit(solution)/shard_map/tail/pallas_call | solution.py:1667
  411.3 3.0 outputs.1
  414.4 1.3 copy.54
  416.7 1.3 copy.55
  (49 shorter events, 4.3 us)
Async XLA Ops:
  7.2 10.6 %copy-start = (bf16[1536,192]{0,1:T(8,128)(2,1)S(1)}, bf16[1536,192]{0,1:T(8,128)(2,1)}, u32[]{:S(2)}) copy-start(bf16[1536,192]{0,1:T(8,128)(2,1)} %param.26) | copy-start | bytes 1769476
  7.2 8.8 %copy-start.12 = (s32[2]{0:T(128)S(1)}, s32[2]{0:T(128)}, u32[]{:S(2)}) copy-start(s32[2]{0:T(128)} %param.20) | copy-start | bytes 28
  7.2 8.8 %copy-start.10 = (f32[1536]{0:T(1024)S(1)}, f32[1536]{0:T(1024)}, u32[]{:S(2)}) copy-start(f32[1536]{0:T(1024)} %param.25) | copy-start | bytes 18436
  7.2 8.8 %copy-start.11 = (s32[2,8]{1,0:T(2,128)S(1)}, s32[2,8]{1,0:T(2,128)}, u32[]{:S(2)}) copy-start(s32[2,8]{1,0:T(2,128)} %param.19) | copy-start | bytes 196
  7.2 9.0 %copy-start.9 = (f32[1536]{0:T(1024)S(1)}, f32[1536]{0:T(1024)}, u32[]{:S(2)}) copy-start(f32[1536]{0:T(1024)} %param.28) | copy-start | bytes 18436
  7.2 9.1 %copy-start.8 = (f32[2,1536]{1,0:T(2,128)S(1)}, f32[2,1536]{1,0:T(2,128)}, u32[]{:S(2)}) copy-start(f32[2,1536]{1,0:T(2,128)} %param.27) | copy-start | bytes 36868
  7.2 9.1 %copy-start.7 = (f32[4,1536]{1,0:T(4,128)S(1)}, f32[4,1536]{1,0:T(4,128)}, u32[]{:S(2)}) copy-start(f32[4,1536]{1,0:T(4,128)} %param.24) | copy-start | bytes 73732
  9.6 33.0 %all-to-all-start = ((bf16[8,1,512,128]{3,2,1,0:T(8,128)(2,1)}), bf16[8,1,512,128]{3,2,1,0:T(8,128)(2,1)}, u32[]{:S(2)}, u32[]{:S(2)}) async-start(bf16[8,1,512,128]{3,2,1,0:T(8,128)(2,1)} %slice.16), calls=%async_computation | async-start | bytes 2097152 | tf_op jit(solution)/shard_map/all_to_all | solution.py:1278
  16.3 3.9 copy-start.3
  20.2 54.6 %copy-start.2 = (s32[2,512,128]{2,1,0:T(8,128)}, s32[2,512,128]{2,1,0:T(8,128)S(1)}, u32[]{:S(2)}) copy-start(s32[2,512,128]{2,1,0:T(8,128)S(1)} %broadcast_in_dim.65.refs_11_.refs_16_.refs_21_) | copy-start | bytes 1572868
  42.7 32.2 %all-to-all-start.1 = ((bf16[8,1,512,128]{3,2,1,0:T(8,128)(2,1)}), bf16[8,1,512,128]{3,2,1,0:T(8,128)(2,1)S(1)}, u32[]{:S(2)}, u32[]{:S(2)}) async-start(bf16[8,1,512,128]{3,2,1,0:T(8,128)(2,1)} %slice.17), calls=%async_computation.1 | async-start | bytes 2097152 | tf_op jit(solution)/shard_map/all_to_all | solution.py:1278
  74.9 1.0 copy-start.6
  75.9 54.0 %all-to-all-start.2 = ((bf16[8,2,512,128]{3,2,1,0:T(8,128)(2,1)}), bf16[8,2,512,128]{3,2,1,0:T(8,128)(2,1)S(1)}, u32[]{:S(2)}, u32[]{:S(2)}) async-start(bf16[8,2,512,128]{3,2,1,0:T(8,128)(2,1)} %bitcast.8), calls=%async_computation.2 | async-start | bytes 4194304 | tf_op jit(solution)/shard_map/all_to_all | solution.py:1278
  80.8 215.0 %reduce-scatter.3.cloned.1.call-start = ((), (), s32[]{:S(2)}) async-start(), calls=%async_computation.6 | async-start | bytes 11796480 | tf_op jit(solution)/shard_map/reduce_scatter | solution.py:2033
  129.9 1.3 copy-start.5
  228.3 81.9 %all-to-all-start.3 = ((bf16[8,2,512,128]{3,2,1,0:T(8,128)(2,1)}), bf16[8,2,512,128]{3,2,1,0:T(8,128)(2,1)S(1)}, u32[]{:S(2)}, u32[]{:S(2)}) async-start(bf16[8,2,512,128]{3,2,1,0:T(8,128)(2,1)} %bitcast.29), calls=%async_computation.3 | async-start | bytes 4194304 | tf_op jit(solution)/shard_map/all_to_all | solution.py:1296
  231.9 179.4 %reduce-scatter.5.cloned.1.call-start = ((), (), s32[]{:S(2)}) async-start(), calls=%async_computation.7 | async-start | bytes 2949120 | tf_op jit(solution)/shard_map/reduce_scatter | solution.py:2064
  414.3 2.3 copy-start.4
  414.3 3.7 copy-start.1
Sparse Core Ops, SparseCore 0:
  196.9 94.4 reduce-scatter.2
  295.9 66.1 reduce-scatter.4

commit v14 on v13

--- a/solution.py
+++ b/solution.py
@@ -951,7 +951,7 @@
             dup_ref[at, own] = (dhid * act).astype(jnp.bfloat16)
         return carry
 
-    lax.fori_loop(0, tokens // tall, tile, 0)
+    lax.fori_loop(0, tokens // tall, tile, 0, unroll=True)
 
 
 def back_kernel(
@@ -1512,6 +1512,7 @@
     width = parts.shape[2]
 
     def back_row(row):
+        tile = 512
         at_row = slice(row * length, (row + 1) * length)
 
         def product(index, carry):
@@ -1524,7 +1525,7 @@
             )
             return carry
 
-        lax.fori_loop(0, model // tile, product, 0)
+        lax.fori_loop(0, model // tile, product, 0, unroll=True)
         slab = 16
 
         def norm(index, carry):
@@ -1548,6 +1549,8 @@
     def weight_product(left, right, made, stream, first):
         columns = made.shape[-1]
         shape = made.shape[1:-1]
+
+        tile = columns
 
         def product(index, carry):
             at = pl.ds(pl.multiple_of(index * tile, tile), tile)
@@ -1715,7 +1718,6 @@
     hidden_ref,
     gout_ref,
     out_ref,
-    turned_ref,
     made_wide,
     made_down,
     come_wide,
@@ -1734,7 +1736,7 @@
 
     def exchange(made, come, index, slot):
         return pltpu.make_async_remote_copy(
-            src_ref=made.at[lax.rem(index, 2), 1 - core],
+            src_ref=made.at[lax.rem(index, 3), 1 - core],
             dst_ref=come.at[index],
             send_sem=send_sem.at[slot],
             recv_sem=recv_sem.at[slot],
@@ -1762,25 +1764,26 @@
         barrier = pltpu.get_barrier_semaphore()
         pl.semaphore_signal(barrier, inc=1, device_id=other, device_id_type=MESH)
         pl.semaphore_wait(barrier, 1)
-        turned_ref[...] = normed_ref[...].T
 
     def product_wide(source, index):
-        made = made_wide.at[lax.rem(index, 2)]
+        made = made_wide.at[lax.rem(index, 3)]
         chips, rows = (made.shape[1], made.shape[2])
         tile = 512
 
         def column(place, carry):
             at = pl.ds(pl.multiple_of(place * tile, tile), tile)
-            part = jnp.dot(turned_ref[...], source[:, at], preferred_element_type=jnp.float32)
+            part = lax.dot_general(
+                normed_ref[...], source[:, at], (((0,), (0,)), ((), ())), preferred_element_type=jnp.float32
+            )
             part = part.astype(jnp.bfloat16).reshape(chips, 2, rows, tile)
             made[0, :, :, at] = part[:, 0]
             made[1, :, :, at] = part[:, 1]
             return carry
 
-        lax.fori_loop(0, source.shape[1] // tile, column, 0)
+        lax.fori_loop(0, source.shape[1] // tile, column, 0, unroll=True)
 
     def product_tall(left, right, made_all, index):
-        made = made_all.at[lax.rem(index, 2)]
+        made = made_all.at[lax.rem(index, 3)]
         chips, rows = (made.shape[1], made.shape[2])
         tile = 512
 
@@ -1794,7 +1797,7 @@
             made[1, :, :, at] = part[:, 1]
             return carry
 
-        lax.fori_loop(0, right.shape[1] // tile, column, 0)
+        lax.fori_loop(0, right.shape[1] // tile, column, 0, unroll=True)
 
     half = wides // 2
 
@@ -1817,7 +1820,7 @@
 
     def finish(made, come, index, slot, store):
         exchange(made, come, index, slot).wait()
-        mine = made.at[lax.rem(index, 2), core]
+        mine = made.at[lax.rem(index, 3), core]
         arrived = come.at[index]
 
         def add(chip, carry):
@@ -1825,10 +1828,10 @@
             arrived[chip] = both.astype(jnp.bfloat16)
             return carry
 
-        lax.fori_loop(0, come.shape[1], add, 0)
+        lax.fori_loop(0, come.shape[1], add, 0, unroll=4)
         store(index).start()
 
-    before = step - 1
+    before = step - 2
 
     @pl.when((before >= 0) & (before < wides))
     def _():
@@ -1838,7 +1841,7 @@
     def _():
         finish(made_down, come_down, before - wides, before, store_down)
 
-    @pl.when(step == total)
+    @pl.when(step == total + 1)
     def _():
         for index in range(wides):
             store_wide(index).wait()
@@ -1872,7 +1875,7 @@
     return pl.pallas_call(
         grads_kernel,
         name="block_gradients",
-        grid=(total + 1,),
+        grid=(total + 2,),
         in_specs=[
             whole(normed),
             part(model, 0, half),
@@ -1883,9 +1886,8 @@
         out_specs=pl.BlockSpec(memory_space=pl.ANY),
         out_shape=jax.ShapeDtypeStruct((chips, rows, model), low),
         scratch_shapes=[
-            pltpu.VMEM((model, tokens), low),
-            pltpu.VMEM((2, 2, chips, wide_rows, model), low),
-            pltpu.VMEM((2, 2, down_chips, down_rows, model), low),
+            pltpu.VMEM((3, 2, chips, wide_rows, model), low),
+            pltpu.VMEM((3, 2, down_chips, down_rows, model), low),
             pltpu.VMEM((wides, chips, wide_rows, model), low),
             pltpu.VMEM((downs, down_chips, down_rows, model), low),
             pltpu.SemaphoreType.DMA((total,)),

time: 425 us -> 426 us (level)
  transfers between devices with their start and end apart: 6 -> 6, of which waited for: 2 -> 2; matrix products, arithmetic and copies ran while one was open for 2% -> 2% of each run, Pallas kernels for 67% -> 68%
where the time goes in v14:
time: 426 us; the launch traced here: 422 us
  Pallas kernels  350 us (82%)
  waiting for transfers between devices  22.9 us (5%)
  starting transfers between devices  19.1 us (4%)
  between operations  14.6 us (3%)
  local copies, waits for them, and re-layouts  12 us (3%)
    pallas_call x1, Pallas kernels, tail(): pl.pallas_call(functools.partial(tail_kernel, corners, orders), name='tai...  102 us
    pallas_call x2, Pallas kernels, channel_call(): pl.pallas_call(kernel, name=name, grid=(blocks,), in_specs=specs, out_spe...  63.5 us
    pallas_call x2, Pallas kernels, front(): pl.pallas_call(front_kernel, name='project_and_scan', grid=(steps,), in_s...  55.3 us
    pallas_call x1, Pallas kernels, block_gradients(): pl.pallas_call(grads_kernel, name='block_gradients', grid=(total + 2,), i...  32 us
    pallas_call x1, Pallas kernels, mlp_back(): pl.pallas_call(back_kernel, name='mlp_back', grid=(ffn // chunk, tokens /...  31.4 us
    pallas_call x1, Pallas kernels, mlp_hidden(): pl.pallas_call(hidden_kernel, name='mlp_hidden', grid=(ffn // MLP_CHUNK,)...  29.8 us
    all_to_all x3, waiting for transfers between devices, features_in(): lax.all_to_all(local, CHAN, 0, 0, tiled=True).reshape(count, -1, width)  22.8 us
    pallas_call x1, Pallas kernels, middle(): pl.pallas_call(functools.partial(middle_kernel, rows), name='mix_and_norm...  19 us
  transfers between devices with their start and end apart: 6, of which 2 were waited for; matrix products, arithmetic and copies ran while one was open for 2% of the time, Pallas kernels for 68%

profile of v14, /device:TPU:0, one launch (start us, length us, event | category | flops | bytes accessed | tf_op | source)
XLA Modules:
  0.0 422.0 jit_solution(883462079552975411)
XLA Ops:
  7.3 2.4 slice.16
  9.6 6.3 %all-to-all-start = ((bf16[8,1,512,128]{3,2,1,0:T(8,128)(2,1)}), bf16[8,1,512,128]{3,2,1,0:T(8,128)(2,1)}, u32[]{:S(2)}, u32[]{:S(2)}) async-start(bf16[8,1,512,128]{3,2,1,0:T(8,128)(2,1)} %slice.16), calls=%async_computation | async-start | bytes 2097152 | tf_op jit(solution)/shard_map/all_to_all | solution.py:1278
  16.3 1.3 concatenate.6.par_ref.refs_12_.refs_21_.refs_26_
  17.8 2.2 fusion.gates_ref.refs_22_.refs_27_
  20.3 1.1 slice.17
  21.4 21.3 %all-to-all-done = bf16[8,1,512,128]{3,2,1,0:T(8,128)(2,1)} async-done(((bf16[8,1,512,128]{3,2,1,0:T(8,128)(2,1)}), bf16[8,1,512,128]{3,2,1,0:T(8,128)(2,1)}, u32[]{:S(2)}, u32[]{:S(2)}) %all-to-all-start) | async-done | bytes 1048608 | tf_op jit(solution)/shard_map/all_to_all | solution.py:1278
  42.7 3.6 all-to-all-start.1
  47.0 27.8 %project_and_scan.2 = (bf16[512,1024]{1,0:T(8,128)(2,1)}, f32[512,128]{1,0:T(8,128)}, bf16[512,1024]{1,0:T(8,128)(2,1)}, f32[1,512,1536]{2,1,0:T(8,128)}, f32[1,...) custom-call(bf16[8,512,128]{2,1,0:T(8,128)(2,1)} %bitcast.1.parts_re, ...), custom_call_target="tpu_custom_call" | custom-call | flops 4026531840 | bytes 20971520 | tf_op jit(solution)/shard_map/project_and_scan/pallas_call | solution.py:740
  75.9 5.0 %all-to-all-start.2 = ((bf16[8,2,512,128]{3,2,1,0:T(8,128)(2,1)}), bf16[8,2,512,128]{3,2,1,0:T(8,128)(2,1)S(1)}, u32[]{:S(2)}, u32[]{:S(2)}) async-start(bf16[8,2,512,128]{3,2,1,0:T(8,128)(2,1)} %bitcast.8), calls=%async_computation.2 | async-start | bytes 4194304 | tf_op jit(solution)/shard_map/all_to_all | solution.py:1278
  81.9 27.5 %project_and_scan.3 = (bf16[512,1024]{1,0:T(8,128)(2,1)}, f32[512,128]{1,0:T(8,128)}, bf16[512,1024]{1,0:T(8,128)(2,1)}, f32[1,512,1536]{2,1,0:T(8,128)}, f32[1,...) custom-call(bf16[8,512,128]{2,1,0:T(8,128)(2,1)} %bitcast.31, ...), custom_call_target="tpu_custom_call" | custom-call | flops 4026531840 | bytes 20971520 | tf_op jit(solution)/shard_map/project_and_scan/pallas_call | solution.py:740
  109.4 19.0 %mix_and_norm.1 = (f32[2,1,1536]{2,1,0:T(1,128)}, bf16[1024,1536]{1,0:T(8,128)(2,1)}, f32[1024,1024]{1,0:T(8,128)}, bf16[1024,1024]{1,0:T(8,128)(2,1)}) custom-call(f32[1,2,1536]{2,1,0:T(2,128)} %get-tuple-element.97.refs_0_.refs_3_.refs_8_, f32[1,2,1536]{2,1,0:T(2,128)} %get-tuple-element.100.refs_1_.refs_4_.refs_9_, ...), custom_call_target="tpu_custom_call" | custom-call | flops 3221225472 | bytes 22020096 | tf_op jit(solution)/shard_map/mix_and_norm/pallas_call | solution.py:863
  128.4 1.5 all-to-all-done.2
  129.9 1.3 copy-done.5
  131.2 29.8 %mlp_hidden.1 = (bf16[1024,1024]{1,0:T(8,128)(2,1)}, bf16[1024,3072]{1,0:T(8,128)(2,1)}, bf16[1024,3072]{1,0:T(8,128)(2,1)}, bf16[1024,3072]{1,0:T(8,128)(2,1)}) custom-call(s32[2]{0:T(128)} %broadcast_subtract_fusion.1.left_ref, bf16[8,1024,128]{2,1,0:T(8,128)(2,1)} %bitcast.30, bf16[1024,1024]{1,0:T(8,128)(2,1)} %get-tuple-element.109.normed_ref, ...), custom_call_target="tpu_custom_call" | custom-call | flops 19327352832 | bytes 44040192 | tf_op jit(solution)/shard_map/mlp_hidden/pallas_call | solution.py:1064
  161.0 32.0 %block_gradients.1 = bf16[16,288,1024]{2,1,0:T(8,128)(2,1)} custom-call(bf16[1024,1024]{1,0:T(8,128)(2,1)} %get-tuple-element.109.normed_ref, bf16[1024,3072]{1,0:T(8,128)(2,1)} %get-tuple-element.113.dgate_ref, bf16[1024,3072]{1,0:T(8,128)(2,1)} %get-tuple-element.114.dup_ref, bf16[1024,3072]{1,0:T(8,128)(2,1)} %get-tuple-element.117.hidden_ref, ...), custom_call_target="tpu_custom_call" | custom-call | flops 19327352832 | bytes 32505856 | tf_op jit(solution)/shard_map/block_gradients/pallas_call | solution.py:1875
  193.0 31.4 %mlp_back.1 = (bf16[8,1024,128]{2,1,0:T(8,128)(2,1)}, bf16[1024,1024]{1,0:T(8,128)(2,1)}) custom-call(bf16[1024,3072]{1,0:T(8,128)(2,1)} %get-tuple-element.117.hidden_ref, bf16[1024,3072]{1,0:T(8,128)(2,1)} %get-tuple-element.113.dgate_ref, bf16[1024,3072]{1,0:T(8,128)(2,1)} %get-tuple-element.114.dup_ref, ...), custom_call_target="tpu_custom_call" | custom-call | flops 19327352832 | bytes 48234496 | tf_op jit(solution)/shard_map/mlp_back/pallas_call | solution.py:1097
  224.4 3.6 all-to-all-start.3
  228.1 25.9 %recurrence_adjoint.1 = (bf16[2,512,1536]{2,1,0:T(8,128)(2,1)}, f32[2,512,1536]{2,1,0:T(8,128)}, f32[2,512,1536]{2,1,0:T(8,128)}, f32[2,1,1536]{2,1,0:T(1,128)}) custom-call(bf16[1024,1024]{1,0:T(8,128)(2,1)} %get-tuple-element.121.refs_0_.dres_hbm, bf16[1536,1024]{1,0:T(8,128)(2,1)} %refs_1_.1, f32[1,512,1536]{2,1,0:T(8,128)} %get-tuple-element.105.refs_6_.refs_2_, ...), custom_call_target="tpu_custom_call" | custom-call | flops 3221225472 | bytes 46784512 | tf_op jit(solution)/shard_map/recurrence_adjoint/pallas_call | solution.py:468
  254.0 37.6 %recurrence_backward.1 = (bf16[2,512,1536]{2,1,0:T(8,128)(2,1)}, f32[2,8,1536]{2,1,0:T(8,128)}, f32[2,8,1536]{2,1,0:T(8,128)}, bf16[1536,256]{1,0:T(8,128)(2,1)}, f32[2,1,1536]{2,1,0:T(1,128)}) custom-call(f32[2,512,1536]{2,1,0:T(8,128)} %get-tuple-element.125.refs_0_.refs_5_, f32[2,512,1536]{2,1,0:T(8,128)} %get-tuple-element.126.refs_1_.refs_6_, ...), custom_call_target="tpu_custom_call" | custom-call | flops 4831838208 | bytes 54456320 | tf_op jit(solution)/shard_map/recurrence_backward/pallas_call | solution.py:468
  291.6 14.3 %recurrence_backward_end.1 = (bf16[2,512,1536]{2,1,0:T(8,128)(2,1)}, f32[2,8,1536]{2,1,0:T(8,128)}, f32[2,8,1536]{2,1,0:T(8,128)}, bf16[1536,256]{1,0:T(8,128)(2,1)}) custom-call(f32[2,1,1536]{2,1,0:T(1,128)} %get-tuple-element.137.refs_0_, ...), custom_call_target="tpu_custom_call", output_to_operand_aliasing={{0}: (1, {}), {1}: (2, {}), {2}: (3, {}), {3}: (4, {})} | custom-call | flops 1207959552 | bytes 100663296 | tf_op jit(solution)/shard_map/recurrence_backward_end/pallas_call | solution.py:609
  306.0 102.2 %tail.1 = (bf16[16,512,128]{2,1,0:T(8,128)(2,1)}, f32[32,1536]{1,0:T(8,128)}, f32[48,1024]{1,0:T(8,128)}, f32[32,1536]{1,0:T(8,128)}, f32[48,256]{1,0:T(8,128)}) custom-call(bf16[1024,1536]{1,0:T(8,128)(2,1)} %bitcast.41, bf16[1024,1536]{1,0:T(8,128)(2,1)} %bitcast.26, f32[2,8,1536]{2,1,0:T(8,128)} %get-tuple-element.146.ending_ref, ...), custom_call_target="tpu_custom_call" | custom-call | flops 16106127360 | bytes 45088768 | tf_op jit(solution)/shard_map/tail/pallas_call | solution.py:1670
  408.2 3.0 outputs.1
  411.2 1.3 copy.54
  413.5 1.3 copy.55
  (49 shorter events, 4.7 us)
Async XLA Ops:
  7.2 10.6 %copy-start = (bf16[1536,192]{0,1:T(8,128)(2,1)S(1)}, bf16[1536,192]{0,1:T(8,128)(2,1)}, u32[]{:S(2)}) copy-start(bf16[1536,192]{0,1:T(8,128)(2,1)} %param.26) | copy-start | bytes 1769476
  7.2 8.8 %copy-start.12 = (s32[2]{0:T(128)S(1)}, s32[2]{0:T(128)}, u32[]{:S(2)}) copy-start(s32[2]{0:T(128)} %param.20) | copy-start | bytes 28
  7.2 8.8 %copy-start.10 = (f32[1536]{0:T(1024)S(1)}, f32[1536]{0:T(1024)}, u32[]{:S(2)}) copy-start(f32[1536]{0:T(1024)} %param.25) | copy-start | bytes 18436
  7.2 8.8 %copy-start.11 = (s32[2,8]{1,0:T(2,128)S(1)}, s32[2,8]{1,0:T(2,128)}, u32[]{:S(2)}) copy-start(s32[2,8]{1,0:T(2,128)} %param.19) | copy-start | bytes 196
  7.2 9.0 %copy-start.9 = (f32[1536]{0:T(1024)S(1)}, f32[1536]{0:T(1024)}, u32[]{:S(2)}) copy-start(f32[1536]{0:T(1024)} %param.28) | copy-start | bytes 18436
  7.2 9.1 %copy-start.8 = (f32[2,1536]{1,0:T(2,128)S(1)}, f32[2,1536]{1,0:T(2,128)}, u32[]{:S(2)}) copy-start(f32[2,1536]{1,0:T(2,128)} %param.27) | copy-start | bytes 36868
  7.2 9.1 %copy-start.7 = (f32[4,1536]{1,0:T(4,128)S(1)}, f32[4,1536]{1,0:T(4,128)}, u32[]{:S(2)}) copy-start(f32[4,1536]{1,0:T(4,128)} %param.24) | copy-start | bytes 73732
  9.6 33.0 %all-to-all-start = ((bf16[8,1,512,128]{3,2,1,0:T(8,128)(2,1)}), bf16[8,1,512,128]{3,2,1,0:T(8,128)(2,1)}, u32[]{:S(2)}, u32[]{:S(2)}) async-start(bf16[8,1,512,128]{3,2,1,0:T(8,128)(2,1)} %slice.16), calls=%async_computation | async-start | bytes 2097152 | tf_op jit(solution)/shard_map/all_to_all | solution.py:1278
  16.3 3.9 copy-start.3
  20.2 54.6 %copy-start.2 = (s32[2,512,128]{2,1,0:T(8,128)}, s32[2,512,128]{2,1,0:T(8,128)S(1)}, u32[]{:S(2)}) copy-start(s32[2,512,128]{2,1,0:T(8,128)S(1)} %broadcast_in_dim.65.refs_11_.refs_16_.refs_21_) | copy-start | bytes 1572868
  42.7 32.2 %all-to-all-start.1 = ((bf16[8,1,512,128]{3,2,1,0:T(8,128)(2,1)}), bf16[8,1,512,128]{3,2,1,0:T(8,128)(2,1)S(1)}, u32[]{:S(2)}, u32[]{:S(2)}) async-start(bf16[8,1,512,128]{3,2,1,0:T(8,128)(2,1)} %slice.17), calls=%async_computation.1 | async-start | bytes 2097152 | tf_op jit(solution)/shard_map/all_to_all | solution.py:1278
  74.9 1.0 copy-start.6
  75.9 54.0 %all-to-all-start.2 = ((bf16[8,2,512,128]{3,2,1,0:T(8,128)(2,1)}), bf16[8,2,512,128]{3,2,1,0:T(8,128)(2,1)S(1)}, u32[]{:S(2)}, u32[]{:S(2)}) async-start(bf16[8,2,512,128]{3,2,1,0:T(8,128)(2,1)} %bitcast.8), calls=%async_computation.2 | async-start | bytes 4194304 | tf_op jit(solution)/shard_map/all_to_all | solution.py:1278
  80.8 210.8 %reduce-scatter.3.cloned.1.call-start = ((), (), s32[]{:S(2)}) async-start(), calls=%async_computation.6 | async-start | bytes 11796480 | tf_op jit(solution)/shard_map/reduce_scatter | solution.py:2035
  129.9 1.3 copy-start.5
  224.4 81.6 %all-to-all-start.3 = ((bf16[8,2,512,128]{3,2,1,0:T(8,128)(2,1)}), bf16[8,2,512,128]{3,2,1,0:T(8,128)(2,1)S(1)}, u32[]{:S(2)}, u32[]{:S(2)}) async-start(bf16[8,2,512,128]{3,2,1,0:T(8,128)(2,1)} %bitcast.29), calls=%async_computation.3 | async-start | bytes 4194304 | tf_op jit(solution)/shard_map/all_to_all | solution.py:1296
  228.0 180.2 %reduce-scatter.5.cloned.1.call-start = ((), (), s32[]{:S(2)}) async-start(), calls=%async_computation.7 | async-start | bytes 2949120 | tf_op jit(solution)/shard_map/reduce_scatter | solution.py:2066
  411.2 2.3 copy-start.4
  411.2 3.7 copy-start.1
Sparse Core Ops, SparseCore 0:
  193.1 95.0 reduce-scatter.2
  291.8 73.0 reduce-scatter.4

commit v15 on v14

--- a/solution.py
+++ b/solution.py
@@ -1512,7 +1512,6 @@
     width = parts.shape[2]
 
     def back_row(row):
-        tile = 512
         at_row = slice(row * length, (row + 1) * length)
 
         def product(index, carry):
@@ -1525,7 +1524,7 @@
             )
             return carry
 
-        lax.fori_loop(0, model // tile, product, 0, unroll=True)
+        lax.fori_loop(0, model // tile, product, 0)
         slab = 16
 
         def norm(index, carry):
@@ -1549,8 +1548,6 @@
     def weight_product(left, right, made, stream, first):
         columns = made.shape[-1]
         shape = made.shape[1:-1]
-
-        tile = columns
 
         def product(index, carry):
             at = pl.ds(pl.multiple_of(index * tile, tile), tile)

time: 426 us -> 426 us (level)
  no operation moved by 1% of the time
where the time goes in v15:
time: 426 us; the launch traced here: 422 us
  Pallas kernels  350 us (82%)
  waiting for transfers between devices  23.3 us (5%)
  starting transfers between devices  18.7 us (4%)
  between operations  14.8 us (3%)
  local copies, waits for them, and re-layouts  12 us (3%)
    pallas_call x1, Pallas kernels, tail(): pl.pallas_call(functools.partial(tail_kernel, corners, orders), name='tai...  101 us
    pallas_call x2, Pallas kernels, channel_call(): pl.pallas_call(kernel, name=name, grid=(blocks,), in_specs=specs, out_spe...  64 us
    pallas_call x2, Pallas kernels, front(): pl.pallas_call(front_kernel, name='project_and_scan', grid=(steps,), in_s...  55.3 us
    pallas_call x1, Pallas kernels, block_gradients(): pl.pallas_call(grads_kernel, name='block_gradients', grid=(total + 2,), i...  32 us
    pallas_call x1, Pallas kernels, mlp_back(): pl.pallas_call(back_kernel, name='mlp_back', grid=(ffn // chunk, tokens /...  31.3 us
    pallas_call x1, Pallas kernels, mlp_hidden(): pl.pallas_call(hidden_kernel, name='mlp_hidden', grid=(ffn // MLP_CHUNK,)...  29.8 us
    all_to_all x3, waiting for transfers between devices, features_in(): lax.all_to_all(local, CHAN, 0, 0, tiled=True).reshape(count, -1, width)  23.2 us
    pallas_call x1, Pallas kernels, middle(): pl.pallas_call(functools.partial(middle_kernel, rows), name='mix_and_norm...  19 us
  transfers between devices with their start and end apart: 6, of which 2 were waited for; matrix products, arithmetic and copies ran while one was open for 2% of the time, Pallas kernels for 68%

profile of v15, /device:TPU:0, one launch (start us, length us, event | category | flops | bytes accessed | tf_op | source)
XLA Modules:
  0.0 421.8 jit_solution(11448600008339840916)
XLA Ops:
  7.3 2.4 slice.16
  9.6 6.3 %all-to-all-start = ((bf16[8,1,512,128]{3,2,1,0:T(8,128)(2,1)}), bf16[8,1,512,128]{3,2,1,0:T(8,128)(2,1)}, u32[]{:S(2)}, u32[]{:S(2)}) async-start(bf16[8,1,512,128]{3,2,1,0:T(8,128)(2,1)} %slice.16), calls=%async_computation | async-start | bytes 2097152 | tf_op jit(solution)/shard_map/all_to_all | solution.py:1278
  16.3 1.3 concatenate.6.par_ref.refs_12_.refs_21_.refs_26_
  17.8 2.2 fusion.gates_ref.refs_22_.refs_27_
  20.3 1.1 slice.17
  21.4 21.3 %all-to-all-done = bf16[8,1,512,128]{3,2,1,0:T(8,128)(2,1)} async-done(((bf16[8,1,512,128]{3,2,1,0:T(8,128)(2,1)}), bf16[8,1,512,128]{3,2,1,0:T(8,128)(2,1)}, u32[]{:S(2)}, u32[]{:S(2)}) %all-to-all-start) | async-done | bytes 1048608 | tf_op jit(solution)/shard_map/all_to_all | solution.py:1278
  42.7 3.6 all-to-all-start.1
  47.0 27.8 %project_and_scan.2 = (bf16[512,1024]{1,0:T(8,128)(2,1)}, f32[512,128]{1,0:T(8,128)}, bf16[512,1024]{1,0:T(8,128)(2,1)}, f32[1,512,1536]{2,1,0:T(8,128)}, f32[1,...) custom-call(bf16[8,512,128]{2,1,0:T(8,128)(2,1)} %bitcast.1.parts_re, ...), custom_call_target="tpu_custom_call" | custom-call | flops 4026531840 | bytes 20971520 | tf_op jit(solution)/shard_map/project_and_scan/pallas_call | solution.py:740
  75.9 5.0 %all-to-all-start.2 = ((bf16[8,2,512,128]{3,2,1,0:T(8,128)(2,1)}), bf16[8,2,512,128]{3,2,1,0:T(8,128)(2,1)S(1)}, u32[]{:S(2)}, u32[]{:S(2)}) async-start(bf16[8,2,512,128]{3,2,1,0:T(8,128)(2,1)} %bitcast.8), calls=%async_computation.2 | async-start | bytes 4194304 | tf_op jit(solution)/shard_map/all_to_all | solution.py:1278
  81.6 27.5 %project_and_scan.3 = (bf16[512,1024]{1,0:T(8,128)(2,1)}, f32[512,128]{1,0:T(8,128)}, bf16[512,1024]{1,0:T(8,128)(2,1)}, f32[1,512,1536]{2,1,0:T(8,128)}, f32[1,...) custom-call(bf16[8,512,128]{2,1,0:T(8,128)(2,1)} %bitcast.31, ...), custom_call_target="tpu_custom_call" | custom-call | flops 4026531840 | bytes 20971520 | tf_op jit(solution)/shard_map/project_and_scan/pallas_call | solution.py:740
  109.0 19.0 %mix_and_norm.1 = (f32[2,1,1536]{2,1,0:T(1,128)}, bf16[1024,1536]{1,0:T(8,128)(2,1)}, f32[1024,1024]{1,0:T(8,128)}, bf16[1024,1024]{1,0:T(8,128)(2,1)}) custom-call(f32[1,2,1536]{2,1,0:T(2,128)} %get-tuple-element.97.refs_0_.refs_3_.refs_8_, f32[1,2,1536]{2,1,0:T(2,128)} %get-tuple-element.100.refs_1_.refs_4_.refs_9_, ...), custom_call_target="tpu_custom_call" | custom-call | flops 3221225472 | bytes 22020096 | tf_op jit(solution)/shard_map/mix_and_norm/pallas_call | solution.py:863
  128.0 1.9 all-to-all-done.2
  129.9 1.3 copy-done.5
  131.2 29.8 %mlp_hidden.1 = (bf16[1024,1024]{1,0:T(8,128)(2,1)}, bf16[1024,3072]{1,0:T(8,128)(2,1)}, bf16[1024,3072]{1,0:T(8,128)(2,1)}, bf16[1024,3072]{1,0:T(8,128)(2,1)}) custom-call(s32[2]{0:T(128)} %broadcast_subtract_fusion.1.left_ref, bf16[8,1024,128]{2,1,0:T(8,128)(2,1)} %bitcast.30, bf16[1024,1024]{1,0:T(8,128)(2,1)} %get-tuple-element.109.normed_ref, ...), custom_call_target="tpu_custom_call" | custom-call | flops 19327352832 | bytes 44040192 | tf_op jit(solution)/shard_map/mlp_hidden/pallas_call | solution.py:1064
  161.0 32.0 %block_gradients.1 = bf16[16,288,1024]{2,1,0:T(8,128)(2,1)} custom-call(bf16[1024,1024]{1,0:T(8,128)(2,1)} %get-tuple-element.109.normed_ref, bf16[1024,3072]{1,0:T(8,128)(2,1)} %get-tuple-element.113.dgate_ref, bf16[1024,3072]{1,0:T(8,128)(2,1)} %get-tuple-element.114.dup_ref, bf16[1024,3072]{1,0:T(8,128)(2,1)} %get-tuple-element.117.hidden_ref, ...), custom_call_target="tpu_custom_call" | custom-call | flops 19327352832 | bytes 32505856 | tf_op jit(solution)/shard_map/block_gradients/pallas_call | solution.py:1872
  193.0 31.3 %mlp_back.1 = (bf16[8,1024,128]{2,1,0:T(8,128)(2,1)}, bf16[1024,1024]{1,0:T(8,128)(2,1)}) custom-call(bf16[1024,3072]{1,0:T(8,128)(2,1)} %get-tuple-element.117.hidden_ref, bf16[1024,3072]{1,0:T(8,128)(2,1)} %get-tuple-element.113.dgate_ref, bf16[1024,3072]{1,0:T(8,128)(2,1)} %get-tuple-element.114.dup_ref, ...), custom_call_target="tpu_custom_call" | custom-call | flops 19327352832 | bytes 48234496 | tf_op jit(solution)/shard_map/mlp_back/pallas_call | solution.py:1097
  224.4 3.6 all-to-all-start.3
  228.0 26.0 %recurrence_adjoint.1 = (bf16[2,512,1536]{2,1,0:T(8,128)(2,1)}, f32[2,512,1536]{2,1,0:T(8,128)}, f32[2,512,1536]{2,1,0:T(8,128)}, f32[2,1,1536]{2,1,0:T(1,128)}) custom-call(bf16[1024,1024]{1,0:T(8,128)(2,1)} %get-tuple-element.121.refs_0_.dres_hbm, bf16[1536,1024]{1,0:T(8,128)(2,1)} %refs_1_.1, f32[1,512,1536]{2,1,0:T(8,128)} %get-tuple-element.105.refs_6_.refs_2_, ...), custom_call_target="tpu_custom_call" | custom-call | flops 3221225472 | bytes 46784512 | tf_op jit(solution)/shard_map/recurrence_adjoint/pallas_call | solution.py:468
  254.0 38.0 %recurrence_backward.1 = (bf16[2,512,1536]{2,1,0:T(8,128)(2,1)}, f32[2,8,1536]{2,1,0:T(8,128)}, f32[2,8,1536]{2,1,0:T(8,128)}, bf16[1536,256]{1,0:T(8,128)(2,1)}, f32[2,1,1536]{2,1,0:T(1,128)}) custom-call(f32[2,512,1536]{2,1,0:T(8,128)} %get-tuple-element.125.refs_0_.refs_5_, f32[2,512,1536]{2,1,0:T(8,128)} %get-tuple-element.126.refs_1_.refs_6_, ...), custom_call_target="tpu_custom_call" | custom-call | flops 4831838208 | bytes 54456320 | tf_op jit(solution)/shard_map/recurrence_backward/pallas_call | solution.py:468
  292.1 14.3 %recurrence_backward_end.1 = (bf16[2,512,1536]{2,1,0:T(8,128)(2,1)}, f32[2,8,1536]{2,1,0:T(8,128)}, f32[2,8,1536]{2,1,0:T(8,128)}, bf16[1536,256]{1,0:T(8,128)(2,1)}) custom-call(f32[2,1,1536]{2,1,0:T(1,128)} %get-tuple-element.137.refs_0_, ...), custom_call_target="tpu_custom_call", output_to_operand_aliasing={{0}: (1, {}), {1}: (2, {}), {2}: (3, {}), {3}: (4, {})} | custom-call | flops 1207959552 | bytes 100663296 | tf_op jit(solution)/shard_map/recurrence_backward_end/pallas_call | solution.py:609
  306.4 101.5 %tail.1 = (bf16[16,512,128]{2,1,0:T(8,128)(2,1)}, f32[32,1536]{1,0:T(8,128)}, f32[48,1024]{1,0:T(8,128)}, f32[32,1536]{1,0:T(8,128)}, f32[48,256]{1,0:T(8,128)}) custom-call(bf16[1024,1536]{1,0:T(8,128)(2,1)} %bitcast.41, bf16[1024,1536]{1,0:T(8,128)(2,1)} %bitcast.26, f32[2,8,1536]{2,1,0:T(8,128)} %get-tuple-element.146.ending_ref, ...), custom_call_target="tpu_custom_call" | custom-call | flops 16106127360 | bytes 45088768 | tf_op jit(solution)/shard_map/tail/pallas_call | solution.py:1667
  407.9 3.0 outputs.1
  410.9 1.3 copy.54
  413.2 1.3 copy.55
  (49 shorter events, 4.3 us)
Async XLA Ops:
  7.2 10.6 %copy-start = (bf16[1536,192]{0,1:T(8,128)(2,1)S(1)}, bf16[1536,192]{0,1:T(8,128)(2,1)}, u32[]{:S(2)}) copy-start(bf16[1536,192]{0,1:T(8,128)(2,1)} %param.26) | copy-start | bytes 1769476
  7.2 8.8 %copy-start.12 = (s32[2]{0:T(128)S(1)}, s32[2]{0:T(128)}, u32[]{:S(2)}) copy-start(s32[2]{0:T(128)} %param.20) | copy-start | bytes 28
  7.2 8.8 %copy-start.10 = (f32[1536]{0:T(1024)S(1)}, f32[1536]{0:T(1024)}, u32[]{:S(2)}) copy-start(f32[1536]{0:T(1024)} %param.25) | copy-start | bytes 18436
  7.2 8.8 %copy-start.11 = (s32[2,8]{1,0:T(2,128)S(1)}, s32[2,8]{1,0:T(2,128)}, u32[]{:S(2)}) copy-start(s32[2,8]{1,0:T(2,128)} %param.19) | copy-start | bytes 196
  7.2 9.0 %copy-start.9 = (f32[1536]{0:T(1024)S(1)}, f32[1536]{0:T(1024)}, u32[]{:S(2)}) copy-start(f32[1536]{0:T(1024)} %param.28) | copy-start | bytes 18436
  7.2 9.1 %copy-start.8 = (f32[2,1536]{1,0:T(2,128)S(1)}, f32[2,1536]{1,0:T(2,128)}, u32[]{:S(2)}) copy-start(f32[2,1536]{1,0:T(2,128)} %param.27) | copy-start | bytes 36868
  7.2 9.1 %copy-start.7 = (f32[4,1536]{1,0:T(4,128)S(1)}, f32[4,1536]{1,0:T(4,128)}, u32[]{:S(2)}) copy-start(f32[4,1536]{1,0:T(4,128)} %param.24) | copy-start | bytes 73732
  9.6 33.0 %all-to-all-start = ((bf16[8,1,512,128]{3,2,1,0:T(8,128)(2,1)}), bf16[8,1,512,128]{3,2,1,0:T(8,128)(2,1)}, u32[]{:S(2)}, u32[]{:S(2)}) async-start(bf16[8,1,512,128]{3,2,1,0:T(8,128)(2,1)} %slice.16), calls=%async_computation | async-start | bytes 2097152 | tf_op jit(solution)/shard_map/all_to_all | solution.py:1278
  16.3 3.9 copy-start.3
  20.2 54.6 %copy-start.2 = (s32[2,512,128]{2,1,0:T(8,128)}, s32[2,512,128]{2,1,0:T(8,128)S(1)}, u32[]{:S(2)}) copy-start(s32[2,512,128]{2,1,0:T(8,128)S(1)} %broadcast_in_dim.65.refs_11_.refs_16_.refs_21_) | copy-start | bytes 1572868
  42.7 32.2 %all-to-all-start.1 = ((bf16[8,1,512,128]{3,2,1,0:T(8,128)(2,1)}), bf16[8,1,512,128]{3,2,1,0:T(8,128)(2,1)S(1)}, u32[]{:S(2)}, u32[]{:S(2)}) async-start(bf16[8,1,512,128]{3,2,1,0:T(8,128)(2,1)} %slice.17), calls=%async_computation.1 | async-start | bytes 2097152 | tf_op jit(solution)/shard_map/all_to_all | solution.py:1278
  74.9 1.0 copy-start.6
  75.9 54.0 %all-to-all-start.2 = ((bf16[8,2,512,128]{3,2,1,0:T(8,128)(2,1)}), bf16[8,2,512,128]{3,2,1,0:T(8,128)(2,1)S(1)}, u32[]{:S(2)}, u32[]{:S(2)}) async-start(bf16[8,2,512,128]{3,2,1,0:T(8,128)(2,1)} %bitcast.8), calls=%async_computation.2 | async-start | bytes 4194304 | tf_op jit(solution)/shard_map/all_to_all | solution.py:1278
  80.8 211.2 %reduce-scatter.3.cloned.1.call-start = ((), (), s32[]{:S(2)}) async-start(), calls=%async_computation.6 | async-start | bytes 11796480 | tf_op jit(solution)/shard_map/reduce_scatter | solution.py:2032
  129.9 1.3 copy-start.5
  224.4 82.0 %all-to-all-start.3 = ((bf16[8,2,512,128]{3,2,1,0:T(8,128)(2,1)}), bf16[8,2,512,128]{3,2,1,0:T(8,128)(2,1)S(1)}, u32[]{:S(2)}, u32[]{:S(2)}) async-start(bf16[8,2,512,128]{3,2,1,0:T(8,128)(2,1)} %bitcast.29), calls=%async_computation.3 | async-start | bytes 4194304 | tf_op jit(solution)/shard_map/all_to_all | solution.py:1296
  228.0 179.9 %reduce-scatter.5.cloned.1.call-start = ((), (), s32[]{:S(2)}) async-start(), calls=%async_computation.7 | async-start | bytes 2949120 | tf_op jit(solution)/shard_map/reduce_scatter | solution.py:2063
  410.9 2.3 copy-start.4
  410.9 3.7 copy-start.1
Sparse Core Ops, SparseCore 0:
  193.2 94.6 reduce-scatter.2
  292.2 66.7 reduce-scatter.4

commit v16 on v15

--- a/solution.py
+++ b/solution.py
@@ -1512,7 +1512,7 @@
     width = parts.shape[2]
 
     def back_row(row):
-        at_row = slice(row * length, (row + 1) * length)
+        at_row = pl.ds(pl.multiple_of(row * length, length), length)
 
         def product(index, carry):
             at = pl.ds(pl.multiple_of(index * tile, tile), tile)
@@ -1598,35 +1598,52 @@
                 advance(stream, reached[stream])
                 reached[stream] += 1
 
-    def compute(item):
-        if item == "gate":
+    def pair(stream):
+        if stream == 4:
+            need("mixed", "dres")
+            left, right, made, slots, first = (mixed, dres, made_out, slots_out[0], 4)
+        elif stream == 0:
             need("normed", "dgate")
-            for stream in (0, 1):
-                weight_product(normed, dgate, made_in, stream, stream * half)
-                begin(stream)
-        elif item == "out":
-            need("mixed", "dres")
-            for stream in (4, 5):
-                weight_product(mixed, dres, made_out, stream - 4, (stream - 4) * half_out)
-                begin(stream)
-        elif item == "in":
+            left, right, made, slots, first = (normed, dgate, made_in, slots_in[0], 0)
+        else:
             need("normed", "dbranch")
-            for stream in (2, 3):
-                weight_product(normed, dbranch, made_in, stream, (stream - 2) * half)
-                begin(stream)
-        else:
-            need("dbranch", "dgate", "win", "wgate", "x", "inverse", "dres")
-            back_row(item)
+            left, right, made, slots, first = (normed, dbranch, made_in, slots_in[0], 0)
+        columns = made.shape[-1]
+        every = (slice(None),) * corners.count
+
+        def one(place, carry):
+            held = stream - first + place
+            weight_product(left, right, made, held, place * columns)
+            pltpu.make_async_remote_copy(
+                src_ref=made.at[(held,) + every + (1 - core,)],
+                dst_ref=slots.at[held],
+                send_sem=send_sem.at[stream + place, 0],
+                recv_sem=recv_sem.at[stream + place, 0],
+                device_id={"core": 1 - core},
+                device_id_type=MESH,
+            ).start()
+            return carry
+
+        lax.fori_loop(0, 2, one, 0)
+        reached[stream] = reached[stream + 1] = 0
+
+    def back_rows():
+        need("dbranch", "dgate", "win", "wgate", "x", "inverse", "dres")
+
+        def one(row, carry):
+            back_row(row)
+            return carry
+
+        lax.fori_loop(0, rows, one, 0)
 
     begin(6)
     fix_rim()
-    compute(0)
-    compute(1)
-    compute('gate')
+    back_rows()
+    pair(0)
     progress((6,))
-    compute('out')
+    pair(4)
     progress((0, 1))
-    compute('in')
+    pair(2)
     progress((0, 1))
     progress((4, 5))
     progress((6,))

time: 426 us -> 422 us (level)
  no operation moved by 1% of the time
where the time goes in v16:
time: 422 us; the launch traced here: 421 us
  Pallas kernels  350 us (83%)
  waiting for transfers between devices  23.2 us (5%)
  starting transfers between devices  18.7 us (4%)
  between operations  14.4 us (3%)
  local copies, waits for them, and re-layouts  12 us (3%)
    pallas_call x1, Pallas kernels, tail(): pl.pallas_call(functools.partial(tail_kernel, corners, orders), name='tai...  101 us
    pallas_call x2, Pallas kernels, channel_call(): pl.pallas_call(kernel, name=name, grid=(blocks,), in_specs=specs, out_spe...  64.1 us
    pallas_call x2, Pallas kernels, front(): pl.pallas_call(front_kernel, name='project_and_scan', grid=(steps,), in_s...  55.3 us
    pallas_call x1, Pallas kernels, block_gradients(): pl.pallas_call(grads_kernel, name='block_gradients', grid=(total + 2,), i...  32 us
    pallas_call x1, Pallas kernels, mlp_back(): pl.pallas_call(back_kernel, name='mlp_back', grid=(ffn // chunk, tokens /...  31.3 us
    pallas_call x1, Pallas kernels, mlp_hidden(): pl.pallas_call(hidden_kernel, name='mlp_hidden', grid=(ffn // MLP_CHUNK,)...  29.8 us
    all_to_all x3, waiting for transfers between devices, features_in(): lax.all_to_all(local, CHAN, 0, 0, tiled=True).reshape(count, -1, width)  23.2 us
    pallas_call x1, Pallas kernels, middle(): pl.pallas_call(functools.partial(middle_kernel, rows), name='mix_and_norm...  19 us
  transfers between devices with their start and end apart: 6, of which 2 were waited for; matrix products, arithmetic and copies ran while one was open for 2% of the time, Pallas kernels for 68%

profile of v16, /device:TPU:0, one launch (start us, length us, event | category | flops | bytes accessed | tf_op | source)
XLA Modules:
  0.0 421.2 jit_solution(6502089395311917946)
XLA Ops:
  7.3 2.4 slice.16
  9.6 6.3 %all-to-all-start = ((bf16[8,1,512,128]{3,2,1,0:T(8,128)(2,1)}), bf16[8,1,512,128]{3,2,1,0:T(8,128)(2,1)}, u32[]{:S(2)}, u32[]{:S(2)}) async-start(bf16[8,1,512,128]{3,2,1,0:T(8,128)(2,1)} %slice.16), calls=%async_computation | async-start | bytes 2097152 | tf_op jit(solution)/shard_map/all_to_all | solution.py:1278
  16.3 1.3 concatenate.6.par_ref.refs_12_.refs_21_.refs_26_
  17.8 2.2 fusion.gates_ref.refs_22_.refs_27_
  20.3 1.1 slice.17
  21.4 21.3 %all-to-all-done = bf16[8,1,512,128]{3,2,1,0:T(8,128)(2,1)} async-done(((bf16[8,1,512,128]{3,2,1,0:T(8,128)(2,1)}), bf16[8,1,512,128]{3,2,1,0:T(8,128)(2,1)}, u32[]{:S(2)}, u32[]{:S(2)}) %all-to-all-start) | async-done | bytes 1048608 | tf_op jit(solution)/shard_map/all_to_all | solution.py:1278
  42.7 3.6 all-to-all-start.1
  47.0 27.8 %project_and_scan.2 = (bf16[512,1024]{1,0:T(8,128)(2,1)}, f32[512,128]{1,0:T(8,128)}, bf16[512,1024]{1,0:T(8,128)(2,1)}, f32[1,512,1536]{2,1,0:T(8,128)}, f32[1,...) custom-call(bf16[8,512,128]{2,1,0:T(8,128)(2,1)} %bitcast.1.parts_re, ...), custom_call_target="tpu_custom_call" | custom-call | flops 4026531840 | bytes 20971520 | tf_op jit(solution)/shard_map/project_and_scan/pallas_call | solution.py:740
  75.9 5.0 %all-to-all-start.2 = ((bf16[8,2,512,128]{3,2,1,0:T(8,128)(2,1)}), bf16[8,2,512,128]{3,2,1,0:T(8,128)(2,1)S(1)}, u32[]{:S(2)}, u32[]{:S(2)}) async-start(bf16[8,2,512,128]{3,2,1,0:T(8,128)(2,1)} %bitcast.8), calls=%async_computation.2 | async-start | bytes 4194304 | tf_op jit(solution)/shard_map/all_to_all | solution.py:1278
  81.6 27.5 %project_and_scan.3 = (bf16[512,1024]{1,0:T(8,128)(2,1)}, f32[512,128]{1,0:T(8,128)}, bf16[512,1024]{1,0:T(8,128)(2,1)}, f32[1,512,1536]{2,1,0:T(8,128)}, f32[1,...) custom-call(bf16[8,512,128]{2,1,0:T(8,128)(2,1)} %bitcast.31, ...), custom_call_target="tpu_custom_call" | custom-call | flops 4026531840 | bytes 20971520 | tf_op jit(solution)/shard_map/project_and_scan/pallas_call | solution.py:740
  109.0 19.0 %mix_and_norm.1 = (f32[2,1,1536]{2,1,0:T(1,128)}, bf16[1024,1536]{1,0:T(8,128)(2,1)}, f32[1024,1024]{1,0:T(8,128)}, bf16[1024,1024]{1,0:T(8,128)(2,1)}) custom-call(f32[1,2,1536]{2,1,0:T(2,128)} %get-tuple-element.97.refs_0_.refs_3_.refs_8_, f32[1,2,1536]{2,1,0:T(2,128)} %get-tuple-element.100.refs_1_.refs_4_.refs_9_, ...), custom_call_target="tpu_custom_call" | custom-call | flops 3221225472 | bytes 22020096 | tf_op jit(solution)/shard_map/mix_and_norm/pallas_call | solution.py:863
  128.0 1.9 all-to-all-done.2
  129.9 1.3 copy-done.5
  131.2 29.8 %mlp_hidden.1 = (bf16[1024,1024]{1,0:T(8,128)(2,1)}, bf16[1024,3072]{1,0:T(8,128)(2,1)}, bf16[1024,3072]{1,0:T(8,128)(2,1)}, bf16[1024,3072]{1,0:T(8,128)(2,1)}) custom-call(s32[2]{0:T(128)} %broadcast_subtract_fusion.1.left_ref, bf16[8,1024,128]{2,1,0:T(8,128)(2,1)} %bitcast.30, bf16[1024,1024]{1,0:T(8,128)(2,1)} %get-tuple-element.109.normed_ref, ...), custom_call_target="tpu_custom_call" | custom-call | flops 19327352832 | bytes 44040192 | tf_op jit(solution)/shard_map/mlp_hidden/pallas_call | solution.py:1064
  161.0 32.0 %block_gradients.1 = bf16[16,288,1024]{2,1,0:T(8,128)(2,1)} custom-call(bf16[1024,1024]{1,0:T(8,128)(2,1)} %get-tuple-element.109.normed_ref, bf16[1024,3072]{1,0:T(8,128)(2,1)} %get-tuple-element.113.dgate_ref, bf16[1024,3072]{1,0:T(8,128)(2,1)} %get-tuple-element.114.dup_ref, bf16[1024,3072]{1,0:T(8,128)(2,1)} %get-tuple-element.117.hidden_ref, ...), custom_call_target="tpu_custom_call" | custom-call | flops 19327352832 | bytes 32505856 | tf_op jit(solution)/shard_map/block_gradients/pallas_call | solution.py:1889
  193.0 31.3 %mlp_back.1 = (bf16[8,1024,128]{2,1,0:T(8,128)(2,1)}, bf16[1024,1024]{1,0:T(8,128)(2,1)}) custom-call(bf16[1024,3072]{1,0:T(8,128)(2,1)} %get-tuple-element.117.hidden_ref, bf16[1024,3072]{1,0:T(8,128)(2,1)} %get-tuple-element.113.dgate_ref, bf16[1024,3072]{1,0:T(8,128)(2,1)} %get-tuple-element.114.dup_ref, ...), custom_call_target="tpu_custom_call" | custom-call | flops 19327352832 | bytes 48234496 | tf_op jit(solution)/shard_map/mlp_back/pallas_call | solution.py:1097
  224.4 3.6 all-to-all-start.3
  228.1 26.0 %recurrence_adjoint.1 = (bf16[2,512,1536]{2,1,0:T(8,128)(2,1)}, f32[2,512,1536]{2,1,0:T(8,128)}, f32[2,512,1536]{2,1,0:T(8,128)}, f32[2,1,1536]{2,1,0:T(1,128)}) custom-call(bf16[1024,1024]{1,0:T(8,128)(2,1)} %get-tuple-element.121.refs_0_.dres_hbm, bf16[1536,1024]{1,0:T(8,128)(2,1)} %refs_1_.1, f32[1,512,1536]{2,1,0:T(8,128)} %get-tuple-element.105.refs_6_.refs_2_, ...), custom_call_target="tpu_custom_call" | custom-call | flops 3221225472 | bytes 46784512 | tf_op jit(solution)/shard_map/recurrence_adjoint/pallas_call | solution.py:468
  254.1 38.1 %recurrence_backward.1 = (bf16[2,512,1536]{2,1,0:T(8,128)(2,1)}, f32[2,8,1536]{2,1,0:T(8,128)}, f32[2,8,1536]{2,1,0:T(8,128)}, bf16[1536,256]{1,0:T(8,128)(2,1)}, f32[2,1,1536]{2,1,0:T(1,128)}) custom-call(f32[2,512,1536]{2,1,0:T(8,128)} %get-tuple-element.125.refs_0_.refs_5_, f32[2,512,1536]{2,1,0:T(8,128)} %get-tuple-element.126.refs_1_.refs_6_, ...), custom_call_target="tpu_custom_call" | custom-call | flops 4831838208 | bytes 54456320 | tf_op jit(solution)/shard_map/recurrence_backward/pallas_call | solution.py:468
  292.2 14.3 %recurrence_backward_end.1 = (bf16[2,512,1536]{2,1,0:T(8,128)(2,1)}, f32[2,8,1536]{2,1,0:T(8,128)}, f32[2,8,1536]{2,1,0:T(8,128)}, bf16[1536,256]{1,0:T(8,128)(2,1)}) custom-call(f32[2,1,1536]{2,1,0:T(1,128)} %get-tuple-element.137.refs_0_, ...), custom_call_target="tpu_custom_call", output_to_operand_aliasing={{0}: (1, {}), {1}: (2, {}), {2}: (3, {}), {3}: (4, {})} | custom-call | flops 1207959552 | bytes 100663296 | tf_op jit(solution)/shard_map/recurrence_backward_end/pallas_call | solution.py:609
  306.5 101.1 %tail.1 = (bf16[16,512,128]{2,1,0:T(8,128)(2,1)}, f32[32,1536]{1,0:T(8,128)}, f32[48,1024]{1,0:T(8,128)}, f32[32,1536]{1,0:T(8,128)}, f32[48,256]{1,0:T(8,128)}) custom-call(bf16[1024,1536]{1,0:T(8,128)(2,1)} %bitcast.41, bf16[1024,1536]{1,0:T(8,128)(2,1)} %bitcast.26, f32[2,8,1536]{2,1,0:T(8,128)} %get-tuple-element.146.ending_ref, ...), custom_call_target="tpu_custom_call" | custom-call | flops 16106127360 | bytes 45088768 | tf_op jit(solution)/shard_map/tail/pallas_call | solution.py:1684
  407.7 3.0 outputs.1
  410.7 1.3 copy.54
  413.0 1.3 copy.55
  (49 shorter events, 4.3 us)
Async XLA Ops:
  7.2 10.6 %copy-start = (bf16[1536,192]{0,1:T(8,128)(2,1)S(1)}, bf16[1536,192]{0,1:T(8,128)(2,1)}, u32[]{:S(2)}) copy-start(bf16[1536,192]{0,1:T(8,128)(2,1)} %param.26) | copy-start | bytes 1769476
  7.2 8.8 %copy-start.12 = (s32[2]{0:T(128)S(1)}, s32[2]{0:T(128)}, u32[]{:S(2)}) copy-start(s32[2]{0:T(128)} %param.20) | copy-start | bytes 28
  7.2 8.8 %copy-start.10 = (f32[1536]{0:T(1024)S(1)}, f32[1536]{0:T(1024)}, u32[]{:S(2)}) copy-start(f32[1536]{0:T(1024)} %param.25) | copy-start | bytes 18436
  7.2 8.8 %copy-start.11 = (s32[2,8]{1,0:T(2,128)S(1)}, s32[2,8]{1,0:T(2,128)}, u32[]{:S(2)}) copy-start(s32[2,8]{1,0:T(2,128)} %param.19) | copy-start | bytes 196
  7.2 9.0 %copy-start.9 = (f32[1536]{0:T(1024)S(1)}, f32[1536]{0:T(1024)}, u32[]{:S(2)}) copy-start(f32[1536]{0:T(1024)} %param.28) | copy-start | bytes 18436
  7.2 9.1 %copy-start.8 = (f32[2,1536]{1,0:T(2,128)S(1)}, f32[2,1536]{1,0:T(2,128)}, u32[]{:S(2)}) copy-start(f32[2,1536]{1,0:T(2,128)} %param.27) | copy-start | bytes 36868
  7.2 9.1 %copy-start.7 = (f32[4,1536]{1,0:T(4,128)S(1)}, f32[4,1536]{1,0:T(4,128)}, u32[]{:S(2)}) copy-start(f32[4,1536]{1,0:T(4,128)} %param.24) | copy-start | bytes 73732
  9.6 33.0 %all-to-all-start = ((bf16[8,1,512,128]{3,2,1,0:T(8,128)(2,1)}), bf16[8,1,512,128]{3,2,1,0:T(8,128)(2,1)}, u32[]{:S(2)}, u32[]{:S(2)}) async-start(bf16[8,1,512,128]{3,2,1,0:T(8,128)(2,1)} %slice.16), calls=%async_computation | async-start | bytes 2097152 | tf_op jit(solution)/shard_map/all_to_all | solution.py:1278
  16.3 3.9 copy-start.3
  20.2 54.6 %copy-start.2 = (s32[2,512,128]{2,1,0:T(8,128)}, s32[2,512,128]{2,1,0:T(8,128)S(1)}, u32[]{:S(2)}) copy-start(s32[2,512,128]{2,1,0:T(8,128)S(1)} %broadcast_in_dim.65.refs_11_.refs_16_.refs_21_) | copy-start | bytes 1572868
  42.7 32.2 %all-to-all-start.1 = ((bf16[8,1,512,128]{3,2,1,0:T(8,128)(2,1)}), bf16[8,1,512,128]{3,2,1,0:T(8,128)(2,1)S(1)}, u32[]{:S(2)}, u32[]{:S(2)}) async-start(bf16[8,1,512,128]{3,2,1,0:T(8,128)(2,1)} %slice.17), calls=%async_computation.1 | async-start | bytes 2097152 | tf_op jit(solution)/shard_map/all_to_all | solution.py:1278
  74.9 1.0 copy-start.6
  75.9 54.0 %all-to-all-start.2 = ((bf16[8,2,512,128]{3,2,1,0:T(8,128)(2,1)}), bf16[8,2,512,128]{3,2,1,0:T(8,128)(2,1)S(1)}, u32[]{:S(2)}, u32[]{:S(2)}) async-start(bf16[8,2,512,128]{3,2,1,0:T(8,128)(2,1)} %bitcast.8), calls=%async_computation.2 | async-start | bytes 4194304 | tf_op jit(solution)/shard_map/all_to_all | solution.py:1278
  80.8 211.4 %reduce-scatter.3.cloned.1.call-start = ((), (), s32[]{:S(2)}) async-start(), calls=%async_computation.6 | async-start | bytes 11796480 | tf_op jit(solution)/shard_map/reduce_scatter | solution.py:2049
  129.9 1.3 copy-start.5
  224.4 82.2 %all-to-all-start.3 = ((bf16[8,2,512,128]{3,2,1,0:T(8,128)(2,1)}), bf16[8,2,512,128]{3,2,1,0:T(8,128)(2,1)S(1)}, u32[]{:S(2)}, u32[]{:S(2)}) async-start(bf16[8,2,512,128]{3,2,1,0:T(8,128)(2,1)} %bitcast.29), calls=%async_computation.3 | async-start | bytes 4194304 | tf_op jit(solution)/shard_map/all_to_all | solution.py:1296
  228.0 179.7 %reduce-scatter.5.cloned.1.call-start = ((), (), s32[]{:S(2)}) async-start(), calls=%async_computation.7 | async-start | bytes 2949120 | tf_op jit(solution)/shard_map/reduce_scatter | solution.py:2080
  410.7 2.3 copy-start.4
  410.7 3.7 copy-start.1
Sparse Core Ops, SparseCore 0:
  193.2 94.4 reduce-scatter.2
  292.3 66.3 reduce-scatter.4
